TPU v7x, 32 devices: a whole 2x2x4 slice. The times are simulated.
32 devices in a mesh: groups: 2 (over y), section: 2 (over x), band: 4 (over z), chan: 2 (over core).
Axes of the slice: x: 2, y: 2, z: 4, core: 2. Of those that a mesh axis runs over, the one named last changes fastest.
Arguments:
- latent: bfloat16 [16, 128, 640], P(('groups', 'band'), None, ('section', 'chan')), parts along dimension 0, may hold values from -6 to 6
- control_hint: bfloat16 [16, 128, 640], P(('groups', 'band'), None, ('section', 'chan')), parts along dimension 0, may hold values from -6 to 6
- control_weight_one: bfloat16 [3, 3, 640, 640], P(None, None, ('section', 'chan')), may hold values from -0.078125 to 0.078125
- control_bias_one: bfloat16 [640], P(('section', 'chan')), may hold values from -3 to 3
- control_weight_two: bfloat16 [3, 3, 640, 640], P(None, None, ('section', 'chan')), may hold values from -0.078125 to 0.078125
- control_bias_two: bfloat16 [640], P(('section', 'chan')), may hold values from -3 to 3
- main_weight_one: bfloat16 [3, 3, 640, 640], P(None, None, ('section', 'chan')), may hold values from -0.078125 to 0.078125
- main_bias_one: bfloat16 [640], P(('section', 'chan')), may hold values from -3 to 3
- main_weight_two: bfloat16 [3, 3, 640, 640], P(None, None, ('section', 'chan')), may hold values from -0.078125 to 0.078125
- main_bias_two: bfloat16 [640], P(('section', 'chan')), may hold values from -3 to 3
- decoder_weight_one: bfloat16 [3, 3, 640, 1280], P(None, None, ('section', 'chan')), may hold values from -0.0546875 to 0.0546875
- decoder_bias_one: bfloat16 [640], P(('section', 'chan')), may hold values from -3 to 3
- decoder_weight_two: bfloat16 [3, 3, 640, 1280], P(None, None, ('section', 'chan')), may hold values from -0.0546875 to 0.0546875
- decoder_bias_two: bfloat16 [640], P(('section', 'chan')), may hold values from -3 to 3
Outputs:
- decoded: bfloat16 [16, 128, 640], P(('groups', 'band'), None, ('section', 'chan')), parts along dimension 0
There are 2 independent parts, one for each index of `groups`. A program takes and returns all parts, laid end to end along the dimension named above; an argument that names none is the same for every part. Nothing has to cross between parts.
All inputs are finite; a program needn't handle non-finite values.
Results may differ from a plain program's by a relative error of at most 0.015.
Values may be sent and summed in bfloat16 or wider, within the bound.
No kernel may reach another device: no remote copies, remote signals or barrier semaphores. Data moves between devices by JAX's collectives and lax.ppermute only.
A program may use at most 64 MiB of HBM per device.

v0:
```python
import jax
import jax.numpy as jnp
from jax import lax
from jax.sharding import PartitionSpec as P

C = 640


def padded_2(cells, sides, width):
    for axis, dim in sides:
        count = lax.axis_size(axis)
        ends = count - 1
        head = lax.slice_in_dim(cells, 0, width, axis=dim)
        tail = lax.slice_in_dim(cells, cells.shape[dim] - width, cells.shape[dim], axis=dim)
        cells = jnp.concatenate(
            [
                lax.ppermute(tail, axis, [(i, (i + 1) % count) for i in range(ends)]),
                cells,
                lax.ppermute(head, axis, [((i + 1) % count, i) for i in range(ends)]),
            ],
            axis=dim,
        )
    return cells


def activate(state):
    value = state.astype(jnp.float32)
    return (value * jax.nn.sigmoid(value)).astype(jnp.bfloat16)


def add_taps(running, portion, anchor, weights):
    height = portion.shape[0] - 2
    breadth = portion.shape[1]
    depth = portion.shape[2]
    outputs = weights.shape[2]
    kernel = lax.dynamic_slice_in_dim(weights, anchor, depth, 3)
    kernel = jnp.transpose(kernel, (3, 0, 1, 2)).reshape(depth, 9 * outputs)
    product = jnp.dot(
        portion.reshape((height + 2) * breadth, depth), kernel, preferred_element_type=jnp.float32
    )
    product = product.reshape(height + 2, breadth, 9 * outputs)
    padded = jnp.pad(product, ((0, 0), (1, 1), (0, 0)))
    for row_step in range(3):
        for col_step in range(3):
            tap_index = row_step * 3 + col_step
            running = (
                running
                + padded[
                    row_step : row_step + height,
                    col_step : col_step + breadth,
                    tap_index * outputs : (tap_index + 1) * outputs,
                ]
            )
    return running


def convolve(activated, weights, skip_bordered):
    height, breadth = (activated.shape[0], activated.shape[1])
    outputs = weights.shape[2]
    empty = jnp.zeros((height, breadth, outputs), jnp.float32)
    bordered = padded_2(activated, (("band", 0),), 1)
    running = add_taps(
        empty,
        lax.all_gather(bordered, ("section", "chan"), axis=2, tiled=True),
        jnp.int32(0),
        weights,
    )
    if skip_bordered is not None:
        running = add_taps(running, skip_bordered, C, weights)
    return running


def residual_layer(state, weights, offset, skip_bordered):
    activated = activate(state)
    result = convolve(activated, weights, skip_bordered)
    total = state.astype(jnp.float32) + result + offset.astype(jnp.float32)
    return total.astype(jnp.bfloat16)


def per_device(
    latent,
    control_hint,
    control_weight_one,
    control_bias_one,
    control_weight_two,
    control_bias_two,
    main_weight_one,
    main_bias_one,
    main_weight_two,
    main_bias_two,
    decoder_weight_one,
    decoder_bias_one,
    decoder_weight_two,
    decoder_bias_two,
):
    control_input = (latent.astype(jnp.float32) + control_hint.astype(jnp.float32)).astype(
        jnp.bfloat16
    )
    control_mid = residual_layer(control_input, control_weight_one, control_bias_one, None)
    control_out = residual_layer(control_mid, control_weight_two, control_bias_two, None)
    main_mid = residual_layer(latent, main_weight_one, main_bias_one, None)
    main_out = residual_layer(main_mid, main_weight_two, main_bias_two, None)
    control_act = activate(control_out)
    skip_whole = lax.all_gather(control_act, ("section", "chan"), axis=2, tiled=True)
    skip_bordered = padded_2(skip_whole, (("band", 0),), 1)
    decoder_mid = residual_layer(main_out, decoder_weight_one, decoder_bias_one, skip_bordered)
    decoded = residual_layer(decoder_mid, decoder_weight_two, decoder_bias_two, skip_bordered)
    return decoded


def solution(mesh):
    placed = (
        P(("groups", "band"), None, ("section", "chan")),
        P(("groups", "band"), None, ("section", "chan")),
        P(None, None, ("section", "chan"), None),
        P(("section", "chan")),
        P(None, None, ("section", "chan"), None),
        P(("section", "chan")),
        P(None, None, ("section", "chan"), None),
        P(("section", "chan")),
        P(None, None, ("section", "chan"), None),
        P(("section", "chan")),
        P(None, None, ("section", "chan"), None),
        P(("section", "chan")),
        P(None, None, ("section", "chan"), None),
        P(("section", "chan")),
    )
    return jax.shard_map(
        per_device,
        mesh=mesh,
        in_specs=placed,
        out_specs=P(("groups", "band"), None, ("section", "chan")),
        check_vma=False,
    )
```

profile of v0, /device:TPU:0, one launch (start us, length us, event | category | flops | bytes accessed | tf_op | source)
XLA Modules:
  0.0 116.4 jit_solution(5973519125874029904)
XLA Ops:
  0.0 1.2 fusion.103
  1.2 5.0 %collective-permute-start = (bf16[1,128,160]{1,2,0:T(8,128)(2,1)S(1)}, bf16[1,128,160]{1,2,0:T(8,128)(2,1)S(1)}, u32[]{:S(2)}, u32[]{:S(2)}) collective-permute-start(bf16[1,128,160]{1,2,0:T(8,128)(2,1)S(1)} %get-tuple-element.27), channel_id=1, source_target_pairs={{0,2},{2,4},{4,6},{1,3},{3,5},{5,7},{8,10},{10,12},{12,14},{9,11},... | collective-permute-start | bytes 122888 | tf_op jit(solution)/shard_map/ppermute | solution.py:17
  6.1 1.3 %collective-permute-start.1 = (bf16[1,128,160]{1,2,0:T(8,128)(2,1)S(1)}, bf16[1,128,160]{1,2,0:T(8,128)(2,1)S(1)}, u32[]{:S(2)}, u32[]{:S(2)}) collective-permute-start(bf16[1,128,160]{1,2,0:T(8,128)(2,1)S(1)} %get-tuple-element.28), channel_id=1, source_target_pairs={{2,0},{4,2},{6,4},{3,1},{5,3},{7,5},{10,8},{12,10},{14,12},{11,9},... | collective-permute-start | bytes 122888 | tf_op jit(solution)/shard_map/ppermute | solution.py:19
  7.5 4.5 %collective-permute-start.6 = (bf16[1,128,160]{1,2,0:T(8,128)(2,1)S(1)}, bf16[1,128,160]{1,2,0:T(8,128)(2,1)S(1)}, u32[]{:S(2)}, u32[]{:S(2)}) collective-permute-start(bf16[1,128,160]{1,2,0:T(8,128)(2,1)S(1)} %get-tuple-element.33), channel_id=1, source_target_pairs={{0,2},{2,4},{4,6},{1,3},{3,5},{5,7},{8,10},{10,12},{12,14},{9,11},... | collective-permute-start | bytes 122888 | tf_op jit(solution)/shard_map/ppermute | solution.py:17
  12.0 0.0 copy-start.1
  12.0 1.6 %collective-permute-start.7 = (bf16[1,128,160]{1,2,0:T(8,128)(2,1)S(1)}, bf16[1,128,160]{1,2,0:T(8,128)(2,1)S(1)}, u32[]{:S(2)}, u32[]{:S(2)}) collective-permute-start(bf16[1,128,160]{1,2,0:T(8,128)(2,1)S(1)} %get-tuple-element.34), channel_id=1, source_target_pairs={{2,0},{4,2},{6,4},{3,1},{5,3},{7,5},{10,8},{12,10},{14,12},{11,9},... | collective-permute-start | bytes 122888 | tf_op jit(solution)/shard_map/ppermute | solution.py:19
  13.6 2.4 %fusion.112 = (bf16[3,3,160,640]{3,2,1,0:T(8,128)(2,1)S(1)}, bf16[3,3,160,640]{3,2,1,0:T(8,128)(2,1)S(1)}) fusion(bf16[3,3,160,1280]{3,2,1,0:T(8,128)(2,1)} %param.24), kind=kLoop, calls=%fused_computation.186 | loop fusion | bytes 7372800 | tf_op jit(solution)/shard_map/dynamic_slice | solution.py:36
  16.0 0.0 copy-start.7
  16.1 0.3 fusion.111
  16.4 0.3 copy-done.7
  16.7 0.0 copy-done.8
  16.7 0.0 copy-done.9
  16.7 0.0 copy-done.10
  16.7 0.0 copy-done.11
  16.7 0.0 copy-done.12
  16.7 1.4 %collective-permute-done.7 = bf16[1,128,160]{1,2,0:T(8,128)(2,1)S(1)} collective-permute-done((bf16[1,128,160]{1,2,0:T(8,128)(2,1)S(1)}, bf16[1,128,160]{1,2,0:T(8,128)(2,1)S(1)}, u32[]{:S(2)}, u32[]{:S(2)}) %collective-permute-start.7) | collective-permute-done | bytes 40992 | tf_op jit(solution)/shard_map/ppermute | solution.py:19
  18.2 7.9 %all_gather.24 = bf16[4,128,640]{1,2,0:T(8,128)(2,1)S(1)} all-gather(bf16[4,128,160]{1,2,0:T(8,128)(2,1)S(1)} %pad_maximum_fusion.3), channel_id=1, replica_groups=mesh['groups'=2,'section'=2,'band'=4,'chan'=2] {'section','chan'}, dimensions={2}, use_global_device_ids=true | all-gather | bytes 819200 | tf_op jit(solution)/shard_map/all_gather | solution.py:64
  26.1 8.0 %all_gather.21 = bf16[4,128,640]{1,2,0:T(8,128)(2,1)S(1)} all-gather(bf16[4,128,160]{1,2,0:T(8,128)(2,1)S(1)} %pad_maximum_fusion), channel_id=1, replica_groups=mesh['groups'=2,'section'=2,'band'=4,'chan'=2] {'section','chan'}, dimensions={2}, use_global_device_ids=true | all-gather | bytes 819200 | tf_op jit(solution)/shard_map/all_gather | solution.py:64
  34.1 1.3 %fusion.120 = f32[4,128,1440]{1,2,0:T(8,128)S(1)} fusion(bf16[640,1440,1]{0,1,2:T(8,128)(2,1)S(1)} %bitcast.56, bf16[4,128,640]{1,2,0:T(8,128)(2,1)S(1)} %all_gather.21), kind=kOutput, calls=%fused_computation.194 | convolution fusion | flops 943718400 | bytes 5447680 | tf_op jit(solution)/shard_map/dot_general | solution.py:38
  35.5 0.2 copy-done.4
  35.6 1.3 %fusion.123 = f32[4,128,1440]{1,2,0:T(8,128)S(1)} fusion(bf16[640,1440,1]{0,1,2:T(8,128)(2,1)S(1)} %bitcast.61, bf16[4,128,640]{1,2,0:T(8,128)(2,1)S(1)} %all_gather.24), kind=kOutput, calls=%fused_computation.197 | convolution fusion | flops 943718400 | bytes 5447680 | tf_op jit(solution)/shard_map/dot_general | solution.py:38
  37.0 0.6 fusion.73
  37.6 3.5 %collective-permute-start.8 = (bf16[1,128,160]{1,2,0:T(8,128)(2,1)S(1)}, bf16[1,128,160]{1,2,0:T(8,128)(2,1)S(1)}, u32[]{:S(2)}, u32[]{:S(2)}) collective-permute-start(bf16[1,128,160]{1,2,0:T(8,128)(2,1)S(1)} %get-tuple-element.31), channel_id=1, source_target_pairs={{0,2},{2,4},{4,6},{1,3},{3,5},{5,7},{8,10},{10,12},{12,14},{9,11},... | collective-permute-start | bytes 122888 | tf_op jit(solution)/shard_map/ppermute | solution.py:17
  41.1 1.3 %collective-permute-start.9 = (bf16[1,128,160]{1,2,0:T(8,128)(2,1)S(1)}, bf16[1,128,160]{1,2,0:T(8,128)(2,1)S(1)}, u32[]{:S(2)}, u32[]{:S(2)}) collective-permute-start(bf16[1,128,160]{1,2,0:T(8,128)(2,1)S(1)} %get-tuple-element.32), channel_id=1, source_target_pairs={{2,0},{4,2},{6,4},{3,1},{5,3},{7,5},{10,8},{12,10},{14,12},{11,9},... | collective-permute-start | bytes 122888 | tf_op jit(solution)/shard_map/ppermute | solution.py:19
  42.5 4.5 %collective-permute-start.2 = (bf16[1,128,160]{1,2,0:T(8,128)(2,1)S(1)}, bf16[1,128,160]{1,2,0:T(8,128)(2,1)S(1)}, u32[]{:S(2)}, u32[]{:S(2)}) collective-permute-start(bf16[1,128,160]{1,2,0:T(8,128)(2,1)S(1)} %get-tuple-element.23), channel_id=1, source_target_pairs={{0,2},{2,4},{4,6},{1,3},{3,5},{5,7},{8,10},{10,12},{12,14},{9,11},... | collective-permute-start | bytes 122888 | tf_op jit(solution)/shard_map/ppermute | solution.py:17
  47.0 1.3 %collective-permute-start.3 = (bf16[1,128,160]{1,2,0:T(8,128)(2,1)S(1)}, bf16[1,128,160]{1,2,0:T(8,128)(2,1)S(1)}, u32[]{:S(2)}, u32[]{:S(2)}) collective-permute-start(bf16[1,128,160]{1,2,0:T(8,128)(2,1)S(1)} %get-tuple-element.24), channel_id=1, source_target_pairs={{2,0},{4,2},{6,4},{3,1},{5,3},{7,5},{10,8},{12,10},{14,12},{11,9},... | collective-permute-start | bytes 122888 | tf_op jit(solution)/shard_map/ppermute | solution.py:19
  48.4 7.2 %all_gather.25 = bf16[4,128,640]{1,2,0:T(8,128)(2,1)S(1)} all-gather(bf16[4,128,160]{1,2,0:T(8,128)(2,1)S(1)} %pad_maximum_fusion.4), channel_id=1, replica_groups=mesh['groups'=2,'section'=2,'band'=4,'chan'=2] {'section','chan'}, dimensions={2}, use_global_device_ids=true | all-gather | bytes 819200 | tf_op jit(solution)/shard_map/all_gather | solution.py:64
  55.6 8.0 %all_gather.22 = bf16[4,128,640]{1,2,0:T(8,128)(2,1)S(1)} all-gather(bf16[4,128,160]{1,2,0:T(8,128)(2,1)S(1)} %pad_maximum_fusion.1), channel_id=1, replica_groups=mesh['groups'=2,'section'=2,'band'=4,'chan'=2] {'section','chan'}, dimensions={2}, use_global_device_ids=true | all-gather | bytes 819200 | tf_op jit(solution)/shard_map/all_gather | solution.py:64
  63.6 1.3 %fusion.121 = f32[4,128,1440]{1,2,0:T(8,128)S(1)} fusion(bf16[640,1440,1]{0,1,2:T(8,128)(2,1)S(1)} %bitcast.62, bf16[4,128,640]{1,2,0:T(8,128)(2,1)S(1)} %all_gather.22), kind=kOutput, calls=%fused_computation.195 | convolution fusion | flops 943718400 | bytes 5447680 | tf_op jit(solution)/shard_map/dot_general | solution.py:38
  64.9 0.4 fusion.79
  65.3 4.5 %collective-permute-start.4 = (bf16[1,128,160]{1,2,0:T(8,128)(2,1)S(1)}, bf16[1,128,160]{1,2,0:T(8,128)(2,1)S(1)}, u32[]{:S(2)}, u32[]{:S(2)}) collective-permute-start(bf16[1,128,160]{1,2,0:T(8,128)(2,1)S(1)} %get-tuple-element.21), channel_id=1, source_target_pairs={{0,2},{2,4},{4,6},{1,3},{3,5},{5,7},{8,10},{10,12},{12,14},{9,11},... | collective-permute-start | bytes 122888 | tf_op jit(solution)/shard_map/ppermute | solution.py:17
  69.7 1.3 %collective-permute-start.5 = (bf16[1,128,160]{1,2,0:T(8,128)(2,1)S(1)}, bf16[1,128,160]{1,2,0:T(8,128)(2,1)S(1)}, u32[]{:S(2)}, u32[]{:S(2)}) collective-permute-start(bf16[1,128,160]{1,2,0:T(8,128)(2,1)S(1)} %get-tuple-element.22), channel_id=1, source_target_pairs={{2,0},{4,2},{6,4},{3,1},{5,3},{7,5},{10,8},{12,10},{14,12},{11,9},... | collective-permute-start | bytes 122888 | tf_op jit(solution)/shard_map/ppermute | solution.py:19
  71.0 1.3 %fusion.124 = f32[4,128,1440]{1,2,0:T(8,128)S(1)} fusion(bf16[640,1440,1]{0,1,2:T(8,128)(2,1)S(1)} %bitcast.63, bf16[4,128,640]{1,2,0:T(8,128)(2,1)S(1)} %all_gather.25), kind=kOutput, calls=%fused_computation.198 | convolution fusion | flops 943718400 | bytes 5447680 | tf_op jit(solution)/shard_map/dot_general | solution.py:38
  72.4 0.4 fusion.69
  72.7 6.1 %all_gather.26 = bf16[2,128,640]{1,2,0:T(8,128)(2,1)S(1)} all-gather(bf16[2,128,160]{1,2,0:T(8,128)(2,1)S(1)} %fusion.69), channel_id=1, replica_groups=mesh['groups'=2,'section'=2,'band'=4,'chan'=2] {'section','chan'}, dimensions={2}, use_global_device_ids=true | all-gather | bytes 409600 | tf_op jit(solution)/shard_map/all_gather | solution.py:104
  78.9 1.3 %collective-permute-start.11 = (bf16[1,128,640]{1,2,0:T(8,128)(2,1)S(1)}, bf16[1,128,640]{1,2,0:T(8,128)(2,1)S(1)}, u32[]{:S(2)}, u32[]{:S(2)}) collective-permute-start(bf16[1,128,640]{1,2,0:T(8,128)(2,1)S(1)} %get-tuple-element.17), channel_id=1, source_target_pairs={{2,0},{4,2},{6,4},{3,1},{5,3},{7,5},{10,8},{12,10},{14,12},{11,9},... | collective-permute-start | bytes 491528 | tf_op jit(solution)/shard_map/ppermute | solution.py:19
  80.2 5.2 %collective-permute-start.10 = (bf16[1,128,640]{1,2,0:T(8,128)(2,1)S(1)}, bf16[1,128,640]{1,2,0:T(8,128)(2,1)S(1)}, u32[]{:S(2)}, u32[]{:S(2)}) collective-permute-start(bf16[1,128,640]{1,2,0:T(8,128)(2,1)S(1)} %get-tuple-element.18), channel_id=1, source_target_pairs={{0,2},{2,4},{4,6},{1,3},{3,5},{5,7},{8,10},{10,12},{12,14},{9,11},... | collective-permute-start | bytes 491528 | tf_op jit(solution)/shard_map/ppermute | solution.py:17
  85.4 7.7 %all_gather.23 = bf16[4,128,640]{1,2,0:T(8,128)(2,1)S(1)} all-gather(bf16[4,128,160]{1,2,0:T(8,128)(2,1)S(1)} %pad_maximum_fusion.2), channel_id=1, replica_groups=mesh['groups'=2,'section'=2,'band'=4,'chan'=2] {'section','chan'}, dimensions={2}, use_global_device_ids=true | all-gather | bytes 819200 | tf_op jit(solution)/shard_map/all_gather | solution.py:64
  93.1 1.3 %fusion.122 = f32[4,128,1440]{1,2,0:T(8,128)S(1)} fusion(bf16[640,1440,1]{0,1,2:T(8,128)(2,1)S(1)} %bitcast.60, bf16[4,128,640]{1,2,0:T(8,128)(2,1)S(1)} %all_gather.23), kind=kOutput, calls=%fused_computation.196 | convolution fusion | flops 943718400 | bytes 5447680 | tf_op jit(solution)/shard_map/dot_general | solution.py:38
  94.6 1.3 %fusion.125 = f32[4,128,1440]{1,2,0:T(8,128)S(1)} fusion(bf16[640,1440,1]{0,1,2:T(8,128)(2,1)S(1)} %bitcast.59, bf16[4,128,640]{1,2,0:T(8,128)(2,1)S(1)} %constant_dynamic-update-slice_fusion), kind=kOutput, calls=%fused_computation.199 | convolution fusion | flops 943718400 | bytes 5447680 | tf_op jit(solution)/shard_map/dot_general | solution.py:38
  95.9 0.6 fusion.97
  96.6 3.9 %collective-permute-start.12 = (bf16[1,128,160]{1,2,0:T(8,128)(2,1)S(1)}, bf16[1,128,160]{1,2,0:T(8,128)(2,1)S(1)}, u32[]{:S(2)}, u32[]{:S(2)}) collective-permute-start(bf16[1,128,160]{1,2,0:T(8,128)(2,1)S(1)} %get-tuple-element.19), channel_id=1, source_target_pairs={{0,2},{2,4},{4,6},{1,3},{3,5},{5,7},{8,10},{10,12},{12,14},{9,11},... | collective-permute-start | bytes 122888 | tf_op jit(solution)/shard_map/ppermute | solution.py:17
  100.5 1.5 %collective-permute-start.13 = (bf16[1,128,160]{1,2,0:T(8,128)(2,1)S(1)}, bf16[1,128,160]{1,2,0:T(8,128)(2,1)S(1)}, u32[]{:S(2)}, u32[]{:S(2)}) collective-permute-start(bf16[1,128,160]{1,2,0:T(8,128)(2,1)S(1)} %get-tuple-element.20), channel_id=1, source_target_pairs={{2,0},{4,2},{6,4},{3,1},{5,3},{7,5},{10,8},{12,10},{14,12},{11,9},... | collective-permute-start | bytes 122888 | tf_op jit(solution)/shard_map/ppermute | solution.py:19
  102.0 1.3 %fusion.127 = f32[4,128,1440]{1,2,0:T(8,128)S(1)} fusion(bf16[640,1440,1]{0,1,2:T(8,128)(2,1)S(1)} %bitcast.58, bf16[4,128,640]{1,2,0:T(8,128)(2,1)S(1)} %constant_dynamic-update-slice_fusion), kind=kOutput, calls=%fused_computation.201 | convolution fusion | flops 943718400 | bytes 5447680 | tf_op jit(solution)/shard_map/dot_general | solution.py:38
  103.3 3.1 %collective-permute-done.13 = bf16[1,128,160]{1,2,0:T(8,128)(2,1)S(1)} collective-permute-done((bf16[1,128,160]{1,2,0:T(8,128)(2,1)S(1)}, bf16[1,128,160]{1,2,0:T(8,128)(2,1)S(1)}, u32[]{:S(2)}, u32[]{:S(2)}) %collective-permute-start.13) | collective-permute-done | bytes 40992 | tf_op jit(solution)/shard_map/ppermute | solution.py:19
  106.4 7.4 %all_gather.27 = bf16[4,128,640]{1,2,0:T(8,128)(2,1)S(1)} all-gather(bf16[4,128,160]{1,2,0:T(8,128)(2,1)S(1)} %pad_maximum_fusion.5), channel_id=1, replica_groups=mesh['groups'=2,'section'=2,'band'=4,'chan'=2] {'section','chan'}, dimensions={2}, use_global_device_ids=true | all-gather | bytes 819200 | tf_op jit(solution)/shard_map/all_gather | solution.py:64
  113.8 1.3 %fusion.126 = f32[4,128,1440]{1,2,0:T(8,128)S(1)} fusion(bf16[640,1440,1]{0,1,2:T(8,128)(2,1)S(1)} %bitcast.57, bf16[4,128,640]{1,2,0:T(8,128)(2,1)S(1)} %all_gather.27), kind=kOutput, calls=%fused_computation.200 | convolution fusion | flops 943718400 | bytes 5447680 | tf_op jit(solution)/shard_map/dot_general | solution.py:38
  115.1 1.2 %fusion.99 = bf16[2,128,160]{1,2,0:T(8,128)(2,1)} fusion(bf16[2,128,160]{1,2,0:T(8,128)(2,1)S(1)} %get-tuple-element.6, f32[4,128,1440]{1,2,0:T(8,128)S(1)} %fusion.127, f32[4,128,1440]{1,2,0:T(8,128)S(1)} %fusion.126, f32[160]{0:T(256)S(1)} %convert_element_type.126), kind=kLoop, calls=%fused_computation.168 | loop fusion | flops 860160 | bytes 7046144 | tf_op jit(solution)/shard_map/convert_element_type | solution.py:77
  (51 shorter events, 0.4 us)
Async XLA Ops:
  0.0 34.1 %copy-start = (bf16[3,3,160,640]{3,2,1,0:T(8,128)(2,1)S(1)}, bf16[3,3,160,640]{3,2,1,0:T(8,128)(2,1)}, u32[]{:S(2)}) copy-start(bf16[3,3,160,640]{3,2,1,0:T(8,128)(2,1)} %param.20) | copy-start | bytes 5529604
  1.2 24.9 %collective-permute-start = (bf16[1,128,160]{1,2,0:T(8,128)(2,1)S(1)}, bf16[1,128,160]{1,2,0:T(8,128)(2,1)S(1)}, u32[]{:S(2)}, u32[]{:S(2)}) collective-permute-start(bf16[1,128,160]{1,2,0:T(8,128)(2,1)S(1)} %get-tuple-element.27), channel_id=1, source_target_pairs={{0,2},{2,4},{4,6},{1,3},{3,5},{5,7},{8,10},{10,12},{12,14},{9,11},... | collective-permute-start | bytes 122888 | tf_op jit(solution)/shard_map/ppermute | solution.py:17
  6.1 20.0 %collective-permute-start.1 = (bf16[1,128,160]{1,2,0:T(8,128)(2,1)S(1)}, bf16[1,128,160]{1,2,0:T(8,128)(2,1)S(1)}, u32[]{:S(2)}, u32[]{:S(2)}) collective-permute-start(bf16[1,128,160]{1,2,0:T(8,128)(2,1)S(1)} %get-tuple-element.28), channel_id=1, source_target_pairs={{2,0},{4,2},{6,4},{3,1},{5,3},{7,5},{10,8},{12,10},{14,12},{11,9},... | collective-permute-start | bytes 122888 | tf_op jit(solution)/shard_map/ppermute | solution.py:19
  7.5 9.3 %collective-permute-start.6 = (bf16[1,128,160]{1,2,0:T(8,128)(2,1)S(1)}, bf16[1,128,160]{1,2,0:T(8,128)(2,1)S(1)}, u32[]{:S(2)}, u32[]{:S(2)}) collective-permute-start(bf16[1,128,160]{1,2,0:T(8,128)(2,1)S(1)} %get-tuple-element.33), channel_id=1, source_target_pairs={{0,2},{2,4},{4,6},{1,3},{3,5},{5,7},{8,10},{10,12},{12,14},{9,11},... | collective-permute-start | bytes 122888 | tf_op jit(solution)/shard_map/ppermute | solution.py:17
  12.0 4.0 %copy-start.1 = (bf16[3,3,160,1280]{3,2,1,0:T(8,128)(2,1)S(1)}, bf16[3,3,160,1280]{3,2,1,0:T(8,128)(2,1)}, u32[]{:S(2)}) copy-start(bf16[3,3,160,1280]{3,2,1,0:T(8,128)(2,1)} %param.26) | copy-start | bytes 11059204
  12.0 6.2 %collective-permute-start.7 = (bf16[1,128,160]{1,2,0:T(8,128)(2,1)S(1)}, bf16[1,128,160]{1,2,0:T(8,128)(2,1)S(1)}, u32[]{:S(2)}, u32[]{:S(2)}) collective-permute-start(bf16[1,128,160]{1,2,0:T(8,128)(2,1)S(1)} %get-tuple-element.34), channel_id=1, source_target_pairs={{2,0},{4,2},{6,4},{3,1},{5,3},{7,5},{10,8},{12,10},{14,12},{11,9},... | collective-permute-start | bytes 122888 | tf_op jit(solution)/shard_map/ppermute | solution.py:19
  16.0 0.7 copy-start.7
  16.0 0.7 copy-start.8
  16.0 0.7 copy-start.9
  16.0 0.7 copy-start.10
  16.0 0.7 copy-start.11
  16.0 0.7 copy-start.12
  34.1 1.5 %copy-start.4 = (bf16[3,3,160,640]{3,2,1,0:T(8,128)(2,1)S(1)}, bf16[3,3,160,640]{3,2,1,0:T(8,128)(2,1)}, u32[]{:S(2)}) copy-start(bf16[3,3,160,640]{3,2,1,0:T(8,128)(2,1)} %param.16) | copy-start | bytes 5529604
  35.4 1.5 %copy-start.2 = (bf16[2,128,160]{1,2,0:T(8,128)(2,1)S(1)}, bf16[2,128,160]{1,2,0:T(8,128)(2,1)}, u32[]{:S(2)}) copy-start(bf16[2,128,160]{1,2,0:T(8,128)(2,1)} %param.14) | copy-start | bytes 245764
  35.5 1.5 %copy-start.3 = (bf16[2,128,160]{1,2,0:T(8,128)(2,1)S(1)}, bf16[2,128,160]{1,2,0:T(8,128)(2,1)}, u32[]{:S(2)}) copy-start(bf16[2,128,160]{1,2,0:T(8,128)(2,1)} %param.15) | copy-start | bytes 245764
  37.0 26.6 %copy-start.5 = (bf16[3,3,160,640]{3,2,1,0:T(8,128)(2,1)S(1)}, bf16[3,3,160,640]{3,2,1,0:T(8,128)(2,1)}, u32[]{:S(2)}) copy-start(bf16[3,3,160,640]{3,2,1,0:T(8,128)(2,1)} %param.22) | copy-start | bytes 5529604
  37.6 10.7 %collective-permute-start.8 = (bf16[1,128,160]{1,2,0:T(8,128)(2,1)S(1)}, bf16[1,128,160]{1,2,0:T(8,128)(2,1)S(1)}, u32[]{:S(2)}, u32[]{:S(2)}) collective-permute-start(bf16[1,128,160]{1,2,0:T(8,128)(2,1)S(1)} %get-tuple-element.31), channel_id=1, source_target_pairs={{0,2},{2,4},{4,6},{1,3},{3,5},{5,7},{8,10},{10,12},{12,14},{9,11},... | collective-permute-start | bytes 122888 | tf_op jit(solution)/shard_map/ppermute | solution.py:17
  41.1 7.2 %collective-permute-start.9 = (bf16[1,128,160]{1,2,0:T(8,128)(2,1)S(1)}, bf16[1,128,160]{1,2,0:T(8,128)(2,1)S(1)}, u32[]{:S(2)}, u32[]{:S(2)}) collective-permute-start(bf16[1,128,160]{1,2,0:T(8,128)(2,1)S(1)} %get-tuple-element.32), channel_id=1, source_target_pairs={{2,0},{4,2},{6,4},{3,1},{5,3},{7,5},{10,8},{12,10},{14,12},{11,9},... | collective-permute-start | bytes 122888 | tf_op jit(solution)/shard_map/ppermute | solution.py:19
  42.5 13.1 %collective-permute-start.2 = (bf16[1,128,160]{1,2,0:T(8,128)(2,1)S(1)}, bf16[1,128,160]{1,2,0:T(8,128)(2,1)S(1)}, u32[]{:S(2)}, u32[]{:S(2)}) collective-permute-start(bf16[1,128,160]{1,2,0:T(8,128)(2,1)S(1)} %get-tuple-element.23), channel_id=1, source_target_pairs={{0,2},{2,4},{4,6},{1,3},{3,5},{5,7},{8,10},{10,12},{12,14},{9,11},... | collective-permute-start | bytes 122888 | tf_op jit(solution)/shard_map/ppermute | solution.py:17
  47.0 8.5 %collective-permute-start.3 = (bf16[1,128,160]{1,2,0:T(8,128)(2,1)S(1)}, bf16[1,128,160]{1,2,0:T(8,128)(2,1)S(1)}, u32[]{:S(2)}, u32[]{:S(2)}) collective-permute-start(bf16[1,128,160]{1,2,0:T(8,128)(2,1)S(1)} %get-tuple-element.24), channel_id=1, source_target_pairs={{2,0},{4,2},{6,4},{3,1},{5,3},{7,5},{10,8},{12,10},{14,12},{11,9},... | collective-permute-start | bytes 122888 | tf_op jit(solution)/shard_map/ppermute | solution.py:19
  64.9 6.2 %copy-start.6 = (bf16[3,3,160,640]{3,2,1,0:T(8,128)(2,1)S(1)}, bf16[3,3,160,640]{3,2,1,0:T(8,128)(2,1)}, u32[]{:S(2)}) copy-start(bf16[3,3,160,640]{3,2,1,0:T(8,128)(2,1)} %param.18) | copy-start | bytes 5529604
  65.3 20.1 %collective-permute-start.4 = (bf16[1,128,160]{1,2,0:T(8,128)(2,1)S(1)}, bf16[1,128,160]{1,2,0:T(8,128)(2,1)S(1)}, u32[]{:S(2)}, u32[]{:S(2)}) collective-permute-start(bf16[1,128,160]{1,2,0:T(8,128)(2,1)S(1)} %get-tuple-element.21), channel_id=1, source_target_pairs={{0,2},{2,4},{4,6},{1,3},{3,5},{5,7},{8,10},{10,12},{12,14},{9,11},... | collective-permute-start | bytes 122888 | tf_op jit(solution)/shard_map/ppermute | solution.py:17
  69.7 15.6 %collective-permute-start.5 = (bf16[1,128,160]{1,2,0:T(8,128)(2,1)S(1)}, bf16[1,128,160]{1,2,0:T(8,128)(2,1)S(1)}, u32[]{:S(2)}, u32[]{:S(2)}) collective-permute-start(bf16[1,128,160]{1,2,0:T(8,128)(2,1)S(1)} %get-tuple-element.22), channel_id=1, source_target_pairs={{2,0},{4,2},{6,4},{3,1},{5,3},{7,5},{10,8},{12,10},{14,12},{11,9},... | collective-permute-start | bytes 122888 | tf_op jit(solution)/shard_map/ppermute | solution.py:19
  78.9 15.7 %collective-permute-start.11 = (bf16[1,128,640]{1,2,0:T(8,128)(2,1)S(1)}, bf16[1,128,640]{1,2,0:T(8,128)(2,1)S(1)}, u32[]{:S(2)}, u32[]{:S(2)}) collective-permute-start(bf16[1,128,640]{1,2,0:T(8,128)(2,1)S(1)} %get-tuple-element.17), channel_id=1, source_target_pairs={{2,0},{4,2},{6,4},{3,1},{5,3},{7,5},{10,8},{12,10},{14,12},{11,9},... | collective-permute-start | bytes 491528 | tf_op jit(solution)/shard_map/ppermute | solution.py:19
  80.2 14.3 %collective-permute-start.10 = (bf16[1,128,640]{1,2,0:T(8,128)(2,1)S(1)}, bf16[1,128,640]{1,2,0:T(8,128)(2,1)S(1)}, u32[]{:S(2)}, u32[]{:S(2)}) collective-permute-start(bf16[1,128,640]{1,2,0:T(8,128)(2,1)S(1)} %get-tuple-element.18), channel_id=1, source_target_pairs={{0,2},{2,4},{4,6},{1,3},{3,5},{5,7},{8,10},{10,12},{12,14},{9,11},... | collective-permute-start | bytes 491528 | tf_op jit(solution)/shard_map/ppermute | solution.py:17
  96.6 6.7 %collective-permute-start.12 = (bf16[1,128,160]{1,2,0:T(8,128)(2,1)S(1)}, bf16[1,128,160]{1,2,0:T(8,128)(2,1)S(1)}, u32[]{:S(2)}, u32[]{:S(2)}) collective-permute-start(bf16[1,128,160]{1,2,0:T(8,128)(2,1)S(1)} %get-tuple-element.19), channel_id=1, source_target_pairs={{0,2},{2,4},{4,6},{1,3},{3,5},{5,7},{8,10},{10,12},{12,14},{9,11},... | collective-permute-start | bytes 122888 | tf_op jit(solution)/shard_map/ppermute | solution.py:17
  100.5 5.9 %collective-permute-start.13 = (bf16[1,128,160]{1,2,0:T(8,128)(2,1)S(1)}, bf16[1,128,160]{1,2,0:T(8,128)(2,1)S(1)}, u32[]{:S(2)}, u32[]{:S(2)}) collective-permute-start(bf16[1,128,160]{1,2,0:T(8,128)(2,1)S(1)} %get-tuple-element.20), channel_id=1, source_target_pairs={{2,0},{4,2},{6,4},{3,1},{5,3},{7,5},{10,8},{12,10},{14,12},{11,9},... | collective-permute-start | bytes 122888 | tf_op jit(solution)/shard_map/ppermute | solution.py:19
where the time goes:
time: 117 us; the launch traced here: 116 us
  blocking collectives  52.3 us (45%)
  starting transfers between devices  40.6 us (35%)
  matrix products  10.5 us (9%)
  waiting for transfers between devices  4.56 us (4%)
  other arithmetic  4.51 us (4%)
  local copies, waits for them, and re-layouts  3.39 us (3%)
    all_gather x6, blocking collectives, convolve(): lax.all_gather(bordered, ('section', 'chan'), axis=2, tiled=True)  46.2 us
    ppermute x7, starting transfers between devices, padded_2(): lax.ppermute(tail, axis, [(i, (i + 1) % count) for i in range(ends)])  31.1 us
    dot_general x8, matrix products, add_taps(): jnp.dot(portion.reshape((height + 2) * breadth, depth), kernel, preferred...  10.5 us
    ppermute x7, starting transfers between devices, padded_2(): lax.ppermute(head, axis, [((i + 1) % count, i) for i in range(ends)])  9.49 us
    all_gather x1, blocking collectives, per_device(): lax.all_gather(control_act, ('section', 'chan'), axis=2, tiled=True)  6.1 us
    ppermute x7, waiting for transfers between devices, padded_2(): lax.ppermute(head, axis, [((i + 1) % count, i) for i in range(ends)])  4.54 us
    convert_element_type x5, other arithmetic, activate(): return (value * jax.nn.sigmoid(value)).astype(jnp.bfloat16)  3.12 us
    dynamic_slice x2, local copies, waits for them, and re-layouts, add_taps(): kernel = lax.dynamic_slice_in_dim(weights, anchor, depth, 3)  2.7 us
  transfers between devices with their start and end apart: 14, of which 2 were waited for; matrix products, arithmetic and copies ran while one was open for 6% of the time, Pallas kernels for 0%

commit v1 on v0

v1 whole, which is shorter than its diff:
```python
import jax
import jax.numpy as jnp
from jax import lax
from jax.sharding import PartitionSpec as P

LAYERS = 4
CHANNEL_AXES = ("section", "chan")


def activate(state):
    value = state.astype(jnp.float32)
    return (value * jax.nn.sigmoid(value)).astype(jnp.bfloat16)


def gather_channels(cells):
    return lax.all_gather(cells, CHANNEL_AXES, axis=cells.ndim - 1, tiled=True)


def convolve(cells, weights):
    return lax.conv_general_dilated(
        cells[None],
        weights,
        (1, 1),
        ((1, 1), (0, 0)),
        dimension_numbers=("NHWC", "HWOI", "NHWC"),
        preferred_element_type=jnp.float32,
    )[0]


def rows_to_columns(cells, halo):
    bands = lax.axis_size("band")
    columns = cells.shape[-2] // bands
    pad = [(0, 0)] * cells.ndim
    pad[-2] = (halo, halo)
    wide = jnp.pad(cells, pad)
    blocks = jnp.stack(
        [
            lax.slice_in_dim(wide, t * columns, (t + 1) * columns + 2 * halo, axis=wide.ndim - 2)
            for t in range(bands)
        ]
    )
    blocks = lax.all_to_all(blocks, "band", 0, 0)
    blocks = jnp.moveaxis(blocks, 0, -4)
    return blocks.reshape(blocks.shape[:-4] + (-1,) + blocks.shape[-2:])


def columns_to_rows(cells):
    bands = lax.axis_size("band")
    rows = cells.shape[0] // bands
    blocks = cells.reshape((bands, rows) + cells.shape[1:])
    blocks = lax.all_to_all(blocks, "band", 0, 0)
    blocks = jnp.moveaxis(blocks, 0, 1)
    return blocks.reshape((rows, -1) + cells.shape[2:])


def per_device(
    latent,
    control_hint,
    control_weight_one,
    control_bias_one,
    control_weight_two,
    control_bias_two,
    main_weight_one,
    main_bias_one,
    main_weight_two,
    main_bias_two,
    decoder_weight_one,
    decoder_bias_one,
    decoder_weight_two,
    decoder_bias_two,
):
    width = latent.shape[1]
    columns = width // lax.axis_size("band")
    first = lax.axis_index("band") * columns

    def masked(cells, halo):
        at = first - halo + jnp.arange(columns + 2 * halo)
        inside = (at >= 0) & (at < width)
        return jnp.where(inside[:, None], cells, jnp.zeros_like(cells))

    def finish(state, result, offset):
        total = state[..., 1:-1, :].astype(jnp.float32) + result + offset.astype(jnp.float32)
        return total.astype(jnp.bfloat16)

    control_input = (latent.astype(jnp.float32) + control_hint.astype(jnp.float32)).astype(
        jnp.bfloat16
    )
    both = rows_to_columns(jnp.stack([control_input, latent]), LAYERS)
    weights = ((control_weight_one, main_weight_one), (control_weight_two, main_weight_two))
    offsets = ((control_bias_one, main_bias_one), (control_bias_two, main_bias_two))
    for step in range(2):
        halo = LAYERS - step
        wide = gather_channels(masked(activate(both), halo))
        both = jnp.stack(
            [
                finish(both[i], convolve(wide[i], weights[step][i]), offsets[step][i])
                for i in range(2)
            ]
        )
    wide = gather_channels(masked(activate(both), 2))
    skip = wide[0]
    joined = jnp.concatenate([wide[1], skip], axis=2)
    state = finish(both[1], convolve(joined, decoder_weight_one), decoder_bias_one)
    wide = gather_channels(masked(activate(state), 1))
    joined = jnp.concatenate([wide, skip[:, 1:-1]], axis=2)
    state = finish(state, convolve(joined, decoder_weight_two), decoder_bias_two)
    return columns_to_rows(state)


def solution(mesh):
    image = P(("groups", "band"), None, CHANNEL_AXES)
    kernel = P(None, None, CHANNEL_AXES, None)
    bias = P(CHANNEL_AXES)
    return jax.shard_map(
        per_device,
        mesh=mesh,
        in_specs=(image, image) + (kernel, bias) * 6,
        out_specs=image,
        check_vma=False,
    )
```

time: 117 us -> 149 us (1.27)
  starting transfers between devices: 40.6 us -> 6.35 us
  local copies, waits for them, and re-layouts: 3.39 us -> 36.3 us
  blocking collectives: 52.3 us -> 76.9 us
  other arithmetic: 4.51 us -> 8.73 us
  waiting for transfers between devices: 4.56 us -> 8.54 us
    ppermute x14 -> x0, starting transfers between devices: 40.6 us -> none  [the longest x7 31.1 us: padded_2(): lax.ppermute(tail, axis, [(i, (i + 1) % count) for i in range(ends)])]
    unnamed x28 -> x64, local copies, waits for them, and re-layouts: 0.6 us -> 20.6 us
    all_gather x7 -> x4, blocking collectives: 52.3 us -> 68 us  [gather_channels(): return lax.all_gather(cells, CHANNEL_AXES, axis=cells.ndim - 1, tiled=True)]
    dot_general x8 -> x0, matrix products: 10.5 us -> none  [add_taps(): jnp.dot(portion.reshape((height + 2) * breadth, depth), kernel, preferred...]
    conv_general_dilated x0 -> x6, matrix products: none -> 10.5 us  [convolve(): lax.conv_general_dilated(cells[None], weights, (1, 1), ((1, 1), (0, 0)),...]
    all_to_all x0 -> x1, blocking collectives: none -> 8.92 us  [columns_to_rows(): blocks = lax.all_to_all(blocks, 'band', 0, 0)]
    all_to_all x0 -> x1, waiting for transfers between devices: none -> 8.54 us  [rows_to_columns(): blocks = lax.all_to_all(blocks, 'band', 0, 0)]
    all_to_all x0 -> x1, starting transfers between devices: none -> 6.35 us  [rows_to_columns(): blocks = lax.all_to_all(blocks, 'band', 0, 0)]
  transfers between devices with their start and end apart: 14 -> 1, of which waited for: 2 -> 1; matrix products, arithmetic and copies ran while one was open for 6% -> 1% of each run, Pallas kernels for 0% -> 0%
where the time goes in v1:
time: 149 us; the launch traced here: 148 us
  blocking collectives  76.9 us (52%)
  local copies, waits for them, and re-layouts  36.3 us (24%)
  matrix products  10.5 us (7%)
  other arithmetic  8.73 us (6%)
  waiting for transfers between devices  8.54 us (6%)
  starting transfers between devices  6.35 us (4%)
    all_gather x4, blocking collectives, gather_channels(): return lax.all_gather(cells, CHANNEL_AXES, axis=cells.ndim - 1, tiled=True)  68 us
    unnamed x64, local copies, waits for them, and re-layouts  20.6 us
    conv_general_dilated x6, matrix products, convolve(): lax.conv_general_dilated(cells[None], weights, (1, 1), ((1, 1), (0, 0)),...  10.5 us
    all_to_all x1, blocking collectives, columns_to_rows(): blocks = lax.all_to_all(blocks, 'band', 0, 0)  8.92 us
    all_to_all x1, waiting for transfers between devices, rows_to_columns(): blocks = lax.all_to_all(blocks, 'band', 0, 0)  8.54 us
    all_to_all x1, starting transfers between devices, rows_to_columns(): blocks = lax.all_to_all(blocks, 'band', 0, 0)  6.35 us
    conv_general_dilated x18, local copies, waits for them, and re-layouts, convolve(): lax.conv_general_dilated(cells[None], weights, (1, 1), ((1, 1), (0, 0)),...  4.9 us
  transfers between devices with their start and end apart: 1, of which 1 were waited for; matrix products, arithmetic and copies ran while one was open for 1% of the time, Pallas kernels for 0%

profile of v1, /device:TPU:0, one launch (start us, length us, event | category | flops | bytes accessed | tf_op | source)
XLA Modules:
  0.0 147.9 jit_solution(17688101977864678801)
XLA Ops:
  0.0 1.1 fusion.93
  1.1 0.9 pad_maximum_fusion.1
  2.0 1.2 fusion.86
  3.5 1.1 copy.84
  4.5 6.3 %all-to-all-start = ((bf16[4,2,2,40,160]{4,3,2,1,0:T(8,128)(2,1)}), bf16[4,2,2,40,160]{4,3,2,1,0:T(8,128)(2,1)S(1)}, u32[]{:S(2)}, u32[]{:S(2)}) async-start(bf16[4,2,2,40,160]{4,3,2,1,0:T(8,128)(2,1)} %copy.84), calls=%async_computation | async-start | bytes 655360 | tf_op jit(solution)/shard_map/all_to_all | solution.py:42
  10.9 0.6 convert_element_type.111
  11.6 0.6 compare_and_fusion.1
  12.7 8.5 %all-to-all-done = bf16[4,2,2,40,160]{4,3,2,1,0:T(8,128)(2,1)S(1)} async-done(((bf16[4,2,2,40,160]{4,3,2,1,0:T(8,128)(2,1)}), bf16[4,2,2,40,160]{4,3,2,1,0:T(8,128)(2,1)S(1)}, u32[]{:S(2)}, u32[]{:S(2)}) %all-to-all-start) | async-done | bytes 204832 | tf_op jit(solution)/shard_map/all_to_all | solution.py:42
  21.4 0.5 copy.87
  22.0 18.6 %all_gather.12 = bf16[2,8,40,640]{2,1,0,3:T(8,128)(2,1)S(1)} all-gather(bf16[2,8,40,160]{2,1,0,3:T(8,128)(2,1)S(1)} %copy.87), channel_id=1, replica_groups=mesh['groups'=2,'section'=2,'band'=4,'chan'=2] {'section','chan'}, dimensions={3}, use_global_device_ids=true | all-gather | bytes 1024000 | tf_op jit(solution)/shard_map/all_gather | solution.py:16
  40.6 1.2 fusion.115
  41.8 2.9 %copy.123 = bf16[1,8,40,640]{3,1,2,0:T(8,128)(2,1)} copy(bf16[1,8,40,640]{2,1,0,3:T(8,128)(2,1)} %get-tuple-element.11) | data formatting | bytes 819200
  44.8 1.0 copy.95
  45.9 1.2 convolution_select_fusion.2
  47.0 0.9 copy.96
  47.9 0.7 fusion.116
  48.6 1.9 %copy.121 = bf16[1,8,40,640]{3,1,2,0:T(8,128)(2,1)} copy(bf16[1,8,40,640]{2,1,0,3:T(8,128)(2,1)S(1)} %get-tuple-element.12) | data formatting | bytes 819200
  50.6 1.0 copy.90
  51.7 2.7 %convolution_select_fusion.3 = f32[8,8,5,160]{3,1,2,0:T(8,128)S(1)} fusion(bf16[3,3,160,640]{3,2,1,0:T(8,128)(2,1)} %param.20, bf16[8,1,7,2,640]{4,2,3,0,1:T(8,128)(2,1)S(1)} %slice.99, bf16[8,1,8,5,640]{4,2,3,0,1:T(8,128)(2,1)S(1)} %copy.90, pred[8,5]{0,1:T(8,128)(4,1)S(1)} %copy-done.28), kind=kOutput, calls=%fused_computation.6 | convolution fusion | flops 542443520 | bytes 2601000 | tf_op jit(solution)/shard_map/conv_general_dilated | solution.py:20
  54.7 0.6 copy-done.1
  55.6 0.7 copy.97
  56.3 18.9 %all_gather.13 = bf16[2,8,38,640]{2,1,0,3:T(8,128)(2,1)S(1)} all-gather(bf16[2,8,38,160]{2,1,0,3:T(8,128)(2,1)S(1)} %copy.97), channel_id=1, replica_groups=mesh['groups'=2,'section'=2,'band'=4,'chan'=2] {'section','chan'}, dimensions={3}, use_global_device_ids=true | all-gather | bytes 972800 | tf_op jit(solution)/shard_map/all_gather | solution.py:16
  75.2 1.2 fusion.114
  76.4 2.4 %copy.125 = bf16[1,8,38,640]{3,1,2,0:T(8,128)(2,1)S(1)} copy(bf16[1,8,38,640]{2,1,0,3:T(8,128)(2,1)} %get-tuple-element.9) | data formatting | bytes 778240
  79.0 1.3 copy-done.16
  80.4 1.2 convolution_select_fusion
  81.5 0.8 copy.105
  82.4 1.4 copy.124
  83.9 1.3 copy-done.17
  85.3 1.2 convolution_select_fusion.1
  86.7 0.6 copy-done.5
  87.6 0.7 copy.106
  88.2 18.7 %all_gather.14 = bf16[2,8,36,640]{2,1,0,3:T(8,128)(2,1)S(1)} all-gather(bf16[2,8,36,160]{2,1,0,3:T(8,128)(2,1)S(1)} %copy.106), channel_id=1, replica_groups=mesh['groups'=2,'section'=2,'band'=4,'chan'=2] {'section','chan'}, dimensions={3}, use_global_device_ids=true | all-gather | bytes 921600 | tf_op jit(solution)/shard_map/all_gather | solution.py:16
  106.9 1.2 fusion.113
  108.2 3.0 %copy.126 = bf16[1,8,36,640]{3,1,2,0:T(8,128)(2,1)} copy(bf16[1,8,36,640]{2,1,0,3:T(8,128)(2,1)} %get-tuple-element.7) | data formatting | bytes 737280
  111.2 1.3 copy.127
  112.5 0.8 slice.120
  113.3 1.0 maximum_bitcast_fusion
  114.6 1.7 %copy-done.14 = bf16[3,3,160,1280]{3,2,1,0:T(8,128)(2,1)S(1)} copy-done((bf16[3,3,160,1280]{3,2,1,0:T(8,128)(2,1)S(1)}, bf16[3,3,160,1280]{3,2,1,0:T(8,128)(2,1)}, u32[]{:S(2)}) %copy-start.14) | copy-done | bytes 3686424
  116.4 2.2 %convolution_select_fusion.5 = f32[8,8,5,160]{3,1,2,0:T(8,128)S(1)} fusion(bf16[3,3,160,1280]{3,2,1,0:T(8,128)(2,1)S(1)} %copy-done.14, bf16[8,1,7,2,1280]{4,2,3,0,1:T(8,128)(2,1)S(1)} %slice.117, bf16[8,1,8,5,1280]{4,2,3,0,1:T(8,128)(2,1)S(1)} %copy.110, pred[8,5]{0,1:T(8,128)(4,1)S(1)} %copy-done.25), kind=kOutput, calls=%fused_computation.8 | convolution fusion | flops 1084835840 | bytes 4997160 | tf_op jit(solution)/shard_map/conv_general_dilated | solution.py:20
  118.7 0.8 fusion.92
  119.7 11.8 %all_gather.15 = bf16[8,34,640]{1,0,2:T(8,128)(2,1)S(1)} all-gather(bf16[8,34,160]{1,0,2:T(8,128)(2,1)S(1)} %copy.112), channel_id=1, replica_groups=mesh['groups'=2,'section'=2,'band'=4,'chan'=2] {'section','chan'}, dimensions={2}, use_global_device_ids=true | all-gather | bytes 435200 | tf_op jit(solution)/shard_map/all_gather | solution.py:16
  131.5 1.3 copy.113
  132.9 1.0 maximum_bitcast_fusion.1
  134.2 1.7 %copy-done.15 = bf16[3,3,160,1280]{3,2,1,0:T(8,128)(2,1)S(1)} copy-done((bf16[3,3,160,1280]{3,2,1,0:T(8,128)(2,1)S(1)}, bf16[3,3,160,1280]{3,2,1,0:T(8,128)(2,1)}, u32[]{:S(2)}) %copy-start.15) | copy-done | bytes 3686424
  136.0 2.1 %convolution_select_fusion.4 = f32[8,8,5,160]{3,1,2,0:T(8,128)S(1)} fusion(bf16[3,3,160,1280]{3,2,1,0:T(8,128)(2,1)S(1)} %copy-done.15, bf16[8,1,7,2,1280]{4,2,3,0,1:T(8,128)(2,1)S(1)} %slice.121, bf16[8,1,8,5,1280]{4,2,3,0,1:T(8,128)(2,1)S(1)} %copy.115, pred[8,5]{0,1:T(8,128)(4,1)S(1)} %copy-done.24), kind=kOutput, calls=%fused_computation.7 | convolution fusion | flops 1084835840 | bytes 4997160 | tf_op jit(solution)/shard_map/conv_general_dilated | solution.py:20
  138.3 8.9 %all_to_all.10 = bf16[4,2,32,160]{3,2,1,0:T(8,128)(2,1)S(1)} all-to-all(bf16[4,2,32,160]{3,2,1,0:T(8,128)(2,1)S(1)} %bitcast.148), channel_id=1, replica_groups=mesh['groups'=2,'section'=2,'band'=4,'chan'=2] {'band'}, dimensions={0} | all-to-all | bytes 163840 | tf_op jit(solution)/shard_map/all_to_all | solution.py:51
  147.2 0.7 copy.119
  (93 shorter events, 3.5 us)
Async XLA Ops:
  0.0 45.9 %copy-start = (bf16[3,3,160,640]{3,2,1,0:T(8,128)(2,1)S(1)}, bf16[3,3,160,640]{3,2,1,0:T(8,128)(2,1)}, u32[]{:S(2)}) copy-start(bf16[3,3,160,640]{3,2,1,0:T(8,128)(2,1)} %param.16) | copy-start | bytes 5529604
  3.2 7.7 %copy-start.18 = (bf16[160]{0:T(256)(128)(2,1)S(1)}, bf16[160]{0:T(256)(128)(2,1)}, u32[]{:S(2)}) copy-start(bf16[160]{0:T(256)(128)(2,1)} %param.17) | copy-start | bytes 964
  3.2 7.7 %copy-start.19 = (bf16[160]{0:T(256)(128)(2,1)S(1)}, bf16[160]{0:T(256)(128)(2,1)}, u32[]{:S(2)}) copy-start(bf16[160]{0:T(256)(128)(2,1)} %param.21) | copy-start | bytes 964
  3.2 7.7 %copy-start.20 = (bf16[160]{0:T(256)(128)(2,1)S(1)}, bf16[160]{0:T(256)(128)(2,1)}, u32[]{:S(2)}) copy-start(bf16[160]{0:T(256)(128)(2,1)} %param.19) | copy-start | bytes 964
  3.2 8.3 %copy-start.21 = (bf16[160]{0:T(256)(128)(2,1)S(1)}, bf16[160]{0:T(256)(128)(2,1)}, u32[]{:S(2)}) copy-start(bf16[160]{0:T(256)(128)(2,1)} %param.23) | copy-start | bytes 964
  3.3 8.3 %copy-start.22 = (bf16[160]{0:T(256)(128)(2,1)S(1)}, bf16[160]{0:T(256)(128)(2,1)}, u32[]{:S(2)}) copy-start(bf16[160]{0:T(256)(128)(2,1)} %param.25) | copy-start | bytes 964
  3.3 8.3 %copy-start.23 = (bf16[160]{0:T(256)(128)(2,1)S(1)}, bf16[160]{0:T(256)(128)(2,1)}, u32[]{:S(2)}) copy-start(bf16[160]{0:T(256)(128)(2,1)} %param.27) | copy-start | bytes 964
  4.5 16.7 %all-to-all-start = ((bf16[4,2,2,40,160]{4,3,2,1,0:T(8,128)(2,1)}), bf16[4,2,2,40,160]{4,3,2,1,0:T(8,128)(2,1)S(1)}, u32[]{:S(2)}, u32[]{:S(2)}) async-start(bf16[4,2,2,40,160]{4,3,2,1,0:T(8,128)(2,1)} %copy.84), calls=%async_computation | async-start | bytes 655360 | tf_op jit(solution)/shard_map/all_to_all | solution.py:42
  41.8 4.1 %copy-start.28 = (pred[8,5]{0,1:T(8,128)(4,1)S(1)}, pred[8,5]{0,1:T(8,128)(4,1)}, u32[]{:S(2)}) copy-start(pred[8,5]{0,1:T(8,128)(4,1)} %constant.68) | copy-start | bytes 124
  51.7 2.9 %copy-start.9 = (bf16[1,4,2,40,160]{4,3,2,1,0:T(8,128)(2,1)S(1)}, bf16[1,4,2,40,160]{4,3,2,1,0:T(8,128)(2,1)}, u32[]{:S(2)}) copy-start(bf16[1,4,2,40,160]{4,3,2,1,0:T(8,128)(2,1)} %get-tuple-element.14) | copy-start | bytes 307204
  51.7 2.9 %copy-start.7 = (f32[8,8,5,160]{3,0,2,1:T(8,128)S(1)}, f32[8,8,5,160]{3,0,2,1:T(8,128)}, u32[]{:S(2)}) copy-start(f32[8,8,5,160]{3,0,2,1:T(8,128)} %copy.96) | copy-start | bytes 614404
  54.7 0.7 copy-start.1
  54.7 0.7 copy-start.3
  78.9 1.5 %copy-start.16 = (bf16[3,3,160,640]{3,2,1,0:T(8,128)(2,1)S(1)}, bf16[3,3,160,640]{3,2,1,0:T(8,128)(2,1)}, u32[]{:S(2)}) copy-start(bf16[3,3,160,640]{3,2,1,0:T(8,128)(2,1)} %param.18) | copy-start | bytes 5529604
  78.9 1.5 %copy-start.26 = (pred[8,5]{0,1:T(8,128)(4,1)S(1)}, pred[8,5]{0,1:T(8,128)(4,1)}, u32[]{:S(2)}) copy-start(pred[8,5]{0,1:T(8,128)(4,1)} %constant.69) | copy-start | bytes 124
  83.7 1.5 %copy-start.17 = (bf16[3,3,160,640]{3,2,1,0:T(8,128)(2,1)S(1)}, bf16[3,3,160,640]{3,2,1,0:T(8,128)(2,1)}, u32[]{:S(2)}) copy-start(bf16[3,3,160,640]{3,2,1,0:T(8,128)(2,1)} %param.22) | copy-start | bytes 5529604
  83.7 1.5 %copy-start.27 = (pred[8,5]{0,1:T(8,128)(4,1)S(1)}, pred[8,5]{0,1:T(8,128)(4,1)}, u32[]{:S(2)}) copy-start(pred[8,5]{0,1:T(8,128)(4,1)} %constant.69) | copy-start | bytes 124
  85.2 1.3 copy-start.2
  85.2 1.3 copy-start.8
  85.2 1.3 copy-start.11
  85.2 1.4 copy-start.4
  86.4 0.9 copy-start.13
  86.7 0.7 copy-start.5
  114.3 2.0 %copy-start.14 = (bf16[3,3,160,1280]{3,2,1,0:T(8,128)(2,1)S(1)}, bf16[3,3,160,1280]{3,2,1,0:T(8,128)(2,1)}, u32[]{:S(2)}) copy-start(bf16[3,3,160,1280]{3,2,1,0:T(8,128)(2,1)} %param.24) | copy-start | bytes 11059204
  114.4 2.0 %copy-start.25 = (pred[8,5]{0,1:T(8,128)(4,1)S(1)}, pred[8,5]{0,1:T(8,128)(4,1)}, u32[]{:S(2)}) copy-start(pred[8,5]{0,1:T(8,128)(4,1)} %constant.71) | copy-start | bytes 124
  116.4 2.3 %copy-start.6 = (bf16[8,36,160]{2,0,1:T(8,128)(2,1)S(1)}, bf16[8,36,160]{2,0,1:T(8,128)(2,1)}, u32[]{:S(2)}) copy-start(bf16[8,36,160]{2,0,1:T(8,128)(2,1)} %copy-done.5) | copy-start | bytes 276484
  116.4 2.3 %copy-start.12 = (pred[34]{0:T(512)(128)(4,1)S(1)}, pred[34]{0:T(512)(128)(4,1)}, u32[]{:S(2)}) copy-start(pred[34]{0:T(512)(128)(4,1)} %compare_and_fusion) | copy-start | bytes 106
  133.9 2.0 %copy-start.15 = (bf16[3,3,160,1280]{3,2,1,0:T(8,128)(2,1)S(1)}, bf16[3,3,160,1280]{3,2,1,0:T(8,128)(2,1)}, u32[]{:S(2)}) copy-start(bf16[3,3,160,1280]{3,2,1,0:T(8,128)(2,1)} %param.26) | copy-start | bytes 11059204
  134.0 2.0 %copy-start.24 = (pred[8,5]{0,1:T(8,128)(4,1)S(1)}, pred[8,5]{0,1:T(8,128)(4,1)}, u32[]{:S(2)}) copy-start(pred[8,5]{0,1:T(8,128)(4,1)} %constant.73) | copy-start | bytes 124
  136.0 2.2 %copy-start.10 = (bf16[8,34,160]{2,0,1:T(8,128)(2,1)S(1)}, bf16[8,34,160]{2,0,1:T(8,128)(2,1)}, u32[]{:S(2)}) copy-start(bf16[8,34,160]{2,0,1:T(8,128)(2,1)} %get-tuple-element.6) | copy-start | bytes 261124

commit v2 on v1

v2 whole, which is shorter than its diff:
```python
import functools

import jax
import jax.numpy as jnp
from jax import lax
from jax.experimental import pallas as pl
from jax.experimental.pallas import tpu as pltpu
from jax.sharding import PartitionSpec as P

LAYERS = 4
CHANNEL_AXES = ("section", "chan")
F32 = jnp.float32
BF16 = jnp.bfloat16
TRANSPOSED = (((1,), (1,)), ((), ()))


def silu(value):
    return value * jax.nn.sigmoid(value)


def exchange(cells, axis, distance):
    count = lax.axis_size(axis)
    return lax.ppermute(cells, axis, [(i, i ^ distance) for i in range(count)])


def channel_place():
    return lax.axis_index("section") * lax.axis_size("chan") + lax.axis_index("chan")


def channel_count():
    return lax.axis_size("section") * lax.axis_size("chan")


def whole(count):
    return [pl.BlockSpec(memory_space=pltpu.VMEM)] * count


def call(kernel, outs, *args, scratch=(), flops=0):
    many = isinstance(outs, (tuple, list))
    moved = sum(a.size * a.dtype.itemsize for a in args)
    moved += sum(o.size * o.dtype.itemsize for o in (outs if many else [outs]))
    return pl.pallas_call(
        kernel,
        out_shape=outs,
        in_specs=whole(len(args)),
        out_specs=whole(len(outs)) if many else whole(1)[0],
        scratch_shapes=list(scratch),
        compiler_params=pltpu.CompilerParams(vmem_limit_bytes=20 << 20),
        cost_estimate=pl.CostEstimate(flops=flops, bytes_accessed=moved, transcendentals=0),
    )(*args)


def sds(shape, dtype=BF16):
    return jax.ShapeDtypeStruct(shape, dtype)


class Sizes:
    def __init__(self, latent):
        self.bands = lax.axis_size("band")
        self.rows, self.width, self.per = latent.shape
        self.columns = self.width // self.bands
        self.wide = self.columns + 2 * LAYERS
        self.height = self.rows * self.bands
        self.cells = self.height * self.wide
        self.shards = channel_count()
        self.depth = self.shards * self.per


def masked_silu(z, state):
    value = silu(state).reshape(-1, z.wide, z.per)
    at = lax.broadcasted_iota(jnp.int32, value.shape, 1)
    at = at + (lax.axis_index("band") * z.columns - LAYERS)
    value = jnp.where((at >= 0) & (at < z.width), value, 0.0)
    return value.reshape(-1, z.per)


def split_kernel(z, latent_ref, hint_ref, *refs):
    outs, spread = refs[:-1], refs[-1]
    latent = latent_ref[...].astype(F32)
    control = (latent + hint_ref[...].astype(F32)).astype(BF16).astype(F32)
    edge = jnp.zeros((2, z.rows, LAYERS, z.per), F32)
    spread[:, :, :LAYERS] = edge
    spread[:, :, LAYERS + z.width :] = edge
    spread[0, :, LAYERS : LAYERS + z.width] = control
    spread[1, :, LAYERS : LAYERS + z.width] = latent
    band = lax.axis_index("band")
    for k, out in enumerate(outs):
        start = pl.multiple_of((band ^ k) * z.columns, 8)
        block = spread[:, :, pl.ds(start, z.wide)]
        out[...] = block.reshape(2, z.rows * z.wide, z.per).astype(BF16)


def join_kernel(z, *refs):
    blocks, (state_ref, act_ref) = refs[:-2], refs[-2:]
    band = lax.axis_index("band")
    size = z.rows * z.wide
    for k, block in enumerate(blocks):
        start = pl.multiple_of((band ^ k) * size, 16)
        for t in range(2):
            cells = block[t]
            state_ref[t, pl.ds(start, size)] = cells
            act_ref[t, pl.ds(start, size)] = masked_silu(z, cells.astype(F32)).astype(BF16)


def in_order(pieces):
    place = channel_place()
    step = 1
    while step < len(pieces):
        flip = (place & step) != 0
        pieces = [
            jnp.where(flip, pieces[j ^ step], pieces[j]) for j in range(len(pieces))
        ]
        step *= 2
    return pieces


def lay_out(z, a_ref, pieces, at=0):
    for j, piece in enumerate(in_order(pieces)):
        a_ref[:, at + j * z.per : at + (j + 1) * z.per] = piece


def convolve(z, cells, weight, left, right):
    n = z.cells
    left[8 : 8 + n] = lax.dot_general(cells, weight(0), TRANSPOSED, preferred_element_type=F32)
    right[8 : 8 + n] = lax.dot_general(cells, weight(2), TRANSPOSED, preferred_element_type=F32)
    middle = lax.dot_general(cells, weight(1), TRANSPOSED, preferred_element_type=F32)
    total = middle + left[7 : 7 + n] + right[9 : 9 + n]
    row = jnp.zeros((z.wide, z.per), F32)
    above = jnp.concatenate([row, total[: n - z.wide, : z.per]], 0)
    below = jnp.concatenate([total[z.wide :, 2 * z.per :], row], 0)
    return total[:, z.per : 2 * z.per] + above + below


def taps(z, w_ref, start, depth):
    def weight(j):
        return w_ref[:, j, :, start : start + depth].reshape(3 * z.per, depth)

    return weight


def clear_edges(z, left, right):
    left[0:8] = jnp.zeros((8, 3 * z.per), F32)
    right[8 + z.cells : 16 + z.cells] = jnp.zeros((8, 3 * z.per), F32)


def pair_kernel(z, *refs):
    n = z.shards
    blocks, refs = refs[:n], refs[n:]
    state_ref, w0, b0, w1, b1, new_ref, act_ref, a_ref, left, right = refs
    clear_edges(z, left, right)
    for t, (w_ref, b_ref) in enumerate(((w0, b0), (w1, b1))):
        lay_out(z, a_ref, [block[t] for block in blocks])
        result = convolve(z, a_ref[...], taps(z, w_ref, 0, z.depth), left, right)
        total = state_ref[t].astype(F32) + result + b_ref[...].astype(F32)
        new = total.astype(BF16)
        new_ref[t] = new
        act_ref[t] = masked_silu(z, new.astype(F32)).astype(BF16)


def decode_kernel(z, *refs):
    n = z.shards
    blocks, refs = refs[:n], refs[n:]
    state_ref, w_ref, b_ref, new_ref, act_ref, skip_ref, a_ref, left, right = refs
    clear_edges(z, left, right)
    lay_out(z, a_ref, [block[1] for block in blocks])
    lay_out(z, a_ref, [block[0] for block in blocks], z.depth)
    skip_ref[...] = a_ref[:, z.depth :]
    result = convolve(z, a_ref[...], taps(z, w_ref, 0, 2 * z.depth), left, right)
    total = state_ref[1].astype(F32) + result + b_ref[...].astype(F32)
    new = total.astype(BF16)
    new_ref[...] = new
    act_ref[...] = masked_silu(z, new.astype(F32)).astype(BF16)


def skip_kernel(z, skip_ref, w_ref, out_ref, left, right):
    clear_edges(z, left, right)
    out_ref[...] = convolve(z, skip_ref[...], taps(z, w_ref, z.depth, z.depth), left, right)


def last_kernel(z, *refs):
    n = z.shards
    blocks, refs = refs[:n], refs[n:]
    state_ref, skip_ref, w_ref, b_ref = refs[:4]
    outs, (a_ref, left, right, image) = refs[4 : 4 + z.bands], refs[4 + z.bands :]
    clear_edges(z, left, right)
    lay_out(z, a_ref, [block[...] for block in blocks])
    result = convolve(z, a_ref[...], taps(z, w_ref, 0, z.depth), left, right)
    total = state_ref[...].astype(F32) + (result + skip_ref[...]) + b_ref[...].astype(F32)
    image[...] = total.reshape(z.height, z.wide, z.per)
    band = lax.axis_index("band")
    for k, out in enumerate(outs):
        rows = image[pl.ds((band ^ k) * z.rows, z.rows), LAYERS : LAYERS + z.columns]
        out[...] = rows.astype(BF16)


def rows_kernel(z, *refs):
    blocks, (out_ref, image) = refs[:-2], refs[-2:]
    band = lax.axis_index("band")
    for k, block in enumerate(blocks):
        start = pl.multiple_of((band ^ k) * z.columns, 8)
        image[:, pl.ds(start, z.columns)] = block[...].astype(F32)
    out_ref[...] = image[...].astype(BF16)


def over_bands(blocks):
    return [blocks[0]] + [exchange(b, "band", k) for k, b in enumerate(blocks) if k]


def gather(cells):
    chips = [cells] + [exchange(cells, "section", k) for k in range(1, lax.axis_size("section"))]
    cores = range(1, lax.axis_size("chan"))
    pieces = []
    for chip in chips:
        pieces += [chip] + [exchange(chip, "chan", k) for k in cores]
    return pieces


def per_device(latent, control_hint, cw1, cb1, cw2, cb2, mw1, mb1, mw2, mb2, dw1, db1, dw2, db2):
    z = Sizes(latent)
    cb1, cb2, mb1, mb2, db1, db2 = [b.reshape(1, -1) for b in (cb1, cb2, mb1, mb2, db1, db2)]
    kernel = lambda f: functools.partial(f, z)
    edges = [pltpu.VMEM((z.cells + 16, 3 * z.per), F32)] * 2
    work = lambda parts: [pltpu.VMEM((z.cells, parts * z.depth), BF16)] + edges
    unit = 2 * 9 * z.cells * z.per * z.depth

    blocks = call(
        kernel(split_kernel),
        [sds((2, z.rows * z.wide, z.per))] * z.bands,
        latent,
        control_hint,
        scratch=[pltpu.VMEM((2, z.rows, z.width + 2 * LAYERS, z.per), F32)],
    )
    pair = sds((2, z.cells, z.per))
    single = sds((z.cells, z.per))
    state, act = call(kernel(join_kernel), [pair, pair], *over_bands(blocks))
    for weights in ((cw1, cb1, mw1, mb1), (cw2, cb2, mw2, mb2)):
        state, act = call(
            kernel(pair_kernel),
            [pair, pair],
            *gather(act),
            state,
            *weights,
            scratch=work(1),
            flops=2 * unit,
        )
    state, act, skip = call(
        kernel(decode_kernel),
        [single, single, sds((z.cells, z.depth))],
        *gather(act),
        state,
        dw1,
        db1,
        scratch=work(2),
        flops=2 * unit,
    )
    part = call(
        kernel(skip_kernel), sds((z.cells, z.per), F32), skip, dw2, scratch=edges, flops=unit
    )
    blocks = call(
        kernel(last_kernel),
        [sds((z.rows, z.columns, z.per))] * z.bands,
        *gather(act),
        state,
        part,
        dw2,
        db2,
        scratch=work(1) + [pltpu.VMEM((z.height, z.wide, z.per), F32)],
        flops=unit,
    )
    return call(
        kernel(rows_kernel),
        sds((z.rows, z.width, z.per)),
        *over_bands(blocks),
        scratch=[pltpu.VMEM((z.rows, z.width, z.per), F32)],
    )


def solution(mesh):
    image = P(("groups", "band"), None, CHANNEL_AXES)
    kernel = P(None, None, CHANNEL_AXES, None)
    bias = P(CHANNEL_AXES)
    return jax.shard_map(
        per_device,
        mesh=mesh,
        in_specs=(image, image) + (kernel, bias) * 6,
        out_specs=image,
        check_vma=False,
    )
```

time: 149 us -> 75.1 us (0.50)
  blocking collectives: 76.9 us -> 0 us
  waiting for transfers between devices: 8.54 us -> 41.8 us
  local copies, waits for them, and re-layouts: 36.3 us -> 7.08 us
  starting transfers between devices: 6.35 us -> 16.9 us
  matrix products: 10.5 us -> 0 us
  Pallas kernels: 0 us -> 8.85 us
  other arithmetic: 8.73 us -> 0 us
    all_gather x4 -> x0, blocking collectives: 68 us -> none  [gather_channels(): return lax.all_gather(cells, CHANNEL_AXES, axis=cells.ndim - 1, tiled=True)]
    ppermute x0 -> x18, waiting for transfers between devices: none -> 41.8 us  [exchange(): return lax.ppermute(cells, axis, [(i, i ^ distance) for i in range(count)])]
    ppermute x0 -> x18, starting transfers between devices: none -> 16.9 us  [exchange(): return lax.ppermute(cells, axis, [(i, i ^ distance) for i in range(count)])]
    unnamed x64 -> x22, local copies, waits for them, and re-layouts: 20.6 us -> 5 us
    conv_general_dilated x6 -> x0, matrix products: 10.5 us -> none  [convolve(): lax.conv_general_dilated(cells[None], weights, (1, 1), ((1, 1), (0, 0)),...]
    all_to_all x1 -> x0, blocking collectives: 8.92 us -> none  [columns_to_rows(): blocks = lax.all_to_all(blocks, 'band', 0, 0)]
    pallas_call x0 -> x8, Pallas kernels: none -> 8.85 us  [call(): pl.pallas_call(kernel, out_shape=outs, in_specs=whole(len(args)), out_spe...]
    all_to_all x1 -> x0, waiting for transfers between devices: 8.54 us -> none  [rows_to_columns(): blocks = lax.all_to_all(blocks, 'band', 0, 0)]
  transfers between devices with their start and end apart: 1 -> 18, of which waited for: 1 -> 11; matrix products, arithmetic and copies ran while one was open for 1% -> 2% of each run, Pallas kernels for 0% -> 2%
where the time goes in v2:
time: 75.1 us; the launch traced here: 74.8 us
  waiting for transfers between devices  41.8 us (56%)
  starting transfers between devices  16.9 us (23%)
  Pallas kernels  8.85 us (12%)
  local copies, waits for them, and re-layouts  7.08 us (9%)
    ppermute x18, waiting for transfers between devices, exchange(): return lax.ppermute(cells, axis, [(i, i ^ distance) for i in range(count)])  41.8 us
    ppermute x18, starting transfers between devices, exchange(): return lax.ppermute(cells, axis, [(i, i ^ distance) for i in range(count)])  16.9 us
    pallas_call x8, Pallas kernels, call(): pl.pallas_call(kernel, out_shape=outs, in_specs=whole(len(args)), out_spe...  8.85 us
    unnamed x22, local copies, waits for them, and re-layouts  5 us
  transfers between devices with their start and end apart: 18, of which 11 were waited for; matrix products, arithmetic and copies ran while one was open for 2% of the time, Pallas kernels for 2%

profile of v2, /device:TPU:0, one launch (start us, length us, event | category | flops | bytes accessed | tf_op | source)
XLA Modules:
  0.0 74.8 jit_solution(13752031694314101076)
XLA Ops:
  0.0 1.0 %copy.15.latent_ref = bf16[2,128,160]{2,1,0:T(8,128)(2,1)S(1)} copy(bf16[2,128,160]{1,2,0:T(8,128)(2,1)} %param.14) | data formatting | bytes 163840 | tf_op args[0]
  1.0 1.0 %copy.16.hint_ref = bf16[2,128,160]{2,1,0:T(8,128)(2,1)S(1)} copy(bf16[2,128,160]{1,2,0:T(8,128)(2,1)} %param.15) | data formatting | bytes 163840 | tf_op args[1]
  2.0 0.1 shard_map.136
  2.1 3.1 %collective-permute-start = (bf16[2,80,160]{2,1,0:T(8,128)(2,1)S(1)}, bf16[2,80,160]{2,1,0:T(8,128)(2,1)S(1)}, u32[]{:S(2)}, u32[]{:S(2)}) collective-permute-start(bf16[2,80,160]{2,1,0:T(8,128)(2,1)S(1)} %get-tuple-element.23), channel_id=1, source_target_pairs={{0,2},{2,0},{4,6},{6,4},{1,3},{3,1},{5,7},{7,5},{8,10},{10,8},{12,... | collective-permute-start | bytes 153608 | tf_op jit(solution)/shard_map/ppermute | solution.py:23
  5.3 2.6 %collective-permute-start.1 = (bf16[2,80,160]{2,1,0:T(8,128)(2,1)S(1)}, bf16[2,80,160]{2,1,0:T(8,128)(2,1)S(1)}, u32[]{:S(2)}, u32[]{:S(2)}) collective-permute-start(bf16[2,80,160]{2,1,0:T(8,128)(2,1)S(1)} %get-tuple-element.24), channel_id=1, source_target_pairs={{0,4},{2,6},{4,0},{6,2},{1,5},{3,7},{5,1},{7,3},{8,12},{10,14},{12... | collective-permute-start | bytes 153608 | tf_op jit(solution)/shard_map/ppermute | solution.py:23
  7.8 0.0 collective-permute-start.2
  7.8 0.0 collective-permute-done.refs_1_
  7.8 6.6 %collective-permute-done.1.refs_2_ = bf16[2,80,160]{2,1,0:T(8,128)(2,1)S(1)} collective-permute-done((bf16[2,80,160]{2,1,0:T(8,128)(2,1)S(1)}, bf16[2,80,160]{2,1,0:T(8,128)(2,1)S(1)}, u32[]{:S(2)}, u32[]{:S(2)}) %collective-permute-start.1) | collective-permute-done | bytes 51232 | tf_op jit(solution)/shard_map/ppermute | solution.py:23
  14.4 0.0 collective-permute-done.2.refs_3_
  14.4 0.2 shard_map.137
  14.6 1.6 %collective-permute-start.4 = (bf16[2,320,160]{2,1,0:T(8,128)(2,1)S(1)}, bf16[2,320,160]{2,1,0:T(8,128)(2,1)S(1)}, u32[]{:S(2)}, u32[]{:S(2)}) collective-permute-start(bf16[2,320,160]{2,1,0:T(8,128)(2,1)S(1)} %get-tuple-element.26.refs_0_), channel_id=1, source_target_pairs={{0,8},{8,0},{1,9},{9,1},{2,10},{10,2},{3,11},{11,3},{4,12},{12,4},... | collective-permute-start | bytes 614408 | tf_op jit(solution)/shard_map/ppermute | solution.py:23
  16.2 0.0 collective-permute-start.3
  16.2 6.0 %collective-permute-done.4.refs_2_ = bf16[2,320,160]{2,1,0:T(8,128)(2,1)S(1)} collective-permute-done((bf16[2,320,160]{2,1,0:T(8,128)(2,1)S(1)}, bf16[2,320,160]{2,1,0:T(8,128)(2,1)S(1)}, u32[]{:S(2)}, u32[]{:S(2)}) %collective-permute-start.4) | collective-permute-done | bytes 204832 | tf_op jit(solution)/shard_map/ppermute | solution.py:23
  22.2 0.0 collective-permute-start.5
  22.2 0.7 reshape.18.refs_6_
  22.8 0.7 reshape.19.refs_8_
  23.5 0.0 collective-permute-done.3.refs_1_
  23.5 0.3 collective-permute-done.5.refs_3_
  23.8 1.5 %copy-done.2 = bf16[3,3,160,640]{3,2,1,0:T(8,128)(2,1)S(1)} copy-done((bf16[3,3,160,640]{3,2,1,0:T(8,128)(2,1)S(1)}, bf16[3,3,160,640]{3,2,1,0:T(8,128)(2,1)}, u32[]{:S(2)}) %copy-start.2) | copy-done | bytes 1843224
  25.3 1.5 %copy-done.3 = bf16[3,3,160,640]{3,2,1,0:T(8,128)(2,1)S(1)} copy-done((bf16[3,3,160,640]{3,2,1,0:T(8,128)(2,1)S(1)}, bf16[3,3,160,640]{3,2,1,0:T(8,128)(2,1)}, u32[]{:S(2)}) %copy-start.3) | copy-done | bytes 1843224
  26.8 2.1 %shard_map.138 = (bf16[2,320,160]{2,1,0:T(8,128)(2,1)S(1)}, bf16[2,320,160]{2,1,0:T(8,128)(2,1)S(1)}) custom-call(bf16[2,320,160]{2,1,0:T(8,128)(2,1)S(1)} %get-tuple-element.26.refs_0_, bf16[2,320,160]{2,1,0:T(8,128)(2,1)S(1)} %collective-permute-done.3.refs_1_, bf16[2,320,160]{2,1,0:T(8,128)(2,1)S(1)} %collective-permute-done.4.refs_2_, ...), custom_call_target="tpu_custom_call" | custom-call | flops 1179648000 | bytes 5120640 | tf_op jit(solution)/shard_map/pallas_call | solution.py:42
  28.9 1.6 %collective-permute-start.7 = (bf16[2,320,160]{2,1,0:T(8,128)(2,1)S(1)}, bf16[2,320,160]{2,1,0:T(8,128)(2,1)S(1)}, u32[]{:S(2)}, u32[]{:S(2)}) collective-permute-start(bf16[2,320,160]{2,1,0:T(8,128)(2,1)S(1)} %get-tuple-element.28.refs_0_), channel_id=1, source_target_pairs={{0,8},{8,0},{1,9},{9,1},{2,10},{10,2},{3,11},{11,3},{4,12},{12,4},... | collective-permute-start | bytes 614408 | tf_op jit(solution)/shard_map/ppermute | solution.py:23
  30.5 0.0 collective-permute-start.6
  30.5 8.3 %collective-permute-done.7.refs_2_ = bf16[2,320,160]{2,1,0:T(8,128)(2,1)S(1)} collective-permute-done((bf16[2,320,160]{2,1,0:T(8,128)(2,1)S(1)}, bf16[2,320,160]{2,1,0:T(8,128)(2,1)S(1)}, u32[]{:S(2)}, u32[]{:S(2)}) %collective-permute-start.7) | collective-permute-done | bytes 204832 | tf_op jit(solution)/shard_map/ppermute | solution.py:23
  38.8 0.0 collective-permute-start.8
  38.9 0.0 collective-permute-done.6.refs_1_
  38.9 1.6 %collective-permute-done.8.refs_3_ = bf16[2,320,160]{2,1,0:T(8,128)(2,1)S(1)} collective-permute-done((bf16[2,320,160]{2,1,0:T(8,128)(2,1)S(1)}, bf16[2,320,160]{2,1,0:T(8,128)(2,1)S(1)}, u32[]{:S(2)}, u32[]{:S(2)}) %collective-permute-start.8) | collective-permute-done | bytes 204832 | tf_op jit(solution)/shard_map/ppermute | solution.py:23
  40.5 2.1 %shard_map.139 = (bf16[2,320,160]{2,1,0:T(8,128)(2,1)S(1)}, bf16[2,320,160]{2,1,0:T(8,128)(2,1)S(1)}) custom-call(bf16[2,320,160]{2,1,0:T(8,128)(2,1)S(1)} %get-tuple-element.28.refs_0_, bf16[2,320,160]{2,1,0:T(8,128)(2,1)S(1)} %collective-permute-done.6.refs_1_, bf16[2,320,160]{2,1,0:T(8,128)(2,1)S(1)} %collective-permute-done.7.refs_2_, ...), custom_call_target="tpu_custom_call" | custom-call | flops 1179648000 | bytes 5120640 | tf_op jit(solution)/shard_map/pallas_call | solution.py:42
  42.6 1.6 %collective-permute-start.10 = (bf16[2,320,160]{2,1,0:T(8,128)(2,1)S(1)}, bf16[2,320,160]{2,1,0:T(8,128)(2,1)S(1)}, u32[]{:S(2)}, u32[]{:S(2)}) collective-permute-start(bf16[2,320,160]{2,1,0:T(8,128)(2,1)S(1)} %get-tuple-element.30.refs_0_), channel_id=1, source_target_pairs={{0,8},{8,0},{1,9},{9,1},{2,10},{10,2},{3,11},{11,3},{4,12},{12,4},... | collective-permute-start | bytes 614408 | tf_op jit(solution)/shard_map/ppermute | solution.py:23
  44.1 0.0 collective-permute-start.9
  44.1 8.3 %collective-permute-done.10.refs_2_ = bf16[2,320,160]{2,1,0:T(8,128)(2,1)S(1)} collective-permute-done((bf16[2,320,160]{2,1,0:T(8,128)(2,1)S(1)}, bf16[2,320,160]{2,1,0:T(8,128)(2,1)S(1)}, u32[]{:S(2)}, u32[]{:S(2)}) %collective-permute-start.10) | collective-permute-done | bytes 204832 | tf_op jit(solution)/shard_map/ppermute | solution.py:23
  52.4 0.0 collective-permute-start.11
  52.4 0.0 collective-permute-done.9.refs_1_
  52.4 1.6 %collective-permute-done.11.refs_3_ = bf16[2,320,160]{2,1,0:T(8,128)(2,1)S(1)} collective-permute-done((bf16[2,320,160]{2,1,0:T(8,128)(2,1)S(1)}, bf16[2,320,160]{2,1,0:T(8,128)(2,1)S(1)}, u32[]{:S(2)}, u32[]{:S(2)}) %collective-permute-start.11) | collective-permute-done | bytes 204832 | tf_op jit(solution)/shard_map/ppermute | solution.py:23
  54.0 1.9 %shard_map.140 = (bf16[320,160]{1,0:T(8,128)(2,1)S(1)}, bf16[320,160]{1,0:T(8,128)(2,1)S(1)}, bf16[320,640]{1,0:T(8,128)(2,1)S(1)}) custom-call(bf16[2,320,160]{2,1,0:T(8,128)(2,1)S(1)} %get-tuple-element.30.refs_0_, bf16[2,320,160]{2,1,0:T(8,128)(2,1)S(1)} %collective-permute-done.9.refs_1_, bf16[2,320,160]{2,1,0:T(8,128)(2,1)S(1)} %collective-permute-done.10.refs_2_, ...), custom_call_target="tpu_custom_call" | custom-call | flops 1179648000 | bytes 5325120 | tf_op jit(solution)/shard_map/pallas_call | solution.py:42
  55.9 1.6 %collective-permute-start.13 = (bf16[320,160]{1,0:T(8,128)(2,1)S(1)}, bf16[320,160]{1,0:T(8,128)(2,1)S(1)}, u32[]{:S(2)}, u32[]{:S(2)}) collective-permute-start(bf16[320,160]{1,0:T(8,128)(2,1)S(1)} %get-tuple-element.32.refs_0_), channel_id=1, source_target_pairs={{0,8},{8,0},{1,9},{9,1},{2,10},{10,2},{3,11},{11,3},{4,12},{12,4},... | collective-permute-start | bytes 307208 | tf_op jit(solution)/shard_map/ppermute | solution.py:23
  57.4 0.0 collective-permute-start.12
  57.4 4.7 %collective-permute-done.13.refs_2_ = bf16[320,160]{1,0:T(8,128)(2,1)S(1)} collective-permute-done((bf16[320,160]{1,0:T(8,128)(2,1)S(1)}, bf16[320,160]{1,0:T(8,128)(2,1)S(1)}, u32[]{:S(2)}, u32[]{:S(2)}) %collective-permute-start.13) | collective-permute-done | bytes 102432 | tf_op jit(solution)/shard_map/ppermute | solution.py:23
  62.2 0.0 collective-permute-start.14
  62.2 1.2 %shard_map.141.refs_5_ = f32[320,160]{1,0:T(8,128)S(1)} custom-call(bf16[320,640]{1,0:T(8,128)(2,1)S(1)} %get-tuple-element.34.skip_ref, bf16[3,3,160,1280]{3,2,1,0:T(8,128)(2,1)S(1)} %copy-done), custom_call_target="tpu_custom_call" | custom-call | flops 589824000 | bytes 4300800 | tf_op jit(solution)/shard_map/pallas_call | solution.py:42
  63.4 0.2 collective-permute-done.14.refs_3_
  63.6 1.3 %shard_map.142 = (bf16[2,32,160]{2,1,0:T(8,128)(2,1)S(1)}, bf16[2,32,160]{2,1,0:T(8,128)(2,1)S(1)}, bf16[2,32,160]{2,1,0:T(8,128)(2,1)S(1)}, bf16[2,32,160]{2,1,0:T(8,128)(2,1)S(1)}) custom-call(bf16[320,160]{1,0:T(8,128)(2,1)S(1)} %get-tuple-element.32.refs_0_, bf16[320,160]{1,0:T(8,128)(2,1)S(1)} %collective-permute-done.12.refs_1_, ...), custom_call_target="tpu_custom_call" | custom-call | flops 589824000 | bytes 4485440 | tf_op jit(solution)/shard_map/pallas_call | solution.py:42
  64.9 2.5 %collective-permute-start.15 = (bf16[2,32,160]{2,1,0:T(8,128)(2,1)S(1)}, bf16[2,32,160]{2,1,0:T(8,128)(2,1)S(1)}, u32[]{:S(2)}, u32[]{:S(2)}) collective-permute-start(bf16[2,32,160]{2,1,0:T(8,128)(2,1)S(1)} %get-tuple-element.36), channel_id=1, source_target_pairs={{0,2},{2,0},{4,6},{6,4},{1,3},{3,1},{5,7},{7,5},{8,10},{10,8},{12,... | collective-permute-start | bytes 61448 | tf_op jit(solution)/shard_map/ppermute | solution.py:23
  67.4 0.9 %collective-permute-start.16 = (bf16[2,32,160]{2,1,0:T(8,128)(2,1)S(1)}, bf16[2,32,160]{2,1,0:T(8,128)(2,1)S(1)}, u32[]{:S(2)}, u32[]{:S(2)}) collective-permute-start(bf16[2,32,160]{2,1,0:T(8,128)(2,1)S(1)} %get-tuple-element.37), channel_id=1, source_target_pairs={{0,4},{2,6},{4,0},{6,2},{1,5},{3,7},{5,1},{7,3},{8,12},{10,14},{12... | collective-permute-start | bytes 61448 | tf_op jit(solution)/shard_map/ppermute | solution.py:23
  68.3 1.5 %collective-permute-start.17 = (bf16[2,32,160]{2,1,0:T(8,128)(2,1)S(1)}, bf16[2,32,160]{2,1,0:T(8,128)(2,1)S(1)}, u32[]{:S(2)}, u32[]{:S(2)}) collective-permute-start(bf16[2,32,160]{2,1,0:T(8,128)(2,1)S(1)} %get-tuple-element.38), channel_id=1, source_target_pairs={{0,6},{2,4},{4,2},{6,0},{1,7},{3,5},{5,3},{7,1},{8,14},{10,12},{12... | collective-permute-start | bytes 61448 | tf_op jit(solution)/shard_map/ppermute | solution.py:23
  69.8 2.8 %collective-permute-done.16.refs_2_ = bf16[2,32,160]{2,1,0:T(8,128)(2,1)S(1)} collective-permute-done((bf16[2,32,160]{2,1,0:T(8,128)(2,1)S(1)}, bf16[2,32,160]{2,1,0:T(8,128)(2,1)S(1)}, u32[]{:S(2)}, u32[]{:S(2)}) %collective-permute-start.16) | collective-permute-done | bytes 20512 | tf_op jit(solution)/shard_map/ppermute | solution.py:23
  72.6 1.4 %collective-permute-done.17.refs_3_ = bf16[2,32,160]{2,1,0:T(8,128)(2,1)S(1)} collective-permute-done((bf16[2,32,160]{2,1,0:T(8,128)(2,1)S(1)}, bf16[2,32,160]{2,1,0:T(8,128)(2,1)S(1)}, u32[]{:S(2)}, u32[]{:S(2)}) %collective-permute-start.17) | collective-permute-done | bytes 20512 | tf_op jit(solution)/shard_map/ppermute | solution.py:23
  74.0 0.7 copy.17
  (25 shorter events, 0.1 us)
Async XLA Ops:
  2.1 5.7 %collective-permute-start = (bf16[2,80,160]{2,1,0:T(8,128)(2,1)S(1)}, bf16[2,80,160]{2,1,0:T(8,128)(2,1)S(1)}, u32[]{:S(2)}, u32[]{:S(2)}) collective-permute-start(bf16[2,80,160]{2,1,0:T(8,128)(2,1)S(1)} %get-tuple-element.23), channel_id=1, source_target_pairs={{0,2},{2,0},{4,6},{6,4},{1,3},{3,1},{5,7},{7,5},{8,10},{10,8},{12,... | collective-permute-start | bytes 153608 | tf_op jit(solution)/shard_map/ppermute | solution.py:23
  5.3 9.2 %collective-permute-start.1 = (bf16[2,80,160]{2,1,0:T(8,128)(2,1)S(1)}, bf16[2,80,160]{2,1,0:T(8,128)(2,1)S(1)}, u32[]{:S(2)}, u32[]{:S(2)}) collective-permute-start(bf16[2,80,160]{2,1,0:T(8,128)(2,1)S(1)} %get-tuple-element.24), channel_id=1, source_target_pairs={{0,4},{2,6},{4,0},{6,2},{1,5},{3,7},{5,1},{7,3},{8,12},{10,14},{12... | collective-permute-start | bytes 153608 | tf_op jit(solution)/shard_map/ppermute | solution.py:23
  7.8 6.6 %collective-permute-start.2 = (bf16[2,80,160]{2,1,0:T(8,128)(2,1)S(1)}, bf16[2,80,160]{2,1,0:T(8,128)(2,1)S(1)}, u32[]{:S(2)}, u32[]{:S(2)}) collective-permute-start(bf16[2,80,160]{2,1,0:T(8,128)(2,1)S(1)} %get-tuple-element.25), channel_id=1, source_target_pairs={{0,6},{2,4},{4,2},{6,0},{1,7},{3,5},{5,3},{7,1},{8,14},{10,12},{12... | collective-permute-start | bytes 153608 | tf_op jit(solution)/shard_map/ppermute | solution.py:23
  14.6 7.6 %collective-permute-start.4 = (bf16[2,320,160]{2,1,0:T(8,128)(2,1)S(1)}, bf16[2,320,160]{2,1,0:T(8,128)(2,1)S(1)}, u32[]{:S(2)}, u32[]{:S(2)}) collective-permute-start(bf16[2,320,160]{2,1,0:T(8,128)(2,1)S(1)} %get-tuple-element.26.refs_0_), channel_id=1, source_target_pairs={{0,8},{8,0},{1,9},{9,1},{2,10},{10,2},{3,11},{11,3},{4,12},{12,4},... | collective-permute-start | bytes 614408 | tf_op jit(solution)/shard_map/ppermute | solution.py:23
  16.2 7.3 %collective-permute-start.3 = (bf16[2,320,160]{2,1,0:T(8,128)(2,1)S(1)}, bf16[2,320,160]{2,1,0:T(8,128)(2,1)S(1)}, u32[]{:S(2)}, u32[]{:S(2)}) collective-permute-start(bf16[2,320,160]{2,1,0:T(8,128)(2,1)S(1)} %get-tuple-element.26.refs_0_), channel_id=1, source_target_pairs={{0,1},{1,0},{2,3},{3,2},{4,5},{5,4},{6,7},{7,6},{8,9},{9,8},{10,11... | collective-permute-start | bytes 614408 | tf_op jit(solution)/shard_map/ppermute | solution.py:23
  22.2 1.6 %collective-permute-start.5 = (bf16[2,320,160]{2,1,0:T(8,128)(2,1)S(1)}, bf16[2,320,160]{2,1,0:T(8,128)(2,1)S(1)}, u32[]{:S(2)}, u32[]{:S(2)}) collective-permute-start(bf16[2,320,160]{2,1,0:T(8,128)(2,1)S(1)} %collective-permute-done.4.refs_2_), channel_id=1, source_target_pairs={{0,1},{1,0},{2,3},{3,2},{4,5},{5,4},{6,7},{7,6},{8,9},{9,8},{10,11... | collective-permute-start | bytes 614408 | tf_op jit(solution)/shard_map/ppermute | solution.py:23
  23.8 1.5 %copy-start.2 = (bf16[3,3,160,640]{3,2,1,0:T(8,128)(2,1)S(1)}, bf16[3,3,160,640]{3,2,1,0:T(8,128)(2,1)}, u32[]{:S(2)}) copy-start(bf16[3,3,160,640]{3,2,1,0:T(8,128)(2,1)} %refs_5_.3) | copy-start | bytes 5529604
  25.3 1.5 %copy-start.3 = (bf16[3,3,160,640]{3,2,1,0:T(8,128)(2,1)S(1)}, bf16[3,3,160,640]{3,2,1,0:T(8,128)(2,1)}, u32[]{:S(2)}) copy-start(bf16[3,3,160,640]{3,2,1,0:T(8,128)(2,1)} %refs_7_.2) | copy-start | bytes 5529604
  26.8 12.0 %copy-start.6 = (bf16[160]{0:T(256)(128)(2,1)S(1)}, bf16[160]{0:T(256)(128)(2,1)}, u32[]{:S(2)}) copy-start(bf16[160]{0:T(256)(128)(2,1)} %param.19) | copy-start | bytes 964
  26.8 12.0 %copy-start.7 = (bf16[160]{0:T(256)(128)(2,1)S(1)}, bf16[160]{0:T(256)(128)(2,1)}, u32[]{:S(2)}) copy-start(bf16[160]{0:T(256)(128)(2,1)} %param.23) | copy-start | bytes 964
  26.8 13.6 %copy-start.4 = (bf16[3,3,160,640]{3,2,1,0:T(8,128)(2,1)S(1)}, bf16[3,3,160,640]{3,2,1,0:T(8,128)(2,1)}, u32[]{:S(2)}) copy-start(bf16[3,3,160,640]{3,2,1,0:T(8,128)(2,1)} %refs_5_.4) | copy-start | bytes 5529604
  26.8 13.6 %copy-start.5 = (bf16[3,3,160,640]{3,2,1,0:T(8,128)(2,1)S(1)}, bf16[3,3,160,640]{3,2,1,0:T(8,128)(2,1)}, u32[]{:S(2)}) copy-start(bf16[3,3,160,640]{3,2,1,0:T(8,128)(2,1)} %refs_7_.3) | copy-start | bytes 5529604
  28.9 9.9 %collective-permute-start.7 = (bf16[2,320,160]{2,1,0:T(8,128)(2,1)S(1)}, bf16[2,320,160]{2,1,0:T(8,128)(2,1)S(1)}, u32[]{:S(2)}, u32[]{:S(2)}) collective-permute-start(bf16[2,320,160]{2,1,0:T(8,128)(2,1)S(1)} %get-tuple-element.28.refs_0_), channel_id=1, source_target_pairs={{0,8},{8,0},{1,9},{9,1},{2,10},{10,2},{3,11},{11,3},{4,12},{12,4},... | collective-permute-start | bytes 614408 | tf_op jit(solution)/shard_map/ppermute | solution.py:23
  30.5 8.4 %collective-permute-start.6 = (bf16[2,320,160]{2,1,0:T(8,128)(2,1)S(1)}, bf16[2,320,160]{2,1,0:T(8,128)(2,1)S(1)}, u32[]{:S(2)}, u32[]{:S(2)}) collective-permute-start(bf16[2,320,160]{2,1,0:T(8,128)(2,1)S(1)} %get-tuple-element.28.refs_0_), channel_id=1, source_target_pairs={{0,1},{1,0},{2,3},{3,2},{4,5},{5,4},{6,7},{7,6},{8,9},{9,8},{10,11... | collective-permute-start | bytes 614408 | tf_op jit(solution)/shard_map/ppermute | solution.py:23
  38.8 1.6 %collective-permute-start.8 = (bf16[2,320,160]{2,1,0:T(8,128)(2,1)S(1)}, bf16[2,320,160]{2,1,0:T(8,128)(2,1)S(1)}, u32[]{:S(2)}, u32[]{:S(2)}) collective-permute-start(bf16[2,320,160]{2,1,0:T(8,128)(2,1)S(1)} %collective-permute-done.7.refs_2_), channel_id=1, source_target_pairs={{0,1},{1,0},{2,3},{3,2},{4,5},{5,4},{6,7},{7,6},{8,9},{9,8},{10,11... | collective-permute-start | bytes 614408 | tf_op jit(solution)/shard_map/ppermute | solution.py:23
  40.5 11.9 %copy-start.8 = (bf16[160]{0:T(256)(128)(2,1)S(1)}, bf16[160]{0:T(256)(128)(2,1)}, u32[]{:S(2)}) copy-start(bf16[160]{0:T(256)(128)(2,1)} %param.25) | copy-start | bytes 964
  40.5 13.6 %copy-start.1 = (bf16[3,3,160,1280]{3,2,1,0:T(8,128)(2,1)S(1)}, bf16[3,3,160,1280]{3,2,1,0:T(8,128)(2,1)}, u32[]{:S(2)}) copy-start(bf16[3,3,160,1280]{3,2,1,0:T(8,128)(2,1)} %refs_5_.5) | copy-start | bytes 11059204
  42.6 9.8 %collective-permute-start.10 = (bf16[2,320,160]{2,1,0:T(8,128)(2,1)S(1)}, bf16[2,320,160]{2,1,0:T(8,128)(2,1)S(1)}, u32[]{:S(2)}, u32[]{:S(2)}) collective-permute-start(bf16[2,320,160]{2,1,0:T(8,128)(2,1)S(1)} %get-tuple-element.30.refs_0_), channel_id=1, source_target_pairs={{0,8},{8,0},{1,9},{9,1},{2,10},{10,2},{3,11},{11,3},{4,12},{12,4},... | collective-permute-start | bytes 614408 | tf_op jit(solution)/shard_map/ppermute | solution.py:23
  44.1 8.3 %collective-permute-start.9 = (bf16[2,320,160]{2,1,0:T(8,128)(2,1)S(1)}, bf16[2,320,160]{2,1,0:T(8,128)(2,1)S(1)}, u32[]{:S(2)}, u32[]{:S(2)}) collective-permute-start(bf16[2,320,160]{2,1,0:T(8,128)(2,1)S(1)} %get-tuple-element.30.refs_0_), channel_id=1, source_target_pairs={{0,1},{1,0},{2,3},{3,2},{4,5},{5,4},{6,7},{7,6},{8,9},{9,8},{10,11... | collective-permute-start | bytes 614408 | tf_op jit(solution)/shard_map/ppermute | solution.py:23
  52.4 1.6 %collective-permute-start.11 = (bf16[2,320,160]{2,1,0:T(8,128)(2,1)S(1)}, bf16[2,320,160]{2,1,0:T(8,128)(2,1)S(1)}, u32[]{:S(2)}, u32[]{:S(2)}) collective-permute-start(bf16[2,320,160]{2,1,0:T(8,128)(2,1)S(1)} %collective-permute-done.10.refs_2_), channel_id=1, source_target_pairs={{0,1},{1,0},{2,3},{3,2},{4,5},{5,4},{6,7},{7,6},{8,9},{9,8},{10,11... | collective-permute-start | bytes 614408 | tf_op jit(solution)/shard_map/ppermute | solution.py:23
  54.0 8.2 %copy-start.9 = (bf16[160]{0:T(256)(128)(2,1)S(1)}, bf16[160]{0:T(256)(128)(2,1)}, u32[]{:S(2)}) copy-start(bf16[160]{0:T(256)(128)(2,1)} %param.27) | copy-start | bytes 964
  54.0 8.2 %copy-start = (bf16[3,3,160,1280]{3,2,1,0:T(8,128)(2,1)S(1)}, bf16[3,3,160,1280]{3,2,1,0:T(8,128)(2,1)}, u32[]{:S(2)}) copy-start(bf16[3,3,160,1280]{3,2,1,0:T(8,128)(2,1)} %refs_6_.1) | copy-start | bytes 11059204
  55.9 6.3 %collective-permute-start.13 = (bf16[320,160]{1,0:T(8,128)(2,1)S(1)}, bf16[320,160]{1,0:T(8,128)(2,1)S(1)}, u32[]{:S(2)}, u32[]{:S(2)}) collective-permute-start(bf16[320,160]{1,0:T(8,128)(2,1)S(1)} %get-tuple-element.32.refs_0_), channel_id=1, source_target_pairs={{0,8},{8,0},{1,9},{9,1},{2,10},{10,2},{3,11},{11,3},{4,12},{12,4},... | collective-permute-start | bytes 307208 | tf_op jit(solution)/shard_map/ppermute | solution.py:23
  57.4 6.0 %collective-permute-start.12 = (bf16[320,160]{1,0:T(8,128)(2,1)S(1)}, bf16[320,160]{1,0:T(8,128)(2,1)S(1)}, u32[]{:S(2)}, u32[]{:S(2)}) collective-permute-start(bf16[320,160]{1,0:T(8,128)(2,1)S(1)} %get-tuple-element.32.refs_0_), channel_id=1, source_target_pairs={{0,1},{1,0},{2,3},{3,2},{4,5},{5,4},{6,7},{7,6},{8,9},{9,8},{10,11... | collective-permute-start | bytes 307208 | tf_op jit(solution)/shard_map/ppermute | solution.py:23
  62.2 1.4 %collective-permute-start.14 = (bf16[320,160]{1,0:T(8,128)(2,1)S(1)}, bf16[320,160]{1,0:T(8,128)(2,1)S(1)}, u32[]{:S(2)}, u32[]{:S(2)}) collective-permute-start(bf16[320,160]{1,0:T(8,128)(2,1)S(1)} %collective-permute-done.13.refs_2_), channel_id=1, source_target_pairs={{0,1},{1,0},{2,3},{3,2},{4,5},{5,4},{6,7},{7,6},{8,9},{9,8},{10,11... | collective-permute-start | bytes 307208 | tf_op jit(solution)/shard_map/ppermute | solution.py:23
  64.9 4.9 %collective-permute-start.15 = (bf16[2,32,160]{2,1,0:T(8,128)(2,1)S(1)}, bf16[2,32,160]{2,1,0:T(8,128)(2,1)S(1)}, u32[]{:S(2)}, u32[]{:S(2)}) collective-permute-start(bf16[2,32,160]{2,1,0:T(8,128)(2,1)S(1)} %get-tuple-element.36), channel_id=1, source_target_pairs={{0,2},{2,0},{4,6},{6,4},{1,3},{3,1},{5,7},{7,5},{8,10},{10,8},{12,... | collective-permute-start | bytes 61448 | tf_op jit(solution)/shard_map/ppermute | solution.py:23
  67.4 5.2 %collective-permute-start.16 = (bf16[2,32,160]{2,1,0:T(8,128)(2,1)S(1)}, bf16[2,32,160]{2,1,0:T(8,128)(2,1)S(1)}, u32[]{:S(2)}, u32[]{:S(2)}) collective-permute-start(bf16[2,32,160]{2,1,0:T(8,128)(2,1)S(1)} %get-tuple-element.37), channel_id=1, source_target_pairs={{0,4},{2,6},{4,0},{6,2},{1,5},{3,7},{5,1},{7,3},{8,12},{10,14},{12... | collective-permute-start | bytes 61448 | tf_op jit(solution)/shard_map/ppermute | solution.py:23
  68.3 5.7 %collective-permute-start.17 = (bf16[2,32,160]{2,1,0:T(8,128)(2,1)S(1)}, bf16[2,32,160]{2,1,0:T(8,128)(2,1)S(1)}, u32[]{:S(2)}, u32[]{:S(2)}) collective-permute-start(bf16[2,32,160]{2,1,0:T(8,128)(2,1)S(1)} %get-tuple-element.38), channel_id=1, source_target_pairs={{0,6},{2,4},{4,2},{6,0},{1,7},{3,5},{5,3},{7,1},{8,14},{10,12},{12... | collective-permute-start | bytes 61448 | tf_op jit(solution)/shard_map/ppermute | solution.py:23

commit v3 on v2

--- a/solution.py
+++ b/solution.py
@@ -7,7 +7,9 @@
 from jax.experimental.pallas import tpu as pltpu
 from jax.sharding import PartitionSpec as P
 
+
 LAYERS = 4
+LANES = 128
 CHANNEL_AXES = ("section", "chan")
 F32 = jnp.float32
 BF16 = jnp.bfloat16
@@ -63,7 +65,46 @@
         self.height = self.rows * self.bands
         self.cells = self.height * self.wide
         self.shards = channel_count()
+        self.rest = self.per % LANES
+        self.groups = LANES // self.rest if self.rest and LANES % self.rest == 0 else 0
+        if self.per < LANES:
+            self.groups = 0
         self.depth = self.shards * self.per
+
+
+    def dense(self, cells):
+        return self.groups and cells % (8 * self.groups) == 0
+
+    def packed(self, cells):
+        if not self.dense(cells):
+            return (cells, self.per)
+        return (cells * (self.per // LANES) + cells // self.groups, LANES)
+
+
+def pack(z, ref, value):
+    cells = value.shape[0]
+    if not z.dense(cells):
+        ref[...] = value.astype(BF16)
+        return
+    full = z.per // LANES
+    for g in range(full):
+        ref[g * cells : (g + 1) * cells] = value[:, g * LANES : (g + 1) * LANES].astype(BF16)
+    part = cells // z.groups
+    rest = [value[g * part : (g + 1) * part, full * LANES :] for g in range(z.groups)]
+    ref[full * cells :] = jnp.concatenate(rest, axis=1).astype(BF16)
+
+
+def unpack(z, cells, message, put):
+    if not z.dense(cells):
+        put(0, 0, message)
+        return
+    full = z.per // LANES
+    for g in range(full):
+        put(0, g * LANES, message[g * cells : (g + 1) * cells])
+    part = cells // z.groups
+    rest = message[full * cells :]
+    for g in range(z.groups):
+        put(g * part, full * LANES, rest[:, g * z.rest : (g + 1) * z.rest])
 
 
 def masked_silu(z, state):
@@ -74,8 +115,20 @@
     return value.reshape(-1, z.per)
 
 
-def split_kernel(z, latent_ref, hint_ref, *refs):
-    outs, spread = refs[:-1], refs[-1]
+def fetch(sources, targets, sems):
+    copies = [
+        pltpu.make_async_copy(source, target, sems.at[i])
+        for i, (source, target) in enumerate(zip(sources, targets))
+    ]
+    for copy in copies:
+        copy.start()
+    for copy in copies:
+        copy.wait()
+
+
+def split_kernel(z, latent_hbm, hint_hbm, *refs):
+    outs, (latent_ref, hint_ref, spread, sems) = refs[:-4], refs[-4:]
+    fetch((latent_hbm, hint_hbm), (latent_ref, hint_ref), sems)
     latent = latent_ref[...].astype(F32)
     control = (latent + hint_ref[...].astype(F32)).astype(BF16).astype(F32)
     edge = jnp.zeros((2, z.rows, LAYERS, z.per), F32)
@@ -86,20 +139,50 @@
     band = lax.axis_index("band")
     for k, out in enumerate(outs):
         start = pl.multiple_of((band ^ k) * z.columns, 8)
-        block = spread[:, :, pl.ds(start, z.wide)]
-        out[...] = block.reshape(2, z.rows * z.wide, z.per).astype(BF16)
+        pack(z, out, spread[:, :, pl.ds(start, z.wide)].reshape(-1, z.per))
+
+
+def in_hbm(array):
+    return pltpu.with_memory_space_constraint(array, pltpu.HBM)
+
+
+def load_kernel(count, *refs):
+    fetch(refs[:count], refs[count : 2 * count], refs[2 * count])
+
+
+def load(*weights):
+    count = len(weights)
+    return pl.pallas_call(
+        functools.partial(load_kernel, count),
+        out_shape=[sds(w.shape) for w in weights],
+        in_specs=[pl.BlockSpec(memory_space=pltpu.HBM)] * count,
+        out_specs=whole(count),
+        scratch_shapes=[pltpu.SemaphoreType.DMA((count,))],
+        compiler_params=pltpu.CompilerParams(vmem_limit_bytes=1 << 20),
+        cost_estimate=pl.CostEstimate(
+            flops=0, bytes_accessed=2 * sum(w.size for w in weights), transcendentals=0
+        ),
+    )(*[in_hbm(w) for w in weights])
 
 
 def join_kernel(z, *refs):
-    blocks, (state_ref, act_ref) = refs[:-2], refs[-2:]
+    blocks, (state_ref, act_ref, image, block_image) = refs[:-4], refs[-4:]
     band = lax.axis_index("band")
     size = z.rows * z.wide
+
+    def put(row, lane, piece):
+        rows, lanes = piece.shape
+        block_image[row : row + rows, lane : lane + lanes] = piece
+
     for k, block in enumerate(blocks):
-        start = pl.multiple_of((band ^ k) * size, 16)
+        start = pl.multiple_of((band ^ k) * size, 8)
+        unpack(z, 2 * size, block[...].astype(F32), put)
         for t in range(2):
-            cells = block[t]
-            state_ref[t, pl.ds(start, size)] = cells
-            act_ref[t, pl.ds(start, size)] = masked_silu(z, cells.astype(F32)).astype(BF16)
+            image[t, pl.ds(start, size)] = block_image[t * size : (t + 1) * size]
+    for t in range(2):
+        value = image[t]
+        state_ref[t] = value.astype(BF16)
+        pack(z, act_ref.at[t], masked_silu(z, value))
 
 
 def in_order(pieces):
@@ -114,9 +197,15 @@
     return pieces
 
 
-def lay_out(z, a_ref, pieces, at=0):
-    for j, piece in enumerate(in_order(pieces)):
-        a_ref[:, at + j * z.per : at + (j + 1) * z.per] = piece
+def lay_out(z, a_ref, messages, at=0):
+    for j, message in enumerate(in_order(messages)):
+
+        def put(row, lane, piece):
+            rows, lanes = piece.shape
+            lane = at + j * z.per + lane
+            a_ref[row : row + rows, lane : lane + lanes] = piece
+
+        unpack(z, z.cells, message, put)
 
 
 def convolve(z, cells, weight, left, right):
@@ -143,7 +232,17 @@
     right[8 + z.cells : 16 + z.cells] = jnp.zeros((8, 3 * z.per), F32)
 
 
-def pair_kernel(z, *refs):
+def finish(z, state, result, bias, new_ref, act_ref):
+    new = (state.astype(F32) + result + bias).astype(BF16)
+    new_ref[...] = new
+    pack(z, act_ref, masked_silu(z, new.astype(F32)))
+
+
+def bias_of(ref):
+    return ref[...].astype(F32).reshape(1, -1)
+
+
+def layer_kernel(z, *refs):
     n = z.shards
     blocks, refs = refs[:n], refs[n:]
     state_ref, w0, b0, w1, b1, new_ref, act_ref, a_ref, left, right = refs
@@ -151,10 +250,7 @@
     for t, (w_ref, b_ref) in enumerate(((w0, b0), (w1, b1))):
         lay_out(z, a_ref, [block[t] for block in blocks])
         result = convolve(z, a_ref[...], taps(z, w_ref, 0, z.depth), left, right)
-        total = state_ref[t].astype(F32) + result + b_ref[...].astype(F32)
-        new = total.astype(BF16)
-        new_ref[t] = new
-        act_ref[t] = masked_silu(z, new.astype(F32)).astype(BF16)
+        finish(z, state_ref[t], result, bias_of(b_ref), new_ref.at[t], act_ref.at[t])
 
 
 def decode_kernel(z, *refs):
@@ -166,10 +262,7 @@
     lay_out(z, a_ref, [block[0] for block in blocks], z.depth)
     skip_ref[...] = a_ref[:, z.depth :]
     result = convolve(z, a_ref[...], taps(z, w_ref, 0, 2 * z.depth), left, right)
-    total = state_ref[1].astype(F32) + result + b_ref[...].astype(F32)
-    new = total.astype(BF16)
-    new_ref[...] = new
-    act_ref[...] = masked_silu(z, new.astype(F32)).astype(BF16)
+    finish(z, state_ref[1], result, bias_of(b_ref), new_ref, act_ref)
 
 
 def skip_kernel(z, skip_ref, w_ref, out_ref, left, right):
@@ -185,7 +278,8 @@
     clear_edges(z, left, right)
     lay_out(z, a_ref, [block[...] for block in blocks])
     result = convolve(z, a_ref[...], taps(z, w_ref, 0, z.depth), left, right)
-    total = state_ref[...].astype(F32) + (result + skip_ref[...]) + b_ref[...].astype(F32)
+    total = state_ref[...].astype(F32) + (result + skip_ref[...])
+    total = total + bias_of(b_ref)
     image[...] = total.reshape(z.height, z.wide, z.per)
     band = lax.axis_index("band")
     for k, out in enumerate(outs):
@@ -203,40 +297,65 @@
 
 
 def over_bands(blocks):
-    return [blocks[0]] + [exchange(b, "band", k) for k, b in enumerate(blocks) if k]
+    moved = [blocks[0]]
+    for k, block in enumerate(blocks):
+        if k:
+            moved.append(exchange(block, "band", k))
+    return moved
 
 
 def gather(cells):
-    chips = [cells] + [exchange(cells, "section", k) for k in range(1, lax.axis_size("section"))]
-    cores = range(1, lax.axis_size("chan"))
+    chips = [cells]
+    for k in range(1, lax.axis_size("section")):
+        chips.append(exchange(cells, "section", k))
     pieces = []
     for chip in chips:
-        pieces += [chip] + [exchange(chip, "chan", k) for k in cores]
+        pieces.append(chip)
+        for k in range(1, lax.axis_size("chan")):
+            pieces.append(exchange(chip, "chan", k))
     return pieces
 
 
 def per_device(latent, control_hint, cw1, cb1, cw2, cb2, mw1, mb1, mw2, mb2, dw1, db1, dw2, db2):
     z = Sizes(latent)
-    cb1, cb2, mb1, mb2, db1, db2 = [b.reshape(1, -1) for b in (cb1, cb2, mb1, mb2, db1, db2)]
-    kernel = lambda f: functools.partial(f, z)
+    kernel = lambda f, *a: functools.partial(f, z, *a)
     edges = [pltpu.VMEM((z.cells + 16, 3 * z.per), F32)] * 2
     work = lambda parts: [pltpu.VMEM((z.cells, parts * z.depth), BF16)] + edges
     unit = 2 * 9 * z.cells * z.per * z.depth
-
-    blocks = call(
+    single = sds((z.cells, z.per))
+    pair = sds((2, z.cells, z.per))
+    message = z.packed(z.cells)
+
+    raw = (z.rows, z.width, z.per)
+    blocks = pl.pallas_call(
         kernel(split_kernel),
-        [sds((2, z.rows * z.wide, z.per))] * z.bands,
-        latent,
-        control_hint,
-        scratch=[pltpu.VMEM((2, z.rows, z.width + 2 * LAYERS, z.per), F32)],
-    )
-    pair = sds((2, z.cells, z.per))
-    single = sds((z.cells, z.per))
-    state, act = call(kernel(join_kernel), [pair, pair], *over_bands(blocks))
+        out_shape=[sds(z.packed(2 * z.rows * z.wide))] * z.bands,
+        in_specs=[pl.BlockSpec(memory_space=pltpu.HBM)] * 2,
+        out_specs=whole(z.bands),
+        scratch_shapes=[pltpu.VMEM(raw, BF16)] * 2
+        + [
+            pltpu.VMEM((2, z.rows, z.width + 2 * LAYERS, z.per), F32),
+            pltpu.SemaphoreType.DMA((2,)),
+        ],
+        compiler_params=pltpu.CompilerParams(vmem_limit_bytes=4 << 20),
+    )(in_hbm(latent), in_hbm(control_hint))
+    blocks = over_bands(blocks)
+    cw1, mw1, cw2, mw2 = load(cw1, mw1, cw2, mw2)
+    (dw1,) = load(dw1)
+    (dw2,) = load(dw2)
+    state, act = call(
+        kernel(join_kernel),
+        [pair, sds((2,) + message)],
+        *blocks,
+        scratch=[
+            pltpu.VMEM((2, z.cells, z.per), F32),
+            pltpu.VMEM((2 * z.rows * z.wide, z.per), F32),
+        ],
+    )
     for weights in ((cw1, cb1, mw1, mb1), (cw2, cb2, mw2, mb2)):
         state, act = call(
-            kernel(pair_kernel),
-            [pair, pair],
+            kernel(layer_kernel),
+            [pair, sds((2,) + message)],
             *gather(act),
             state,
             *weights,
@@ -245,7 +364,7 @@
         )
     state, act, skip = call(
         kernel(decode_kernel),
-        [single, single, sds((z.cells, z.depth))],
+        [single, sds(message), sds((z.cells, z.depth))],
         *gather(act),
         state,
         dw1,
@@ -269,9 +388,9 @@
     )
     return call(
         kernel(rows_kernel),
-        sds((z.rows, z.width, z.per)),
+        sds(raw),
         *over_bands(blocks),
-        scratch=[pltpu.VMEM((z.rows, z.width, z.per), F32)],
+        scratch=[pltpu.VMEM(raw, F32)],
     )
 
 
@@ -279,6 +398,7 @@
     image = P(("groups", "band"), None, CHANNEL_AXES)
     kernel = P(None, None, CHANNEL_AXES, None)
     bias = P(CHANNEL_AXES)
+
     return jax.shard_map(
         per_device,
         mesh=mesh,

time: 75.1 us -> 68.8 us (0.916)
  waiting for transfers between devices: 41.8 us -> 29.4 us
  Pallas kernels: 8.85 us -> 18 us
  local copies, waits for them, and re-layouts: 7.08 us -> 4.05 us
    ppermute x18, waiting for transfers between devices: 41.8 us -> 29.4 us  [exchange(): return lax.ppermute(cells, axis, [(i, i ^ distance) for i in range(count)])]
    pallas_call x0 -> x4, Pallas kernels: none -> 8.5 us  [the longest x3 7.3 us: load(): pl.pallas_call(functools.partial(load_kernel, count), out_shape=[sds(w.sh...]
    unnamed x22 -> x14, local copies, waits for them, and re-layouts: 5 us -> 3.31 us
    reshape x6 -> x0, local copies, waits for them, and re-layouts: 1.33 us -> none  [per_device(): b.reshape(1, -1)]
    pallas_call x8 -> x7, Pallas kernels: 8.85 us -> 9.53 us  [call(): pl.pallas_call(kernel, out_shape=outs, in_specs=whole(len(args)), out_spe...]
  transfers between devices with their start and end apart: 18 -> 18, of which waited for: 11 -> 9; matrix products, arithmetic and copies ran while one was open for 2% -> 0% of each run, Pallas kernels for 2% -> 12%
where the time goes in v3:
time: 68.8 us; the launch traced here: 68.5 us
  waiting for transfers between devices  29.4 us (43%)
  Pallas kernels  18 us (26%)
  starting transfers between devices  16.8 us (24%)
  local copies, waits for them, and re-layouts  4.05 us (6%)
    ppermute x18, waiting for transfers between devices, exchange(): return lax.ppermute(cells, axis, [(i, i ^ distance) for i in range(count)])  29.4 us
    ppermute x18, starting transfers between devices, exchange(): return lax.ppermute(cells, axis, [(i, i ^ distance) for i in range(count)])  16.8 us
    pallas_call x7, Pallas kernels, call(): pl.pallas_call(kernel, out_shape=outs, in_specs=whole(len(args)), out_spe...  9.53 us
    pallas_call x3, Pallas kernels, load(): pl.pallas_call(functools.partial(load_kernel, count), out_shape=[sds(w.sh...  7.3 us
    unnamed x14, local copies, waits for them, and re-layouts  3.31 us
  transfers between devices with their start and end apart: 18, of which 9 were waited for; matrix products, arithmetic and copies ran while one was open for 0% of the time, Pallas kernels for 12%

profile of v3, /device:TPU:0, one launch (start us, length us, event | category | flops | bytes accessed | tf_op | source)
XLA Modules:
  0.0 68.5 jit_solution(9206206335373965935)
XLA Ops:
  0.0 1.6 %copy.15.latent_hbm = bf16[2,128,160]{2,1,0:T(8,128)(2,1)} copy(bf16[2,128,160]{1,2,0:T(8,128)(2,1)} %param.14) | data formatting | bytes 163840 | tf_op args[0]
  1.6 1.6 %copy.16.hint_hbm = bf16[2,128,160]{2,1,0:T(8,128)(2,1)} copy(bf16[2,128,160]{1,2,0:T(8,128)(2,1)} %param.15) | data formatting | bytes 163840 | tf_op args[1]
  3.3 1.2 %shard_map.136 = (bf16[200,128]{1,0:T(8,128)(2,1)S(1)}, bf16[200,128]{1,0:T(8,128)(2,1)S(1)}, bf16[200,128]{1,0:T(8,128)(2,1)S(1)}, bf16[200,128]{1,0:T(8,128)(2,1)S(1)}) custom-call(bf16[2,128,160]{2,1,0:T(8,128)(2,1)} %copy.15.latent_hbm, bf16[2,128,160]{2,1,0:T(8,128)(2,1)} %copy.16.hint_hbm), custom_call_target="tpu_custom_call" | custom-call | tf_op jit(solution)/shard_map/pallas_call | solution.py:330
  4.5 3.1 %collective-permute-start = (bf16[200,128]{1,0:T(8,128)(2,1)S(1)}, bf16[200,128]{1,0:T(8,128)(2,1)S(1)}, u32[]{:S(2)}, u32[]{:S(2)}) collective-permute-start(bf16[200,128]{1,0:T(8,128)(2,1)S(1)} %get-tuple-element.27), channel_id=1, source_target_pairs={{0,2},{2,0},{4,6},{6,4},{1,3},{3,1},{5,7},{7,5},{8,10},{10,8},{12,... | collective-permute-start | bytes 153608 | tf_op jit(solution)/shard_map/ppermute | solution.py:25
  7.6 2.6 %collective-permute-start.1 = (bf16[200,128]{1,0:T(8,128)(2,1)S(1)}, bf16[200,128]{1,0:T(8,128)(2,1)S(1)}, u32[]{:S(2)}, u32[]{:S(2)}) collective-permute-start(bf16[200,128]{1,0:T(8,128)(2,1)S(1)} %get-tuple-element.28), channel_id=1, source_target_pairs={{0,4},{2,6},{4,0},{6,2},{1,5},{3,7},{5,1},{7,3},{8,12},{10,14},{12... | collective-permute-start | bytes 153608 | tf_op jit(solution)/shard_map/ppermute | solution.py:25
  10.2 0.0 collective-permute-start.2
  10.2 0.0 collective-permute-done.refs_1_
  10.2 3.4 %collective-permute-done.1.refs_2_ = bf16[200,128]{1,0:T(8,128)(2,1)S(1)} collective-permute-done((bf16[200,128]{1,0:T(8,128)(2,1)S(1)}, bf16[200,128]{1,0:T(8,128)(2,1)S(1)}, u32[]{:S(2)}, u32[]{:S(2)}) %collective-permute-start.1) | collective-permute-done | bytes 51232 | tf_op jit(solution)/shard_map/ppermute | solution.py:25
  13.6 2.5 %collective-permute-done.2.refs_3_ = bf16[200,128]{1,0:T(8,128)(2,1)S(1)} collective-permute-done((bf16[200,128]{1,0:T(8,128)(2,1)S(1)}, bf16[200,128]{1,0:T(8,128)(2,1)S(1)}, u32[]{:S(2)}, u32[]{:S(2)}) %collective-permute-start.2) | collective-permute-done | bytes 51232 | tf_op jit(solution)/shard_map/ppermute | solution.py:25
  16.1 0.3 shard_map.137
  16.4 0.0 copy-start.2
  16.4 0.0 copy-start.3
  16.4 1.6 %collective-permute-start.4 = (bf16[2,400,128]{2,1,0:T(8,128)(2,1)S(1)}, bf16[2,400,128]{2,1,0:T(8,128)(2,1)S(1)}, u32[]{:S(2)}, u32[]{:S(2)}) collective-permute-start(bf16[2,400,128]{2,1,0:T(8,128)(2,1)S(1)} %get-tuple-element.30.refs_0_), channel_id=1, source_target_pairs={{0,8},{8,0},{1,9},{9,1},{2,10},{10,2},{3,11},{11,3},{4,12},{12,4},... | collective-permute-start | bytes 614408 | tf_op jit(solution)/shard_map/ppermute | solution.py:25
  18.0 0.0 collective-permute-start.3
  18.0 4.3 %collective-permute-done.4.refs_2_ = bf16[2,400,128]{2,1,0:T(8,128)(2,1)S(1)} collective-permute-done((bf16[2,400,128]{2,1,0:T(8,128)(2,1)S(1)}, bf16[2,400,128]{2,1,0:T(8,128)(2,1)S(1)}, u32[]{:S(2)}, u32[]{:S(2)}) %collective-permute-start.4) | collective-permute-done | bytes 204832 | tf_op jit(solution)/shard_map/ppermute | solution.py:25
  22.3 0.0 collective-permute-start.5
  22.3 3.2 %shard_map.138 = (bf16[3,3,160,640]{3,2,1,0:T(8,128)(2,1)S(1)}, bf16[3,3,160,640]{3,2,1,0:T(8,128)(2,1)S(1)}, bf16[3,3,160,640]{3,2,1,0:T(8,128)(2,1)S(1)}, bf16[3,3,160,640]{3,2,1,0:T(8,128)(2,1)S(1)}) custom-call(bf16[3,3,160,640]{3,2,1,0:T(8,128)(2,1)} %refs_0_.3, bf16[3,3,160,640]{3,2,1,0:T(8,128)(2,1)} %refs_1_.1, bf16[3,3,160,640]{3,2,1,0:T(8,128)(2,1)} %refs_2_.1, ...), custom_call_target="tpu_custom_call" | custom-call | bytes 7372800 | tf_op jit(solution)/shard_map/pallas_call | solution.py:155
  25.5 0.0 collective-permute-done.3.refs_1_
  25.5 0.0 collective-permute-done.5.refs_3_
  25.5 0.0 copy-start.4
  25.5 0.0 copy-start.5
  25.5 2.2 %shard_map.139 = (bf16[2,320,160]{2,1,0:T(8,128)(2,1)S(1)}, bf16[2,400,128]{2,1,0:T(8,128)(2,1)S(1)}) custom-call(bf16[2,400,128]{2,1,0:T(8,128)(2,1)S(1)} %get-tuple-element.30.refs_0_, bf16[2,400,128]{2,1,0:T(8,128)(2,1)S(1)} %collective-permute-done.3.refs_1_, bf16[2,400,128]{2,1,0:T(8,128)(2,1)S(1)} %collective-permute-done.4.refs_2_, ...), custom_call_target="tpu_custom_call" | custom-call | flops 1179648000 | bytes 5120640 | tf_op jit(solution)/shard_map/pallas_call | solution.py:44
  27.8 1.6 %collective-permute-start.7 = (bf16[2,400,128]{2,1,0:T(8,128)(2,1)S(1)}, bf16[2,400,128]{2,1,0:T(8,128)(2,1)S(1)}, u32[]{:S(2)}, u32[]{:S(2)}) collective-permute-start(bf16[2,400,128]{2,1,0:T(8,128)(2,1)S(1)} %get-tuple-element.34.refs_0_), channel_id=1, source_target_pairs={{0,8},{8,0},{1,9},{9,1},{2,10},{10,2},{3,11},{11,3},{4,12},{12,4},... | collective-permute-start | bytes 614408 | tf_op jit(solution)/shard_map/ppermute | solution.py:25
  29.3 0.2 collective-permute-start.6
  29.6 5.8 %collective-permute-done.7.refs_2_ = bf16[2,400,128]{2,1,0:T(8,128)(2,1)S(1)} collective-permute-done((bf16[2,400,128]{2,1,0:T(8,128)(2,1)S(1)}, bf16[2,400,128]{2,1,0:T(8,128)(2,1)S(1)}, u32[]{:S(2)}, u32[]{:S(2)}) %collective-permute-start.7) | collective-permute-done | bytes 204832 | tf_op jit(solution)/shard_map/ppermute | solution.py:25
  35.3 1.4 %collective-permute-done.8.refs_3_ = bf16[2,400,128]{2,1,0:T(8,128)(2,1)S(1)} collective-permute-done((bf16[2,400,128]{2,1,0:T(8,128)(2,1)S(1)}, bf16[2,400,128]{2,1,0:T(8,128)(2,1)S(1)}, u32[]{:S(2)}, u32[]{:S(2)}) %collective-permute-start.8) | collective-permute-done | bytes 204832 | tf_op jit(solution)/shard_map/ppermute | solution.py:25
  36.8 2.3 %shard_map.140 = (bf16[2,320,160]{2,1,0:T(8,128)(2,1)S(1)}, bf16[2,400,128]{2,1,0:T(8,128)(2,1)S(1)}) custom-call(bf16[2,400,128]{2,1,0:T(8,128)(2,1)S(1)} %get-tuple-element.34.refs_0_, bf16[2,400,128]{2,1,0:T(8,128)(2,1)S(1)} %collective-permute-done.6.refs_1_, bf16[2,400,128]{2,1,0:T(8,128)(2,1)S(1)} %collective-permute-done.7.refs_2_, ...), custom_call_target="tpu_custom_call" | custom-call | flops 1179648000 | bytes 5120640 | tf_op jit(solution)/shard_map/pallas_call | solution.py:44
  39.1 1.6 %collective-permute-start.10 = (bf16[2,400,128]{2,1,0:T(8,128)(2,1)S(1)}, bf16[2,400,128]{2,1,0:T(8,128)(2,1)S(1)}, u32[]{:S(2)}, u32[]{:S(2)}) collective-permute-start(bf16[2,400,128]{2,1,0:T(8,128)(2,1)S(1)} %get-tuple-element.38.refs_0_), channel_id=1, source_target_pairs={{0,8},{8,0},{1,9},{9,1},{2,10},{10,2},{3,11},{11,3},{4,12},{12,4},... | collective-permute-start | bytes 614408 | tf_op jit(solution)/shard_map/ppermute | solution.py:25
  40.6 5.6 %collective-permute-done.10.refs_2_ = bf16[2,400,128]{2,1,0:T(8,128)(2,1)S(1)} collective-permute-done((bf16[2,400,128]{2,1,0:T(8,128)(2,1)S(1)}, bf16[2,400,128]{2,1,0:T(8,128)(2,1)S(1)}, u32[]{:S(2)}, u32[]{:S(2)}) %collective-permute-start.10) | collective-permute-done | bytes 204832 | tf_op jit(solution)/shard_map/ppermute | solution.py:25
  46.2 0.0 collective-permute-start.11
  46.2 2.1 %shard_map.141.refs_5_ = bf16[3,3,160,1280]{3,2,1,0:T(8,128)(2,1)S(1)} custom-call(bf16[3,3,160,1280]{3,2,1,0:T(8,128)(2,1)} %refs_0_.4), custom_call_target="tpu_custom_call" | custom-call | bytes 3686400 | tf_op jit(solution)/shard_map/pallas_call | solution.py:155
  48.3 0.0 collective-permute-done.11.refs_3_
  48.3 2.1 %shard_map.142 = (bf16[320,160]{1,0:T(8,128)(2,1)S(1)}, bf16[400,128]{1,0:T(8,128)(2,1)S(1)}, bf16[320,640]{1,0:T(8,128)(2,1)S(1)}) custom-call(bf16[2,400,128]{2,1,0:T(8,128)(2,1)S(1)} %get-tuple-element.38.refs_0_, bf16[2,400,128]{2,1,0:T(8,128)(2,1)S(1)} %collective-permute-done.9.refs_1_, bf16[2,400,128]{2,1,0:T(8,128)(2,1)S(1)} %collective-permute-done.10.refs_2_, ...), custom_call_target="tpu_custom_call" | custom-call | flops 1179648000 | bytes 5325120 | tf_op jit(solution)/shard_map/pallas_call | solution.py:44
  50.4 1.6 %collective-permute-start.13 = (bf16[400,128]{1,0:T(8,128)(2,1)S(1)}, bf16[400,128]{1,0:T(8,128)(2,1)S(1)}, u32[]{:S(2)}, u32[]{:S(2)}) collective-permute-start(bf16[400,128]{1,0:T(8,128)(2,1)S(1)} %get-tuple-element.40.refs_0_), channel_id=1, source_target_pairs={{0,8},{8,0},{1,9},{9,1},{2,10},{10,2},{3,11},{11,3},{4,12},{12,4},... | collective-permute-start | bytes 307208 | tf_op jit(solution)/shard_map/ppermute | solution.py:25
  52.0 0.2 collective-permute-start.12
  52.2 3.6 %collective-permute-done.13.refs_2_ = bf16[400,128]{1,0:T(8,128)(2,1)S(1)} collective-permute-done((bf16[400,128]{1,0:T(8,128)(2,1)S(1)}, bf16[400,128]{1,0:T(8,128)(2,1)S(1)}, u32[]{:S(2)}, u32[]{:S(2)}) %collective-permute-start.13) | collective-permute-done | bytes 102432 | tf_op jit(solution)/shard_map/ppermute | solution.py:25
  55.8 0.0 collective-permute-start.14
  55.8 2.1 %shard_map.143.w_ref.refs_6_ = bf16[3,3,160,1280]{3,2,1,0:T(8,128)(2,1)S(1)} custom-call(bf16[3,3,160,1280]{3,2,1,0:T(8,128)(2,1)} %refs_0_.5), custom_call_target="tpu_custom_call" | custom-call | bytes 3686400 | tf_op jit(solution)/shard_map/pallas_call | solution.py:155
  57.8 0.0 copy-start.1
  57.9 1.2 %shard_map.144.refs_5_ = f32[320,160]{1,0:T(8,128)S(1)} custom-call(bf16[320,640]{1,0:T(8,128)(2,1)S(1)} %get-tuple-element.42.skip_ref, bf16[3,3,160,1280]{3,2,1,0:T(8,128)(2,1)S(1)} %shard_map.143.w_ref.refs_6_), custom_call_target="tpu_custom_call" | custom-call | flops 589824000 | bytes 4300800 | tf_op jit(solution)/shard_map/pallas_call | solution.py:44
  59.0 0.0 collective-permute-done.12.refs_1_
  59.1 1.4 %shard_map.145 = (bf16[2,32,160]{2,1,0:T(8,128)(2,1)S(1)}, bf16[2,32,160]{2,1,0:T(8,128)(2,1)S(1)}, bf16[2,32,160]{2,1,0:T(8,128)(2,1)S(1)}, bf16[2,32,160]{2,1,0:T(8,128)(2,1)S(1)}) custom-call(bf16[400,128]{1,0:T(8,128)(2,1)S(1)} %get-tuple-element.40.refs_0_, bf16[400,128]{1,0:T(8,128)(2,1)S(1)} %collective-permute-done.12.refs_1_, ...), custom_call_target="tpu_custom_call" | custom-call | flops 589824000 | bytes 4485440 | tf_op jit(solution)/shard_map/pallas_call | solution.py:44
  60.5 0.1 collective-permute-start.15
  60.6 1.4 %collective-permute-start.16 = (bf16[2,32,160]{2,1,0:T(8,128)(2,1)S(1)}, bf16[2,32,160]{2,1,0:T(8,128)(2,1)S(1)}, u32[]{:S(2)}, u32[]{:S(2)}) collective-permute-start(bf16[2,32,160]{2,1,0:T(8,128)(2,1)S(1)} %get-tuple-element.45), channel_id=1, source_target_pairs={{0,4},{2,6},{4,0},{6,2},{1,5},{3,7},{5,1},{7,3},{8,12},{10,14},{12... | collective-permute-start | bytes 61448 | tf_op jit(solution)/shard_map/ppermute | solution.py:25
  62.0 3.0 %collective-permute-start.17 = (bf16[2,32,160]{2,1,0:T(8,128)(2,1)S(1)}, bf16[2,32,160]{2,1,0:T(8,128)(2,1)S(1)}, u32[]{:S(2)}, u32[]{:S(2)}) collective-permute-start(bf16[2,32,160]{2,1,0:T(8,128)(2,1)S(1)} %get-tuple-element.46), channel_id=1, source_target_pairs={{0,6},{2,4},{4,2},{6,0},{1,7},{3,5},{5,3},{7,1},{8,14},{10,12},{12... | collective-permute-start | bytes 61448 | tf_op jit(solution)/shard_map/ppermute | solution.py:25
  64.9 0.8 %collective-permute-done.16.refs_2_ = bf16[2,32,160]{2,1,0:T(8,128)(2,1)S(1)} collective-permute-done((bf16[2,32,160]{2,1,0:T(8,128)(2,1)S(1)}, bf16[2,32,160]{2,1,0:T(8,128)(2,1)S(1)}, u32[]{:S(2)}, u32[]{:S(2)}) %collective-permute-start.16) | collective-permute-done | bytes 20512 | tf_op jit(solution)/shard_map/ppermute | solution.py:25
  65.8 1.9 %collective-permute-done.17.refs_3_ = bf16[2,32,160]{2,1,0:T(8,128)(2,1)S(1)} collective-permute-done((bf16[2,32,160]{2,1,0:T(8,128)(2,1)S(1)}, bf16[2,32,160]{2,1,0:T(8,128)(2,1)S(1)}, u32[]{:S(2)}, u32[]{:S(2)}) %collective-permute-start.17) | collective-permute-done | bytes 20512 | tf_op jit(solution)/shard_map/ppermute | solution.py:25
  67.7 0.7 %copy.17 = bf16[2,128,160]{1,2,0:T(8,128)(2,1)} copy(bf16[2,128,160]{2,1,0:T(8,128)(2,1)S(1)} %shard_map.146) | data formatting | bytes 163840 | tf_op jit(solution)/shard_map/pallas_call | solution.py:44
  (14 shorter events, 0.1 us)
Async XLA Ops:
  4.5 5.7 %collective-permute-start = (bf16[200,128]{1,0:T(8,128)(2,1)S(1)}, bf16[200,128]{1,0:T(8,128)(2,1)S(1)}, u32[]{:S(2)}, u32[]{:S(2)}) collective-permute-start(bf16[200,128]{1,0:T(8,128)(2,1)S(1)} %get-tuple-element.27), channel_id=1, source_target_pairs={{0,2},{2,0},{4,6},{6,4},{1,3},{3,1},{5,7},{7,5},{8,10},{10,8},{12,... | collective-permute-start | bytes 153608 | tf_op jit(solution)/shard_map/ppermute | solution.py:25
  7.6 6.0 %collective-permute-start.1 = (bf16[200,128]{1,0:T(8,128)(2,1)S(1)}, bf16[200,128]{1,0:T(8,128)(2,1)S(1)}, u32[]{:S(2)}, u32[]{:S(2)}) collective-permute-start(bf16[200,128]{1,0:T(8,128)(2,1)S(1)} %get-tuple-element.28), channel_id=1, source_target_pairs={{0,4},{2,6},{4,0},{6,2},{1,5},{3,7},{5,1},{7,3},{8,12},{10,14},{12... | collective-permute-start | bytes 153608 | tf_op jit(solution)/shard_map/ppermute | solution.py:25
  10.2 5.9 %collective-permute-start.2 = (bf16[200,128]{1,0:T(8,128)(2,1)S(1)}, bf16[200,128]{1,0:T(8,128)(2,1)S(1)}, u32[]{:S(2)}, u32[]{:S(2)}) collective-permute-start(bf16[200,128]{1,0:T(8,128)(2,1)S(1)} %get-tuple-element.29), channel_id=1, source_target_pairs={{0,6},{2,4},{4,2},{6,0},{1,7},{3,5},{5,3},{7,1},{8,14},{10,12},{12... | collective-permute-start | bytes 153608 | tf_op jit(solution)/shard_map/ppermute | solution.py:25
  16.4 9.1 %copy-start.2 = (bf16[160]{0:T(256)(128)(2,1)S(1)}, bf16[160]{0:T(256)(128)(2,1)}, u32[]{:S(2)}) copy-start(bf16[160]{0:T(256)(128)(2,1)} %refs_6_.3) | copy-start | bytes 964
  16.4 9.1 %copy-start.3 = (bf16[160]{0:T(256)(128)(2,1)S(1)}, bf16[160]{0:T(256)(128)(2,1)}, u32[]{:S(2)}) copy-start(bf16[160]{0:T(256)(128)(2,1)} %refs_8_.2) | copy-start | bytes 964
  16.4 5.8 %collective-permute-start.4 = (bf16[2,400,128]{2,1,0:T(8,128)(2,1)S(1)}, bf16[2,400,128]{2,1,0:T(8,128)(2,1)S(1)}, u32[]{:S(2)}, u32[]{:S(2)}) collective-permute-start(bf16[2,400,128]{2,1,0:T(8,128)(2,1)S(1)} %get-tuple-element.30.refs_0_), channel_id=1, source_target_pairs={{0,8},{8,0},{1,9},{9,1},{2,10},{10,2},{3,11},{11,3},{4,12},{12,4},... | collective-permute-start | bytes 614408 | tf_op jit(solution)/shard_map/ppermute | solution.py:25
  18.0 7.5 %collective-permute-start.3 = (bf16[2,400,128]{2,1,0:T(8,128)(2,1)S(1)}, bf16[2,400,128]{2,1,0:T(8,128)(2,1)S(1)}, u32[]{:S(2)}, u32[]{:S(2)}) collective-permute-start(bf16[2,400,128]{2,1,0:T(8,128)(2,1)S(1)} %get-tuple-element.30.refs_0_), channel_id=1, source_target_pairs={{0,1},{1,0},{2,3},{3,2},{4,5},{5,4},{6,7},{7,6},{8,9},{9,8},{10,11... | collective-permute-start | bytes 614408 | tf_op jit(solution)/shard_map/ppermute | solution.py:25
  22.3 3.2 %collective-permute-start.5 = (bf16[2,400,128]{2,1,0:T(8,128)(2,1)S(1)}, bf16[2,400,128]{2,1,0:T(8,128)(2,1)S(1)}, u32[]{:S(2)}, u32[]{:S(2)}) collective-permute-start(bf16[2,400,128]{2,1,0:T(8,128)(2,1)S(1)} %collective-permute-done.4.refs_2_), channel_id=1, source_target_pairs={{0,1},{1,0},{2,3},{3,2},{4,5},{5,4},{6,7},{7,6},{8,9},{9,8},{10,11... | collective-permute-start | bytes 614408 | tf_op jit(solution)/shard_map/ppermute | solution.py:25
  25.5 11.3 %copy-start.4 = (bf16[160]{0:T(256)(128)(2,1)S(1)}, bf16[160]{0:T(256)(128)(2,1)}, u32[]{:S(2)}) copy-start(bf16[160]{0:T(256)(128)(2,1)} %refs_6_.4) | copy-start | bytes 964
  25.5 11.3 %copy-start.5 = (bf16[160]{0:T(256)(128)(2,1)S(1)}, bf16[160]{0:T(256)(128)(2,1)}, u32[]{:S(2)}) copy-start(bf16[160]{0:T(256)(128)(2,1)} %refs_8_.3) | copy-start | bytes 964
  27.8 7.6 %collective-permute-start.7 = (bf16[2,400,128]{2,1,0:T(8,128)(2,1)S(1)}, bf16[2,400,128]{2,1,0:T(8,128)(2,1)S(1)}, u32[]{:S(2)}, u32[]{:S(2)}) collective-permute-start(bf16[2,400,128]{2,1,0:T(8,128)(2,1)S(1)} %get-tuple-element.34.refs_0_), channel_id=1, source_target_pairs={{0,8},{8,0},{1,9},{9,1},{2,10},{10,2},{3,11},{11,3},{4,12},{12,4},... | collective-permute-start | bytes 614408 | tf_op jit(solution)/shard_map/ppermute | solution.py:25
  29.3 6.0 %collective-permute-start.6 = (bf16[2,400,128]{2,1,0:T(8,128)(2,1)S(1)}, bf16[2,400,128]{2,1,0:T(8,128)(2,1)S(1)}, u32[]{:S(2)}, u32[]{:S(2)}) collective-permute-start(bf16[2,400,128]{2,1,0:T(8,128)(2,1)S(1)} %get-tuple-element.34.refs_0_), channel_id=1, source_target_pairs={{0,1},{1,0},{2,3},{3,2},{4,5},{5,4},{6,7},{7,6},{8,9},{9,8},{10,11... | collective-permute-start | bytes 614408 | tf_op jit(solution)/shard_map/ppermute | solution.py:25
  35.3 1.5 %collective-permute-start.8 = (bf16[2,400,128]{2,1,0:T(8,128)(2,1)S(1)}, bf16[2,400,128]{2,1,0:T(8,128)(2,1)S(1)}, u32[]{:S(2)}, u32[]{:S(2)}) collective-permute-start(bf16[2,400,128]{2,1,0:T(8,128)(2,1)S(1)} %collective-permute-done.7.refs_2_), channel_id=1, source_target_pairs={{0,1},{1,0},{2,3},{3,2},{4,5},{5,4},{6,7},{7,6},{8,9},{9,8},{10,11... | collective-permute-start | bytes 614408 | tf_op jit(solution)/shard_map/ppermute | solution.py:25
  39.0 9.3 %copy-start = (bf16[160]{0:T(256)(128)(2,1)S(1)}, bf16[160]{0:T(256)(128)(2,1)}, u32[]{:S(2)}) copy-start(bf16[160]{0:T(256)(128)(2,1)} %refs_6_.5) | copy-start | bytes 964
  39.1 7.2 %collective-permute-start.10 = (bf16[2,400,128]{2,1,0:T(8,128)(2,1)S(1)}, bf16[2,400,128]{2,1,0:T(8,128)(2,1)S(1)}, u32[]{:S(2)}, u32[]{:S(2)}) collective-permute-start(bf16[2,400,128]{2,1,0:T(8,128)(2,1)S(1)} %get-tuple-element.38.refs_0_), channel_id=1, source_target_pairs={{0,8},{8,0},{1,9},{9,1},{2,10},{10,2},{3,11},{11,3},{4,12},{12,4},... | collective-permute-start | bytes 614408 | tf_op jit(solution)/shard_map/ppermute | solution.py:25
  40.6 7.7 %collective-permute-start.9 = (bf16[2,400,128]{2,1,0:T(8,128)(2,1)S(1)}, bf16[2,400,128]{2,1,0:T(8,128)(2,1)S(1)}, u32[]{:S(2)}, u32[]{:S(2)}) collective-permute-start(bf16[2,400,128]{2,1,0:T(8,128)(2,1)S(1)} %get-tuple-element.38.refs_0_), channel_id=1, source_target_pairs={{0,1},{1,0},{2,3},{3,2},{4,5},{5,4},{6,7},{7,6},{8,9},{9,8},{10,11... | collective-permute-start | bytes 614408 | tf_op jit(solution)/shard_map/ppermute | solution.py:25
  46.2 2.1 %collective-permute-start.11 = (bf16[2,400,128]{2,1,0:T(8,128)(2,1)S(1)}, bf16[2,400,128]{2,1,0:T(8,128)(2,1)S(1)}, u32[]{:S(2)}, u32[]{:S(2)}) collective-permute-start(bf16[2,400,128]{2,1,0:T(8,128)(2,1)S(1)} %collective-permute-done.10.refs_2_), channel_id=1, source_target_pairs={{0,1},{1,0},{2,3},{3,2},{4,5},{5,4},{6,7},{7,6},{8,9},{9,8},{10,11... | collective-permute-start | bytes 614408 | tf_op jit(solution)/shard_map/ppermute | solution.py:25
  50.4 5.4 %collective-permute-start.13 = (bf16[400,128]{1,0:T(8,128)(2,1)S(1)}, bf16[400,128]{1,0:T(8,128)(2,1)S(1)}, u32[]{:S(2)}, u32[]{:S(2)}) collective-permute-start(bf16[400,128]{1,0:T(8,128)(2,1)S(1)} %get-tuple-element.40.refs_0_), channel_id=1, source_target_pairs={{0,8},{8,0},{1,9},{9,1},{2,10},{10,2},{3,11},{11,3},{4,12},{12,4},... | collective-permute-start | bytes 307208 | tf_op jit(solution)/shard_map/ppermute | solution.py:25
  52.0 7.1 %collective-permute-start.12 = (bf16[400,128]{1,0:T(8,128)(2,1)S(1)}, bf16[400,128]{1,0:T(8,128)(2,1)S(1)}, u32[]{:S(2)}, u32[]{:S(2)}) collective-permute-start(bf16[400,128]{1,0:T(8,128)(2,1)S(1)} %get-tuple-element.40.refs_0_), channel_id=1, source_target_pairs={{0,1},{1,0},{2,3},{3,2},{4,5},{5,4},{6,7},{7,6},{8,9},{9,8},{10,11... | collective-permute-start | bytes 307208 | tf_op jit(solution)/shard_map/ppermute | solution.py:25
  55.8 3.3 %collective-permute-start.14 = (bf16[400,128]{1,0:T(8,128)(2,1)S(1)}, bf16[400,128]{1,0:T(8,128)(2,1)S(1)}, u32[]{:S(2)}, u32[]{:S(2)}) collective-permute-start(bf16[400,128]{1,0:T(8,128)(2,1)S(1)} %collective-permute-done.13.refs_2_), channel_id=1, source_target_pairs={{0,1},{1,0},{2,3},{3,2},{4,5},{5,4},{6,7},{7,6},{8,9},{9,8},{10,11... | collective-permute-start | bytes 307208 | tf_op jit(solution)/shard_map/ppermute | solution.py:25
  57.8 1.2 %copy-start.1 = (bf16[160]{0:T(256)(128)(2,1)S(1)}, bf16[160]{0:T(256)(128)(2,1)}, u32[]{:S(2)}) copy-start(bf16[160]{0:T(256)(128)(2,1)} %refs_7_.1) | copy-start | bytes 964
  60.5 4.5 %collective-permute-start.15 = (bf16[2,32,160]{2,1,0:T(8,128)(2,1)S(1)}, bf16[2,32,160]{2,1,0:T(8,128)(2,1)S(1)}, u32[]{:S(2)}, u32[]{:S(2)}) collective-permute-start(bf16[2,32,160]{2,1,0:T(8,128)(2,1)S(1)} %get-tuple-element.44), channel_id=1, source_target_pairs={{0,2},{2,0},{4,6},{6,4},{1,3},{3,1},{5,7},{7,5},{8,10},{10,8},{12,... | collective-permute-start | bytes 61448 | tf_op jit(solution)/shard_map/ppermute | solution.py:25
  60.6 5.2 %collective-permute-start.16 = (bf16[2,32,160]{2,1,0:T(8,128)(2,1)S(1)}, bf16[2,32,160]{2,1,0:T(8,128)(2,1)S(1)}, u32[]{:S(2)}, u32[]{:S(2)}) collective-permute-start(bf16[2,32,160]{2,1,0:T(8,128)(2,1)S(1)} %get-tuple-element.45), channel_id=1, source_target_pairs={{0,4},{2,6},{4,0},{6,2},{1,5},{3,7},{5,1},{7,3},{8,12},{10,14},{12... | collective-permute-start | bytes 61448 | tf_op jit(solution)/shard_map/ppermute | solution.py:25
  62.0 5.7 %collective-permute-start.17 = (bf16[2,32,160]{2,1,0:T(8,128)(2,1)S(1)}, bf16[2,32,160]{2,1,0:T(8,128)(2,1)S(1)}, u32[]{:S(2)}, u32[]{:S(2)}) collective-permute-start(bf16[2,32,160]{2,1,0:T(8,128)(2,1)S(1)} %get-tuple-element.46), channel_id=1, source_target_pairs={{0,6},{2,4},{4,2},{6,0},{1,7},{3,5},{5,3},{7,1},{8,14},{10,12},{12... | collective-permute-start | bytes 61448 | tf_op jit(solution)/shard_map/ppermute | solution.py:25

commit v4 on v3

--- a/solution.py
+++ b/solution.py
@@ -134,8 +134,9 @@
     edge = jnp.zeros((2, z.rows, LAYERS, z.per), F32)
     spread[:, :, :LAYERS] = edge
     spread[:, :, LAYERS + z.width :] = edge
-    spread[0, :, LAYERS : LAYERS + z.width] = control
-    spread[1, :, LAYERS : LAYERS + z.width] = latent
+    for row in range(z.rows):
+        spread[0, row, LAYERS : LAYERS + z.width] = control[row].T
+        spread[1, row, LAYERS : LAYERS + z.width] = latent[row].T
     band = lax.axis_index("band")
     for k, out in enumerate(outs):
         start = pl.multiple_of((band ^ k) * z.columns, 8)
@@ -284,16 +285,26 @@
     band = lax.axis_index("band")
     for k, out in enumerate(outs):
         rows = image[pl.ds((band ^ k) * z.rows, z.rows), LAYERS : LAYERS + z.columns]
-        out[...] = rows.astype(BF16)
+        pack(z, out, rows.reshape(-1, z.per))
 
 
 def rows_kernel(z, *refs):
-    blocks, (out_ref, image) = refs[:-2], refs[-2:]
+    blocks, (out_ref, image, block_image) = refs[:-3], refs[-3:]
     band = lax.axis_index("band")
+
+    def put(row, lane, piece):
+        rows, lanes = piece.shape
+        block_image[row : row + rows, lane : lane + lanes] = piece
+
     for k, block in enumerate(blocks):
         start = pl.multiple_of((band ^ k) * z.columns, 8)
-        image[:, pl.ds(start, z.columns)] = block[...].astype(F32)
-    out_ref[...] = image[...].astype(BF16)
+        unpack(z, z.rows * z.columns, block[...].astype(F32), put)
+        for row in range(z.rows):
+            image[row, pl.ds(start, z.columns)] = block_image[
+                row * z.columns : (row + 1) * z.columns
+            ]
+    for row in range(z.rows):
+        out_ref[row] = image[row].T.astype(BF16)
 
 
 def over_bands(blocks):
@@ -326,7 +337,7 @@
     pair = sds((2, z.cells, z.per))
     message = z.packed(z.cells)
 
-    raw = (z.rows, z.width, z.per)
+    raw = (z.rows, z.per, z.width)
     blocks = pl.pallas_call(
         kernel(split_kernel),
         out_shape=[sds(z.packed(2 * z.rows * z.wide))] * z.bands,
@@ -338,9 +349,10 @@
             pltpu.SemaphoreType.DMA((2,)),
         ],
         compiler_params=pltpu.CompilerParams(vmem_limit_bytes=4 << 20),
-    )(in_hbm(latent), in_hbm(control_hint))
+    )(in_hbm(latent.swapaxes(1, 2)), in_hbm(control_hint.swapaxes(1, 2)))
     blocks = over_bands(blocks)
-    cw1, mw1, cw2, mw2 = load(cw1, mw1, cw2, mw2)
+    cw1, mw1 = load(cw1, mw1)
+    cw2, mw2 = load(cw2, mw2)
     (dw1,) = load(dw1)
     (dw2,) = load(dw2)
     state, act = call(
@@ -377,7 +389,7 @@
     )
     blocks = call(
         kernel(last_kernel),
-        [sds((z.rows, z.columns, z.per))] * z.bands,
+        [sds(z.packed(z.rows * z.columns))] * z.bands,
         *gather(act),
         state,
         part,
@@ -386,12 +398,16 @@
         scratch=work(1) + [pltpu.VMEM((z.height, z.wide, z.per), F32)],
         flops=unit,
     )
-    return call(
+    out = call(
         kernel(rows_kernel),
         sds(raw),
         *over_bands(blocks),
-        scratch=[pltpu.VMEM(raw, F32)],
-    )
+        scratch=[
+            pltpu.VMEM((z.rows, z.width, z.per), F32),
+            pltpu.VMEM((z.rows * z.columns, z.per), F32),
+        ],
+    )
+    return out.swapaxes(1, 2)
 
 
 def solution(mesh):

time: 68.8 us -> 65.3 us (0.949)
  local copies, waits for them, and re-layouts: 4.05 us -> 0.03 us
  Pallas kernels: 18 us -> 19.8 us
  waiting for transfers between devices: 29.4 us -> 27.9 us
    unnamed x14 -> x12, local copies, waits for them, and re-layouts: 3.31 us -> 0.03 us
    ppermute x18, waiting for transfers between devices: 29.4 us -> 27.9 us  [exchange(): return lax.ppermute(cells, axis, [(i, i ^ distance) for i in range(count)])]
    pallas_call x3 -> x4, Pallas kernels: 7.3 us -> 8.25 us  [load(): pl.pallas_call(functools.partial(load_kernel, count), out_shape=[sds(w.sh...]
    pallas_call x7, Pallas kernels: 9.53 us -> 10.4 us  [call(): pl.pallas_call(kernel, out_shape=outs, in_specs=whole(len(args)), out_spe...]
    pallas_call x1 -> x0, local copies, waits for them, and re-layouts: 0.74 us -> none  [call(): pl.pallas_call(kernel, out_shape=outs, in_specs=whole(len(args)), out_spe...]
  transfers between devices with their start and end apart: 18 -> 18, of which waited for: 9 -> 8; matrix products, arithmetic and copies ran while one was open for 0% -> 0% of each run, Pallas kernels for 12% -> 14%
where the time goes in v4:
time: 65.3 us; the launch traced here: 65.1 us
  waiting for transfers between devices  27.9 us (43%)
  Pallas kernels  19.8 us (30%)
  starting transfers between devices  17.1 us (26%)
    ppermute x18, waiting for transfers between devices, exchange(): return lax.ppermute(cells, axis, [(i, i ^ distance) for i in range(count)])  27.9 us
    ppermute x18, starting transfers between devices, exchange(): return lax.ppermute(cells, axis, [(i, i ^ distance) for i in range(count)])  17.1 us
    pallas_call x7, Pallas kernels, call(): pl.pallas_call(kernel, out_shape=outs, in_specs=whole(len(args)), out_spe...  10.4 us
    pallas_call x4, Pallas kernels, load(): pl.pallas_call(functools.partial(load_kernel, count), out_shape=[sds(w.sh...  8.25 us
  transfers between devices with their start and end apart: 18, of which 8 were waited for; matrix products, arithmetic and copies ran while one was open for 0% of the time, Pallas kernels for 14%

profile of v4, /device:TPU:0, one launch (start us, length us, event | category | flops | bytes accessed | tf_op | source)
XLA Modules:
  0.0 65.1 jit_solution(13543166131388377966)
XLA Ops:
  0.0 1.2 %shard_map.136 = (bf16[200,128]{1,0:T(8,128)(2,1)S(1)}, bf16[200,128]{1,0:T(8,128)(2,1)S(1)}, bf16[200,128]{1,0:T(8,128)(2,1)S(1)}, bf16[200,128]{1,0:T(8,128)(2,1)S(1)}) custom-call(bf16[2,160,128]{2,1,0:T(8,128)(2,1)} %bitcast.3, bf16[2,160,128]{2,1,0:T(8,128)(2,1)} %bitcast.4), custom_call_target="tpu_custom_call" | custom-call | tf_op jit(solution)/shard_map/pallas_call | solution.py:341
  1.2 3.1 %collective-permute-start = (bf16[200,128]{1,0:T(8,128)(2,1)S(1)}, bf16[200,128]{1,0:T(8,128)(2,1)S(1)}, u32[]{:S(2)}, u32[]{:S(2)}) collective-permute-start(bf16[200,128]{1,0:T(8,128)(2,1)S(1)} %get-tuple-element.27), channel_id=1, source_target_pairs={{0,2},{2,0},{4,6},{6,4},{1,3},{3,1},{5,7},{7,5},{8,10},{10,8},{12,... | collective-permute-start | bytes 153608 | tf_op jit(solution)/shard_map/ppermute | solution.py:25
  4.3 2.6 %collective-permute-start.1 = (bf16[200,128]{1,0:T(8,128)(2,1)S(1)}, bf16[200,128]{1,0:T(8,128)(2,1)S(1)}, u32[]{:S(2)}, u32[]{:S(2)}) collective-permute-start(bf16[200,128]{1,0:T(8,128)(2,1)S(1)} %get-tuple-element.28), channel_id=1, source_target_pairs={{0,4},{2,6},{4,0},{6,2},{1,5},{3,7},{5,1},{7,3},{8,12},{10,14},{12... | collective-permute-start | bytes 153608 | tf_op jit(solution)/shard_map/ppermute | solution.py:25
  6.9 0.0 collective-permute-start.2
  6.9 0.0 collective-permute-done.refs_1_
  6.9 3.4 %collective-permute-done.1.refs_2_ = bf16[200,128]{1,0:T(8,128)(2,1)S(1)} collective-permute-done((bf16[200,128]{1,0:T(8,128)(2,1)S(1)}, bf16[200,128]{1,0:T(8,128)(2,1)S(1)}, u32[]{:S(2)}, u32[]{:S(2)}) %collective-permute-start.1) | collective-permute-done | bytes 51232 | tf_op jit(solution)/shard_map/ppermute | solution.py:25
  10.3 2.5 %collective-permute-done.2.refs_3_ = bf16[200,128]{1,0:T(8,128)(2,1)S(1)} collective-permute-done((bf16[200,128]{1,0:T(8,128)(2,1)S(1)}, bf16[200,128]{1,0:T(8,128)(2,1)S(1)}, u32[]{:S(2)}, u32[]{:S(2)}) %collective-permute-start.2) | collective-permute-done | bytes 51232 | tf_op jit(solution)/shard_map/ppermute | solution.py:25
  12.8 0.3 shard_map.137
  13.1 0.0 copy-start.2
  13.2 0.0 copy-start.3
  13.2 1.6 %collective-permute-start.4 = (bf16[2,400,128]{2,1,0:T(8,128)(2,1)S(1)}, bf16[2,400,128]{2,1,0:T(8,128)(2,1)S(1)}, u32[]{:S(2)}, u32[]{:S(2)}) collective-permute-start(bf16[2,400,128]{2,1,0:T(8,128)(2,1)S(1)} %get-tuple-element.30.refs_0_), channel_id=1, source_target_pairs={{0,8},{8,0},{1,9},{9,1},{2,10},{10,2},{3,11},{11,3},{4,12},{12,4},... | collective-permute-start | bytes 614408 | tf_op jit(solution)/shard_map/ppermute | solution.py:25
  14.7 0.0 collective-permute-start.3
  14.7 4.3 %collective-permute-done.4.refs_2_ = bf16[2,400,128]{2,1,0:T(8,128)(2,1)S(1)} collective-permute-done((bf16[2,400,128]{2,1,0:T(8,128)(2,1)S(1)}, bf16[2,400,128]{2,1,0:T(8,128)(2,1)S(1)}, u32[]{:S(2)}, u32[]{:S(2)}) %collective-permute-start.4) | collective-permute-done | bytes 204832 | tf_op jit(solution)/shard_map/ppermute | solution.py:25
  19.0 0.0 collective-permute-start.5
  19.0 2.1 %shard_map.138 = (bf16[3,3,160,640]{3,2,1,0:T(8,128)(2,1)S(1)}, bf16[3,3,160,640]{3,2,1,0:T(8,128)(2,1)S(1)}) custom-call(bf16[3,3,160,640]{3,2,1,0:T(8,128)(2,1)} %refs_0_.4, bf16[3,3,160,640]{3,2,1,0:T(8,128)(2,1)} %refs_1_.2), custom_call_target="tpu_custom_call" | custom-call | bytes 3686400 | tf_op jit(solution)/shard_map/pallas_call | solution.py:156
  21.1 0.0 collective-permute-done.3.refs_1_
  21.1 0.0 collective-permute-done.5.refs_3_
  21.1 2.2 %shard_map.139 = (bf16[2,320,160]{2,1,0:T(8,128)(2,1)S(1)}, bf16[2,400,128]{2,1,0:T(8,128)(2,1)S(1)}) custom-call(bf16[2,400,128]{2,1,0:T(8,128)(2,1)S(1)} %get-tuple-element.30.refs_0_, bf16[2,400,128]{2,1,0:T(8,128)(2,1)S(1)} %collective-permute-done.3.refs_1_, bf16[2,400,128]{2,1,0:T(8,128)(2,1)S(1)} %collective-permute-done.4.refs_2_, ...), custom_call_target="tpu_custom_call" | custom-call | flops 1179648000 | bytes 5120640 | tf_op jit(solution)/shard_map/pallas_call | solution.py:44
  23.4 0.0 copy-start.5
  23.4 1.6 %collective-permute-start.7 = (bf16[2,400,128]{2,1,0:T(8,128)(2,1)S(1)}, bf16[2,400,128]{2,1,0:T(8,128)(2,1)S(1)}, u32[]{:S(2)}, u32[]{:S(2)}) collective-permute-start(bf16[2,400,128]{2,1,0:T(8,128)(2,1)S(1)} %get-tuple-element.34.refs_0_), channel_id=1, source_target_pairs={{0,8},{8,0},{1,9},{9,1},{2,10},{10,2},{3,11},{11,3},{4,12},{12,4},... | collective-permute-start | bytes 614408 | tf_op jit(solution)/shard_map/ppermute | solution.py:25
  24.9 0.2 collective-permute-start.6
  25.2 5.8 %collective-permute-done.7.refs_2_ = bf16[2,400,128]{2,1,0:T(8,128)(2,1)S(1)} collective-permute-done((bf16[2,400,128]{2,1,0:T(8,128)(2,1)S(1)}, bf16[2,400,128]{2,1,0:T(8,128)(2,1)S(1)}, u32[]{:S(2)}, u32[]{:S(2)}) %collective-permute-start.7) | collective-permute-done | bytes 204832 | tf_op jit(solution)/shard_map/ppermute | solution.py:25
  30.9 0.0 collective-permute-start.8
  30.9 2.1 %shard_map.140 = (bf16[3,3,160,640]{3,2,1,0:T(8,128)(2,1)S(1)}, bf16[3,3,160,640]{3,2,1,0:T(8,128)(2,1)S(1)}) custom-call(bf16[3,3,160,640]{3,2,1,0:T(8,128)(2,1)} %refs_0_.5, bf16[3,3,160,640]{3,2,1,0:T(8,128)(2,1)} %refs_1_.3), custom_call_target="tpu_custom_call" | custom-call | bytes 3686400 | tf_op jit(solution)/shard_map/pallas_call | solution.py:156
  33.0 0.0 collective-permute-done.8.refs_3_
  33.1 2.3 %shard_map.141 = (bf16[2,320,160]{2,1,0:T(8,128)(2,1)S(1)}, bf16[2,400,128]{2,1,0:T(8,128)(2,1)S(1)}) custom-call(bf16[2,400,128]{2,1,0:T(8,128)(2,1)S(1)} %get-tuple-element.34.refs_0_, bf16[2,400,128]{2,1,0:T(8,128)(2,1)S(1)} %collective-permute-done.6.refs_1_, bf16[2,400,128]{2,1,0:T(8,128)(2,1)S(1)} %collective-permute-done.7.refs_2_, ...), custom_call_target="tpu_custom_call" | custom-call | flops 1179648000 | bytes 5120640 | tf_op jit(solution)/shard_map/pallas_call | solution.py:44
  35.3 1.6 %collective-permute-start.10 = (bf16[2,400,128]{2,1,0:T(8,128)(2,1)S(1)}, bf16[2,400,128]{2,1,0:T(8,128)(2,1)S(1)}, u32[]{:S(2)}, u32[]{:S(2)}) collective-permute-start(bf16[2,400,128]{2,1,0:T(8,128)(2,1)S(1)} %get-tuple-element.38.refs_0_), channel_id=1, source_target_pairs={{0,8},{8,0},{1,9},{9,1},{2,10},{10,2},{3,11},{11,3},{4,12},{12,4},... | collective-permute-start | bytes 614408 | tf_op jit(solution)/shard_map/ppermute | solution.py:25
  36.9 0.2 collective-permute-start.9
  37.1 5.8 %collective-permute-done.10.refs_2_ = bf16[2,400,128]{2,1,0:T(8,128)(2,1)S(1)} collective-permute-done((bf16[2,400,128]{2,1,0:T(8,128)(2,1)S(1)}, bf16[2,400,128]{2,1,0:T(8,128)(2,1)S(1)}, u32[]{:S(2)}, u32[]{:S(2)}) %collective-permute-start.10) | collective-permute-done | bytes 204832 | tf_op jit(solution)/shard_map/ppermute | solution.py:25
  42.9 2.1 %shard_map.142.refs_5_ = bf16[3,3,160,1280]{3,2,1,0:T(8,128)(2,1)S(1)} custom-call(bf16[3,3,160,1280]{3,2,1,0:T(8,128)(2,1)} %refs_0_.6), custom_call_target="tpu_custom_call" | custom-call | bytes 3686400 | tf_op jit(solution)/shard_map/pallas_call | solution.py:156
  44.9 0.0 collective-permute-done.9.refs_1_
  45.0 0.0 collective-permute-done.11.refs_3_
  45.0 2.1 %shard_map.143 = (bf16[320,160]{1,0:T(8,128)(2,1)S(1)}, bf16[400,128]{1,0:T(8,128)(2,1)S(1)}, bf16[320,640]{1,0:T(8,128)(2,1)S(1)}) custom-call(bf16[2,400,128]{2,1,0:T(8,128)(2,1)S(1)} %get-tuple-element.38.refs_0_, bf16[2,400,128]{2,1,0:T(8,128)(2,1)S(1)} %collective-permute-done.9.refs_1_, bf16[2,400,128]{2,1,0:T(8,128)(2,1)S(1)} %collective-permute-done.10.refs_2_, ...), custom_call_target="tpu_custom_call" | custom-call | flops 1179648000 | bytes 5325120 | tf_op jit(solution)/shard_map/pallas_call | solution.py:44
  47.1 1.6 %collective-permute-start.13 = (bf16[400,128]{1,0:T(8,128)(2,1)S(1)}, bf16[400,128]{1,0:T(8,128)(2,1)S(1)}, u32[]{:S(2)}, u32[]{:S(2)}) collective-permute-start(bf16[400,128]{1,0:T(8,128)(2,1)S(1)} %get-tuple-element.40.refs_0_), channel_id=1, source_target_pairs={{0,8},{8,0},{1,9},{9,1},{2,10},{10,2},{3,11},{11,3},{4,12},{12,4},... | collective-permute-start | bytes 307208 | tf_op jit(solution)/shard_map/ppermute | solution.py:25
  48.6 0.2 collective-permute-start.12
  48.8 3.6 %collective-permute-done.13.refs_2_ = bf16[400,128]{1,0:T(8,128)(2,1)S(1)} collective-permute-done((bf16[400,128]{1,0:T(8,128)(2,1)S(1)}, bf16[400,128]{1,0:T(8,128)(2,1)S(1)}, u32[]{:S(2)}, u32[]{:S(2)}) %collective-permute-start.13) | collective-permute-done | bytes 102432 | tf_op jit(solution)/shard_map/ppermute | solution.py:25
  52.4 0.0 collective-permute-start.14
  52.4 2.1 %shard_map.144.w_ref.refs_6_ = bf16[3,3,160,1280]{3,2,1,0:T(8,128)(2,1)S(1)} custom-call(bf16[3,3,160,1280]{3,2,1,0:T(8,128)(2,1)} %refs_0_.7), custom_call_target="tpu_custom_call" | custom-call | bytes 3686400 | tf_op jit(solution)/shard_map/pallas_call | solution.py:156
  54.5 0.0 copy-start.1
  54.5 1.2 %shard_map.145.refs_5_ = f32[320,160]{1,0:T(8,128)S(1)} custom-call(bf16[320,640]{1,0:T(8,128)(2,1)S(1)} %get-tuple-element.42.skip_ref, bf16[3,3,160,1280]{3,2,1,0:T(8,128)(2,1)S(1)} %shard_map.144.w_ref.refs_6_), custom_call_target="tpu_custom_call" | custom-call | flops 589824000 | bytes 4300800 | tf_op jit(solution)/shard_map/pallas_call | solution.py:44
  55.7 1.5 %shard_map.146 = (bf16[80,128]{1,0:T(8,128)(2,1)S(1)}, bf16[80,128]{1,0:T(8,128)(2,1)S(1)}, bf16[80,128]{1,0:T(8,128)(2,1)S(1)}, bf16[80,128]{1,0:T(8,128)(2,1)S(1)}) custom-call(bf16[400,128]{1,0:T(8,128)(2,1)S(1)} %get-tuple-element.40.refs_0_, bf16[400,128]{1,0:T(8,128)(2,1)S(1)} %collective-permute-done.12.refs_1_, ...), custom_call_target="tpu_custom_call" | custom-call | flops 589824000 | bytes 4485440 | tf_op jit(solution)/shard_map/pallas_call | solution.py:44
  57.2 0.1 collective-permute-start.15
  57.3 1.4 %collective-permute-start.16 = (bf16[80,128]{1,0:T(8,128)(2,1)S(1)}, bf16[80,128]{1,0:T(8,128)(2,1)S(1)}, u32[]{:S(2)}, u32[]{:S(2)}) collective-permute-start(bf16[80,128]{1,0:T(8,128)(2,1)S(1)} %get-tuple-element.45), channel_id=1, source_target_pairs={{0,4},{2,6},{4,0},{6,2},{1,5},{3,7},{5,1},{7,3},{8,12},{10,14},{12... | collective-permute-start | bytes 61448 | tf_op jit(solution)/shard_map/ppermute | solution.py:25
  58.7 3.0 %collective-permute-start.17 = (bf16[80,128]{1,0:T(8,128)(2,1)S(1)}, bf16[80,128]{1,0:T(8,128)(2,1)S(1)}, u32[]{:S(2)}, u32[]{:S(2)}) collective-permute-start(bf16[80,128]{1,0:T(8,128)(2,1)S(1)} %get-tuple-element.46), channel_id=1, source_target_pairs={{0,6},{2,4},{4,2},{6,0},{1,7},{3,5},{5,3},{7,1},{8,14},{10,12},{12... | collective-permute-start | bytes 61448 | tf_op jit(solution)/shard_map/ppermute | solution.py:25
  61.6 0.0 collective-permute-done.15.refs_1_
  61.6 0.6 collective-permute-done.16.refs_2_
  62.2 2.0 %collective-permute-done.17.refs_3_ = bf16[80,128]{1,0:T(8,128)(2,1)S(1)} collective-permute-done((bf16[80,128]{1,0:T(8,128)(2,1)S(1)}, bf16[80,128]{1,0:T(8,128)(2,1)S(1)}, u32[]{:S(2)}, u32[]{:S(2)}) %collective-permute-start.17) | collective-permute-done | bytes 20512 | tf_op jit(solution)/shard_map/ppermute | solution.py:25
  64.3 0.8 %shard_map.147 = bf16[2,160,128]{2,1,0:T(8,128)(2,1)} custom-call(bf16[80,128]{1,0:T(8,128)(2,1)S(1)} %get-tuple-element.43.refs_0_, bf16[80,128]{1,0:T(8,128)(2,1)S(1)} %collective-permute-done.15.refs_1_, bf16[80,128]{1,0:T(8,128)(2,1)S(1)} %collective-permute-done.16.refs_2_, bf16[80,128]{1,0:T(8,128)(2,1)S(1)} %collective-permute-done.17.refs_3_), custom_call_target="tpu_custom_call" | custom-call | bytes 163840 | tf_op jit(solution)/shard_map/pallas_call | solution.py:44
  (12 shorter events, 0.0 us)
Async XLA Ops:
  1.2 5.7 %collective-permute-start = (bf16[200,128]{1,0:T(8,128)(2,1)S(1)}, bf16[200,128]{1,0:T(8,128)(2,1)S(1)}, u32[]{:S(2)}, u32[]{:S(2)}) collective-permute-start(bf16[200,128]{1,0:T(8,128)(2,1)S(1)} %get-tuple-element.27), channel_id=1, source_target_pairs={{0,2},{2,0},{4,6},{6,4},{1,3},{3,1},{5,7},{7,5},{8,10},{10,8},{12,... | collective-permute-start | bytes 153608 | tf_op jit(solution)/shard_map/ppermute | solution.py:25
  4.3 6.0 %collective-permute-start.1 = (bf16[200,128]{1,0:T(8,128)(2,1)S(1)}, bf16[200,128]{1,0:T(8,128)(2,1)S(1)}, u32[]{:S(2)}, u32[]{:S(2)}) collective-permute-start(bf16[200,128]{1,0:T(8,128)(2,1)S(1)} %get-tuple-element.28), channel_id=1, source_target_pairs={{0,4},{2,6},{4,0},{6,2},{1,5},{3,7},{5,1},{7,3},{8,12},{10,14},{12... | collective-permute-start | bytes 153608 | tf_op jit(solution)/shard_map/ppermute | solution.py:25
  6.9 5.9 %collective-permute-start.2 = (bf16[200,128]{1,0:T(8,128)(2,1)S(1)}, bf16[200,128]{1,0:T(8,128)(2,1)S(1)}, u32[]{:S(2)}, u32[]{:S(2)}) collective-permute-start(bf16[200,128]{1,0:T(8,128)(2,1)S(1)} %get-tuple-element.29), channel_id=1, source_target_pairs={{0,6},{2,4},{4,2},{6,0},{1,7},{3,5},{5,3},{7,1},{8,14},{10,12},{12... | collective-permute-start | bytes 153608 | tf_op jit(solution)/shard_map/ppermute | solution.py:25
  13.1 8.0 %copy-start.2 = (bf16[160]{0:T(256)(128)(2,1)S(1)}, bf16[160]{0:T(256)(128)(2,1)}, u32[]{:S(2)}) copy-start(bf16[160]{0:T(256)(128)(2,1)} %refs_6_.3) | copy-start | bytes 964
  13.2 8.0 %copy-start.3 = (bf16[160]{0:T(256)(128)(2,1)S(1)}, bf16[160]{0:T(256)(128)(2,1)}, u32[]{:S(2)}) copy-start(bf16[160]{0:T(256)(128)(2,1)} %refs_8_.2) | copy-start | bytes 964
  13.2 5.8 %collective-permute-start.4 = (bf16[2,400,128]{2,1,0:T(8,128)(2,1)S(1)}, bf16[2,400,128]{2,1,0:T(8,128)(2,1)S(1)}, u32[]{:S(2)}, u32[]{:S(2)}) collective-permute-start(bf16[2,400,128]{2,1,0:T(8,128)(2,1)S(1)} %get-tuple-element.30.refs_0_), channel_id=1, source_target_pairs={{0,8},{8,0},{1,9},{9,1},{2,10},{10,2},{3,11},{11,3},{4,12},{12,4},... | collective-permute-start | bytes 614408 | tf_op jit(solution)/shard_map/ppermute | solution.py:25
  14.7 6.4 %collective-permute-start.3 = (bf16[2,400,128]{2,1,0:T(8,128)(2,1)S(1)}, bf16[2,400,128]{2,1,0:T(8,128)(2,1)S(1)}, u32[]{:S(2)}, u32[]{:S(2)}) collective-permute-start(bf16[2,400,128]{2,1,0:T(8,128)(2,1)S(1)} %get-tuple-element.30.refs_0_), channel_id=1, source_target_pairs={{0,1},{1,0},{2,3},{3,2},{4,5},{5,4},{6,7},{7,6},{8,9},{9,8},{10,11... | collective-permute-start | bytes 614408 | tf_op jit(solution)/shard_map/ppermute | solution.py:25
  19.0 2.1 %collective-permute-start.5 = (bf16[2,400,128]{2,1,0:T(8,128)(2,1)S(1)}, bf16[2,400,128]{2,1,0:T(8,128)(2,1)S(1)}, u32[]{:S(2)}, u32[]{:S(2)}) collective-permute-start(bf16[2,400,128]{2,1,0:T(8,128)(2,1)S(1)} %collective-permute-done.4.refs_2_), channel_id=1, source_target_pairs={{0,1},{1,0},{2,3},{3,2},{4,5},{5,4},{6,7},{7,6},{8,9},{9,8},{10,11... | collective-permute-start | bytes 614408 | tf_op jit(solution)/shard_map/ppermute | solution.py:25
  23.4 9.7 %copy-start.4 = (bf16[160]{0:T(256)(128)(2,1)S(1)}, bf16[160]{0:T(256)(128)(2,1)}, u32[]{:S(2)}) copy-start(bf16[160]{0:T(256)(128)(2,1)} %refs_6_.4) | copy-start | bytes 964
  23.4 9.7 %copy-start.5 = (bf16[160]{0:T(256)(128)(2,1)S(1)}, bf16[160]{0:T(256)(128)(2,1)}, u32[]{:S(2)}) copy-start(bf16[160]{0:T(256)(128)(2,1)} %refs_8_.3) | copy-start | bytes 964
  23.4 7.5 %collective-permute-start.7 = (bf16[2,400,128]{2,1,0:T(8,128)(2,1)S(1)}, bf16[2,400,128]{2,1,0:T(8,128)(2,1)S(1)}, u32[]{:S(2)}, u32[]{:S(2)}) collective-permute-start(bf16[2,400,128]{2,1,0:T(8,128)(2,1)S(1)} %get-tuple-element.34.refs_0_), channel_id=1, source_target_pairs={{0,8},{8,0},{1,9},{9,1},{2,10},{10,2},{3,11},{11,3},{4,12},{12,4},... | collective-permute-start | bytes 614408 | tf_op jit(solution)/shard_map/ppermute | solution.py:25
  24.9 8.1 %collective-permute-start.6 = (bf16[2,400,128]{2,1,0:T(8,128)(2,1)S(1)}, bf16[2,400,128]{2,1,0:T(8,128)(2,1)S(1)}, u32[]{:S(2)}, u32[]{:S(2)}) collective-permute-start(bf16[2,400,128]{2,1,0:T(8,128)(2,1)S(1)} %get-tuple-element.34.refs_0_), channel_id=1, source_target_pairs={{0,1},{1,0},{2,3},{3,2},{4,5},{5,4},{6,7},{7,6},{8,9},{9,8},{10,11... | collective-permute-start | bytes 614408 | tf_op jit(solution)/shard_map/ppermute | solution.py:25
  30.9 2.1 %collective-permute-start.8 = (bf16[2,400,128]{2,1,0:T(8,128)(2,1)S(1)}, bf16[2,400,128]{2,1,0:T(8,128)(2,1)S(1)}, u32[]{:S(2)}, u32[]{:S(2)}) collective-permute-start(bf16[2,400,128]{2,1,0:T(8,128)(2,1)S(1)} %collective-permute-done.7.refs_2_), channel_id=1, source_target_pairs={{0,1},{1,0},{2,3},{3,2},{4,5},{5,4},{6,7},{7,6},{8,9},{9,8},{10,11... | collective-permute-start | bytes 614408 | tf_op jit(solution)/shard_map/ppermute | solution.py:25
  35.3 9.6 %copy-start = (bf16[160]{0:T(256)(128)(2,1)S(1)}, bf16[160]{0:T(256)(128)(2,1)}, u32[]{:S(2)}) copy-start(bf16[160]{0:T(256)(128)(2,1)} %refs_6_.5) | copy-start | bytes 964
  35.3 7.6 %collective-permute-start.10 = (bf16[2,400,128]{2,1,0:T(8,128)(2,1)S(1)}, bf16[2,400,128]{2,1,0:T(8,128)(2,1)S(1)}, u32[]{:S(2)}, u32[]{:S(2)}) collective-permute-start(bf16[2,400,128]{2,1,0:T(8,128)(2,1)S(1)} %get-tuple-element.38.refs_0_), channel_id=1, source_target_pairs={{0,8},{8,0},{1,9},{9,1},{2,10},{10,2},{3,11},{11,3},{4,12},{12,4},... | collective-permute-start | bytes 614408 | tf_op jit(solution)/shard_map/ppermute | solution.py:25
  36.9 8.1 %collective-permute-start.9 = (bf16[2,400,128]{2,1,0:T(8,128)(2,1)S(1)}, bf16[2,400,128]{2,1,0:T(8,128)(2,1)S(1)}, u32[]{:S(2)}, u32[]{:S(2)}) collective-permute-start(bf16[2,400,128]{2,1,0:T(8,128)(2,1)S(1)} %get-tuple-element.38.refs_0_), channel_id=1, source_target_pairs={{0,1},{1,0},{2,3},{3,2},{4,5},{5,4},{6,7},{7,6},{8,9},{9,8},{10,11... | collective-permute-start | bytes 614408 | tf_op jit(solution)/shard_map/ppermute | solution.py:25
  42.9 2.1 %collective-permute-start.11 = (bf16[2,400,128]{2,1,0:T(8,128)(2,1)S(1)}, bf16[2,400,128]{2,1,0:T(8,128)(2,1)S(1)}, u32[]{:S(2)}, u32[]{:S(2)}) collective-permute-start(bf16[2,400,128]{2,1,0:T(8,128)(2,1)S(1)} %collective-permute-done.10.refs_2_), channel_id=1, source_target_pairs={{0,1},{1,0},{2,3},{3,2},{4,5},{5,4},{6,7},{7,6},{8,9},{9,8},{10,11... | collective-permute-start | bytes 614408 | tf_op jit(solution)/shard_map/ppermute | solution.py:25
  47.1 5.4 %collective-permute-start.13 = (bf16[400,128]{1,0:T(8,128)(2,1)S(1)}, bf16[400,128]{1,0:T(8,128)(2,1)S(1)}, u32[]{:S(2)}, u32[]{:S(2)}) collective-permute-start(bf16[400,128]{1,0:T(8,128)(2,1)S(1)} %get-tuple-element.40.refs_0_), channel_id=1, source_target_pairs={{0,8},{8,0},{1,9},{9,1},{2,10},{10,2},{3,11},{11,3},{4,12},{12,4},... | collective-permute-start | bytes 307208 | tf_op jit(solution)/shard_map/ppermute | solution.py:25
  48.6 7.1 %collective-permute-start.12 = (bf16[400,128]{1,0:T(8,128)(2,1)S(1)}, bf16[400,128]{1,0:T(8,128)(2,1)S(1)}, u32[]{:S(2)}, u32[]{:S(2)}) collective-permute-start(bf16[400,128]{1,0:T(8,128)(2,1)S(1)} %get-tuple-element.40.refs_0_), channel_id=1, source_target_pairs={{0,1},{1,0},{2,3},{3,2},{4,5},{5,4},{6,7},{7,6},{8,9},{9,8},{10,11... | collective-permute-start | bytes 307208 | tf_op jit(solution)/shard_map/ppermute | solution.py:25
  52.4 3.3 %collective-permute-start.14 = (bf16[400,128]{1,0:T(8,128)(2,1)S(1)}, bf16[400,128]{1,0:T(8,128)(2,1)S(1)}, u32[]{:S(2)}, u32[]{:S(2)}) collective-permute-start(bf16[400,128]{1,0:T(8,128)(2,1)S(1)} %collective-permute-done.13.refs_2_), channel_id=1, source_target_pairs={{0,1},{1,0},{2,3},{3,2},{4,5},{5,4},{6,7},{7,6},{8,9},{9,8},{10,11... | collective-permute-start | bytes 307208 | tf_op jit(solution)/shard_map/ppermute | solution.py:25
  54.5 1.2 %copy-start.1 = (bf16[160]{0:T(256)(128)(2,1)S(1)}, bf16[160]{0:T(256)(128)(2,1)}, u32[]{:S(2)}) copy-start(bf16[160]{0:T(256)(128)(2,1)} %refs_7_.1) | copy-start | bytes 964
  57.2 4.5 %collective-permute-start.15 = (bf16[80,128]{1,0:T(8,128)(2,1)S(1)}, bf16[80,128]{1,0:T(8,128)(2,1)S(1)}, u32[]{:S(2)}, u32[]{:S(2)}) collective-permute-start(bf16[80,128]{1,0:T(8,128)(2,1)S(1)} %get-tuple-element.44), channel_id=1, source_target_pairs={{0,2},{2,0},{4,6},{6,4},{1,3},{3,1},{5,7},{7,5},{8,10},{10,8},{12,... | collective-permute-start | bytes 61448 | tf_op jit(solution)/shard_map/ppermute | solution.py:25
  57.3 4.9 %collective-permute-start.16 = (bf16[80,128]{1,0:T(8,128)(2,1)S(1)}, bf16[80,128]{1,0:T(8,128)(2,1)S(1)}, u32[]{:S(2)}, u32[]{:S(2)}) collective-permute-start(bf16[80,128]{1,0:T(8,128)(2,1)S(1)} %get-tuple-element.45), channel_id=1, source_target_pairs={{0,4},{2,6},{4,0},{6,2},{1,5},{3,7},{5,1},{7,3},{8,12},{10,14},{12... | collective-permute-start | bytes 61448 | tf_op jit(solution)/shard_map/ppermute | solution.py:25
  58.7 5.6 %collective-permute-start.17 = (bf16[80,128]{1,0:T(8,128)(2,1)S(1)}, bf16[80,128]{1,0:T(8,128)(2,1)S(1)}, u32[]{:S(2)}, u32[]{:S(2)}) collective-permute-start(bf16[80,128]{1,0:T(8,128)(2,1)S(1)} %get-tuple-element.46), channel_id=1, source_target_pairs={{0,6},{2,4},{4,2},{6,0},{1,7},{3,5},{5,3},{7,1},{8,14},{10,12},{12... | collective-permute-start | bytes 61448 | tf_op jit(solution)/shard_map/ppermute | solution.py:25

commit v5 on v4

--- a/solution.py
+++ b/solution.py
@@ -64,6 +64,7 @@
         self.wide = self.columns + 2 * LAYERS
         self.height = self.rows * self.bands
         self.cells = self.height * self.wide
+        self.held = self.cells + 2 * self.height
         self.shards = channel_count()
         self.rest = self.per % LANES
         self.groups = LANES // self.rest if self.rest and LANES % self.rest == 0 else 0
@@ -108,8 +109,8 @@
 
 
 def masked_silu(z, state):
-    value = silu(state).reshape(-1, z.wide, z.per)
-    at = lax.broadcasted_iota(jnp.int32, value.shape, 1)
+    value = silu(state).reshape(z.wide, z.height, z.per)
+    at = lax.broadcasted_iota(jnp.int32, value.shape, 0)
     at = at + (lax.axis_index("band") * z.columns - LAYERS)
     value = jnp.where((at >= 0) & (at < z.width), value, 0.0)
     return value.reshape(-1, z.per)
@@ -166,6 +167,10 @@
     )(*[in_hbm(w) for w in weights])
 
 
+def lane_groups(z):
+    return [(at, min(LANES, z.per - at)) for at in range(0, z.per, LANES)]
+
+
 def join_kernel(z, *refs):
     blocks, (state_ref, act_ref, image, block_image) = refs[:-4], refs[-4:]
     band = lax.axis_index("band")
@@ -173,15 +178,20 @@
 
     def put(row, lane, piece):
         rows, lanes = piece.shape
-        block_image[row : row + rows, lane : lane + lanes] = piece
+        group, lane = lane // LANES, lane % LANES
+        block_image[group, row : row + rows, lane : lane + lanes] = piece
 
     for k, block in enumerate(blocks):
-        start = pl.multiple_of((band ^ k) * size, 8)
         unpack(z, 2 * size, block[...].astype(F32), put)
         for t in range(2):
-            image[t, pl.ds(start, size)] = block_image[t * size : (t + 1) * size]
+            for row in range(z.rows):
+                to = pl.ds((band ^ k) * z.rows + row, z.wide, stride=z.height)
+                at = t * size + row * z.wide
+                for g in range(len(lane_groups(z))):
+                    image[t, g, to] = block_image[g, at : at + z.wide]
     for t in range(2):
-        value = image[t]
+        parts = [image[t, g][:, :n] for g, (_, n) in enumerate(lane_groups(z))]
+        value = jnp.concatenate(parts, axis=1)
         state_ref[t] = value.astype(BF16)
         pack(z, act_ref.at[t], masked_silu(z, value))
 
@@ -204,21 +214,27 @@
         def put(row, lane, piece):
             rows, lanes = piece.shape
             lane = at + j * z.per + lane
+            row = row + z.height
             a_ref[row : row + rows, lane : lane + lanes] = piece
 
         unpack(z, z.cells, message, put)
 
 
-def convolve(z, cells, weight, left, right):
-    n = z.cells
-    left[8 : 8 + n] = lax.dot_general(cells, weight(0), TRANSPOSED, preferred_element_type=F32)
-    right[8 : 8 + n] = lax.dot_general(cells, weight(2), TRANSPOSED, preferred_element_type=F32)
-    middle = lax.dot_general(cells, weight(1), TRANSPOSED, preferred_element_type=F32)
-    total = middle + left[7 : 7 + n] + right[9 : 9 + n]
-    row = jnp.zeros((z.wide, z.per), F32)
-    above = jnp.concatenate([row, total[: n - z.wide, : z.per]], 0)
-    below = jnp.concatenate([total[z.wide :, 2 * z.per :], row], 0)
-    return total[:, z.per : 2 * z.per] + above + below
+def convolve(z, cells, weight):
+    moved = jnp.concatenate([cells(j) for j in range(3)], axis=1)
+    weights = jnp.concatenate([weight(j) for j in range(3)], axis=1)
+    total = lax.dot_general(moved, weights, TRANSPOSED, preferred_element_type=F32)
+    above, middle, below = [
+        total[:, i * z.per : (i + 1) * z.per].reshape(z.wide, z.height, z.per) for i in range(3)
+    ]
+    row = lax.broadcasted_iota(jnp.int32, middle.shape, 1)
+    above = jnp.where(row == 0, 0.0, pltpu.roll(above, 1, 1))
+    below = jnp.where(row == z.height - 1, 0.0, pltpu.roll(below, z.height - 1, 1))
+    return (middle + above + below).reshape(-1, z.per)
+
+
+def moves(z, a_ref):
+    return lambda j: a_ref[j * z.height : j * z.height + z.cells]
 
 
 def taps(z, w_ref, start, depth):
@@ -228,9 +244,10 @@
     return weight
 
 
-def clear_edges(z, left, right):
-    left[0:8] = jnp.zeros((8, 3 * z.per), F32)
-    right[8 + z.cells : 16 + z.cells] = jnp.zeros((8, 3 * z.per), F32)
+def clear_edges(z, a_ref):
+    edge = jnp.zeros((z.height, a_ref.shape[1]), BF16)
+    a_ref[: z.height] = edge
+    a_ref[z.height + z.cells :] = edge
 
 
 def finish(z, state, result, bias, new_ref, act_ref):
@@ -246,46 +263,53 @@
 def layer_kernel(z, *refs):
     n = z.shards
     blocks, refs = refs[:n], refs[n:]
-    state_ref, w0, b0, w1, b1, new_ref, act_ref, a_ref, left, right = refs
-    clear_edges(z, left, right)
+    state_ref, w0, b0, w1, b1, new_ref, act_ref, a_ref = refs
     for t, (w_ref, b_ref) in enumerate(((w0, b0), (w1, b1))):
-        lay_out(z, a_ref, [block[t] for block in blocks])
-        result = convolve(z, a_ref[...], taps(z, w_ref, 0, z.depth), left, right)
+        clear_edges(z, a_ref.at[t])
+        lay_out(z, a_ref.at[t], [block[t] for block in blocks])
+        result = convolve(z, moves(z, a_ref.at[t]), taps(z, w_ref, 0, z.depth))
         finish(z, state_ref[t], result, bias_of(b_ref), new_ref.at[t], act_ref.at[t])
 
 
 def decode_kernel(z, *refs):
     n = z.shards
     blocks, refs = refs[:n], refs[n:]
-    state_ref, w_ref, b_ref, new_ref, act_ref, skip_ref, a_ref, left, right = refs
-    clear_edges(z, left, right)
+    state_ref, w_ref, b_ref, new_ref, act_ref, skip_ref, a_ref = refs
+    clear_edges(z, a_ref)
     lay_out(z, a_ref, [block[1] for block in blocks])
     lay_out(z, a_ref, [block[0] for block in blocks], z.depth)
     skip_ref[...] = a_ref[:, z.depth :]
-    result = convolve(z, a_ref[...], taps(z, w_ref, 0, 2 * z.depth), left, right)
+    result = convolve(z, moves(z, a_ref), taps(z, w_ref, 0, 2 * z.depth))
     finish(z, state_ref[1], result, bias_of(b_ref), new_ref, act_ref)
 
 
-def skip_kernel(z, skip_ref, w_ref, out_ref, left, right):
-    clear_edges(z, left, right)
-    out_ref[...] = convolve(z, skip_ref[...], taps(z, w_ref, z.depth, z.depth), left, right)
+def skip_kernel(z, skip_ref, w_ref, out_ref):
+    out_ref[...] = convolve(z, moves(z, skip_ref), taps(z, w_ref, z.depth, z.depth))
 
 
 def last_kernel(z, *refs):
     n = z.shards
     blocks, refs = refs[:n], refs[n:]
     state_ref, skip_ref, w_ref, b_ref = refs[:4]
-    outs, (a_ref, left, right, image) = refs[4 : 4 + z.bands], refs[4 + z.bands :]
-    clear_edges(z, left, right)
+    outs, (a_ref, image) = refs[4 : 4 + z.bands], refs[4 + z.bands :]
+    clear_edges(z, a_ref)
     lay_out(z, a_ref, [block[...] for block in blocks])
-    result = convolve(z, a_ref[...], taps(z, w_ref, 0, z.depth), left, right)
+    result = convolve(z, moves(z, a_ref), taps(z, w_ref, 0, z.depth))
     total = state_ref[...].astype(F32) + (result + skip_ref[...])
     total = total + bias_of(b_ref)
-    image[...] = total.reshape(z.height, z.wide, z.per)
+    groups = lane_groups(z)
+    for g, (lane, n) in enumerate(groups):
+        image[g, :, :n] = total[:, lane : lane + n]
     band = lax.axis_index("band")
     for k, out in enumerate(outs):
-        rows = image[pl.ds((band ^ k) * z.rows, z.rows), LAYERS : LAYERS + z.columns]
-        pack(z, out, rows.reshape(-1, z.per))
+        rows = []
+        for row in range(z.rows):
+            first = LAYERS * z.height + (band ^ k) * z.rows + row
+            at = pl.ds(first, z.columns, stride=z.height)
+            rows.append(
+                jnp.concatenate([image[g, at][:, :n] for g, (_, n) in enumerate(groups)], axis=1)
+            )
+        pack(z, out, jnp.concatenate(rows, axis=0))
 
 
 def rows_kernel(z, *refs):
@@ -330,8 +354,8 @@
 def per_device(latent, control_hint, cw1, cb1, cw2, cb2, mw1, mb1, mw2, mb2, dw1, db1, dw2, db2):
     z = Sizes(latent)
     kernel = lambda f, *a: functools.partial(f, z, *a)
-    edges = [pltpu.VMEM((z.cells + 16, 3 * z.per), F32)] * 2
-    work = lambda parts: [pltpu.VMEM((z.cells, parts * z.depth), BF16)] + edges
+    held = lambda *parts: [pltpu.VMEM(parts[:-1] + (z.held, parts[-1] * z.depth), BF16)]
+    groups = len(lane_groups(z))
     unit = 2 * 9 * z.cells * z.per * z.depth
     single = sds((z.cells, z.per))
     pair = sds((2, z.cells, z.per))
@@ -360,8 +384,8 @@
         [pair, sds((2,) + message)],
         *blocks,
         scratch=[
-            pltpu.VMEM((2, z.cells, z.per), F32),
-            pltpu.VMEM((2 * z.rows * z.wide, z.per), F32),
+            pltpu.VMEM((2, groups, z.cells, LANES), F32),
+            pltpu.VMEM((groups, 2 * z.rows * z.wide, LANES), F32),
         ],
     )
     for weights in ((cw1, cb1, mw1, mb1), (cw2, cb2, mw2, mb2)):
@@ -371,22 +395,20 @@
             *gather(act),
             state,
             *weights,
-            scratch=work(1),
+            scratch=held(2, 1),
             flops=2 * unit,
         )
     state, act, skip = call(
         kernel(decode_kernel),
-        [single, sds(message), sds((z.cells, z.depth))],
+        [single, sds(message), sds((z.held, z.depth))],
         *gather(act),
         state,
         dw1,
         db1,
-        scratch=work(2),
+        scratch=held(2),
         flops=2 * unit,
     )
-    part = call(
-        kernel(skip_kernel), sds((z.cells, z.per), F32), skip, dw2, scratch=edges, flops=unit
-    )
+    part = call(kernel(skip_kernel), sds((z.cells, z.per), F32), skip, dw2, flops=unit)
     blocks = call(
         kernel(last_kernel),
         [sds(z.packed(z.rows * z.columns))] * z.bands,
@@ -395,7 +417,7 @@
         part,
         dw2,
         db2,
-        scratch=work(1) + [pltpu.VMEM((z.height, z.wide, z.per), F32)],
+        scratch=held(1) + [pltpu.VMEM((groups, z.cells, LANES), F32)],
         flops=unit,
     )
     out = call(

time: 65.3 us -> 65.5 us (level)
  no operation moved by 1% of the time
where the time goes in v5:
time: 65.5 us; the launch traced here: 65.3 us
  waiting for transfers between devices  27.9 us (43%)
  Pallas kernels  20 us (31%)
  starting transfers between devices  17 us (26%)
    ppermute x18, waiting for transfers between devices, exchange(): return lax.ppermute(cells, axis, [(i, i ^ distance) for i in range(count)])  27.9 us
    ppermute x18, starting transfers between devices, exchange(): return lax.ppermute(cells, axis, [(i, i ^ distance) for i in range(count)])  17 us
    pallas_call x7, Pallas kernels, call(): pl.pallas_call(kernel, out_shape=outs, in_specs=whole(len(args)), out_spe...  10.6 us
    pallas_call x4, Pallas kernels, load(): pl.pallas_call(functools.partial(load_kernel, count), out_shape=[sds(w.sh...  8.25 us
  transfers between devices with their start and end apart: 18, of which 8 were waited for; matrix products, arithmetic and copies ran while one was open for 0% of the time, Pallas kernels for 14%

profile of v5, /device:TPU:0, one launch (start us, length us, event | category | flops | bytes accessed | tf_op | source)
XLA Modules:
  0.0 65.3 jit_solution(16666571722010197234)
XLA Ops:
  0.0 1.2 %shard_map.136 = (bf16[200,128]{1,0:T(8,128)(2,1)S(1)}, bf16[200,128]{1,0:T(8,128)(2,1)S(1)}, bf16[200,128]{1,0:T(8,128)(2,1)S(1)}, bf16[200,128]{1,0:T(8,128)(2,1)S(1)}) custom-call(bf16[2,160,128]{2,1,0:T(8,128)(2,1)} %bitcast.3, bf16[2,160,128]{2,1,0:T(8,128)(2,1)} %bitcast.4), custom_call_target="tpu_custom_call" | custom-call | tf_op jit(solution)/shard_map/pallas_call | solution.py:365
  1.2 3.1 %collective-permute-start = (bf16[200,128]{1,0:T(8,128)(2,1)S(1)}, bf16[200,128]{1,0:T(8,128)(2,1)S(1)}, u32[]{:S(2)}, u32[]{:S(2)}) collective-permute-start(bf16[200,128]{1,0:T(8,128)(2,1)S(1)} %get-tuple-element.27), channel_id=1, source_target_pairs={{0,2},{2,0},{4,6},{6,4},{1,3},{3,1},{5,7},{7,5},{8,10},{10,8},{12,... | collective-permute-start | bytes 153608 | tf_op jit(solution)/shard_map/ppermute | solution.py:25
  4.3 2.6 %collective-permute-start.1 = (bf16[200,128]{1,0:T(8,128)(2,1)S(1)}, bf16[200,128]{1,0:T(8,128)(2,1)S(1)}, u32[]{:S(2)}, u32[]{:S(2)}) collective-permute-start(bf16[200,128]{1,0:T(8,128)(2,1)S(1)} %get-tuple-element.28), channel_id=1, source_target_pairs={{0,4},{2,6},{4,0},{6,2},{1,5},{3,7},{5,1},{7,3},{8,12},{10,14},{12... | collective-permute-start | bytes 153608 | tf_op jit(solution)/shard_map/ppermute | solution.py:25
  6.9 0.0 collective-permute-start.2
  6.9 0.0 collective-permute-done.refs_1_
  6.9 3.4 %collective-permute-done.1.refs_2_ = bf16[200,128]{1,0:T(8,128)(2,1)S(1)} collective-permute-done((bf16[200,128]{1,0:T(8,128)(2,1)S(1)}, bf16[200,128]{1,0:T(8,128)(2,1)S(1)}, u32[]{:S(2)}, u32[]{:S(2)}) %collective-permute-start.1) | collective-permute-done | bytes 51232 | tf_op jit(solution)/shard_map/ppermute | solution.py:25
  10.3 2.5 %collective-permute-done.2.refs_3_ = bf16[200,128]{1,0:T(8,128)(2,1)S(1)} collective-permute-done((bf16[200,128]{1,0:T(8,128)(2,1)S(1)}, bf16[200,128]{1,0:T(8,128)(2,1)S(1)}, u32[]{:S(2)}, u32[]{:S(2)}) %collective-permute-start.2) | collective-permute-done | bytes 51232 | tf_op jit(solution)/shard_map/ppermute | solution.py:25
  12.8 0.4 shard_map.137
  13.2 0.0 copy-start.2
  13.2 0.0 copy-start.3
  13.3 1.6 %collective-permute-start.4 = (bf16[2,400,128]{2,1,0:T(8,128)(2,1)S(1)}, bf16[2,400,128]{2,1,0:T(8,128)(2,1)S(1)}, u32[]{:S(2)}, u32[]{:S(2)}) collective-permute-start(bf16[2,400,128]{2,1,0:T(8,128)(2,1)S(1)} %get-tuple-element.30.refs_0_), channel_id=1, source_target_pairs={{0,8},{8,0},{1,9},{9,1},{2,10},{10,2},{3,11},{11,3},{4,12},{12,4},... | collective-permute-start | bytes 614408 | tf_op jit(solution)/shard_map/ppermute | solution.py:25
  14.8 0.0 collective-permute-start.3
  14.8 4.3 %collective-permute-done.4.refs_2_ = bf16[2,400,128]{2,1,0:T(8,128)(2,1)S(1)} collective-permute-done((bf16[2,400,128]{2,1,0:T(8,128)(2,1)S(1)}, bf16[2,400,128]{2,1,0:T(8,128)(2,1)S(1)}, u32[]{:S(2)}, u32[]{:S(2)}) %collective-permute-start.4) | collective-permute-done | bytes 204832 | tf_op jit(solution)/shard_map/ppermute | solution.py:25
  19.1 0.0 collective-permute-start.5
  19.1 2.1 %shard_map.138 = (bf16[3,3,160,640]{3,2,1,0:T(8,128)(2,1)S(1)}, bf16[3,3,160,640]{3,2,1,0:T(8,128)(2,1)S(1)}) custom-call(bf16[3,3,160,640]{3,2,1,0:T(8,128)(2,1)} %refs_0_.4, bf16[3,3,160,640]{3,2,1,0:T(8,128)(2,1)} %refs_1_.2), custom_call_target="tpu_custom_call" | custom-call | bytes 3686400 | tf_op jit(solution)/shard_map/pallas_call | solution.py:157
  21.2 0.0 collective-permute-done.3.refs_1_
  21.2 0.0 collective-permute-done.5.refs_3_
  21.2 2.2 %shard_map.139 = (bf16[2,320,160]{2,1,0:T(8,128)(2,1)S(1)}, bf16[2,400,128]{2,1,0:T(8,128)(2,1)S(1)}) custom-call(bf16[2,400,128]{2,1,0:T(8,128)(2,1)S(1)} %get-tuple-element.30.refs_0_, bf16[2,400,128]{2,1,0:T(8,128)(2,1)S(1)} %collective-permute-done.3.refs_1_, bf16[2,400,128]{2,1,0:T(8,128)(2,1)S(1)} %collective-permute-done.4.refs_2_, ...), custom_call_target="tpu_custom_call" | custom-call | flops 1179648000 | bytes 5120640 | tf_op jit(solution)/shard_map/pallas_call | solution.py:44
  23.4 1.6 %collective-permute-start.7 = (bf16[2,400,128]{2,1,0:T(8,128)(2,1)S(1)}, bf16[2,400,128]{2,1,0:T(8,128)(2,1)S(1)}, u32[]{:S(2)}, u32[]{:S(2)}) collective-permute-start(bf16[2,400,128]{2,1,0:T(8,128)(2,1)S(1)} %get-tuple-element.34.refs_0_), channel_id=1, source_target_pairs={{0,8},{8,0},{1,9},{9,1},{2,10},{10,2},{3,11},{11,3},{4,12},{12,4},... | collective-permute-start | bytes 614408 | tf_op jit(solution)/shard_map/ppermute | solution.py:25
  25.0 0.2 collective-permute-start.6
  25.2 5.8 %collective-permute-done.7.refs_2_ = bf16[2,400,128]{2,1,0:T(8,128)(2,1)S(1)} collective-permute-done((bf16[2,400,128]{2,1,0:T(8,128)(2,1)S(1)}, bf16[2,400,128]{2,1,0:T(8,128)(2,1)S(1)}, u32[]{:S(2)}, u32[]{:S(2)}) %collective-permute-start.7) | collective-permute-done | bytes 204832 | tf_op jit(solution)/shard_map/ppermute | solution.py:25
  31.0 0.0 collective-permute-start.8
  31.0 2.1 %shard_map.140 = (bf16[3,3,160,640]{3,2,1,0:T(8,128)(2,1)S(1)}, bf16[3,3,160,640]{3,2,1,0:T(8,128)(2,1)S(1)}) custom-call(bf16[3,3,160,640]{3,2,1,0:T(8,128)(2,1)} %refs_0_.5, bf16[3,3,160,640]{3,2,1,0:T(8,128)(2,1)} %refs_1_.3), custom_call_target="tpu_custom_call" | custom-call | bytes 3686400 | tf_op jit(solution)/shard_map/pallas_call | solution.py:157
  33.1 0.0 collective-permute-done.6.refs_1_
  33.1 0.0 collective-permute-done.8.refs_3_
  33.1 2.2 %shard_map.141 = (bf16[2,320,160]{2,1,0:T(8,128)(2,1)S(1)}, bf16[2,400,128]{2,1,0:T(8,128)(2,1)S(1)}) custom-call(bf16[2,400,128]{2,1,0:T(8,128)(2,1)S(1)} %get-tuple-element.34.refs_0_, bf16[2,400,128]{2,1,0:T(8,128)(2,1)S(1)} %collective-permute-done.6.refs_1_, bf16[2,400,128]{2,1,0:T(8,128)(2,1)S(1)} %collective-permute-done.7.refs_2_, ...), custom_call_target="tpu_custom_call" | custom-call | flops 1179648000 | bytes 5120640 | tf_op jit(solution)/shard_map/pallas_call | solution.py:44
  35.3 1.6 %collective-permute-start.10 = (bf16[2,400,128]{2,1,0:T(8,128)(2,1)S(1)}, bf16[2,400,128]{2,1,0:T(8,128)(2,1)S(1)}, u32[]{:S(2)}, u32[]{:S(2)}) collective-permute-start(bf16[2,400,128]{2,1,0:T(8,128)(2,1)S(1)} %get-tuple-element.38.refs_0_), channel_id=1, source_target_pairs={{0,8},{8,0},{1,9},{9,1},{2,10},{10,2},{3,11},{11,3},{4,12},{12,4},... | collective-permute-start | bytes 614408 | tf_op jit(solution)/shard_map/ppermute | solution.py:25
  36.9 0.2 collective-permute-start.9
  37.1 5.8 %collective-permute-done.10.refs_2_ = bf16[2,400,128]{2,1,0:T(8,128)(2,1)S(1)} collective-permute-done((bf16[2,400,128]{2,1,0:T(8,128)(2,1)S(1)}, bf16[2,400,128]{2,1,0:T(8,128)(2,1)S(1)}, u32[]{:S(2)}, u32[]{:S(2)}) %collective-permute-start.10) | collective-permute-done | bytes 204832 | tf_op jit(solution)/shard_map/ppermute | solution.py:25
  42.9 0.0 collective-permute-start.11
  42.9 2.1 %shard_map.142.refs_5_ = bf16[3,3,160,1280]{3,2,1,0:T(8,128)(2,1)S(1)} custom-call(bf16[3,3,160,1280]{3,2,1,0:T(8,128)(2,1)} %refs_0_.6), custom_call_target="tpu_custom_call" | custom-call | bytes 3686400 | tf_op jit(solution)/shard_map/pallas_call | solution.py:157
  45.0 2.3 %shard_map.143 = (bf16[320,160]{1,0:T(8,128)(2,1)S(1)}, bf16[400,128]{1,0:T(8,128)(2,1)S(1)}, bf16[336,640]{1,0:T(8,128)(2,1)S(1)}) custom-call(bf16[2,400,128]{2,1,0:T(8,128)(2,1)S(1)} %get-tuple-element.38.refs_0_, bf16[2,400,128]{2,1,0:T(8,128)(2,1)S(1)} %collective-permute-done.9.refs_1_, bf16[2,400,128]{2,1,0:T(8,128)(2,1)S(1)} %collective-permute-done.10.refs_2_, ...), custom_call_target="tpu_custom_call" | custom-call | flops 1179648000 | bytes 5345600 | tf_op jit(solution)/shard_map/pallas_call | solution.py:44
  47.2 1.5 %collective-permute-start.13 = (bf16[400,128]{1,0:T(8,128)(2,1)S(1)}, bf16[400,128]{1,0:T(8,128)(2,1)S(1)}, u32[]{:S(2)}, u32[]{:S(2)}) collective-permute-start(bf16[400,128]{1,0:T(8,128)(2,1)S(1)} %get-tuple-element.40.refs_0_), channel_id=1, source_target_pairs={{0,8},{8,0},{1,9},{9,1},{2,10},{10,2},{3,11},{11,3},{4,12},{12,4},... | collective-permute-start | bytes 307208 | tf_op jit(solution)/shard_map/ppermute | solution.py:25
  48.8 0.2 collective-permute-start.12
  49.0 3.6 %collective-permute-done.13.refs_2_ = bf16[400,128]{1,0:T(8,128)(2,1)S(1)} collective-permute-done((bf16[400,128]{1,0:T(8,128)(2,1)S(1)}, bf16[400,128]{1,0:T(8,128)(2,1)S(1)}, u32[]{:S(2)}, u32[]{:S(2)}) %collective-permute-start.13) | collective-permute-done | bytes 102432 | tf_op jit(solution)/shard_map/ppermute | solution.py:25
  52.6 0.0 collective-permute-start.14
  52.6 2.1 %shard_map.144.w_ref.refs_6_ = bf16[3,3,160,1280]{3,2,1,0:T(8,128)(2,1)S(1)} custom-call(bf16[3,3,160,1280]{3,2,1,0:T(8,128)(2,1)} %refs_0_.7), custom_call_target="tpu_custom_call" | custom-call | bytes 3686400 | tf_op jit(solution)/shard_map/pallas_call | solution.py:157
  54.6 0.0 copy-start.1
  54.6 1.2 %shard_map.145.refs_5_ = f32[320,160]{1,0:T(8,128)S(1)} custom-call(bf16[336,640]{1,0:T(8,128)(2,1)S(1)} %get-tuple-element.42.skip_ref, bf16[3,3,160,1280]{3,2,1,0:T(8,128)(2,1)S(1)} %shard_map.144.w_ref.refs_6_), custom_call_target="tpu_custom_call" | custom-call | flops 589824000 | bytes 4321280 | tf_op jit(solution)/shard_map/pallas_call | solution.py:44
  55.8 0.0 collective-permute-done.14.refs_3_
  55.9 1.5 %shard_map.146 = (bf16[80,128]{1,0:T(8,128)(2,1)S(1)}, bf16[80,128]{1,0:T(8,128)(2,1)S(1)}, bf16[80,128]{1,0:T(8,128)(2,1)S(1)}, bf16[80,128]{1,0:T(8,128)(2,1)S(1)}) custom-call(bf16[400,128]{1,0:T(8,128)(2,1)S(1)} %get-tuple-element.40.refs_0_, bf16[400,128]{1,0:T(8,128)(2,1)S(1)} %collective-permute-done.12.refs_1_, ...), custom_call_target="tpu_custom_call" | custom-call | flops 589824000 | bytes 4485440 | tf_op jit(solution)/shard_map/pallas_call | solution.py:44
  57.4 0.1 collective-permute-start.15
  57.4 1.4 %collective-permute-start.16 = (bf16[80,128]{1,0:T(8,128)(2,1)S(1)}, bf16[80,128]{1,0:T(8,128)(2,1)S(1)}, u32[]{:S(2)}, u32[]{:S(2)}) collective-permute-start(bf16[80,128]{1,0:T(8,128)(2,1)S(1)} %get-tuple-element.45), channel_id=1, source_target_pairs={{0,4},{2,6},{4,0},{6,2},{1,5},{3,7},{5,1},{7,3},{8,12},{10,14},{12... | collective-permute-start | bytes 61448 | tf_op jit(solution)/shard_map/ppermute | solution.py:25
  58.9 3.0 %collective-permute-start.17 = (bf16[80,128]{1,0:T(8,128)(2,1)S(1)}, bf16[80,128]{1,0:T(8,128)(2,1)S(1)}, u32[]{:S(2)}, u32[]{:S(2)}) collective-permute-start(bf16[80,128]{1,0:T(8,128)(2,1)S(1)} %get-tuple-element.46), channel_id=1, source_target_pairs={{0,6},{2,4},{4,2},{6,0},{1,7},{3,5},{5,3},{7,1},{8,14},{10,12},{12... | collective-permute-start | bytes 61448 | tf_op jit(solution)/shard_map/ppermute | solution.py:25
  61.8 0.0 collective-permute-done.15.refs_1_
  61.8 0.6 collective-permute-done.16.refs_2_
  62.4 2.1 %collective-permute-done.17.refs_3_ = bf16[80,128]{1,0:T(8,128)(2,1)S(1)} collective-permute-done((bf16[80,128]{1,0:T(8,128)(2,1)S(1)}, bf16[80,128]{1,0:T(8,128)(2,1)S(1)}, u32[]{:S(2)}, u32[]{:S(2)}) %collective-permute-start.17) | collective-permute-done | bytes 20512 | tf_op jit(solution)/shard_map/ppermute | solution.py:25
  64.4 0.8 %shard_map.147 = bf16[2,160,128]{2,1,0:T(8,128)(2,1)} custom-call(bf16[80,128]{1,0:T(8,128)(2,1)S(1)} %get-tuple-element.43.refs_0_, bf16[80,128]{1,0:T(8,128)(2,1)S(1)} %collective-permute-done.15.refs_1_, bf16[80,128]{1,0:T(8,128)(2,1)S(1)} %collective-permute-done.16.refs_2_, bf16[80,128]{1,0:T(8,128)(2,1)S(1)} %collective-permute-done.17.refs_3_), custom_call_target="tpu_custom_call" | custom-call | bytes 163840 | tf_op jit(solution)/shard_map/pallas_call | solution.py:44
  (12 shorter events, 0.0 us)
Async XLA Ops:
  1.2 5.7 %collective-permute-start = (bf16[200,128]{1,0:T(8,128)(2,1)S(1)}, bf16[200,128]{1,0:T(8,128)(2,1)S(1)}, u32[]{:S(2)}, u32[]{:S(2)}) collective-permute-start(bf16[200,128]{1,0:T(8,128)(2,1)S(1)} %get-tuple-element.27), channel_id=1, source_target_pairs={{0,2},{2,0},{4,6},{6,4},{1,3},{3,1},{5,7},{7,5},{8,10},{10,8},{12,... | collective-permute-start | bytes 153608 | tf_op jit(solution)/shard_map/ppermute | solution.py:25
  4.3 6.0 %collective-permute-start.1 = (bf16[200,128]{1,0:T(8,128)(2,1)S(1)}, bf16[200,128]{1,0:T(8,128)(2,1)S(1)}, u32[]{:S(2)}, u32[]{:S(2)}) collective-permute-start(bf16[200,128]{1,0:T(8,128)(2,1)S(1)} %get-tuple-element.28), channel_id=1, source_target_pairs={{0,4},{2,6},{4,0},{6,2},{1,5},{3,7},{5,1},{7,3},{8,12},{10,14},{12... | collective-permute-start | bytes 153608 | tf_op jit(solution)/shard_map/ppermute | solution.py:25
  6.9 5.9 %collective-permute-start.2 = (bf16[200,128]{1,0:T(8,128)(2,1)S(1)}, bf16[200,128]{1,0:T(8,128)(2,1)S(1)}, u32[]{:S(2)}, u32[]{:S(2)}) collective-permute-start(bf16[200,128]{1,0:T(8,128)(2,1)S(1)} %get-tuple-element.29), channel_id=1, source_target_pairs={{0,6},{2,4},{4,2},{6,0},{1,7},{3,5},{5,3},{7,1},{8,14},{10,12},{12... | collective-permute-start | bytes 153608 | tf_op jit(solution)/shard_map/ppermute | solution.py:25
  13.2 8.0 %copy-start.2 = (bf16[160]{0:T(256)(128)(2,1)S(1)}, bf16[160]{0:T(256)(128)(2,1)}, u32[]{:S(2)}) copy-start(bf16[160]{0:T(256)(128)(2,1)} %refs_6_.3) | copy-start | bytes 964
  13.2 8.0 %copy-start.3 = (bf16[160]{0:T(256)(128)(2,1)S(1)}, bf16[160]{0:T(256)(128)(2,1)}, u32[]{:S(2)}) copy-start(bf16[160]{0:T(256)(128)(2,1)} %refs_8_.2) | copy-start | bytes 964
  13.3 5.8 %collective-permute-start.4 = (bf16[2,400,128]{2,1,0:T(8,128)(2,1)S(1)}, bf16[2,400,128]{2,1,0:T(8,128)(2,1)S(1)}, u32[]{:S(2)}, u32[]{:S(2)}) collective-permute-start(bf16[2,400,128]{2,1,0:T(8,128)(2,1)S(1)} %get-tuple-element.30.refs_0_), channel_id=1, source_target_pairs={{0,8},{8,0},{1,9},{9,1},{2,10},{10,2},{3,11},{11,3},{4,12},{12,4},... | collective-permute-start | bytes 614408 | tf_op jit(solution)/shard_map/ppermute | solution.py:25
  14.8 6.4 %collective-permute-start.3 = (bf16[2,400,128]{2,1,0:T(8,128)(2,1)S(1)}, bf16[2,400,128]{2,1,0:T(8,128)(2,1)S(1)}, u32[]{:S(2)}, u32[]{:S(2)}) collective-permute-start(bf16[2,400,128]{2,1,0:T(8,128)(2,1)S(1)} %get-tuple-element.30.refs_0_), channel_id=1, source_target_pairs={{0,1},{1,0},{2,3},{3,2},{4,5},{5,4},{6,7},{7,6},{8,9},{9,8},{10,11... | collective-permute-start | bytes 614408 | tf_op jit(solution)/shard_map/ppermute | solution.py:25
  19.1 2.1 %collective-permute-start.5 = (bf16[2,400,128]{2,1,0:T(8,128)(2,1)S(1)}, bf16[2,400,128]{2,1,0:T(8,128)(2,1)S(1)}, u32[]{:S(2)}, u32[]{:S(2)}) collective-permute-start(bf16[2,400,128]{2,1,0:T(8,128)(2,1)S(1)} %collective-permute-done.4.refs_2_), channel_id=1, source_target_pairs={{0,1},{1,0},{2,3},{3,2},{4,5},{5,4},{6,7},{7,6},{8,9},{9,8},{10,11... | collective-permute-start | bytes 614408 | tf_op jit(solution)/shard_map/ppermute | solution.py:25
  23.4 9.7 %copy-start.4 = (bf16[160]{0:T(256)(128)(2,1)S(1)}, bf16[160]{0:T(256)(128)(2,1)}, u32[]{:S(2)}) copy-start(bf16[160]{0:T(256)(128)(2,1)} %refs_6_.4) | copy-start | bytes 964
  23.4 9.7 %copy-start.5 = (bf16[160]{0:T(256)(128)(2,1)S(1)}, bf16[160]{0:T(256)(128)(2,1)}, u32[]{:S(2)}) copy-start(bf16[160]{0:T(256)(128)(2,1)} %refs_8_.3) | copy-start | bytes 964
  23.4 7.6 %collective-permute-start.7 = (bf16[2,400,128]{2,1,0:T(8,128)(2,1)S(1)}, bf16[2,400,128]{2,1,0:T(8,128)(2,1)S(1)}, u32[]{:S(2)}, u32[]{:S(2)}) collective-permute-start(bf16[2,400,128]{2,1,0:T(8,128)(2,1)S(1)} %get-tuple-element.34.refs_0_), channel_id=1, source_target_pairs={{0,8},{8,0},{1,9},{9,1},{2,10},{10,2},{3,11},{11,3},{4,12},{12,4},... | collective-permute-start | bytes 614408 | tf_op jit(solution)/shard_map/ppermute | solution.py:25
  25.0 8.1 %collective-permute-start.6 = (bf16[2,400,128]{2,1,0:T(8,128)(2,1)S(1)}, bf16[2,400,128]{2,1,0:T(8,128)(2,1)S(1)}, u32[]{:S(2)}, u32[]{:S(2)}) collective-permute-start(bf16[2,400,128]{2,1,0:T(8,128)(2,1)S(1)} %get-tuple-element.34.refs_0_), channel_id=1, source_target_pairs={{0,1},{1,0},{2,3},{3,2},{4,5},{5,4},{6,7},{7,6},{8,9},{9,8},{10,11... | collective-permute-start | bytes 614408 | tf_op jit(solution)/shard_map/ppermute | solution.py:25
  31.0 2.1 %collective-permute-start.8 = (bf16[2,400,128]{2,1,0:T(8,128)(2,1)S(1)}, bf16[2,400,128]{2,1,0:T(8,128)(2,1)S(1)}, u32[]{:S(2)}, u32[]{:S(2)}) collective-permute-start(bf16[2,400,128]{2,1,0:T(8,128)(2,1)S(1)} %collective-permute-done.7.refs_2_), channel_id=1, source_target_pairs={{0,1},{1,0},{2,3},{3,2},{4,5},{5,4},{6,7},{7,6},{8,9},{9,8},{10,11... | collective-permute-start | bytes 614408 | tf_op jit(solution)/shard_map/ppermute | solution.py:25
  35.3 9.6 %copy-start = (bf16[160]{0:T(256)(128)(2,1)S(1)}, bf16[160]{0:T(256)(128)(2,1)}, u32[]{:S(2)}) copy-start(bf16[160]{0:T(256)(128)(2,1)} %refs_6_.5) | copy-start | bytes 964
  35.3 7.5 %collective-permute-start.10 = (bf16[2,400,128]{2,1,0:T(8,128)(2,1)S(1)}, bf16[2,400,128]{2,1,0:T(8,128)(2,1)S(1)}, u32[]{:S(2)}, u32[]{:S(2)}) collective-permute-start(bf16[2,400,128]{2,1,0:T(8,128)(2,1)S(1)} %get-tuple-element.38.refs_0_), channel_id=1, source_target_pairs={{0,8},{8,0},{1,9},{9,1},{2,10},{10,2},{3,11},{11,3},{4,12},{12,4},... | collective-permute-start | bytes 614408 | tf_op jit(solution)/shard_map/ppermute | solution.py:25
  36.9 8.1 %collective-permute-start.9 = (bf16[2,400,128]{2,1,0:T(8,128)(2,1)S(1)}, bf16[2,400,128]{2,1,0:T(8,128)(2,1)S(1)}, u32[]{:S(2)}, u32[]{:S(2)}) collective-permute-start(bf16[2,400,128]{2,1,0:T(8,128)(2,1)S(1)} %get-tuple-element.38.refs_0_), channel_id=1, source_target_pairs={{0,1},{1,0},{2,3},{3,2},{4,5},{5,4},{6,7},{7,6},{8,9},{9,8},{10,11... | collective-permute-start | bytes 614408 | tf_op jit(solution)/shard_map/ppermute | solution.py:25
  42.9 2.1 %collective-permute-start.11 = (bf16[2,400,128]{2,1,0:T(8,128)(2,1)S(1)}, bf16[2,400,128]{2,1,0:T(8,128)(2,1)S(1)}, u32[]{:S(2)}, u32[]{:S(2)}) collective-permute-start(bf16[2,400,128]{2,1,0:T(8,128)(2,1)S(1)} %collective-permute-done.10.refs_2_), channel_id=1, source_target_pairs={{0,1},{1,0},{2,3},{3,2},{4,5},{5,4},{6,7},{7,6},{8,9},{9,8},{10,11... | collective-permute-start | bytes 614408 | tf_op jit(solution)/shard_map/ppermute | solution.py:25
  47.2 5.3 %collective-permute-start.13 = (bf16[400,128]{1,0:T(8,128)(2,1)S(1)}, bf16[400,128]{1,0:T(8,128)(2,1)S(1)}, u32[]{:S(2)}, u32[]{:S(2)}) collective-permute-start(bf16[400,128]{1,0:T(8,128)(2,1)S(1)} %get-tuple-element.40.refs_0_), channel_id=1, source_target_pairs={{0,8},{8,0},{1,9},{9,1},{2,10},{10,2},{3,11},{11,3},{4,12},{12,4},... | collective-permute-start | bytes 307208 | tf_op jit(solution)/shard_map/ppermute | solution.py:25
  48.8 7.1 %collective-permute-start.12 = (bf16[400,128]{1,0:T(8,128)(2,1)S(1)}, bf16[400,128]{1,0:T(8,128)(2,1)S(1)}, u32[]{:S(2)}, u32[]{:S(2)}) collective-permute-start(bf16[400,128]{1,0:T(8,128)(2,1)S(1)} %get-tuple-element.40.refs_0_), channel_id=1, source_target_pairs={{0,1},{1,0},{2,3},{3,2},{4,5},{5,4},{6,7},{7,6},{8,9},{9,8},{10,11... | collective-permute-start | bytes 307208 | tf_op jit(solution)/shard_map/ppermute | solution.py:25
  52.6 3.3 %collective-permute-start.14 = (bf16[400,128]{1,0:T(8,128)(2,1)S(1)}, bf16[400,128]{1,0:T(8,128)(2,1)S(1)}, u32[]{:S(2)}, u32[]{:S(2)}) collective-permute-start(bf16[400,128]{1,0:T(8,128)(2,1)S(1)} %collective-permute-done.13.refs_2_), channel_id=1, source_target_pairs={{0,1},{1,0},{2,3},{3,2},{4,5},{5,4},{6,7},{7,6},{8,9},{9,8},{10,11... | collective-permute-start | bytes 307208 | tf_op jit(solution)/shard_map/ppermute | solution.py:25
  54.6 1.2 %copy-start.1 = (bf16[160]{0:T(256)(128)(2,1)S(1)}, bf16[160]{0:T(256)(128)(2,1)}, u32[]{:S(2)}) copy-start(bf16[160]{0:T(256)(128)(2,1)} %refs_7_.1) | copy-start | bytes 964
  57.4 4.5 %collective-permute-start.15 = (bf16[80,128]{1,0:T(8,128)(2,1)S(1)}, bf16[80,128]{1,0:T(8,128)(2,1)S(1)}, u32[]{:S(2)}, u32[]{:S(2)}) collective-permute-start(bf16[80,128]{1,0:T(8,128)(2,1)S(1)} %get-tuple-element.44), channel_id=1, source_target_pairs={{0,2},{2,0},{4,6},{6,4},{1,3},{3,1},{5,7},{7,5},{8,10},{10,8},{12,... | collective-permute-start | bytes 61448 | tf_op jit(solution)/shard_map/ppermute | solution.py:25
  57.4 4.9 %collective-permute-start.16 = (bf16[80,128]{1,0:T(8,128)(2,1)S(1)}, bf16[80,128]{1,0:T(8,128)(2,1)S(1)}, u32[]{:S(2)}, u32[]{:S(2)}) collective-permute-start(bf16[80,128]{1,0:T(8,128)(2,1)S(1)} %get-tuple-element.45), channel_id=1, source_target_pairs={{0,4},{2,6},{4,0},{6,2},{1,5},{3,7},{5,1},{7,3},{8,12},{10,14},{12... | collective-permute-start | bytes 61448 | tf_op jit(solution)/shard_map/ppermute | solution.py:25
  58.9 5.6 %collective-permute-start.17 = (bf16[80,128]{1,0:T(8,128)(2,1)S(1)}, bf16[80,128]{1,0:T(8,128)(2,1)S(1)}, u32[]{:S(2)}, u32[]{:S(2)}) collective-permute-start(bf16[80,128]{1,0:T(8,128)(2,1)S(1)} %get-tuple-element.46), channel_id=1, source_target_pairs={{0,6},{2,4},{4,2},{6,0},{1,7},{3,5},{5,3},{7,1},{8,14},{10,12},{12... | collective-permute-start | bytes 61448 | tf_op jit(solution)/shard_map/ppermute | solution.py:25

commit v6 on v5

--- a/solution.py
+++ b/solution.py
@@ -220,17 +220,34 @@
         unpack(z, z.cells, message, put)
 
 
+def up(z, value):
+    value = value.reshape(z.wide, z.height, -1)
+    row = lax.broadcasted_iota(jnp.int32, value.shape, 1)
+    return jnp.where(row == 0, 0.0, pltpu.roll(value, 1, 1)).reshape(z.cells, -1)
+
+
+def down(z, value):
+    value = value.reshape(z.wide, z.height, -1)
+    row = lax.broadcasted_iota(jnp.int32, value.shape, 1)
+    last = z.height - 1
+    return jnp.where(row == last, 0.0, pltpu.roll(value, last, 1)).reshape(z.cells, -1)
+
+
 def convolve(z, cells, weight):
     moved = jnp.concatenate([cells(j) for j in range(3)], axis=1)
     weights = jnp.concatenate([weight(j) for j in range(3)], axis=1)
     total = lax.dot_general(moved, weights, TRANSPOSED, preferred_element_type=F32)
-    above, middle, below = [
-        total[:, i * z.per : (i + 1) * z.per].reshape(z.wide, z.height, z.per) for i in range(3)
-    ]
-    row = lax.broadcasted_iota(jnp.int32, middle.shape, 1)
-    above = jnp.where(row == 0, 0.0, pltpu.roll(above, 1, 1))
-    below = jnp.where(row == z.height - 1, 0.0, pltpu.roll(below, z.height - 1, 1))
-    return (middle + above + below).reshape(-1, z.per)
+    full = z.per - z.rest
+    parts = []
+    if full:
+        above, middle, below = [total[:, i * full : (i + 1) * full] for i in range(3)]
+        parts.append(middle + up(z, above) + down(z, below))
+    if z.rest:
+        middle, above, below = [
+            total[:, 3 * full + i * z.rest : 3 * full + (i + 1) * z.rest] for i in range(3)
+        ]
+        parts.append(middle + up(z, above) + down(z, below))
+    return jnp.concatenate(parts, axis=1) if len(parts) > 1 else parts[0]
 
 
 def moves(z, a_ref):
@@ -238,8 +255,13 @@
 
 
 def taps(z, w_ref, start, depth):
+    full = z.per - z.rest
+
     def weight(j):
-        return w_ref[:, j, :, start : start + depth].reshape(3 * z.per, depth)
+        rows = [w_ref[i, j, :full, start : start + depth] for i in range(3) if full]
+        if z.rest:
+            rows += [w_ref[i, j, full:, start : start + depth] for i in (1, 0, 2)]
+        return jnp.concatenate(rows, axis=0)
 
     return weight
 
@@ -408,7 +430,9 @@
         scratch=held(2),
         flops=2 * unit,
     )
-    part = call(kernel(skip_kernel), sds((z.cells, z.per), F32), skip, dw2, flops=unit)
+    part = call(
+        kernel(skip_kernel), sds((z.cells, z.per), F32), skip, dw2, flops=unit
+    )
     blocks = call(
         kernel(last_kernel),
         [sds(z.packed(z.rows * z.columns))] * z.bands,

time: 65.5 us -> 64.3 us (0.982)
  Pallas kernels: 20 us -> 18.8 us
    pallas_call x7, Pallas kernels: 10.6 us -> 9.33 us  [call(): pl.pallas_call(kernel, out_shape=outs, in_specs=whole(len(args)), out_spe...]
where the time goes in v6:
time: 64.3 us; the launch traced here: 64.1 us
  waiting for transfers between devices  27.9 us (43%)
  Pallas kernels  18.8 us (29%)
  starting transfers between devices  17.1 us (27%)
    ppermute x18, waiting for transfers between devices, exchange(): return lax.ppermute(cells, axis, [(i, i ^ distance) for i in range(count)])  27.9 us
    ppermute x18, starting transfers between devices, exchange(): return lax.ppermute(cells, axis, [(i, i ^ distance) for i in range(count)])  17.1 us
    pallas_call x7, Pallas kernels, call(): pl.pallas_call(kernel, out_shape=outs, in_specs=whole(len(args)), out_spe...  9.33 us
    pallas_call x4, Pallas kernels, load(): pl.pallas_call(functools.partial(load_kernel, count), out_shape=[sds(w.sh...  8.25 us
  transfers between devices with their start and end apart: 18, of which 8 were waited for; matrix products, arithmetic and copies ran while one was open for 0% of the time, Pallas kernels for 14%

profile of v6, /device:TPU:0, one launch (start us, length us, event | category | flops | bytes accessed | tf_op | source)
XLA Modules:
  0.0 64.1 jit_solution(5985858500570451275)
XLA Ops:
  0.0 1.2 %shard_map.136 = (bf16[200,128]{1,0:T(8,128)(2,1)S(1)}, bf16[200,128]{1,0:T(8,128)(2,1)S(1)}, bf16[200,128]{1,0:T(8,128)(2,1)S(1)}, bf16[200,128]{1,0:T(8,128)(2,1)S(1)}) custom-call(bf16[2,160,128]{2,1,0:T(8,128)(2,1)} %bitcast.3, bf16[2,160,128]{2,1,0:T(8,128)(2,1)} %bitcast.4), custom_call_target="tpu_custom_call" | custom-call | tf_op jit(solution)/shard_map/pallas_call | solution.py:387
  1.2 3.1 %collective-permute-start = (bf16[200,128]{1,0:T(8,128)(2,1)S(1)}, bf16[200,128]{1,0:T(8,128)(2,1)S(1)}, u32[]{:S(2)}, u32[]{:S(2)}) collective-permute-start(bf16[200,128]{1,0:T(8,128)(2,1)S(1)} %get-tuple-element.27), channel_id=1, source_target_pairs={{0,2},{2,0},{4,6},{6,4},{1,3},{3,1},{5,7},{7,5},{8,10},{10,8},{12,... | collective-permute-start | bytes 153608 | tf_op jit(solution)/shard_map/ppermute | solution.py:25
  4.3 2.6 %collective-permute-start.1 = (bf16[200,128]{1,0:T(8,128)(2,1)S(1)}, bf16[200,128]{1,0:T(8,128)(2,1)S(1)}, u32[]{:S(2)}, u32[]{:S(2)}) collective-permute-start(bf16[200,128]{1,0:T(8,128)(2,1)S(1)} %get-tuple-element.28), channel_id=1, source_target_pairs={{0,4},{2,6},{4,0},{6,2},{1,5},{3,7},{5,1},{7,3},{8,12},{10,14},{12... | collective-permute-start | bytes 153608 | tf_op jit(solution)/shard_map/ppermute | solution.py:25
  6.9 0.0 collective-permute-start.2
  6.9 0.0 collective-permute-done.refs_1_
  6.9 3.4 %collective-permute-done.1.refs_2_ = bf16[200,128]{1,0:T(8,128)(2,1)S(1)} collective-permute-done((bf16[200,128]{1,0:T(8,128)(2,1)S(1)}, bf16[200,128]{1,0:T(8,128)(2,1)S(1)}, u32[]{:S(2)}, u32[]{:S(2)}) %collective-permute-start.1) | collective-permute-done | bytes 51232 | tf_op jit(solution)/shard_map/ppermute | solution.py:25
  10.3 2.5 %collective-permute-done.2.refs_3_ = bf16[200,128]{1,0:T(8,128)(2,1)S(1)} collective-permute-done((bf16[200,128]{1,0:T(8,128)(2,1)S(1)}, bf16[200,128]{1,0:T(8,128)(2,1)S(1)}, u32[]{:S(2)}, u32[]{:S(2)}) %collective-permute-start.2) | collective-permute-done | bytes 51232 | tf_op jit(solution)/shard_map/ppermute | solution.py:25
  12.8 0.4 shard_map.137
  13.2 0.0 copy-start.2
  13.2 0.0 copy-start.3
  13.3 1.6 %collective-permute-start.4 = (bf16[2,400,128]{2,1,0:T(8,128)(2,1)S(1)}, bf16[2,400,128]{2,1,0:T(8,128)(2,1)S(1)}, u32[]{:S(2)}, u32[]{:S(2)}) collective-permute-start(bf16[2,400,128]{2,1,0:T(8,128)(2,1)S(1)} %get-tuple-element.30.refs_0_), channel_id=1, source_target_pairs={{0,8},{8,0},{1,9},{9,1},{2,10},{10,2},{3,11},{11,3},{4,12},{12,4},... | collective-permute-start | bytes 614408 | tf_op jit(solution)/shard_map/ppermute | solution.py:25
  14.8 4.3 %collective-permute-done.4.refs_2_ = bf16[2,400,128]{2,1,0:T(8,128)(2,1)S(1)} collective-permute-done((bf16[2,400,128]{2,1,0:T(8,128)(2,1)S(1)}, bf16[2,400,128]{2,1,0:T(8,128)(2,1)S(1)}, u32[]{:S(2)}, u32[]{:S(2)}) %collective-permute-start.4) | collective-permute-done | bytes 204832 | tf_op jit(solution)/shard_map/ppermute | solution.py:25
  19.1 2.1 %shard_map.138 = (bf16[3,3,160,640]{3,2,1,0:T(8,128)(2,1)S(1)}, bf16[3,3,160,640]{3,2,1,0:T(8,128)(2,1)S(1)}) custom-call(bf16[3,3,160,640]{3,2,1,0:T(8,128)(2,1)} %refs_0_.4, bf16[3,3,160,640]{3,2,1,0:T(8,128)(2,1)} %refs_1_.2), custom_call_target="tpu_custom_call" | custom-call | bytes 3686400 | tf_op jit(solution)/shard_map/pallas_call | solution.py:157
  21.2 0.0 collective-permute-done.3.refs_1_
  21.2 2.0 %shard_map.139 = (bf16[2,320,160]{2,1,0:T(8,128)(2,1)S(1)}, bf16[2,400,128]{2,1,0:T(8,128)(2,1)S(1)}) custom-call(bf16[2,400,128]{2,1,0:T(8,128)(2,1)S(1)} %get-tuple-element.30.refs_0_, bf16[2,400,128]{2,1,0:T(8,128)(2,1)S(1)} %collective-permute-done.3.refs_1_, bf16[2,400,128]{2,1,0:T(8,128)(2,1)S(1)} %collective-permute-done.4.refs_2_, ...), custom_call_target="tpu_custom_call" | custom-call | flops 1179648000 | bytes 5120640 | tf_op jit(solution)/shard_map/pallas_call | solution.py:44
  23.2 0.0 copy-start.4
  23.2 0.0 copy-start.5
  23.2 1.6 %collective-permute-start.7 = (bf16[2,400,128]{2,1,0:T(8,128)(2,1)S(1)}, bf16[2,400,128]{2,1,0:T(8,128)(2,1)S(1)}, u32[]{:S(2)}, u32[]{:S(2)}) collective-permute-start(bf16[2,400,128]{2,1,0:T(8,128)(2,1)S(1)} %get-tuple-element.34.refs_0_), channel_id=1, source_target_pairs={{0,8},{8,0},{1,9},{9,1},{2,10},{10,2},{3,11},{11,3},{4,12},{12,4},... | collective-permute-start | bytes 614408 | tf_op jit(solution)/shard_map/ppermute | solution.py:25
  24.7 0.2 collective-permute-start.6
  25.0 5.8 %collective-permute-done.7.refs_2_ = bf16[2,400,128]{2,1,0:T(8,128)(2,1)S(1)} collective-permute-done((bf16[2,400,128]{2,1,0:T(8,128)(2,1)S(1)}, bf16[2,400,128]{2,1,0:T(8,128)(2,1)S(1)}, u32[]{:S(2)}, u32[]{:S(2)}) %collective-permute-start.7) | collective-permute-done | bytes 204832 | tf_op jit(solution)/shard_map/ppermute | solution.py:25
  30.7 0.0 collective-permute-start.8
  30.7 2.1 %shard_map.140 = (bf16[3,3,160,640]{3,2,1,0:T(8,128)(2,1)S(1)}, bf16[3,3,160,640]{3,2,1,0:T(8,128)(2,1)S(1)}) custom-call(bf16[3,3,160,640]{3,2,1,0:T(8,128)(2,1)} %refs_0_.5, bf16[3,3,160,640]{3,2,1,0:T(8,128)(2,1)} %refs_1_.3), custom_call_target="tpu_custom_call" | custom-call | bytes 3686400 | tf_op jit(solution)/shard_map/pallas_call | solution.py:157
  32.8 0.0 collective-permute-done.6.refs_1_
  32.8 0.0 collective-permute-done.8.refs_3_
  32.9 2.0 %shard_map.141 = (bf16[2,320,160]{2,1,0:T(8,128)(2,1)S(1)}, bf16[2,400,128]{2,1,0:T(8,128)(2,1)S(1)}) custom-call(bf16[2,400,128]{2,1,0:T(8,128)(2,1)S(1)} %get-tuple-element.34.refs_0_, bf16[2,400,128]{2,1,0:T(8,128)(2,1)S(1)} %collective-permute-done.6.refs_1_, bf16[2,400,128]{2,1,0:T(8,128)(2,1)S(1)} %collective-permute-done.7.refs_2_, ...), custom_call_target="tpu_custom_call" | custom-call | flops 1179648000 | bytes 5120640 | tf_op jit(solution)/shard_map/pallas_call | solution.py:44
  34.8 0.0 copy-start
  34.8 1.6 %collective-permute-start.10 = (bf16[2,400,128]{2,1,0:T(8,128)(2,1)S(1)}, bf16[2,400,128]{2,1,0:T(8,128)(2,1)S(1)}, u32[]{:S(2)}, u32[]{:S(2)}) collective-permute-start(bf16[2,400,128]{2,1,0:T(8,128)(2,1)S(1)} %get-tuple-element.38.refs_0_), channel_id=1, source_target_pairs={{0,8},{8,0},{1,9},{9,1},{2,10},{10,2},{3,11},{11,3},{4,12},{12,4},... | collective-permute-start | bytes 614408 | tf_op jit(solution)/shard_map/ppermute | solution.py:25
  36.4 0.2 collective-permute-start.9
  36.6 5.8 %collective-permute-done.10.refs_2_ = bf16[2,400,128]{2,1,0:T(8,128)(2,1)S(1)} collective-permute-done((bf16[2,400,128]{2,1,0:T(8,128)(2,1)S(1)}, bf16[2,400,128]{2,1,0:T(8,128)(2,1)S(1)}, u32[]{:S(2)}, u32[]{:S(2)}) %collective-permute-start.10) | collective-permute-done | bytes 204832 | tf_op jit(solution)/shard_map/ppermute | solution.py:25
  42.4 2.1 %shard_map.142.refs_5_ = bf16[3,3,160,1280]{3,2,1,0:T(8,128)(2,1)S(1)} custom-call(bf16[3,3,160,1280]{3,2,1,0:T(8,128)(2,1)} %refs_0_.6), custom_call_target="tpu_custom_call" | custom-call | bytes 3686400 | tf_op jit(solution)/shard_map/pallas_call | solution.py:157
  44.5 0.0 collective-permute-done.9.refs_1_
  44.5 0.0 collective-permute-done.11.refs_3_
  44.5 2.0 %shard_map.143 = (bf16[320,160]{1,0:T(8,128)(2,1)S(1)}, bf16[400,128]{1,0:T(8,128)(2,1)S(1)}, bf16[336,640]{1,0:T(8,128)(2,1)S(1)}) custom-call(bf16[2,400,128]{2,1,0:T(8,128)(2,1)S(1)} %get-tuple-element.38.refs_0_, bf16[2,400,128]{2,1,0:T(8,128)(2,1)S(1)} %collective-permute-done.9.refs_1_, bf16[2,400,128]{2,1,0:T(8,128)(2,1)S(1)} %collective-permute-done.10.refs_2_, ...), custom_call_target="tpu_custom_call" | custom-call | flops 1179648000 | bytes 5345600 | tf_op jit(solution)/shard_map/pallas_call | solution.py:44
  46.5 1.5 %collective-permute-start.13 = (bf16[400,128]{1,0:T(8,128)(2,1)S(1)}, bf16[400,128]{1,0:T(8,128)(2,1)S(1)}, u32[]{:S(2)}, u32[]{:S(2)}) collective-permute-start(bf16[400,128]{1,0:T(8,128)(2,1)S(1)} %get-tuple-element.40.refs_0_), channel_id=1, source_target_pairs={{0,8},{8,0},{1,9},{9,1},{2,10},{10,2},{3,11},{11,3},{4,12},{12,4},... | collective-permute-start | bytes 307208 | tf_op jit(solution)/shard_map/ppermute | solution.py:25
  48.0 0.2 collective-permute-start.12
  48.3 3.6 %collective-permute-done.13.refs_2_ = bf16[400,128]{1,0:T(8,128)(2,1)S(1)} collective-permute-done((bf16[400,128]{1,0:T(8,128)(2,1)S(1)}, bf16[400,128]{1,0:T(8,128)(2,1)S(1)}, u32[]{:S(2)}, u32[]{:S(2)}) %collective-permute-start.13) | collective-permute-done | bytes 102432 | tf_op jit(solution)/shard_map/ppermute | solution.py:25
  51.9 2.1 %shard_map.144.w_ref.refs_6_ = bf16[3,3,160,1280]{3,2,1,0:T(8,128)(2,1)S(1)} custom-call(bf16[3,3,160,1280]{3,2,1,0:T(8,128)(2,1)} %refs_0_.7), custom_call_target="tpu_custom_call" | custom-call | bytes 3686400 | tf_op jit(solution)/shard_map/pallas_call | solution.py:157
  53.9 0.0 copy-start.1
  53.9 0.9 %shard_map.145.refs_5_ = f32[320,160]{1,0:T(8,128)S(1)} custom-call(bf16[336,640]{1,0:T(8,128)(2,1)S(1)} %get-tuple-element.42.skip_ref, bf16[3,3,160,1280]{3,2,1,0:T(8,128)(2,1)S(1)} %shard_map.144.w_ref.refs_6_), custom_call_target="tpu_custom_call" | custom-call | flops 589824000 | bytes 4321280 | tf_op jit(solution)/shard_map/pallas_call | solution.py:44
  54.9 0.0 collective-permute-done.12.refs_1_
  54.9 0.0 collective-permute-done.14.refs_3_
  54.9 1.2 %shard_map.146 = (bf16[80,128]{1,0:T(8,128)(2,1)S(1)}, bf16[80,128]{1,0:T(8,128)(2,1)S(1)}, bf16[80,128]{1,0:T(8,128)(2,1)S(1)}, bf16[80,128]{1,0:T(8,128)(2,1)S(1)}) custom-call(bf16[400,128]{1,0:T(8,128)(2,1)S(1)} %get-tuple-element.40.refs_0_, bf16[400,128]{1,0:T(8,128)(2,1)S(1)} %collective-permute-done.12.refs_1_, ...), custom_call_target="tpu_custom_call" | custom-call | flops 589824000 | bytes 4485440 | tf_op jit(solution)/shard_map/pallas_call | solution.py:44
  56.1 0.1 collective-permute-start.15
  56.2 1.4 %collective-permute-start.16 = (bf16[80,128]{1,0:T(8,128)(2,1)S(1)}, bf16[80,128]{1,0:T(8,128)(2,1)S(1)}, u32[]{:S(2)}, u32[]{:S(2)}) collective-permute-start(bf16[80,128]{1,0:T(8,128)(2,1)S(1)} %get-tuple-element.45), channel_id=1, source_target_pairs={{0,4},{2,6},{4,0},{6,2},{1,5},{3,7},{5,1},{7,3},{8,12},{10,14},{12... | collective-permute-start | bytes 61448 | tf_op jit(solution)/shard_map/ppermute | solution.py:25
  57.6 3.0 %collective-permute-start.17 = (bf16[80,128]{1,0:T(8,128)(2,1)S(1)}, bf16[80,128]{1,0:T(8,128)(2,1)S(1)}, u32[]{:S(2)}, u32[]{:S(2)}) collective-permute-start(bf16[80,128]{1,0:T(8,128)(2,1)S(1)} %get-tuple-element.46), channel_id=1, source_target_pairs={{0,6},{2,4},{4,2},{6,0},{1,7},{3,5},{5,3},{7,1},{8,14},{10,12},{12... | collective-permute-start | bytes 61448 | tf_op jit(solution)/shard_map/ppermute | solution.py:25
  60.6 0.6 collective-permute-done.16.refs_2_
  61.2 2.1 %collective-permute-done.17.refs_3_ = bf16[80,128]{1,0:T(8,128)(2,1)S(1)} collective-permute-done((bf16[80,128]{1,0:T(8,128)(2,1)S(1)}, bf16[80,128]{1,0:T(8,128)(2,1)S(1)}, u32[]{:S(2)}, u32[]{:S(2)}) %collective-permute-start.17) | collective-permute-done | bytes 20512 | tf_op jit(solution)/shard_map/ppermute | solution.py:25
  63.2 0.8 %shard_map.147 = bf16[2,160,128]{2,1,0:T(8,128)(2,1)} custom-call(bf16[80,128]{1,0:T(8,128)(2,1)S(1)} %get-tuple-element.43.refs_0_, bf16[80,128]{1,0:T(8,128)(2,1)S(1)} %collective-permute-done.15.refs_1_, bf16[80,128]{1,0:T(8,128)(2,1)S(1)} %collective-permute-done.16.refs_2_, bf16[80,128]{1,0:T(8,128)(2,1)S(1)} %collective-permute-done.17.refs_3_), custom_call_target="tpu_custom_call" | custom-call | bytes 163840 | tf_op jit(solution)/shard_map/pallas_call | solution.py:44
  (12 shorter events, 0.0 us)
Async XLA Ops:
  1.2 5.7 %collective-permute-start = (bf16[200,128]{1,0:T(8,128)(2,1)S(1)}, bf16[200,128]{1,0:T(8,128)(2,1)S(1)}, u32[]{:S(2)}, u32[]{:S(2)}) collective-permute-start(bf16[200,128]{1,0:T(8,128)(2,1)S(1)} %get-tuple-element.27), channel_id=1, source_target_pairs={{0,2},{2,0},{4,6},{6,4},{1,3},{3,1},{5,7},{7,5},{8,10},{10,8},{12,... | collective-permute-start | bytes 153608 | tf_op jit(solution)/shard_map/ppermute | solution.py:25
  4.3 6.0 %collective-permute-start.1 = (bf16[200,128]{1,0:T(8,128)(2,1)S(1)}, bf16[200,128]{1,0:T(8,128)(2,1)S(1)}, u32[]{:S(2)}, u32[]{:S(2)}) collective-permute-start(bf16[200,128]{1,0:T(8,128)(2,1)S(1)} %get-tuple-element.28), channel_id=1, source_target_pairs={{0,4},{2,6},{4,0},{6,2},{1,5},{3,7},{5,1},{7,3},{8,12},{10,14},{12... | collective-permute-start | bytes 153608 | tf_op jit(solution)/shard_map/ppermute | solution.py:25
  6.9 5.9 %collective-permute-start.2 = (bf16[200,128]{1,0:T(8,128)(2,1)S(1)}, bf16[200,128]{1,0:T(8,128)(2,1)S(1)}, u32[]{:S(2)}, u32[]{:S(2)}) collective-permute-start(bf16[200,128]{1,0:T(8,128)(2,1)S(1)} %get-tuple-element.29), channel_id=1, source_target_pairs={{0,6},{2,4},{4,2},{6,0},{1,7},{3,5},{5,3},{7,1},{8,14},{10,12},{12... | collective-permute-start | bytes 153608 | tf_op jit(solution)/shard_map/ppermute | solution.py:25
  13.2 8.0 %copy-start.2 = (bf16[160]{0:T(256)(128)(2,1)S(1)}, bf16[160]{0:T(256)(128)(2,1)}, u32[]{:S(2)}) copy-start(bf16[160]{0:T(256)(128)(2,1)} %refs_6_.3) | copy-start | bytes 964
  13.2 8.0 %copy-start.3 = (bf16[160]{0:T(256)(128)(2,1)S(1)}, bf16[160]{0:T(256)(128)(2,1)}, u32[]{:S(2)}) copy-start(bf16[160]{0:T(256)(128)(2,1)} %refs_8_.2) | copy-start | bytes 964
  13.3 5.8 %collective-permute-start.4 = (bf16[2,400,128]{2,1,0:T(8,128)(2,1)S(1)}, bf16[2,400,128]{2,1,0:T(8,128)(2,1)S(1)}, u32[]{:S(2)}, u32[]{:S(2)}) collective-permute-start(bf16[2,400,128]{2,1,0:T(8,128)(2,1)S(1)} %get-tuple-element.30.refs_0_), channel_id=1, source_target_pairs={{0,8},{8,0},{1,9},{9,1},{2,10},{10,2},{3,11},{11,3},{4,12},{12,4},... | collective-permute-start | bytes 614408 | tf_op jit(solution)/shard_map/ppermute | solution.py:25
  14.8 6.4 %collective-permute-start.3 = (bf16[2,400,128]{2,1,0:T(8,128)(2,1)S(1)}, bf16[2,400,128]{2,1,0:T(8,128)(2,1)S(1)}, u32[]{:S(2)}, u32[]{:S(2)}) collective-permute-start(bf16[2,400,128]{2,1,0:T(8,128)(2,1)S(1)} %get-tuple-element.30.refs_0_), channel_id=1, source_target_pairs={{0,1},{1,0},{2,3},{3,2},{4,5},{5,4},{6,7},{7,6},{8,9},{9,8},{10,11... | collective-permute-start | bytes 614408 | tf_op jit(solution)/shard_map/ppermute | solution.py:25
  19.1 2.1 %collective-permute-start.5 = (bf16[2,400,128]{2,1,0:T(8,128)(2,1)S(1)}, bf16[2,400,128]{2,1,0:T(8,128)(2,1)S(1)}, u32[]{:S(2)}, u32[]{:S(2)}) collective-permute-start(bf16[2,400,128]{2,1,0:T(8,128)(2,1)S(1)} %collective-permute-done.4.refs_2_), channel_id=1, source_target_pairs={{0,1},{1,0},{2,3},{3,2},{4,5},{5,4},{6,7},{7,6},{8,9},{9,8},{10,11... | collective-permute-start | bytes 614408 | tf_op jit(solution)/shard_map/ppermute | solution.py:25
  23.2 9.7 %copy-start.4 = (bf16[160]{0:T(256)(128)(2,1)S(1)}, bf16[160]{0:T(256)(128)(2,1)}, u32[]{:S(2)}) copy-start(bf16[160]{0:T(256)(128)(2,1)} %refs_6_.4) | copy-start | bytes 964
  23.2 9.7 %copy-start.5 = (bf16[160]{0:T(256)(128)(2,1)S(1)}, bf16[160]{0:T(256)(128)(2,1)}, u32[]{:S(2)}) copy-start(bf16[160]{0:T(256)(128)(2,1)} %refs_8_.3) | copy-start | bytes 964
  23.2 7.6 %collective-permute-start.7 = (bf16[2,400,128]{2,1,0:T(8,128)(2,1)S(1)}, bf16[2,400,128]{2,1,0:T(8,128)(2,1)S(1)}, u32[]{:S(2)}, u32[]{:S(2)}) collective-permute-start(bf16[2,400,128]{2,1,0:T(8,128)(2,1)S(1)} %get-tuple-element.34.refs_0_), channel_id=1, source_target_pairs={{0,8},{8,0},{1,9},{9,1},{2,10},{10,2},{3,11},{11,3},{4,12},{12,4},... | collective-permute-start | bytes 614408 | tf_op jit(solution)/shard_map/ppermute | solution.py:25
  24.7 8.1 %collective-permute-start.6 = (bf16[2,400,128]{2,1,0:T(8,128)(2,1)S(1)}, bf16[2,400,128]{2,1,0:T(8,128)(2,1)S(1)}, u32[]{:S(2)}, u32[]{:S(2)}) collective-permute-start(bf16[2,400,128]{2,1,0:T(8,128)(2,1)S(1)} %get-tuple-element.34.refs_0_), channel_id=1, source_target_pairs={{0,1},{1,0},{2,3},{3,2},{4,5},{5,4},{6,7},{7,6},{8,9},{9,8},{10,11... | collective-permute-start | bytes 614408 | tf_op jit(solution)/shard_map/ppermute | solution.py:25
  30.7 2.1 %collective-permute-start.8 = (bf16[2,400,128]{2,1,0:T(8,128)(2,1)S(1)}, bf16[2,400,128]{2,1,0:T(8,128)(2,1)S(1)}, u32[]{:S(2)}, u32[]{:S(2)}) collective-permute-start(bf16[2,400,128]{2,1,0:T(8,128)(2,1)S(1)} %collective-permute-done.7.refs_2_), channel_id=1, source_target_pairs={{0,1},{1,0},{2,3},{3,2},{4,5},{5,4},{6,7},{7,6},{8,9},{9,8},{10,11... | collective-permute-start | bytes 614408 | tf_op jit(solution)/shard_map/ppermute | solution.py:25
  34.8 9.6 %copy-start = (bf16[160]{0:T(256)(128)(2,1)S(1)}, bf16[160]{0:T(256)(128)(2,1)}, u32[]{:S(2)}) copy-start(bf16[160]{0:T(256)(128)(2,1)} %refs_6_.5) | copy-start | bytes 964
  34.8 7.5 %collective-permute-start.10 = (bf16[2,400,128]{2,1,0:T(8,128)(2,1)S(1)}, bf16[2,400,128]{2,1,0:T(8,128)(2,1)S(1)}, u32[]{:S(2)}, u32[]{:S(2)}) collective-permute-start(bf16[2,400,128]{2,1,0:T(8,128)(2,1)S(1)} %get-tuple-element.38.refs_0_), channel_id=1, source_target_pairs={{0,8},{8,0},{1,9},{9,1},{2,10},{10,2},{3,11},{11,3},{4,12},{12,4},... | collective-permute-start | bytes 614408 | tf_op jit(solution)/shard_map/ppermute | solution.py:25
  36.4 8.1 %collective-permute-start.9 = (bf16[2,400,128]{2,1,0:T(8,128)(2,1)S(1)}, bf16[2,400,128]{2,1,0:T(8,128)(2,1)S(1)}, u32[]{:S(2)}, u32[]{:S(2)}) collective-permute-start(bf16[2,400,128]{2,1,0:T(8,128)(2,1)S(1)} %get-tuple-element.38.refs_0_), channel_id=1, source_target_pairs={{0,1},{1,0},{2,3},{3,2},{4,5},{5,4},{6,7},{7,6},{8,9},{9,8},{10,11... | collective-permute-start | bytes 614408 | tf_op jit(solution)/shard_map/ppermute | solution.py:25
  42.4 2.1 %collective-permute-start.11 = (bf16[2,400,128]{2,1,0:T(8,128)(2,1)S(1)}, bf16[2,400,128]{2,1,0:T(8,128)(2,1)S(1)}, u32[]{:S(2)}, u32[]{:S(2)}) collective-permute-start(bf16[2,400,128]{2,1,0:T(8,128)(2,1)S(1)} %collective-permute-done.10.refs_2_), channel_id=1, source_target_pairs={{0,1},{1,0},{2,3},{3,2},{4,5},{5,4},{6,7},{7,6},{8,9},{9,8},{10,11... | collective-permute-start | bytes 614408 | tf_op jit(solution)/shard_map/ppermute | solution.py:25
  46.5 5.4 %collective-permute-start.13 = (bf16[400,128]{1,0:T(8,128)(2,1)S(1)}, bf16[400,128]{1,0:T(8,128)(2,1)S(1)}, u32[]{:S(2)}, u32[]{:S(2)}) collective-permute-start(bf16[400,128]{1,0:T(8,128)(2,1)S(1)} %get-tuple-element.40.refs_0_), channel_id=1, source_target_pairs={{0,8},{8,0},{1,9},{9,1},{2,10},{10,2},{3,11},{11,3},{4,12},{12,4},... | collective-permute-start | bytes 307208 | tf_op jit(solution)/shard_map/ppermute | solution.py:25
  48.0 6.8 %collective-permute-start.12 = (bf16[400,128]{1,0:T(8,128)(2,1)S(1)}, bf16[400,128]{1,0:T(8,128)(2,1)S(1)}, u32[]{:S(2)}, u32[]{:S(2)}) collective-permute-start(bf16[400,128]{1,0:T(8,128)(2,1)S(1)} %get-tuple-element.40.refs_0_), channel_id=1, source_target_pairs={{0,1},{1,0},{2,3},{3,2},{4,5},{5,4},{6,7},{7,6},{8,9},{9,8},{10,11... | collective-permute-start | bytes 307208 | tf_op jit(solution)/shard_map/ppermute | solution.py:25
  51.8 3.0 %collective-permute-start.14 = (bf16[400,128]{1,0:T(8,128)(2,1)S(1)}, bf16[400,128]{1,0:T(8,128)(2,1)S(1)}, u32[]{:S(2)}, u32[]{:S(2)}) collective-permute-start(bf16[400,128]{1,0:T(8,128)(2,1)S(1)} %collective-permute-done.13.refs_2_), channel_id=1, source_target_pairs={{0,1},{1,0},{2,3},{3,2},{4,5},{5,4},{6,7},{7,6},{8,9},{9,8},{10,11... | collective-permute-start | bytes 307208 | tf_op jit(solution)/shard_map/ppermute | solution.py:25
  53.9 1.0 %copy-start.1 = (bf16[160]{0:T(256)(128)(2,1)S(1)}, bf16[160]{0:T(256)(128)(2,1)}, u32[]{:S(2)}) copy-start(bf16[160]{0:T(256)(128)(2,1)} %refs_7_.1) | copy-start | bytes 964
  56.1 4.5 %collective-permute-start.15 = (bf16[80,128]{1,0:T(8,128)(2,1)S(1)}, bf16[80,128]{1,0:T(8,128)(2,1)S(1)}, u32[]{:S(2)}, u32[]{:S(2)}) collective-permute-start(bf16[80,128]{1,0:T(8,128)(2,1)S(1)} %get-tuple-element.44), channel_id=1, source_target_pairs={{0,2},{2,0},{4,6},{6,4},{1,3},{3,1},{5,7},{7,5},{8,10},{10,8},{12,... | collective-permute-start | bytes 61448 | tf_op jit(solution)/shard_map/ppermute | solution.py:25
  56.2 4.9 %collective-permute-start.16 = (bf16[80,128]{1,0:T(8,128)(2,1)S(1)}, bf16[80,128]{1,0:T(8,128)(2,1)S(1)}, u32[]{:S(2)}, u32[]{:S(2)}) collective-permute-start(bf16[80,128]{1,0:T(8,128)(2,1)S(1)} %get-tuple-element.45), channel_id=1, source_target_pairs={{0,4},{2,6},{4,0},{6,2},{1,5},{3,7},{5,1},{7,3},{8,12},{10,14},{12... | collective-permute-start | bytes 61448 | tf_op jit(solution)/shard_map/ppermute | solution.py:25
  57.6 5.6 %collective-permute-start.17 = (bf16[80,128]{1,0:T(8,128)(2,1)S(1)}, bf16[80,128]{1,0:T(8,128)(2,1)S(1)}, u32[]{:S(2)}, u32[]{:S(2)}) collective-permute-start(bf16[80,128]{1,0:T(8,128)(2,1)S(1)} %get-tuple-element.46), channel_id=1, source_target_pairs={{0,6},{2,4},{4,2},{6,0},{1,7},{3,5},{5,3},{7,1},{8,14},{10,12},{12... | collective-permute-start | bytes 61448 | tf_op jit(solution)/shard_map/ppermute | solution.py:25

commit v7 on v6

--- a/solution.py
+++ b/solution.py
@@ -66,46 +66,62 @@
         self.cells = self.height * self.wide
         self.held = self.cells + 2 * self.height
         self.shards = channel_count()
+        self.depth = self.shards * self.per
         self.rest = self.per % LANES
         self.groups = LANES // self.rest if self.rest and LANES % self.rest == 0 else 0
         if self.per < LANES:
             self.groups = 0
-        self.depth = self.shards * self.per
-
-
-    def dense(self, cells):
-        return self.groups and cells % (8 * self.groups) == 0
+        self.span = LANES
+        while not self.fits():
+            self.span += LANES
+
+    def fits(self):
+        last = self.depth - self.span
+        self.starts = [min(j * self.per // LANES * LANES, last) for j in range(self.shards)]
+        self.offsets = [j * self.per - start for j, start in enumerate(self.starts)]
+        return all(offset + self.per <= self.span for offset in self.offsets)
+
+
+    def part(self, cells):
+        return -(-cells // (8 * self.groups)) * 8
 
     def packed(self, cells):
-        if not self.dense(cells):
+        if not self.groups:
             return (cells, self.per)
-        return (cells * (self.per // LANES) + cells // self.groups, LANES)
+        return (cells * (self.per // LANES) + self.part(cells), LANES)
+
+    def kept(self, trim):
+        return self.cells - 2 * trim * self.height
 
 
 def pack(z, ref, value):
     cells = value.shape[0]
-    if not z.dense(cells):
+    if not z.groups:
         ref[...] = value.astype(BF16)
         return
     full = z.per // LANES
     for g in range(full):
         ref[g * cells : (g + 1) * cells] = value[:, g * LANES : (g + 1) * LANES].astype(BF16)
-    part = cells // z.groups
+    part = z.part(cells)
     rest = [value[g * part : (g + 1) * part, full * LANES :] for g in range(z.groups)]
+    short = part - rest[-1].shape[0]
+    if short:
+        rest[-1] = jnp.concatenate([rest[-1], jnp.zeros((short, z.rest), F32)], axis=0)
     ref[full * cells :] = jnp.concatenate(rest, axis=1).astype(BF16)
 
 
 def unpack(z, cells, message, put):
-    if not z.dense(cells):
+    if not z.groups:
         put(0, 0, message)
         return
     full = z.per // LANES
     for g in range(full):
         put(0, g * LANES, message[g * cells : (g + 1) * cells])
-    part = cells // z.groups
+    part = z.part(cells)
     rest = message[full * cells :]
     for g in range(z.groups):
-        put(g * part, full * LANES, rest[:, g * z.rest : (g + 1) * z.rest])
+        rows = min(part, cells - g * part)
+        put(g * part, full * LANES, rest[:rows, g * z.rest : (g + 1) * z.rest])
 
 
 def masked_silu(z, state):
@@ -208,16 +224,51 @@
     return pieces
 
 
-def lay_out(z, a_ref, messages, at=0):
+def lay_out(z, trim, a_ref, messages):
+    first = (1 + trim) * z.height
+    a_ref[:first] = jnp.zeros((first, a_ref.shape[1]), BF16)
+    a_ref[z.held - first :] = jnp.zeros((first, a_ref.shape[1]), BF16)
     for j, message in enumerate(in_order(messages)):
 
         def put(row, lane, piece):
             rows, lanes = piece.shape
-            lane = at + j * z.per + lane
-            row = row + z.height
+            lane = j * z.per + lane
+            row = row + first
             a_ref[row : row + rows, lane : lane + lanes] = piece
 
-        unpack(z, z.cells, message, put)
+        unpack(z, z.kept(trim), message, put)
+
+
+def place(z, trim, a_ref, at, message, distance):
+    first = (1 + trim) * z.height
+    owner = channel_place() ^ distance
+    start = offset = jnp.int32(0)
+    for j in range(z.shards):
+        start = jnp.where(owner == j, z.starts[j], start)
+        offset = jnp.where(owner == j, z.offsets[j], offset)
+    for known in sorted(set(z.offsets)):
+
+        @pl.when(offset == known)
+        def _():
+            def put(row, lane, piece):
+                rows, lanes = piece.shape
+                lane = at + known + lane
+                row = row + first
+                a_ref[row : row + rows, lane : lane + lanes] = piece
+
+            unpack(z, z.kept(trim), message, put)
+
+    return start
+
+
+def accumulate(z, trim, distances, sources, w_ref, a_ref):
+    a_ref[...] = jnp.zeros(a_ref.shape, BF16)
+    slices = []
+    for base, messages in sources:
+        for distance, message in zip(distances, messages):
+            start = place(z, trim, a_ref, len(slices) * z.span, message, distance)
+            slices.append(pl.ds(pl.multiple_of(base + start, LANES), z.span))
+    return convolve(z, moves(z, a_ref), taps(z, w_ref, slices))
 
 
 def up(z, value):
@@ -254,71 +305,90 @@
     return lambda j: a_ref[j * z.height : j * z.height + z.cells]
 
 
-def taps(z, w_ref, start, depth):
+def taps(z, w_ref, slices):
     full = z.per - z.rest
 
-    def weight(j):
-        rows = [w_ref[i, j, :full, start : start + depth] for i in range(3) if full]
+    def rows(j, at):
+        rows = [w_ref[i, j, :full, at] for i in range(3) if full]
         if z.rest:
-            rows += [w_ref[i, j, full:, start : start + depth] for i in (1, 0, 2)]
+            rows += [w_ref[i, j, full:, at] for i in (1, 0, 2)]
         return jnp.concatenate(rows, axis=0)
 
-    return weight
-
-
-def clear_edges(z, a_ref):
-    edge = jnp.zeros((z.height, a_ref.shape[1]), BF16)
-    a_ref[: z.height] = edge
-    a_ref[z.height + z.cells :] = edge
-
-
-def finish(z, state, result, bias, new_ref, act_ref):
+    return lambda j: jnp.concatenate([rows(j, at) for at in slices], axis=1)
+
+
+def finish(z, trim, state, result, bias, new_ref, act_ref):
     new = (state.astype(F32) + result + bias).astype(BF16)
     new_ref[...] = new
-    pack(z, act_ref, masked_silu(z, new.astype(F32)))
+    edge = trim * z.height
+    pack(z, act_ref, masked_silu(z, new.astype(F32))[edge : z.cells - edge])
 
 
 def bias_of(ref):
     return ref[...].astype(F32).reshape(1, -1)
 
 
-def layer_kernel(z, *refs):
-    n = z.shards
+def pair_kernel(z, trim, distances, add, end, *refs):
+    n = len(distances)
     blocks, refs = refs[:n], refs[n:]
-    state_ref, w0, b0, w1, b1, new_ref, act_ref, a_ref = refs
-    for t, (w_ref, b_ref) in enumerate(((w0, b0), (w1, b1))):
-        clear_edges(z, a_ref.at[t])
-        lay_out(z, a_ref.at[t], [block[t] for block in blocks])
-        result = convolve(z, moves(z, a_ref.at[t]), taps(z, w_ref, 0, z.depth))
-        finish(z, state_ref[t], result, bias_of(b_ref), new_ref.at[t], act_ref.at[t])
-
-
-def decode_kernel(z, *refs):
-    n = z.shards
+    sums, refs = refs[:add], refs[add:]
+    w0, w1, *refs = refs
+    if end:
+        state_ref, b0, b1, new_ref, act_ref, a_ref = refs
+    else:
+        out_ref, a_ref = refs
+    for t, w_ref in enumerate((w0, w1)):
+        sources = [(0, [block[t] for block in blocks])]
+        total = accumulate(z, trim, distances, sources, w_ref, a_ref.at[t])
+        for other in sums:
+            total = total + other[t]
+        if end:
+            bias = bias_of((b0, b1)[t])
+            finish(z, trim + 1, state_ref[t], total, bias, new_ref.at[t], act_ref.at[t])
+        else:
+            out_ref[t] = total
+
+
+def decode_kernel(z, trim, distances, add, end, *refs):
+    n = len(distances)
     blocks, refs = refs[:n], refs[n:]
-    state_ref, w_ref, b_ref, new_ref, act_ref, skip_ref, a_ref = refs
-    clear_edges(z, a_ref)
-    lay_out(z, a_ref, [block[1] for block in blocks])
-    lay_out(z, a_ref, [block[0] for block in blocks], z.depth)
-    skip_ref[...] = a_ref[:, z.depth :]
-    result = convolve(z, moves(z, a_ref), taps(z, w_ref, 0, 2 * z.depth))
-    finish(z, state_ref[1], result, bias_of(b_ref), new_ref, act_ref)
-
-
-def skip_kernel(z, skip_ref, w_ref, out_ref):
-    out_ref[...] = convolve(z, moves(z, skip_ref), taps(z, w_ref, z.depth, z.depth))
-
-
-def last_kernel(z, *refs):
-    n = z.shards
+    sums, refs = refs[:add], refs[add:]
+    w_ref, *refs = refs
+    a_ref = refs.pop()
+    sources = [(0, [block[1] for block in blocks]), (z.depth, [block[0] for block in blocks])]
+    total = accumulate(z, trim, distances, sources, w_ref, a_ref)
+    for other in sums:
+        total = total + other[...]
+    if end:
+        state_ref, b_ref, new_ref, act_ref = refs
+        finish(z, trim + 1, state_ref[1], total, bias_of(b_ref), new_ref, act_ref)
+    else:
+        refs[0][...] = total
+
+
+def skip_kernel(z, trim, *refs):
+    blocks, (w_ref, out_ref, a_ref) = refs[: z.shards], refs[z.shards :]
+    lay_out(z, trim, a_ref, [block[0] for block in blocks])
+    weights = taps(z, w_ref, [slice(z.depth, 2 * z.depth)])
+    out_ref[...] = convolve(z, moves(z, a_ref), weights)
+
+
+def last_kernel(z, trim, distances, add, end, *refs):
+    n = len(distances)
     blocks, refs = refs[:n], refs[n:]
-    state_ref, skip_ref, w_ref, b_ref = refs[:4]
-    outs, (a_ref, image) = refs[4 : 4 + z.bands], refs[4 + z.bands :]
-    clear_edges(z, a_ref)
-    lay_out(z, a_ref, [block[...] for block in blocks])
-    result = convolve(z, moves(z, a_ref), taps(z, w_ref, 0, z.depth))
-    total = state_ref[...].astype(F32) + (result + skip_ref[...])
-    total = total + bias_of(b_ref)
+    sums, refs = refs[:add], refs[add:]
+    w_ref, *refs = refs
+    a_ref = refs.pop()
+    sources = [(0, [block[...] for block in blocks])]
+    total = accumulate(z, trim, distances, sources, w_ref, a_ref)
+    for other in sums:
+        total = total + other[...]
+    if not end:
+        refs[0][...] = total
+        return
+    image = refs.pop()
+    state_ref, b_ref, *outs = refs
+    total = state_ref[...].astype(F32) + total + bias_of(b_ref)
     groups = lane_groups(z)
     for g, (lane, n) in enumerate(groups):
         image[g, :, :n] = total[:, lane : lane + n]
@@ -362,26 +432,33 @@
 
 
 def gather(cells):
-    chips = [cells]
+    cores = lax.axis_size("chan")
+    near, far = [cells], []
+    for k in range(1, cores):
+        near.append(exchange(cells, "chan", k))
+    chips = []
     for k in range(1, lax.axis_size("section")):
         chips.append(exchange(cells, "section", k))
-    pieces = []
     for chip in chips:
-        pieces.append(chip)
-        for k in range(1, lax.axis_size("chan")):
-            pieces.append(exchange(chip, "chan", k))
-    return pieces
+        for k in range(1, cores):
+            far.append(exchange(chip, "chan", k))
+    names = (
+        tuple(range(cores)),
+        tuple(at * cores for at in range(1, len(chips) + 1)),
+        tuple(at * cores + k for at in range(1, len(chips) + 1) for k in range(1, cores)),
+    )
+    return list(zip(names, (near, chips, far)))
 
 
 def per_device(latent, control_hint, cw1, cb1, cw2, cb2, mw1, mb1, mw2, mb2, dw1, db1, dw2, db2):
     z = Sizes(latent)
     kernel = lambda f, *a: functools.partial(f, z, *a)
-    held = lambda *parts: [pltpu.VMEM(parts[:-1] + (z.held, parts[-1] * z.depth), BF16)]
     groups = len(lane_groups(z))
-    unit = 2 * 9 * z.cells * z.per * z.depth
     single = sds((z.cells, z.per))
     pair = sds((2, z.cells, z.per))
-    message = z.packed(z.cells)
+    total = sds((z.cells, z.per), F32)
+    totals = sds((2, z.cells, z.per), F32)
+    message = lambda trim: z.packed(z.kept(trim))
 
     raw = (z.rows, z.per, z.width)
     blocks = pl.pallas_call(
@@ -403,46 +480,61 @@
     (dw2,) = load(dw2)
     state, act = call(
         kernel(join_kernel),
-        [pair, sds((2,) + message)],
+        [pair, sds((2,) + message(0))],
         *blocks,
         scratch=[
             pltpu.VMEM((2, groups, z.cells, LANES), F32),
             pltpu.VMEM((groups, 2 * z.rows * z.wide, LANES), F32),
         ],
     )
-    for weights in ((cw1, cb1, mw1, mb1), (cw2, cb2, mw2, mb2)):
-        state, act = call(
-            kernel(layer_kernel),
-            [pair, sds((2,) + message)],
-            *gather(act),
-            state,
-            *weights,
-            scratch=held(2, 1),
-            flops=2 * unit,
-        )
-    state, act, skip = call(
-        kernel(decode_kernel),
-        [single, sds(message), sds((z.held, z.depth))],
-        *gather(act),
-        state,
-        dw1,
-        db1,
-        scratch=held(2),
-        flops=2 * unit,
+
+    def layer(step, body, received, weights, rest, partial_out, outs, sums=(), extra=(), wide=1):
+        received = [(names, pieces) for names, pieces in received if names]
+        for at, (names, pieces) in enumerate(received):
+            end = at == len(received) - 1
+            shape = (z.held, len(names) * z.span * wide)
+            if len(weights) > 1:
+                shape = (len(weights),) + shape
+            result = call(
+                kernel(body, step, names, len(sums), end),
+                outs if end else partial_out,
+                *pieces,
+                *sums,
+                *weights,
+                *(rest if end else ()),
+                scratch=(list(extra) if end else []) + [pltpu.VMEM(shape, BF16)],
+                flops=2 * 9 * z.cells * z.per * z.per * len(names) * len(weights) * wide,
+            )
+            sums = (result,)
+        return result
+
+    for step, (cw, cb, mw, mb) in enumerate(((cw1, cb1, mw1, mb1), (cw2, cb2, mw2, mb2))):
+        received = gather(act)
+        outs = [pair, sds((2,) + message(step + 1))]
+        rest = (state, cb, mb)
+        state, act = layer(step, pair_kernel, received, (cw, mw), rest, totals, outs)
+    received = gather(act)
+    skips = {d: p for names, pieces in received for d, p in zip(names, pieces)}
+    outs = [single, sds(message(3))]
+    state, act = layer(2, decode_kernel, received, (dw1,), (state, db1), total, outs, wide=2)
+    part = call(
+        kernel(skip_kernel, 2),
+        total,
+        *[skips[d] for d in range(z.shards)],
+        dw2,
+        scratch=[pltpu.VMEM((z.held, z.depth), BF16)],
+        flops=2 * 9 * z.cells * z.per * z.depth,
     )
-    part = call(
-        kernel(skip_kernel), sds((z.cells, z.per), F32), skip, dw2, flops=unit
-    )
-    blocks = call(
-        kernel(last_kernel),
+    blocks = layer(
+        3,
+        last_kernel,
+        gather(act),
+        (dw2,),
+        (state, db2),
+        total,
         [sds(z.packed(z.rows * z.columns))] * z.bands,
-        *gather(act),
-        state,
-        part,
-        dw2,
-        db2,
-        scratch=held(1) + [pltpu.VMEM((groups, z.cells, LANES), F32)],
-        flops=unit,
+        sums=(part,),
+        extra=[pltpu.VMEM((groups, z.cells, LANES), F32)],
     )
     out = call(
         kernel(rows_kernel),

time: 64.3 us -> 71.3 us (1.11)
  Pallas kernels: 18.8 us -> 28.7 us
  waiting for transfers between devices: 27.9 us -> 25.2 us
    pallas_call x7 -> x15, Pallas kernels: 9.33 us -> 19.3 us  [call(): pl.pallas_call(kernel, out_shape=outs, in_specs=whole(len(args)), out_spe...]
    ppermute x18, waiting for transfers between devices: 27.9 us -> 25.2 us  [exchange(): return lax.ppermute(cells, axis, [(i, i ^ distance) for i in range(count)])]
  transfers between devices with their start and end apart: 18 -> 18, of which waited for: 8 -> 8; matrix products, arithmetic and copies ran while one was open for 0% -> 0% of each run, Pallas kernels for 14% -> 30%
where the time goes in v7:
time: 71.3 us; the launch traced here: 71.1 us
  Pallas kernels  28.7 us (40%)
  waiting for transfers between devices  25.2 us (35%)
  starting transfers between devices  16.9 us (24%)
    ppermute x18, waiting for transfers between devices, exchange(): return lax.ppermute(cells, axis, [(i, i ^ distance) for i in range(count)])  25.2 us
    pallas_call x15, Pallas kernels, call(): pl.pallas_call(kernel, out_shape=outs, in_specs=whole(len(args)), out_spe...  19.3 us
    ppermute x18, starting transfers between devices, exchange(): return lax.ppermute(cells, axis, [(i, i ^ distance) for i in range(count)])  16.9 us
    pallas_call x4, Pallas kernels, load(): pl.pallas_call(functools.partial(load_kernel, count), out_shape=[sds(w.sh...  8.25 us
  transfers between devices with their start and end apart: 18, of which 8 were waited for; matrix products, arithmetic and copies ran while one was open for 0% of the time, Pallas kernels for 30%

profile of v7, /device:TPU:0, one launch (start us, length us, event | category | flops | bytes accessed | tf_op | source)
XLA Modules:
  0.0 71.1 jit_solution(9313532320496798108)
XLA Ops:
  0.0 1.2 %shard_map.136 = (bf16[200,128]{1,0:T(8,128)(2,1)S(1)}, bf16[200,128]{1,0:T(8,128)(2,1)S(1)}, bf16[200,128]{1,0:T(8,128)(2,1)S(1)}, bf16[200,128]{1,0:T(8,128)(2,1)S(1)}) custom-call(bf16[2,160,128]{2,1,0:T(8,128)(2,1)} %bitcast.3, bf16[2,160,128]{2,1,0:T(8,128)(2,1)} %bitcast.4), custom_call_target="tpu_custom_call" | custom-call | tf_op jit(solution)/shard_map/pallas_call | solution.py:464
  1.2 3.1 %collective-permute-start = (bf16[200,128]{1,0:T(8,128)(2,1)S(1)}, bf16[200,128]{1,0:T(8,128)(2,1)S(1)}, u32[]{:S(2)}, u32[]{:S(2)}) collective-permute-start(bf16[200,128]{1,0:T(8,128)(2,1)S(1)} %get-tuple-element.26), channel_id=1, source_target_pairs={{0,2},{2,0},{4,6},{6,4},{1,3},{3,1},{5,7},{7,5},{8,10},{10,8},{12,... | collective-permute-start | bytes 153608 | tf_op jit(solution)/shard_map/ppermute | solution.py:25
  4.3 2.6 %collective-permute-start.1 = (bf16[200,128]{1,0:T(8,128)(2,1)S(1)}, bf16[200,128]{1,0:T(8,128)(2,1)S(1)}, u32[]{:S(2)}, u32[]{:S(2)}) collective-permute-start(bf16[200,128]{1,0:T(8,128)(2,1)S(1)} %get-tuple-element.27), channel_id=1, source_target_pairs={{0,4},{2,6},{4,0},{6,2},{1,5},{3,7},{5,1},{7,3},{8,12},{10,14},{12... | collective-permute-start | bytes 153608 | tf_op jit(solution)/shard_map/ppermute | solution.py:25
  6.9 0.0 collective-permute-start.2
  6.9 0.0 collective-permute-done.refs_1_
  6.9 3.4 %collective-permute-done.1.refs_2_ = bf16[200,128]{1,0:T(8,128)(2,1)S(1)} collective-permute-done((bf16[200,128]{1,0:T(8,128)(2,1)S(1)}, bf16[200,128]{1,0:T(8,128)(2,1)S(1)}, u32[]{:S(2)}, u32[]{:S(2)}) %collective-permute-start.1) | collective-permute-done | bytes 51232 | tf_op jit(solution)/shard_map/ppermute | solution.py:25
  10.3 2.5 %collective-permute-done.2.refs_3_ = bf16[200,128]{1,0:T(8,128)(2,1)S(1)} collective-permute-done((bf16[200,128]{1,0:T(8,128)(2,1)S(1)}, bf16[200,128]{1,0:T(8,128)(2,1)S(1)}, u32[]{:S(2)}, u32[]{:S(2)}) %collective-permute-start.2) | collective-permute-done | bytes 51232 | tf_op jit(solution)/shard_map/ppermute | solution.py:25
  12.8 0.4 shard_map.137
  13.2 1.6 %collective-permute-start.3 = (bf16[2,400,128]{2,1,0:T(8,128)(2,1)S(1)}, bf16[2,400,128]{2,1,0:T(8,128)(2,1)S(1)}, u32[]{:S(2)}, u32[]{:S(2)}) collective-permute-start(bf16[2,400,128]{2,1,0:T(8,128)(2,1)S(1)} %get-tuple-element.29.refs_0_), channel_id=1, source_target_pairs={{0,8},{8,0},{1,9},{9,1},{2,10},{10,2},{3,11},{11,3},{4,12},{12,4},... | collective-permute-start | bytes 614408 | tf_op jit(solution)/shard_map/ppermute | solution.py:25
  14.8 4.3 %collective-permute-done.3.refs_0_ = bf16[2,400,128]{2,1,0:T(8,128)(2,1)S(1)} collective-permute-done((bf16[2,400,128]{2,1,0:T(8,128)(2,1)S(1)}, bf16[2,400,128]{2,1,0:T(8,128)(2,1)S(1)}, u32[]{:S(2)}, u32[]{:S(2)}) %collective-permute-start.3) | collective-permute-done | bytes 204832 | tf_op jit(solution)/shard_map/ppermute | solution.py:25
  19.1 0.0 collective-permute-start.4
  19.1 2.1 %shard_map.138 = (bf16[3,3,160,640]{3,2,1,0:T(8,128)(2,1)S(1)}, bf16[3,3,160,640]{3,2,1,0:T(8,128)(2,1)S(1)}) custom-call(bf16[3,3,160,640]{3,2,1,0:T(8,128)(2,1)} %refs_0_.4, bf16[3,3,160,640]{3,2,1,0:T(8,128)(2,1)} %refs_1_.2), custom_call_target="tpu_custom_call" | custom-call | bytes 3686400 | tf_op jit(solution)/shard_map/pallas_call | solution.py:173
  21.1 2.1 %shard_map.139.refs_1_ = f32[2,320,160]{2,1,0:T(8,128)S(1)} custom-call(bf16[2,400,128]{2,1,0:T(8,128)(2,1)S(1)} %get-tuple-element.29.refs_0_, bf16[2,400,128]{2,1,0:T(8,128)(2,1)S(1)} %collective-permute-done.5.refs_1_, bf16[3,3,160,640]{3,2,1,0:T(8,128)(2,1)S(1)} %get-tuple-element.30.refs_2_, bf16[3,3,160,640]{3,2,1,0:T(8,128)(2,1)S(1)} %get-tuple-element.31.refs_3_), custom_call_target="tpu_custom_call" | custom-call | flops 589824000 | bytes 4505600 | tf_op jit(solution)/shard_map/pallas_call | solution.py:44
  23.2 0.0 copy-start.2
  23.2 1.4 %shard_map.140.refs_1_ = f32[2,320,160]{2,1,0:T(8,128)S(1)} custom-call(bf16[2,400,128]{2,1,0:T(8,128)(2,1)S(1)} %collective-permute-done.3.refs_0_, f32[2,320,160]{2,1,0:T(8,128)S(1)} %shard_map.139.refs_1_, bf16[3,3,160,640]{3,2,1,0:T(8,128)(2,1)S(1)} %get-tuple-element.30.refs_2_, bf16[3,3,160,640]{3,2,1,0:T(8,128)(2,1)S(1)} %get-tuple-element.31.refs_3_), custom_call_target="tpu_custom_call" | custom-call | flops 294912000 | bytes 4710400 | tf_op jit(solution)/shard_map/pallas_call | solution.py:44
  24.6 1.6 %shard_map.141 = (bf16[2,320,160]{2,1,0:T(8,128)(2,1)S(1)}, bf16[2,384,128]{2,1,0:T(8,128)(2,1)S(1)}) custom-call(bf16[2,400,128]{2,1,0:T(8,128)(2,1)S(1)} %collective-permute-done.4.refs_0_, f32[2,320,160]{2,1,0:T(8,128)S(1)} %shard_map.140.refs_1_, bf16[3,3,160,640]{3,2,1,0:T(8,128)(2,1)S(1)} %get-tuple-element.30.refs_2_, ...), custom_call_target="tpu_custom_call" | custom-call | flops 294912000 | bytes 4907648 | tf_op jit(solution)/shard_map/pallas_call | solution.py:44
  26.2 1.5 %collective-permute-start.6 = (bf16[2,384,128]{2,1,0:T(8,128)(2,1)S(1)}, bf16[2,384,128]{2,1,0:T(8,128)(2,1)S(1)}, u32[]{:S(2)}, u32[]{:S(2)}) collective-permute-start(bf16[2,384,128]{2,1,0:T(8,128)(2,1)S(1)} %get-tuple-element.33.refs_0_), channel_id=1, source_target_pairs={{0,8},{8,0},{1,9},{9,1},{2,10},{10,2},{3,11},{11,3},{4,12},{12,4},... | collective-permute-start | bytes 589832 | tf_op jit(solution)/shard_map/ppermute | solution.py:25
  27.8 0.2 collective-permute-start.8
  28.0 5.6 %collective-permute-done.6.refs_0_ = bf16[2,384,128]{2,1,0:T(8,128)(2,1)S(1)} collective-permute-done((bf16[2,384,128]{2,1,0:T(8,128)(2,1)S(1)}, bf16[2,384,128]{2,1,0:T(8,128)(2,1)S(1)}, u32[]{:S(2)}, u32[]{:S(2)}) %collective-permute-start.6) | collective-permute-done | bytes 196640 | tf_op jit(solution)/shard_map/ppermute | solution.py:25
  33.6 0.0 collective-permute-start.7
  33.6 2.1 %shard_map.142 = (bf16[3,3,160,640]{3,2,1,0:T(8,128)(2,1)S(1)}, bf16[3,3,160,640]{3,2,1,0:T(8,128)(2,1)S(1)}) custom-call(bf16[3,3,160,640]{3,2,1,0:T(8,128)(2,1)} %refs_0_.5, bf16[3,3,160,640]{3,2,1,0:T(8,128)(2,1)} %refs_1_.3), custom_call_target="tpu_custom_call" | custom-call | bytes 3686400 | tf_op jit(solution)/shard_map/pallas_call | solution.py:173
  35.7 2.1 %shard_map.143.refs_1_ = f32[2,320,160]{2,1,0:T(8,128)S(1)} custom-call(bf16[2,384,128]{2,1,0:T(8,128)(2,1)S(1)} %get-tuple-element.33.refs_0_, bf16[2,384,128]{2,1,0:T(8,128)(2,1)S(1)} %collective-permute-done.8.refs_1_, bf16[3,3,160,640]{3,2,1,0:T(8,128)(2,1)S(1)} %get-tuple-element.34.refs_2_, bf16[3,3,160,640]{3,2,1,0:T(8,128)(2,1)S(1)} %get-tuple-element.35.refs_3_), custom_call_target="tpu_custom_call" | custom-call | flops 589824000 | bytes 4489216 | tf_op jit(solution)/shard_map/pallas_call | solution.py:44
  37.8 0.0 copy-start.4
  37.8 1.3 %shard_map.144.refs_1_ = f32[2,320,160]{2,1,0:T(8,128)S(1)} custom-call(bf16[2,384,128]{2,1,0:T(8,128)(2,1)S(1)} %collective-permute-done.6.refs_0_, f32[2,320,160]{2,1,0:T(8,128)S(1)} %shard_map.143.refs_1_, bf16[3,3,160,640]{3,2,1,0:T(8,128)(2,1)S(1)} %get-tuple-element.34.refs_2_, bf16[3,3,160,640]{3,2,1,0:T(8,128)(2,1)S(1)} %get-tuple-element.35.refs_3_), custom_call_target="tpu_custom_call" | custom-call | flops 294912000 | bytes 4702208 | tf_op jit(solution)/shard_map/pallas_call | solution.py:44
  39.2 1.6 %shard_map.145 = (bf16[2,320,160]{2,1,0:T(8,128)(2,1)S(1)}, bf16[2,360,128]{2,1,0:T(8,128)(2,1)S(1)}) custom-call(bf16[2,384,128]{2,1,0:T(8,128)(2,1)S(1)} %collective-permute-done.7.refs_0_, f32[2,320,160]{2,1,0:T(8,128)S(1)} %shard_map.144.refs_1_, bf16[3,3,160,640]{3,2,1,0:T(8,128)(2,1)S(1)} %get-tuple-element.34.refs_2_, ...), custom_call_target="tpu_custom_call" | custom-call | flops 294912000 | bytes 4887168 | tf_op jit(solution)/shard_map/pallas_call | solution.py:44
  40.8 1.5 %collective-permute-start.9 = (bf16[2,360,128]{2,1,0:T(8,128)(2,1)S(1)}, bf16[2,360,128]{2,1,0:T(8,128)(2,1)S(1)}, u32[]{:S(2)}, u32[]{:S(2)}) collective-permute-start(bf16[2,360,128]{2,1,0:T(8,128)(2,1)S(1)} %get-tuple-element.37.refs_0_), channel_id=1, source_target_pairs={{0,8},{8,0},{1,9},{9,1},{2,10},{10,2},{3,11},{11,3},{4,12},{12,4},... | collective-permute-start | bytes 552968 | tf_op jit(solution)/shard_map/ppermute | solution.py:25
  42.3 0.2 collective-permute-start.11
  42.5 5.4 %collective-permute-done.9.refs_0_.refs_2_ = bf16[2,360,128]{2,1,0:T(8,128)(2,1)S(1)} collective-permute-done((bf16[2,360,128]{2,1,0:T(8,128)(2,1)S(1)}, bf16[2,360,128]{2,1,0:T(8,128)(2,1)S(1)}, u32[]{:S(2)}, u32[]{:S(2)}) %collective-permute-start.9) | collective-permute-done | bytes 184352 | tf_op jit(solution)/shard_map/ppermute | solution.py:25
  47.9 2.1 %shard_map.146.refs_2_ = bf16[3,3,160,1280]{3,2,1,0:T(8,128)(2,1)S(1)} custom-call(bf16[3,3,160,1280]{3,2,1,0:T(8,128)(2,1)} %refs_0_.6), custom_call_target="tpu_custom_call" | custom-call | bytes 3686400 | tf_op jit(solution)/shard_map/pallas_call | solution.py:173
  50.0 2.0 %shard_map.147.refs_1_ = f32[320,160]{1,0:T(8,128)S(1)} custom-call(bf16[2,360,128]{2,1,0:T(8,128)(2,1)S(1)} %get-tuple-element.37.refs_0_, bf16[2,360,128]{2,1,0:T(8,128)(2,1)S(1)} %collective-permute-done.11.refs_1_, bf16[3,3,160,1280]{3,2,1,0:T(8,128)(2,1)S(1)} %shard_map.146.refs_2_), custom_call_target="tpu_custom_call" | custom-call | flops 589824000 | bytes 4259840 | tf_op jit(solution)/shard_map/pallas_call | solution.py:44
  52.0 0.0 copy-start.5
  52.1 1.1 %shard_map.148.refs_1_ = f32[320,160]{1,0:T(8,128)S(1)} custom-call(bf16[2,360,128]{2,1,0:T(8,128)(2,1)S(1)} %collective-permute-done.9.refs_0_.refs_2_, f32[320,160]{1,0:T(8,128)S(1)} %shard_map.147.refs_1_, bf16[3,3,160,1280]{3,2,1,0:T(8,128)(2,1)S(1)} %shard_map.146.refs_2_), custom_call_target="tpu_custom_call" | custom-call | flops 294912000 | bytes 4280320 | tf_op jit(solution)/shard_map/pallas_call | solution.py:44
  53.2 1.2 %shard_map.149 = (bf16[320,160]{1,0:T(8,128)(2,1)S(1)}, bf16[344,128]{1,0:T(8,128)(2,1)S(1)}) custom-call(bf16[2,360,128]{2,1,0:T(8,128)(2,1)S(1)} %collective-permute-done.10.refs_0_.refs_3_, f32[320,160]{1,0:T(8,128)S(1)} %shard_map.148.refs_1_, bf16[3,3,160,1280]{3,2,1,0:T(8,128)(2,1)S(1)} %shard_map.146.refs_2_, ...), custom_call_target="tpu_custom_call" | custom-call | flops 294912000 | bytes 4471104 | tf_op jit(solution)/shard_map/pallas_call | solution.py:44
  54.4 1.5 %collective-permute-start.12 = (bf16[344,128]{1,0:T(8,128)(2,1)S(1)}, bf16[344,128]{1,0:T(8,128)(2,1)S(1)}, u32[]{:S(2)}, u32[]{:S(2)}) collective-permute-start(bf16[344,128]{1,0:T(8,128)(2,1)S(1)} %get-tuple-element.39.refs_0_), channel_id=1, source_target_pairs={{0,8},{8,0},{1,9},{9,1},{2,10},{10,2},{3,11},{11,3},{4,12},{12,4},... | collective-permute-start | bytes 264200 | tf_op jit(solution)/shard_map/ppermute | solution.py:25
  55.9 0.2 collective-permute-start.14
  56.1 2.1 %shard_map.150.refs_4_.refs_3_.refs_2_ = bf16[3,3,160,1280]{3,2,1,0:T(8,128)(2,1)S(1)} custom-call(bf16[3,3,160,1280]{3,2,1,0:T(8,128)(2,1)} %refs_0_.7), custom_call_target="tpu_custom_call" | custom-call | bytes 3686400 | tf_op jit(solution)/shard_map/pallas_call | solution.py:173
  58.1 1.3 %collective-permute-done.12.refs_0_ = bf16[344,128]{1,0:T(8,128)(2,1)S(1)} collective-permute-done((bf16[344,128]{1,0:T(8,128)(2,1)S(1)}, bf16[344,128]{1,0:T(8,128)(2,1)S(1)}, u32[]{:S(2)}, u32[]{:S(2)}) %collective-permute-start.12) | collective-permute-done | bytes 88096 | tf_op jit(solution)/shard_map/ppermute | solution.py:25
  59.5 1.1 %shard_map.151.refs_2_ = f32[320,160]{1,0:T(8,128)S(1)} custom-call(bf16[2,360,128]{2,1,0:T(8,128)(2,1)S(1)} %get-tuple-element.37.refs_0_, bf16[2,360,128]{2,1,0:T(8,128)(2,1)S(1)} %collective-permute-done.11.refs_1_, bf16[2,360,128]{2,1,0:T(8,128)(2,1)S(1)} %collective-permute-done.9.refs_0_.refs_2_, ...), custom_call_target="tpu_custom_call" | custom-call | flops 589824000 | bytes 4628480 | tf_op jit(solution)/shard_map/pallas_call | solution.py:44
  60.6 1.0 %shard_map.152.refs_1_ = f32[320,160]{1,0:T(8,128)S(1)} custom-call(bf16[344,128]{1,0:T(8,128)(2,1)S(1)} %get-tuple-element.39.refs_0_, bf16[344,128]{1,0:T(8,128)(2,1)S(1)} %collective-permute-done.14.refs_1_, f32[320,160]{1,0:T(8,128)S(1)} %shard_map.151.refs_2_, bf16[3,3,160,1280]{3,2,1,0:T(8,128)(2,1)S(1)} %shard_map.150.refs_4_.refs_3_.refs_2_), custom_call_target="tpu_custom_call" | custom-call | flops 294912000 | bytes 4272128 | tf_op jit(solution)/shard_map/pallas_call | solution.py:44
  61.6 0.0 copy-start
  61.7 0.7 shard_map.153.refs_1_
  62.4 0.8 %shard_map.154 = (bf16[80,128]{1,0:T(8,128)(2,1)S(1)}, bf16[80,128]{1,0:T(8,128)(2,1)S(1)}, bf16[80,128]{1,0:T(8,128)(2,1)S(1)}, bf16[80,128]{1,0:T(8,128)(2,1)S(1)}) custom-call(bf16[344,128]{1,0:T(8,128)(2,1)S(1)} %collective-permute-done.13.refs_0_, f32[320,160]{1,0:T(8,128)S(1)} %shard_map.153.refs_1_, ...), custom_call_target="tpu_custom_call" | custom-call | flops 147456000 | bytes 4163904 | tf_op jit(solution)/shard_map/pallas_call | solution.py:44
  63.2 0.1 collective-permute-start.15
  63.3 1.4 %collective-permute-start.16 = (bf16[80,128]{1,0:T(8,128)(2,1)S(1)}, bf16[80,128]{1,0:T(8,128)(2,1)S(1)}, u32[]{:S(2)}, u32[]{:S(2)}) collective-permute-start(bf16[80,128]{1,0:T(8,128)(2,1)S(1)} %get-tuple-element.43), channel_id=1, source_target_pairs={{0,4},{2,6},{4,0},{6,2},{1,5},{3,7},{5,1},{7,3},{8,12},{10,14},{12... | collective-permute-start | bytes 61448 | tf_op jit(solution)/shard_map/ppermute | solution.py:25
  64.7 3.0 %collective-permute-start.17 = (bf16[80,128]{1,0:T(8,128)(2,1)S(1)}, bf16[80,128]{1,0:T(8,128)(2,1)S(1)}, u32[]{:S(2)}, u32[]{:S(2)}) collective-permute-start(bf16[80,128]{1,0:T(8,128)(2,1)S(1)} %get-tuple-element.44), channel_id=1, source_target_pairs={{0,6},{2,4},{4,2},{6,0},{1,7},{3,5},{5,3},{7,1},{8,14},{10,12},{12... | collective-permute-start | bytes 61448 | tf_op jit(solution)/shard_map/ppermute | solution.py:25
  67.6 0.6 collective-permute-done.16.refs_2_
  68.2 2.0 %collective-permute-done.17.refs_3_ = bf16[80,128]{1,0:T(8,128)(2,1)S(1)} collective-permute-done((bf16[80,128]{1,0:T(8,128)(2,1)S(1)}, bf16[80,128]{1,0:T(8,128)(2,1)S(1)}, u32[]{:S(2)}, u32[]{:S(2)}) %collective-permute-start.17) | collective-permute-done | bytes 20512 | tf_op jit(solution)/shard_map/ppermute | solution.py:25
  70.3 0.8 %shard_map.155 = bf16[2,160,128]{2,1,0:T(8,128)(2,1)} custom-call(bf16[80,128]{1,0:T(8,128)(2,1)S(1)} %get-tuple-element.41.refs_0_, bf16[80,128]{1,0:T(8,128)(2,1)S(1)} %collective-permute-done.15.refs_1_, bf16[80,128]{1,0:T(8,128)(2,1)S(1)} %collective-permute-done.16.refs_2_, bf16[80,128]{1,0:T(8,128)(2,1)S(1)} %collective-permute-done.17.refs_3_), custom_call_target="tpu_custom_call" | custom-call | bytes 163840 | tf_op jit(solution)/shard_map/pallas_call | solution.py:44
  (20 shorter events, 0.0 us)
Async XLA Ops:
  1.2 5.7 %collective-permute-start = (bf16[200,128]{1,0:T(8,128)(2,1)S(1)}, bf16[200,128]{1,0:T(8,128)(2,1)S(1)}, u32[]{:S(2)}, u32[]{:S(2)}) collective-permute-start(bf16[200,128]{1,0:T(8,128)(2,1)S(1)} %get-tuple-element.26), channel_id=1, source_target_pairs={{0,2},{2,0},{4,6},{6,4},{1,3},{3,1},{5,7},{7,5},{8,10},{10,8},{12,... | collective-permute-start | bytes 153608 | tf_op jit(solution)/shard_map/ppermute | solution.py:25
  4.3 6.0 %collective-permute-start.1 = (bf16[200,128]{1,0:T(8,128)(2,1)S(1)}, bf16[200,128]{1,0:T(8,128)(2,1)S(1)}, u32[]{:S(2)}, u32[]{:S(2)}) collective-permute-start(bf16[200,128]{1,0:T(8,128)(2,1)S(1)} %get-tuple-element.27), channel_id=1, source_target_pairs={{0,4},{2,6},{4,0},{6,2},{1,5},{3,7},{5,1},{7,3},{8,12},{10,14},{12... | collective-permute-start | bytes 153608 | tf_op jit(solution)/shard_map/ppermute | solution.py:25
  6.9 5.9 %collective-permute-start.2 = (bf16[200,128]{1,0:T(8,128)(2,1)S(1)}, bf16[200,128]{1,0:T(8,128)(2,1)S(1)}, u32[]{:S(2)}, u32[]{:S(2)}) collective-permute-start(bf16[200,128]{1,0:T(8,128)(2,1)S(1)} %get-tuple-element.28), channel_id=1, source_target_pairs={{0,6},{2,4},{4,2},{6,0},{1,7},{3,5},{5,3},{7,1},{8,14},{10,12},{12... | collective-permute-start | bytes 153608 | tf_op jit(solution)/shard_map/ppermute | solution.py:25
  13.2 5.8 %collective-permute-start.3 = (bf16[2,400,128]{2,1,0:T(8,128)(2,1)S(1)}, bf16[2,400,128]{2,1,0:T(8,128)(2,1)S(1)}, u32[]{:S(2)}, u32[]{:S(2)}) collective-permute-start(bf16[2,400,128]{2,1,0:T(8,128)(2,1)S(1)} %get-tuple-element.29.refs_0_), channel_id=1, source_target_pairs={{0,8},{8,0},{1,9},{9,1},{2,10},{10,2},{3,11},{11,3},{4,12},{12,4},... | collective-permute-start | bytes 614408 | tf_op jit(solution)/shard_map/ppermute | solution.py:25
  14.8 6.4 %collective-permute-start.5 = (bf16[2,400,128]{2,1,0:T(8,128)(2,1)S(1)}, bf16[2,400,128]{2,1,0:T(8,128)(2,1)S(1)}, u32[]{:S(2)}, u32[]{:S(2)}) collective-permute-start(bf16[2,400,128]{2,1,0:T(8,128)(2,1)S(1)} %get-tuple-element.29.refs_0_), channel_id=1, source_target_pairs={{0,1},{1,0},{2,3},{3,2},{4,5},{5,4},{6,7},{7,6},{8,9},{9,8},{10,11... | collective-permute-start | bytes 614408 | tf_op jit(solution)/shard_map/ppermute | solution.py:25
  19.1 5.6 %collective-permute-start.4 = (bf16[2,400,128]{2,1,0:T(8,128)(2,1)S(1)}, bf16[2,400,128]{2,1,0:T(8,128)(2,1)S(1)}, u32[]{:S(2)}, u32[]{:S(2)}) collective-permute-start(bf16[2,400,128]{2,1,0:T(8,128)(2,1)S(1)} %collective-permute-done.3.refs_0_), channel_id=1, source_target_pairs={{0,1},{1,0},{2,3},{3,2},{4,5},{5,4},{6,7},{7,6},{8,9},{9,8},{10,11... | collective-permute-start | bytes 614408 | tf_op jit(solution)/shard_map/ppermute | solution.py:25
  23.2 1.4 %copy-start.1 = (bf16[160]{0:T(256)(128)(2,1)S(1)}, bf16[160]{0:T(256)(128)(2,1)}, u32[]{:S(2)}) copy-start(bf16[160]{0:T(256)(128)(2,1)} %refs_5_.2) | copy-start | bytes 964
  23.2 1.4 %copy-start.2 = (bf16[160]{0:T(256)(128)(2,1)S(1)}, bf16[160]{0:T(256)(128)(2,1)}, u32[]{:S(2)}) copy-start(bf16[160]{0:T(256)(128)(2,1)} %refs_6_.2) | copy-start | bytes 964
  26.2 7.4 %collective-permute-start.6 = (bf16[2,384,128]{2,1,0:T(8,128)(2,1)S(1)}, bf16[2,384,128]{2,1,0:T(8,128)(2,1)S(1)}, u32[]{:S(2)}, u32[]{:S(2)}) collective-permute-start(bf16[2,384,128]{2,1,0:T(8,128)(2,1)S(1)} %get-tuple-element.33.refs_0_), channel_id=1, source_target_pairs={{0,8},{8,0},{1,9},{9,1},{2,10},{10,2},{3,11},{11,3},{4,12},{12,4},... | collective-permute-start | bytes 589832 | tf_op jit(solution)/shard_map/ppermute | solution.py:25
  27.8 7.9 %collective-permute-start.8 = (bf16[2,384,128]{2,1,0:T(8,128)(2,1)S(1)}, bf16[2,384,128]{2,1,0:T(8,128)(2,1)S(1)}, u32[]{:S(2)}, u32[]{:S(2)}) collective-permute-start(bf16[2,384,128]{2,1,0:T(8,128)(2,1)S(1)} %get-tuple-element.33.refs_0_), channel_id=1, source_target_pairs={{0,1},{1,0},{2,3},{3,2},{4,5},{5,4},{6,7},{7,6},{8,9},{9,8},{10,11... | collective-permute-start | bytes 589832 | tf_op jit(solution)/shard_map/ppermute | solution.py:25
  33.6 5.5 %collective-permute-start.7 = (bf16[2,384,128]{2,1,0:T(8,128)(2,1)S(1)}, bf16[2,384,128]{2,1,0:T(8,128)(2,1)S(1)}, u32[]{:S(2)}, u32[]{:S(2)}) collective-permute-start(bf16[2,384,128]{2,1,0:T(8,128)(2,1)S(1)} %collective-permute-done.6.refs_0_), channel_id=1, source_target_pairs={{0,1},{1,0},{2,3},{3,2},{4,5},{5,4},{6,7},{7,6},{8,9},{9,8},{10,11... | collective-permute-start | bytes 589832 | tf_op jit(solution)/shard_map/ppermute | solution.py:25
  37.8 1.4 %copy-start.3 = (bf16[160]{0:T(256)(128)(2,1)S(1)}, bf16[160]{0:T(256)(128)(2,1)}, u32[]{:S(2)}) copy-start(bf16[160]{0:T(256)(128)(2,1)} %refs_5_.3) | copy-start | bytes 964
  37.8 1.4 %copy-start.4 = (bf16[160]{0:T(256)(128)(2,1)S(1)}, bf16[160]{0:T(256)(128)(2,1)}, u32[]{:S(2)}) copy-start(bf16[160]{0:T(256)(128)(2,1)} %refs_6_.3) | copy-start | bytes 964
  40.8 7.1 %collective-permute-start.9 = (bf16[2,360,128]{2,1,0:T(8,128)(2,1)S(1)}, bf16[2,360,128]{2,1,0:T(8,128)(2,1)S(1)}, u32[]{:S(2)}, u32[]{:S(2)}) collective-permute-start(bf16[2,360,128]{2,1,0:T(8,128)(2,1)S(1)} %get-tuple-element.37.refs_0_), channel_id=1, source_target_pairs={{0,8},{8,0},{1,9},{9,1},{2,10},{10,2},{3,11},{11,3},{4,12},{12,4},... | collective-permute-start | bytes 552968 | tf_op jit(solution)/shard_map/ppermute | solution.py:25
  42.3 7.7 %collective-permute-start.11 = (bf16[2,360,128]{2,1,0:T(8,128)(2,1)S(1)}, bf16[2,360,128]{2,1,0:T(8,128)(2,1)S(1)}, u32[]{:S(2)}, u32[]{:S(2)}) collective-permute-start(bf16[2,360,128]{2,1,0:T(8,128)(2,1)S(1)} %get-tuple-element.37.refs_0_), channel_id=1, source_target_pairs={{0,1},{1,0},{2,3},{3,2},{4,5},{5,4},{6,7},{7,6},{8,9},{9,8},{10,11... | collective-permute-start | bytes 552968 | tf_op jit(solution)/shard_map/ppermute | solution.py:25
  47.9 5.2 %collective-permute-start.10 = (bf16[2,360,128]{2,1,0:T(8,128)(2,1)S(1)}, bf16[2,360,128]{2,1,0:T(8,128)(2,1)S(1)}, u32[]{:S(2)}, u32[]{:S(2)}) collective-permute-start(bf16[2,360,128]{2,1,0:T(8,128)(2,1)S(1)} %collective-permute-done.9.refs_0_.refs_2_), channel_id=1, source_target_pairs={{0,1},{1,0},{2,3},{3,2},{4,5},{5,4},{6,7},{7,6},{8,9},{9,8},{10,11... | collective-permute-start | bytes 552968 | tf_op jit(solution)/shard_map/ppermute | solution.py:25
  52.0 1.1 %copy-start.5 = (bf16[160]{0:T(256)(128)(2,1)S(1)}, bf16[160]{0:T(256)(128)(2,1)}, u32[]{:S(2)}) copy-start(bf16[160]{0:T(256)(128)(2,1)} %refs_4_.2) | copy-start | bytes 964
  54.4 5.1 %collective-permute-start.12 = (bf16[344,128]{1,0:T(8,128)(2,1)S(1)}, bf16[344,128]{1,0:T(8,128)(2,1)S(1)}, u32[]{:S(2)}, u32[]{:S(2)}) collective-permute-start(bf16[344,128]{1,0:T(8,128)(2,1)S(1)} %get-tuple-element.39.refs_0_), channel_id=1, source_target_pairs={{0,8},{8,0},{1,9},{9,1},{2,10},{10,2},{3,11},{11,3},{4,12},{12,4},... | collective-permute-start | bytes 264200 | tf_op jit(solution)/shard_map/ppermute | solution.py:25
  55.9 4.7 %collective-permute-start.14 = (bf16[344,128]{1,0:T(8,128)(2,1)S(1)}, bf16[344,128]{1,0:T(8,128)(2,1)S(1)}, u32[]{:S(2)}, u32[]{:S(2)}) collective-permute-start(bf16[344,128]{1,0:T(8,128)(2,1)S(1)} %get-tuple-element.39.refs_0_), channel_id=1, source_target_pairs={{0,1},{1,0},{2,3},{3,2},{4,5},{5,4},{6,7},{7,6},{8,9},{9,8},{10,11... | collective-permute-start | bytes 264200 | tf_op jit(solution)/shard_map/ppermute | solution.py:25
  59.5 2.9 %collective-permute-start.13 = (bf16[344,128]{1,0:T(8,128)(2,1)S(1)}, bf16[344,128]{1,0:T(8,128)(2,1)S(1)}, u32[]{:S(2)}, u32[]{:S(2)}) collective-permute-start(bf16[344,128]{1,0:T(8,128)(2,1)S(1)} %collective-permute-done.12.refs_0_), channel_id=1, source_target_pairs={{0,1},{1,0},{2,3},{3,2},{4,5},{5,4},{6,7},{7,6},{8,9},{9,8},{10,11... | collective-permute-start | bytes 264200 | tf_op jit(solution)/shard_map/ppermute | solution.py:25
  61.6 0.7 copy-start
  63.2 4.5 %collective-permute-start.15 = (bf16[80,128]{1,0:T(8,128)(2,1)S(1)}, bf16[80,128]{1,0:T(8,128)(2,1)S(1)}, u32[]{:S(2)}, u32[]{:S(2)}) collective-permute-start(bf16[80,128]{1,0:T(8,128)(2,1)S(1)} %get-tuple-element.42), channel_id=1, source_target_pairs={{0,2},{2,0},{4,6},{6,4},{1,3},{3,1},{5,7},{7,5},{8,10},{10,8},{12,... | collective-permute-start | bytes 61448 | tf_op jit(solution)/shard_map/ppermute | solution.py:25
  63.3 5.0 %collective-permute-start.16 = (bf16[80,128]{1,0:T(8,128)(2,1)S(1)}, bf16[80,128]{1,0:T(8,128)(2,1)S(1)}, u32[]{:S(2)}, u32[]{:S(2)}) collective-permute-start(bf16[80,128]{1,0:T(8,128)(2,1)S(1)} %get-tuple-element.43), channel_id=1, source_target_pairs={{0,4},{2,6},{4,0},{6,2},{1,5},{3,7},{5,1},{7,3},{8,12},{10,14},{12... | collective-permute-start | bytes 61448 | tf_op jit(solution)/shard_map/ppermute | solution.py:25
  64.7 5.6 %collective-permute-start.17 = (bf16[80,128]{1,0:T(8,128)(2,1)S(1)}, bf16[80,128]{1,0:T(8,128)(2,1)S(1)}, u32[]{:S(2)}, u32[]{:S(2)}) collective-permute-start(bf16[80,128]{1,0:T(8,128)(2,1)S(1)} %get-tuple-element.44), channel_id=1, source_target_pairs={{0,6},{2,4},{4,2},{6,0},{1,7},{3,5},{5,3},{7,1},{8,14},{10,12},{12... | collective-permute-start | bytes 61448 | tf_op jit(solution)/shard_map/ppermute | solution.py:25

commit v8 on v7

--- a/solution.py
+++ b/solution.py
@@ -82,6 +82,14 @@
         return all(offset + self.per <= self.span for offset in self.offsets)
 
 
+    def rolled(self):
+        return (
+            self.groups > 0
+            and self.per // LANES == 1
+            and self.span == 2 * LANES
+            and all(o % self.rest == 0 and o + self.rest <= LANES for o in self.offsets)
+        )
+
     def part(self, cells):
         return -(-cells // (8 * self.groups)) * 8
 
@@ -94,20 +102,32 @@
         return self.cells - 2 * trim * self.height
 
 
-def pack(z, ref, value):
+def pick(values, owner):
+    chosen = jnp.int32(values[0])
+    for j, value in enumerate(values):
+        chosen = jnp.where(owner == j, value, chosen)
+    return chosen
+
+
+def pack(z, ref, value, roll=False):
     cells = value.shape[0]
     if not z.groups:
         ref[...] = value.astype(BF16)
         return
+    turn = lambda lanes: lanes
+    if roll and z.rolled():
+        offset = pick(z.offsets, channel_place())
+        turn = lambda lanes: pltpu.roll(lanes, offset, 1)
     full = z.per // LANES
     for g in range(full):
-        ref[g * cells : (g + 1) * cells] = value[:, g * LANES : (g + 1) * LANES].astype(BF16)
+        lanes = turn(value[:, g * LANES : (g + 1) * LANES])
+        ref[g * cells : (g + 1) * cells] = lanes.astype(BF16)
     part = z.part(cells)
     rest = [value[g * part : (g + 1) * part, full * LANES :] for g in range(z.groups)]
     short = part - rest[-1].shape[0]
     if short:
         rest[-1] = jnp.concatenate([rest[-1], jnp.zeros((short, z.rest), F32)], axis=0)
-    ref[full * cells :] = jnp.concatenate(rest, axis=1).astype(BF16)
+    ref[full * cells :] = turn(jnp.concatenate(rest, axis=1)).astype(BF16)
 
 
 def unpack(z, cells, message, put):
@@ -209,60 +229,56 @@
         parts = [image[t, g][:, :n] for g, (_, n) in enumerate(lane_groups(z))]
         value = jnp.concatenate(parts, axis=1)
         state_ref[t] = value.astype(BF16)
-        pack(z, act_ref.at[t], masked_silu(z, value))
-
-
-def in_order(pieces):
-    place = channel_place()
-    step = 1
-    while step < len(pieces):
-        flip = (place & step) != 0
-        pieces = [
-            jnp.where(flip, pieces[j ^ step], pieces[j]) for j in range(len(pieces))
-        ]
-        step *= 2
-    return pieces
-
-
-def lay_out(z, trim, a_ref, messages):
-    first = (1 + trim) * z.height
-    a_ref[:first] = jnp.zeros((first, a_ref.shape[1]), BF16)
-    a_ref[z.held - first :] = jnp.zeros((first, a_ref.shape[1]), BF16)
-    for j, message in enumerate(in_order(messages)):
-
-        def put(row, lane, piece):
-            rows, lanes = piece.shape
-            lane = j * z.per + lane
-            row = row + first
-            a_ref[row : row + rows, lane : lane + lanes] = piece
-
-        unpack(z, z.kept(trim), message, put)
+        pack(z, act_ref.at[t], masked_silu(z, value), roll=True)
 
 
 def place(z, trim, a_ref, at, message, distance):
     first = (1 + trim) * z.height
     owner = channel_place() ^ distance
-    start = offset = jnp.int32(0)
-    for j in range(z.shards):
-        start = jnp.where(owner == j, z.starts[j], start)
-        offset = jnp.where(owner == j, z.offsets[j], offset)
-    for known in sorted(set(z.offsets)):
-
-        @pl.when(offset == known)
-        def _():
-            def put(row, lane, piece):
-                rows, lanes = piece.shape
-                lane = at + known + lane
-                row = row + first
-                a_ref[row : row + rows, lane : lane + lanes] = piece
-
-            unpack(z, z.kept(trim), message, put)
-
-    return start
+    offset = pick(z.offsets, owner)
+    cells = z.kept(trim)
+    if z.rolled():
+        main = message[:cells].astype(F32)
+        rest = message[cells:].astype(F32)
+        part = z.part(cells)
+        turned = [rest] + [
+            pltpu.roll(rest, LANES - g * z.rest, 1)[: min(part, cells - g * part)]
+            for g in range(1, z.groups)
+        ]
+        rest = jnp.concatenate(turned, axis=0)
+        lane = lax.broadcasted_iota(jnp.int32, main.shape, 1)
+        low = jnp.where(lane >= offset, main, 0.0)
+        high = jnp.where(lane < offset, main, jnp.where(lane < offset + z.rest, rest, 0.0))
+        a_ref[first : first + cells, at : at + LANES] = low.astype(BF16)
+        a_ref[first : first + cells, at + LANES : at + 2 * LANES] = high.astype(BF16)
+    else:
+        for known in sorted(set(z.offsets)):
+
+            @pl.when(offset == known)
+            def _():
+                def put(row, lane, piece):
+                    rows, lanes = piece.shape
+                    lane = at + known + lane
+                    row = row + first
+                    a_ref[row : row + rows, lane : lane + lanes] = piece
+
+                unpack(z, cells, message, put)
+
+    return pick(z.starts, owner)
+
+
+def clear(z, trim, a_ref):
+    if z.rolled():
+        first = (1 + trim) * z.height
+        edge = jnp.zeros((first, a_ref.shape[1]), BF16)
+        a_ref[:first] = edge
+        a_ref[z.held - first :] = edge
+    else:
+        a_ref[...] = jnp.zeros(a_ref.shape, BF16)
 
 
 def accumulate(z, trim, distances, sources, w_ref, a_ref):
-    a_ref[...] = jnp.zeros(a_ref.shape, BF16)
+    clear(z, trim, a_ref)
     slices = []
     for base, messages in sources:
         for distance, message in zip(distances, messages):
@@ -321,7 +337,8 @@
     new = (state.astype(F32) + result + bias).astype(BF16)
     new_ref[...] = new
     edge = trim * z.height
-    pack(z, act_ref, masked_silu(z, new.astype(F32))[edge : z.cells - edge])
+    act = masked_silu(z, new.astype(F32))[edge : z.cells - edge]
+    pack(z, act_ref, act, roll=True)
 
 
 def bias_of(ref):
@@ -368,9 +385,8 @@
 
 def skip_kernel(z, trim, *refs):
     blocks, (w_ref, out_ref, a_ref) = refs[: z.shards], refs[z.shards :]
-    lay_out(z, trim, a_ref, [block[0] for block in blocks])
-    weights = taps(z, w_ref, [slice(z.depth, 2 * z.depth)])
-    out_ref[...] = convolve(z, moves(z, a_ref), weights)
+    sources = [(z.depth, [block[0] for block in blocks])]
+    out_ref[...] = accumulate(z, trim, range(z.shards), sources, w_ref, a_ref)
 
 
 def last_kernel(z, trim, distances, add, end, *refs):
@@ -522,7 +538,7 @@
         total,
         *[skips[d] for d in range(z.shards)],
         dw2,
-        scratch=[pltpu.VMEM((z.held, z.depth), BF16)],
+        scratch=[pltpu.VMEM((z.held, z.shards * z.span), BF16)],
         flops=2 * 9 * z.cells * z.per * z.depth,
     )
     blocks = layer(

time: 71.3 us -> 66.3 us (0.930)
  Pallas kernels: 28.7 us -> 23.7 us
    pallas_call x15, Pallas kernels: 19.3 us -> 14.2 us  [call(): pl.pallas_call(kernel, out_shape=outs, in_specs=whole(len(args)), out_spe...]
  transfers between devices with their start and end apart: 18 -> 18, of which waited for: 8 -> 8; matrix products, arithmetic and copies ran while one was open for 0% -> 0% of each run, Pallas kernels for 30% -> 26%
where the time goes in v8:
time: 66.3 us; the launch traced here: 66.1 us
  waiting for transfers between devices  24.9 us (38%)
  Pallas kernels  23.7 us (36%)
  starting transfers between devices  17 us (26%)
    ppermute x18, waiting for transfers between devices, exchange(): return lax.ppermute(cells, axis, [(i, i ^ distance) for i in range(count)])  24.9 us
    ppermute x18, starting transfers between devices, exchange(): return lax.ppermute(cells, axis, [(i, i ^ distance) for i in range(count)])  17 us
    pallas_call x15, Pallas kernels, call(): pl.pallas_call(kernel, out_shape=outs, in_specs=whole(len(args)), out_spe...  14.2 us
    pallas_call x4, Pallas kernels, load(): pl.pallas_call(functools.partial(load_kernel, count), out_shape=[sds(w.sh...  8.25 us
  transfers between devices with their start and end apart: 18, of which 8 were waited for; matrix products, arithmetic and copies ran while one was open for 0% of the time, Pallas kernels for 26%

profile of v8, /device:TPU:0, one launch (start us, length us, event | category | flops | bytes accessed | tf_op | source)
XLA Modules:
  0.0 66.1 jit_solution(14654901804962713486)
XLA Ops:
  0.0 1.2 %shard_map.136 = (bf16[200,128]{1,0:T(8,128)(2,1)S(1)}, bf16[200,128]{1,0:T(8,128)(2,1)S(1)}, bf16[200,128]{1,0:T(8,128)(2,1)S(1)}, bf16[200,128]{1,0:T(8,128)(2,1)S(1)}) custom-call(bf16[2,160,128]{2,1,0:T(8,128)(2,1)} %bitcast.3, bf16[2,160,128]{2,1,0:T(8,128)(2,1)} %bitcast.4), custom_call_target="tpu_custom_call" | custom-call | tf_op jit(solution)/shard_map/pallas_call | solution.py:480
  1.2 3.1 %collective-permute-start = (bf16[200,128]{1,0:T(8,128)(2,1)S(1)}, bf16[200,128]{1,0:T(8,128)(2,1)S(1)}, u32[]{:S(2)}, u32[]{:S(2)}) collective-permute-start(bf16[200,128]{1,0:T(8,128)(2,1)S(1)} %get-tuple-element.26), channel_id=1, source_target_pairs={{0,2},{2,0},{4,6},{6,4},{1,3},{3,1},{5,7},{7,5},{8,10},{10,8},{12,... | collective-permute-start | bytes 153608 | tf_op jit(solution)/shard_map/ppermute | solution.py:25
  4.3 2.6 %collective-permute-start.1 = (bf16[200,128]{1,0:T(8,128)(2,1)S(1)}, bf16[200,128]{1,0:T(8,128)(2,1)S(1)}, u32[]{:S(2)}, u32[]{:S(2)}) collective-permute-start(bf16[200,128]{1,0:T(8,128)(2,1)S(1)} %get-tuple-element.27), channel_id=1, source_target_pairs={{0,4},{2,6},{4,0},{6,2},{1,5},{3,7},{5,1},{7,3},{8,12},{10,14},{12... | collective-permute-start | bytes 153608 | tf_op jit(solution)/shard_map/ppermute | solution.py:25
  6.9 0.0 collective-permute-start.2
  6.9 3.4 %collective-permute-done.1.refs_2_ = bf16[200,128]{1,0:T(8,128)(2,1)S(1)} collective-permute-done((bf16[200,128]{1,0:T(8,128)(2,1)S(1)}, bf16[200,128]{1,0:T(8,128)(2,1)S(1)}, u32[]{:S(2)}, u32[]{:S(2)}) %collective-permute-start.1) | collective-permute-done | bytes 51232 | tf_op jit(solution)/shard_map/ppermute | solution.py:25
  10.3 2.5 %collective-permute-done.2.refs_3_ = bf16[200,128]{1,0:T(8,128)(2,1)S(1)} collective-permute-done((bf16[200,128]{1,0:T(8,128)(2,1)S(1)}, bf16[200,128]{1,0:T(8,128)(2,1)S(1)}, u32[]{:S(2)}, u32[]{:S(2)}) %collective-permute-start.2) | collective-permute-done | bytes 51232 | tf_op jit(solution)/shard_map/ppermute | solution.py:25
  12.8 0.5 shard_map.137
  13.3 1.5 %collective-permute-start.3 = (bf16[2,400,128]{2,1,0:T(8,128)(2,1)S(1)}, bf16[2,400,128]{2,1,0:T(8,128)(2,1)S(1)}, u32[]{:S(2)}, u32[]{:S(2)}) collective-permute-start(bf16[2,400,128]{2,1,0:T(8,128)(2,1)S(1)} %get-tuple-element.29.refs_0_), channel_id=1, source_target_pairs={{0,8},{8,0},{1,9},{9,1},{2,10},{10,2},{3,11},{11,3},{4,12},{12,4},... | collective-permute-start | bytes 614408 | tf_op jit(solution)/shard_map/ppermute | solution.py:25
  14.9 4.3 %collective-permute-done.3.refs_0_ = bf16[2,400,128]{2,1,0:T(8,128)(2,1)S(1)} collective-permute-done((bf16[2,400,128]{2,1,0:T(8,128)(2,1)S(1)}, bf16[2,400,128]{2,1,0:T(8,128)(2,1)S(1)}, u32[]{:S(2)}, u32[]{:S(2)}) %collective-permute-start.3) | collective-permute-done | bytes 204832 | tf_op jit(solution)/shard_map/ppermute | solution.py:25
  19.1 2.1 %shard_map.138 = (bf16[3,3,160,640]{3,2,1,0:T(8,128)(2,1)S(1)}, bf16[3,3,160,640]{3,2,1,0:T(8,128)(2,1)S(1)}) custom-call(bf16[3,3,160,640]{3,2,1,0:T(8,128)(2,1)} %refs_0_.4, bf16[3,3,160,640]{3,2,1,0:T(8,128)(2,1)} %refs_1_.2), custom_call_target="tpu_custom_call" | custom-call | bytes 3686400 | tf_op jit(solution)/shard_map/pallas_call | solution.py:193
  21.2 1.3 %shard_map.139.refs_1_ = f32[2,320,160]{2,1,0:T(8,128)S(1)} custom-call(bf16[2,400,128]{2,1,0:T(8,128)(2,1)S(1)} %get-tuple-element.29.refs_0_, bf16[2,400,128]{2,1,0:T(8,128)(2,1)S(1)} %collective-permute-done.5.refs_1_, bf16[3,3,160,640]{3,2,1,0:T(8,128)(2,1)S(1)} %get-tuple-element.30.refs_2_, bf16[3,3,160,640]{3,2,1,0:T(8,128)(2,1)S(1)} %get-tuple-element.31.refs_3_), custom_call_target="tpu_custom_call" | custom-call | flops 589824000 | bytes 4505600 | tf_op jit(solution)/shard_map/pallas_call | solution.py:44
  22.6 0.0 copy-start.1
  22.6 0.0 copy-start.2
  22.6 0.8 %shard_map.140.refs_1_ = f32[2,320,160]{2,1,0:T(8,128)S(1)} custom-call(bf16[2,400,128]{2,1,0:T(8,128)(2,1)S(1)} %collective-permute-done.3.refs_0_, f32[2,320,160]{2,1,0:T(8,128)S(1)} %shard_map.139.refs_1_, bf16[3,3,160,640]{3,2,1,0:T(8,128)(2,1)S(1)} %get-tuple-element.30.refs_2_, bf16[3,3,160,640]{3,2,1,0:T(8,128)(2,1)S(1)} %get-tuple-element.31.refs_3_), custom_call_target="tpu_custom_call" | custom-call | flops 294912000 | bytes 4710400 | tf_op jit(solution)/shard_map/pallas_call | solution.py:44
  23.5 1.1 %shard_map.141 = (bf16[2,320,160]{2,1,0:T(8,128)(2,1)S(1)}, bf16[2,384,128]{2,1,0:T(8,128)(2,1)S(1)}) custom-call(bf16[2,400,128]{2,1,0:T(8,128)(2,1)S(1)} %collective-permute-done.4.refs_0_, f32[2,320,160]{2,1,0:T(8,128)S(1)} %shard_map.140.refs_1_, bf16[3,3,160,640]{3,2,1,0:T(8,128)(2,1)S(1)} %get-tuple-element.30.refs_2_, ...), custom_call_target="tpu_custom_call" | custom-call | flops 294912000 | bytes 4907648 | tf_op jit(solution)/shard_map/pallas_call | solution.py:44
  24.5 1.5 %collective-permute-start.6 = (bf16[2,384,128]{2,1,0:T(8,128)(2,1)S(1)}, bf16[2,384,128]{2,1,0:T(8,128)(2,1)S(1)}, u32[]{:S(2)}, u32[]{:S(2)}) collective-permute-start(bf16[2,384,128]{2,1,0:T(8,128)(2,1)S(1)} %get-tuple-element.33.refs_0_), channel_id=1, source_target_pairs={{0,8},{8,0},{1,9},{9,1},{2,10},{10,2},{3,11},{11,3},{4,12},{12,4},... | collective-permute-start | bytes 589832 | tf_op jit(solution)/shard_map/ppermute | solution.py:25
  26.1 0.2 collective-permute-start.8
  26.3 5.6 %collective-permute-done.6.refs_0_ = bf16[2,384,128]{2,1,0:T(8,128)(2,1)S(1)} collective-permute-done((bf16[2,384,128]{2,1,0:T(8,128)(2,1)S(1)}, bf16[2,384,128]{2,1,0:T(8,128)(2,1)S(1)}, u32[]{:S(2)}, u32[]{:S(2)}) %collective-permute-start.6) | collective-permute-done | bytes 196640 | tf_op jit(solution)/shard_map/ppermute | solution.py:25
  31.9 2.1 %shard_map.142 = (bf16[3,3,160,640]{3,2,1,0:T(8,128)(2,1)S(1)}, bf16[3,3,160,640]{3,2,1,0:T(8,128)(2,1)S(1)}) custom-call(bf16[3,3,160,640]{3,2,1,0:T(8,128)(2,1)} %refs_0_.5, bf16[3,3,160,640]{3,2,1,0:T(8,128)(2,1)} %refs_1_.3), custom_call_target="tpu_custom_call" | custom-call | bytes 3686400 | tf_op jit(solution)/shard_map/pallas_call | solution.py:193
  34.0 1.4 %shard_map.143.refs_1_ = f32[2,320,160]{2,1,0:T(8,128)S(1)} custom-call(bf16[2,384,128]{2,1,0:T(8,128)(2,1)S(1)} %get-tuple-element.33.refs_0_, bf16[2,384,128]{2,1,0:T(8,128)(2,1)S(1)} %collective-permute-done.8.refs_1_, bf16[3,3,160,640]{3,2,1,0:T(8,128)(2,1)S(1)} %get-tuple-element.34.refs_2_, bf16[3,3,160,640]{3,2,1,0:T(8,128)(2,1)S(1)} %get-tuple-element.35.refs_3_), custom_call_target="tpu_custom_call" | custom-call | flops 589824000 | bytes 4489216 | tf_op jit(solution)/shard_map/pallas_call | solution.py:44
  35.3 0.0 copy-start.3
  35.3 0.0 copy-start.4
  35.4 0.8 %shard_map.144.refs_1_ = f32[2,320,160]{2,1,0:T(8,128)S(1)} custom-call(bf16[2,384,128]{2,1,0:T(8,128)(2,1)S(1)} %collective-permute-done.6.refs_0_, f32[2,320,160]{2,1,0:T(8,128)S(1)} %shard_map.143.refs_1_, bf16[3,3,160,640]{3,2,1,0:T(8,128)(2,1)S(1)} %get-tuple-element.34.refs_2_, bf16[3,3,160,640]{3,2,1,0:T(8,128)(2,1)S(1)} %get-tuple-element.35.refs_3_), custom_call_target="tpu_custom_call" | custom-call | flops 294912000 | bytes 4702208 | tf_op jit(solution)/shard_map/pallas_call | solution.py:44
  36.2 1.0 %shard_map.145 = (bf16[2,320,160]{2,1,0:T(8,128)(2,1)S(1)}, bf16[2,360,128]{2,1,0:T(8,128)(2,1)S(1)}) custom-call(bf16[2,384,128]{2,1,0:T(8,128)(2,1)S(1)} %collective-permute-done.7.refs_0_, f32[2,320,160]{2,1,0:T(8,128)S(1)} %shard_map.144.refs_1_, bf16[3,3,160,640]{3,2,1,0:T(8,128)(2,1)S(1)} %get-tuple-element.34.refs_2_, ...), custom_call_target="tpu_custom_call" | custom-call | flops 294912000 | bytes 4887168 | tf_op jit(solution)/shard_map/pallas_call | solution.py:44
  37.3 1.5 %collective-permute-start.9 = (bf16[2,360,128]{2,1,0:T(8,128)(2,1)S(1)}, bf16[2,360,128]{2,1,0:T(8,128)(2,1)S(1)}, u32[]{:S(2)}, u32[]{:S(2)}) collective-permute-start(bf16[2,360,128]{2,1,0:T(8,128)(2,1)S(1)} %get-tuple-element.37.refs_0_), channel_id=1, source_target_pairs={{0,8},{8,0},{1,9},{9,1},{2,10},{10,2},{3,11},{11,3},{4,12},{12,4},... | collective-permute-start | bytes 552968 | tf_op jit(solution)/shard_map/ppermute | solution.py:25
  38.8 0.2 collective-permute-start.11
  39.0 5.3 %collective-permute-done.9.refs_0_.refs_2_ = bf16[2,360,128]{2,1,0:T(8,128)(2,1)S(1)} collective-permute-done((bf16[2,360,128]{2,1,0:T(8,128)(2,1)S(1)}, bf16[2,360,128]{2,1,0:T(8,128)(2,1)S(1)}, u32[]{:S(2)}, u32[]{:S(2)}) %collective-permute-start.9) | collective-permute-done | bytes 184352 | tf_op jit(solution)/shard_map/ppermute | solution.py:25
  44.4 2.1 %shard_map.146.refs_2_ = bf16[3,3,160,1280]{3,2,1,0:T(8,128)(2,1)S(1)} custom-call(bf16[3,3,160,1280]{3,2,1,0:T(8,128)(2,1)} %refs_0_.6), custom_call_target="tpu_custom_call" | custom-call | bytes 3686400 | tf_op jit(solution)/shard_map/pallas_call | solution.py:193
  46.4 1.3 %shard_map.147.refs_1_ = f32[320,160]{1,0:T(8,128)S(1)} custom-call(bf16[2,360,128]{2,1,0:T(8,128)(2,1)S(1)} %get-tuple-element.37.refs_0_, bf16[2,360,128]{2,1,0:T(8,128)(2,1)S(1)} %collective-permute-done.11.refs_1_, bf16[3,3,160,1280]{3,2,1,0:T(8,128)(2,1)S(1)} %shard_map.146.refs_2_), custom_call_target="tpu_custom_call" | custom-call | flops 589824000 | bytes 4259840 | tf_op jit(solution)/shard_map/pallas_call | solution.py:44
  47.8 0.0 copy-start.5
  47.8 0.8 %shard_map.148.refs_1_ = f32[320,160]{1,0:T(8,128)S(1)} custom-call(bf16[2,360,128]{2,1,0:T(8,128)(2,1)S(1)} %collective-permute-done.9.refs_0_.refs_2_, f32[320,160]{1,0:T(8,128)S(1)} %shard_map.147.refs_1_, bf16[3,3,160,1280]{3,2,1,0:T(8,128)(2,1)S(1)} %shard_map.146.refs_2_), custom_call_target="tpu_custom_call" | custom-call | flops 294912000 | bytes 4280320 | tf_op jit(solution)/shard_map/pallas_call | solution.py:44
  48.6 1.0 %shard_map.149 = (bf16[320,160]{1,0:T(8,128)(2,1)S(1)}, bf16[344,128]{1,0:T(8,128)(2,1)S(1)}) custom-call(bf16[2,360,128]{2,1,0:T(8,128)(2,1)S(1)} %collective-permute-done.10.refs_0_.refs_3_, f32[320,160]{1,0:T(8,128)S(1)} %shard_map.148.refs_1_, bf16[3,3,160,1280]{3,2,1,0:T(8,128)(2,1)S(1)} %shard_map.146.refs_2_, ...), custom_call_target="tpu_custom_call" | custom-call | flops 294912000 | bytes 4471104 | tf_op jit(solution)/shard_map/pallas_call | solution.py:44
  49.6 1.5 %collective-permute-start.12 = (bf16[344,128]{1,0:T(8,128)(2,1)S(1)}, bf16[344,128]{1,0:T(8,128)(2,1)S(1)}, u32[]{:S(2)}, u32[]{:S(2)}) collective-permute-start(bf16[344,128]{1,0:T(8,128)(2,1)S(1)} %get-tuple-element.39.refs_0_), channel_id=1, source_target_pairs={{0,8},{8,0},{1,9},{9,1},{2,10},{10,2},{3,11},{11,3},{4,12},{12,4},... | collective-permute-start | bytes 264200 | tf_op jit(solution)/shard_map/ppermute | solution.py:25
  51.2 0.2 collective-permute-start.14
  51.4 2.1 %shard_map.150.refs_4_.refs_3_.refs_2_ = bf16[3,3,160,1280]{3,2,1,0:T(8,128)(2,1)S(1)} custom-call(bf16[3,3,160,1280]{3,2,1,0:T(8,128)(2,1)} %refs_0_.7), custom_call_target="tpu_custom_call" | custom-call | bytes 3686400 | tf_op jit(solution)/shard_map/pallas_call | solution.py:193
  53.4 1.2 %collective-permute-done.12.refs_0_ = bf16[344,128]{1,0:T(8,128)(2,1)S(1)} collective-permute-done((bf16[344,128]{1,0:T(8,128)(2,1)S(1)}, bf16[344,128]{1,0:T(8,128)(2,1)S(1)}, u32[]{:S(2)}, u32[]{:S(2)}) %collective-permute-start.12) | collective-permute-done | bytes 88096 | tf_op jit(solution)/shard_map/ppermute | solution.py:25
  54.7 1.3 %shard_map.151.refs_2_ = f32[320,160]{1,0:T(8,128)S(1)} custom-call(bf16[2,360,128]{2,1,0:T(8,128)(2,1)S(1)} %get-tuple-element.37.refs_0_, bf16[2,360,128]{2,1,0:T(8,128)(2,1)S(1)} %collective-permute-done.11.refs_1_, bf16[2,360,128]{2,1,0:T(8,128)(2,1)S(1)} %collective-permute-done.9.refs_0_.refs_2_, ...), custom_call_target="tpu_custom_call" | custom-call | flops 589824000 | bytes 4628480 | tf_op jit(solution)/shard_map/pallas_call | solution.py:44
  56.0 0.8 %shard_map.152.refs_1_ = f32[320,160]{1,0:T(8,128)S(1)} custom-call(bf16[344,128]{1,0:T(8,128)(2,1)S(1)} %get-tuple-element.39.refs_0_, bf16[344,128]{1,0:T(8,128)(2,1)S(1)} %collective-permute-done.14.refs_1_, f32[320,160]{1,0:T(8,128)S(1)} %shard_map.151.refs_2_, bf16[3,3,160,1280]{3,2,1,0:T(8,128)(2,1)S(1)} %shard_map.150.refs_4_.refs_3_.refs_2_), custom_call_target="tpu_custom_call" | custom-call | flops 294912000 | bytes 4272128 | tf_op jit(solution)/shard_map/pallas_call | solution.py:44
  56.8 0.0 copy-start
  56.8 0.5 shard_map.153.refs_1_
  57.4 0.1 copy-done
  57.5 0.6 shard_map.154
  58.1 0.1 collective-permute-start.15
  58.2 1.4 %collective-permute-start.16 = (bf16[80,128]{1,0:T(8,128)(2,1)S(1)}, bf16[80,128]{1,0:T(8,128)(2,1)S(1)}, u32[]{:S(2)}, u32[]{:S(2)}) collective-permute-start(bf16[80,128]{1,0:T(8,128)(2,1)S(1)} %get-tuple-element.43), channel_id=1, source_target_pairs={{0,4},{2,6},{4,0},{6,2},{1,5},{3,7},{5,1},{7,3},{8,12},{10,14},{12... | collective-permute-start | bytes 61448 | tf_op jit(solution)/shard_map/ppermute | solution.py:25
  59.6 3.0 %collective-permute-start.17 = (bf16[80,128]{1,0:T(8,128)(2,1)S(1)}, bf16[80,128]{1,0:T(8,128)(2,1)S(1)}, u32[]{:S(2)}, u32[]{:S(2)}) collective-permute-start(bf16[80,128]{1,0:T(8,128)(2,1)S(1)} %get-tuple-element.44), channel_id=1, source_target_pairs={{0,6},{2,4},{4,2},{6,0},{1,7},{3,5},{5,3},{7,1},{8,14},{10,12},{12... | collective-permute-start | bytes 61448 | tf_op jit(solution)/shard_map/ppermute | solution.py:25
  62.6 0.5 collective-permute-done.16.refs_2_
  63.1 2.1 %collective-permute-done.17.refs_3_ = bf16[80,128]{1,0:T(8,128)(2,1)S(1)} collective-permute-done((bf16[80,128]{1,0:T(8,128)(2,1)S(1)}, bf16[80,128]{1,0:T(8,128)(2,1)S(1)}, u32[]{:S(2)}, u32[]{:S(2)}) %collective-permute-start.17) | collective-permute-done | bytes 20512 | tf_op jit(solution)/shard_map/ppermute | solution.py:25
  65.2 0.8 %shard_map.155 = bf16[2,160,128]{2,1,0:T(8,128)(2,1)} custom-call(bf16[80,128]{1,0:T(8,128)(2,1)S(1)} %get-tuple-element.41.refs_0_, bf16[80,128]{1,0:T(8,128)(2,1)S(1)} %collective-permute-done.15.refs_1_, bf16[80,128]{1,0:T(8,128)(2,1)S(1)} %collective-permute-done.16.refs_2_, bf16[80,128]{1,0:T(8,128)(2,1)S(1)} %collective-permute-done.17.refs_3_), custom_call_target="tpu_custom_call" | custom-call | bytes 163840 | tf_op jit(solution)/shard_map/pallas_call | solution.py:44
  (20 shorter events, 0.1 us)
Async XLA Ops:
  1.2 5.7 %collective-permute-start = (bf16[200,128]{1,0:T(8,128)(2,1)S(1)}, bf16[200,128]{1,0:T(8,128)(2,1)S(1)}, u32[]{:S(2)}, u32[]{:S(2)}) collective-permute-start(bf16[200,128]{1,0:T(8,128)(2,1)S(1)} %get-tuple-element.26), channel_id=1, source_target_pairs={{0,2},{2,0},{4,6},{6,4},{1,3},{3,1},{5,7},{7,5},{8,10},{10,8},{12,... | collective-permute-start | bytes 153608 | tf_op jit(solution)/shard_map/ppermute | solution.py:25
  4.3 6.0 %collective-permute-start.1 = (bf16[200,128]{1,0:T(8,128)(2,1)S(1)}, bf16[200,128]{1,0:T(8,128)(2,1)S(1)}, u32[]{:S(2)}, u32[]{:S(2)}) collective-permute-start(bf16[200,128]{1,0:T(8,128)(2,1)S(1)} %get-tuple-element.27), channel_id=1, source_target_pairs={{0,4},{2,6},{4,0},{6,2},{1,5},{3,7},{5,1},{7,3},{8,12},{10,14},{12... | collective-permute-start | bytes 153608 | tf_op jit(solution)/shard_map/ppermute | solution.py:25
  6.9 5.9 %collective-permute-start.2 = (bf16[200,128]{1,0:T(8,128)(2,1)S(1)}, bf16[200,128]{1,0:T(8,128)(2,1)S(1)}, u32[]{:S(2)}, u32[]{:S(2)}) collective-permute-start(bf16[200,128]{1,0:T(8,128)(2,1)S(1)} %get-tuple-element.28), channel_id=1, source_target_pairs={{0,6},{2,4},{4,2},{6,0},{1,7},{3,5},{5,3},{7,1},{8,14},{10,12},{12... | collective-permute-start | bytes 153608 | tf_op jit(solution)/shard_map/ppermute | solution.py:25
  13.3 5.8 %collective-permute-start.3 = (bf16[2,400,128]{2,1,0:T(8,128)(2,1)S(1)}, bf16[2,400,128]{2,1,0:T(8,128)(2,1)S(1)}, u32[]{:S(2)}, u32[]{:S(2)}) collective-permute-start(bf16[2,400,128]{2,1,0:T(8,128)(2,1)S(1)} %get-tuple-element.29.refs_0_), channel_id=1, source_target_pairs={{0,8},{8,0},{1,9},{9,1},{2,10},{10,2},{3,11},{11,3},{4,12},{12,4},... | collective-permute-start | bytes 614408 | tf_op jit(solution)/shard_map/ppermute | solution.py:25
  14.9 6.4 %collective-permute-start.5 = (bf16[2,400,128]{2,1,0:T(8,128)(2,1)S(1)}, bf16[2,400,128]{2,1,0:T(8,128)(2,1)S(1)}, u32[]{:S(2)}, u32[]{:S(2)}) collective-permute-start(bf16[2,400,128]{2,1,0:T(8,128)(2,1)S(1)} %get-tuple-element.29.refs_0_), channel_id=1, source_target_pairs={{0,1},{1,0},{2,3},{3,2},{4,5},{5,4},{6,7},{7,6},{8,9},{9,8},{10,11... | collective-permute-start | bytes 614408 | tf_op jit(solution)/shard_map/ppermute | solution.py:25
  19.1 4.3 %collective-permute-start.4 = (bf16[2,400,128]{2,1,0:T(8,128)(2,1)S(1)}, bf16[2,400,128]{2,1,0:T(8,128)(2,1)S(1)}, u32[]{:S(2)}, u32[]{:S(2)}) collective-permute-start(bf16[2,400,128]{2,1,0:T(8,128)(2,1)S(1)} %collective-permute-done.3.refs_0_), channel_id=1, source_target_pairs={{0,1},{1,0},{2,3},{3,2},{4,5},{5,4},{6,7},{7,6},{8,9},{9,8},{10,11... | collective-permute-start | bytes 614408 | tf_op jit(solution)/shard_map/ppermute | solution.py:25
  22.6 0.9 %copy-start.1 = (bf16[160]{0:T(256)(128)(2,1)S(1)}, bf16[160]{0:T(256)(128)(2,1)}, u32[]{:S(2)}) copy-start(bf16[160]{0:T(256)(128)(2,1)} %refs_5_.2) | copy-start | bytes 964
  22.6 0.9 %copy-start.2 = (bf16[160]{0:T(256)(128)(2,1)S(1)}, bf16[160]{0:T(256)(128)(2,1)}, u32[]{:S(2)}) copy-start(bf16[160]{0:T(256)(128)(2,1)} %refs_6_.2) | copy-start | bytes 964
  24.5 7.4 %collective-permute-start.6 = (bf16[2,384,128]{2,1,0:T(8,128)(2,1)S(1)}, bf16[2,384,128]{2,1,0:T(8,128)(2,1)S(1)}, u32[]{:S(2)}, u32[]{:S(2)}) collective-permute-start(bf16[2,384,128]{2,1,0:T(8,128)(2,1)S(1)} %get-tuple-element.33.refs_0_), channel_id=1, source_target_pairs={{0,8},{8,0},{1,9},{9,1},{2,10},{10,2},{3,11},{11,3},{4,12},{12,4},... | collective-permute-start | bytes 589832 | tf_op jit(solution)/shard_map/ppermute | solution.py:25
  26.1 7.9 %collective-permute-start.8 = (bf16[2,384,128]{2,1,0:T(8,128)(2,1)S(1)}, bf16[2,384,128]{2,1,0:T(8,128)(2,1)S(1)}, u32[]{:S(2)}, u32[]{:S(2)}) collective-permute-start(bf16[2,384,128]{2,1,0:T(8,128)(2,1)S(1)} %get-tuple-element.33.refs_0_), channel_id=1, source_target_pairs={{0,1},{1,0},{2,3},{3,2},{4,5},{5,4},{6,7},{7,6},{8,9},{9,8},{10,11... | collective-permute-start | bytes 589832 | tf_op jit(solution)/shard_map/ppermute | solution.py:25
  31.9 4.3 %collective-permute-start.7 = (bf16[2,384,128]{2,1,0:T(8,128)(2,1)S(1)}, bf16[2,384,128]{2,1,0:T(8,128)(2,1)S(1)}, u32[]{:S(2)}, u32[]{:S(2)}) collective-permute-start(bf16[2,384,128]{2,1,0:T(8,128)(2,1)S(1)} %collective-permute-done.6.refs_0_), channel_id=1, source_target_pairs={{0,1},{1,0},{2,3},{3,2},{4,5},{5,4},{6,7},{7,6},{8,9},{9,8},{10,11... | collective-permute-start | bytes 589832 | tf_op jit(solution)/shard_map/ppermute | solution.py:25
  35.3 0.9 %copy-start.3 = (bf16[160]{0:T(256)(128)(2,1)S(1)}, bf16[160]{0:T(256)(128)(2,1)}, u32[]{:S(2)}) copy-start(bf16[160]{0:T(256)(128)(2,1)} %refs_5_.3) | copy-start | bytes 964
  35.3 0.9 %copy-start.4 = (bf16[160]{0:T(256)(128)(2,1)S(1)}, bf16[160]{0:T(256)(128)(2,1)}, u32[]{:S(2)}) copy-start(bf16[160]{0:T(256)(128)(2,1)} %refs_6_.3) | copy-start | bytes 964
  37.3 7.1 %collective-permute-start.9 = (bf16[2,360,128]{2,1,0:T(8,128)(2,1)S(1)}, bf16[2,360,128]{2,1,0:T(8,128)(2,1)S(1)}, u32[]{:S(2)}, u32[]{:S(2)}) collective-permute-start(bf16[2,360,128]{2,1,0:T(8,128)(2,1)S(1)} %get-tuple-element.37.refs_0_), channel_id=1, source_target_pairs={{0,8},{8,0},{1,9},{9,1},{2,10},{10,2},{3,11},{11,3},{4,12},{12,4},... | collective-permute-start | bytes 552968 | tf_op jit(solution)/shard_map/ppermute | solution.py:25
  38.8 7.6 %collective-permute-start.11 = (bf16[2,360,128]{2,1,0:T(8,128)(2,1)S(1)}, bf16[2,360,128]{2,1,0:T(8,128)(2,1)S(1)}, u32[]{:S(2)}, u32[]{:S(2)}) collective-permute-start(bf16[2,360,128]{2,1,0:T(8,128)(2,1)S(1)} %get-tuple-element.37.refs_0_), channel_id=1, source_target_pairs={{0,1},{1,0},{2,3},{3,2},{4,5},{5,4},{6,7},{7,6},{8,9},{9,8},{10,11... | collective-permute-start | bytes 552968 | tf_op jit(solution)/shard_map/ppermute | solution.py:25
  44.4 4.2 %collective-permute-start.10 = (bf16[2,360,128]{2,1,0:T(8,128)(2,1)S(1)}, bf16[2,360,128]{2,1,0:T(8,128)(2,1)S(1)}, u32[]{:S(2)}, u32[]{:S(2)}) collective-permute-start(bf16[2,360,128]{2,1,0:T(8,128)(2,1)S(1)} %collective-permute-done.9.refs_0_.refs_2_), channel_id=1, source_target_pairs={{0,1},{1,0},{2,3},{3,2},{4,5},{5,4},{6,7},{7,6},{8,9},{9,8},{10,11... | collective-permute-start | bytes 552968 | tf_op jit(solution)/shard_map/ppermute | solution.py:25
  47.8 0.8 %copy-start.5 = (bf16[160]{0:T(256)(128)(2,1)S(1)}, bf16[160]{0:T(256)(128)(2,1)}, u32[]{:S(2)}) copy-start(bf16[160]{0:T(256)(128)(2,1)} %refs_4_.2) | copy-start | bytes 964
  49.6 5.0 %collective-permute-start.12 = (bf16[344,128]{1,0:T(8,128)(2,1)S(1)}, bf16[344,128]{1,0:T(8,128)(2,1)S(1)}, u32[]{:S(2)}, u32[]{:S(2)}) collective-permute-start(bf16[344,128]{1,0:T(8,128)(2,1)S(1)} %get-tuple-element.39.refs_0_), channel_id=1, source_target_pairs={{0,8},{8,0},{1,9},{9,1},{2,10},{10,2},{3,11},{11,3},{4,12},{12,4},... | collective-permute-start | bytes 264200 | tf_op jit(solution)/shard_map/ppermute | solution.py:25
  51.2 4.9 %collective-permute-start.14 = (bf16[344,128]{1,0:T(8,128)(2,1)S(1)}, bf16[344,128]{1,0:T(8,128)(2,1)S(1)}, u32[]{:S(2)}, u32[]{:S(2)}) collective-permute-start(bf16[344,128]{1,0:T(8,128)(2,1)S(1)} %get-tuple-element.39.refs_0_), channel_id=1, source_target_pairs={{0,1},{1,0},{2,3},{3,2},{4,5},{5,4},{6,7},{7,6},{8,9},{9,8},{10,11... | collective-permute-start | bytes 264200 | tf_op jit(solution)/shard_map/ppermute | solution.py:25
  54.7 2.7 %collective-permute-start.13 = (bf16[344,128]{1,0:T(8,128)(2,1)S(1)}, bf16[344,128]{1,0:T(8,128)(2,1)S(1)}, u32[]{:S(2)}, u32[]{:S(2)}) collective-permute-start(bf16[344,128]{1,0:T(8,128)(2,1)S(1)} %collective-permute-done.12.refs_0_), channel_id=1, source_target_pairs={{0,1},{1,0},{2,3},{3,2},{4,5},{5,4},{6,7},{7,6},{8,9},{9,8},{10,11... | collective-permute-start | bytes 264200 | tf_op jit(solution)/shard_map/ppermute | solution.py:25
  56.8 0.7 copy-start
  58.1 4.5 %collective-permute-start.15 = (bf16[80,128]{1,0:T(8,128)(2,1)S(1)}, bf16[80,128]{1,0:T(8,128)(2,1)S(1)}, u32[]{:S(2)}, u32[]{:S(2)}) collective-permute-start(bf16[80,128]{1,0:T(8,128)(2,1)S(1)} %get-tuple-element.42), channel_id=1, source_target_pairs={{0,2},{2,0},{4,6},{6,4},{1,3},{3,1},{5,7},{7,5},{8,10},{10,8},{12,... | collective-permute-start | bytes 61448 | tf_op jit(solution)/shard_map/ppermute | solution.py:25
  58.2 4.9 %collective-permute-start.16 = (bf16[80,128]{1,0:T(8,128)(2,1)S(1)}, bf16[80,128]{1,0:T(8,128)(2,1)S(1)}, u32[]{:S(2)}, u32[]{:S(2)}) collective-permute-start(bf16[80,128]{1,0:T(8,128)(2,1)S(1)} %get-tuple-element.43), channel_id=1, source_target_pairs={{0,4},{2,6},{4,0},{6,2},{1,5},{3,7},{5,1},{7,3},{8,12},{10,14},{12... | collective-permute-start | bytes 61448 | tf_op jit(solution)/shard_map/ppermute | solution.py:25
  59.6 5.6 %collective-permute-start.17 = (bf16[80,128]{1,0:T(8,128)(2,1)S(1)}, bf16[80,128]{1,0:T(8,128)(2,1)S(1)}, u32[]{:S(2)}, u32[]{:S(2)}) collective-permute-start(bf16[80,128]{1,0:T(8,128)(2,1)S(1)} %get-tuple-element.44), channel_id=1, source_target_pairs={{0,6},{2,4},{4,2},{6,0},{1,7},{3,5},{5,3},{7,1},{8,14},{10,12},{12... | collective-permute-start | bytes 61448 | tf_op jit(solution)/shard_map/ppermute | solution.py:25

commit v9 on v8

--- a/solution.py
+++ b/solution.py
@@ -208,7 +208,8 @@
 
 
 def join_kernel(z, *refs):
-    blocks, (state_ref, act_ref, image, block_image) = refs[:-4], refs[-4:]
+    blocks, (*states, act_zero, act_one, image, block_image) = refs[: z.bands], refs[z.bands :]
+    acts = (act_zero, act_one)
     band = lax.axis_index("band")
     size = z.rows * z.wide
 
@@ -228,8 +229,8 @@
     for t in range(2):
         parts = [image[t, g][:, :n] for g, (_, n) in enumerate(lane_groups(z))]
         value = jnp.concatenate(parts, axis=1)
-        state_ref[t] = value.astype(BF16)
-        pack(z, act_ref.at[t], masked_silu(z, value), roll=True)
+        states[t][...] = value.astype(BF16)
+        pack(z, acts[t], masked_silu(z, value), roll=True)
 
 
 def place(z, trim, a_ref, at, message, distance):
@@ -345,65 +346,28 @@
     return ref[...].astype(F32).reshape(1, -1)
 
 
-def pair_kernel(z, trim, distances, add, end, *refs):
-    n = len(distances)
-    blocks, refs = refs[:n], refs[n:]
-    sums, refs = refs[:add], refs[add:]
-    w0, w1, *refs = refs
-    if end:
-        state_ref, b0, b1, new_ref, act_ref, a_ref = refs
-    else:
-        out_ref, a_ref = refs
-    for t, w_ref in enumerate((w0, w1)):
-        sources = [(0, [block[t] for block in blocks])]
-        total = accumulate(z, trim, distances, sources, w_ref, a_ref.at[t])
-        for other in sums:
-            total = total + other[t]
-        if end:
-            bias = bias_of((b0, b1)[t])
-            finish(z, trim + 1, state_ref[t], total, bias, new_ref.at[t], act_ref.at[t])
-        else:
-            out_ref[t] = total
-
-
-def decode_kernel(z, trim, distances, add, end, *refs):
+def block_kernel(z, trim, base, distances, add, end, *refs):
     n = len(distances)
     blocks, refs = refs[:n], refs[n:]
     sums, refs = refs[:add], refs[add:]
     w_ref, *refs = refs
     a_ref = refs.pop()
-    sources = [(0, [block[1] for block in blocks]), (z.depth, [block[0] for block in blocks])]
+    sources = [(base, [block[...] for block in blocks])]
     total = accumulate(z, trim, distances, sources, w_ref, a_ref)
     for other in sums:
         total = total + other[...]
     if end:
-        state_ref, b_ref, new_ref, act_ref = refs
-        finish(z, trim + 1, state_ref[1], total, bias_of(b_ref), new_ref, act_ref)
+        end(z, trim, total, *refs)
     else:
         refs[0][...] = total
 
 
-def skip_kernel(z, trim, *refs):
-    blocks, (w_ref, out_ref, a_ref) = refs[: z.shards], refs[z.shards :]
-    sources = [(z.depth, [block[0] for block in blocks])]
-    out_ref[...] = accumulate(z, trim, range(z.shards), sources, w_ref, a_ref)
-
-
-def last_kernel(z, trim, distances, add, end, *refs):
-    n = len(distances)
-    blocks, refs = refs[:n], refs[n:]
-    sums, refs = refs[:add], refs[add:]
-    w_ref, *refs = refs
-    a_ref = refs.pop()
-    sources = [(0, [block[...] for block in blocks])]
-    total = accumulate(z, trim, distances, sources, w_ref, a_ref)
-    for other in sums:
-        total = total + other[...]
-    if not end:
-        refs[0][...] = total
-        return
-    image = refs.pop()
-    state_ref, b_ref, *outs = refs
+def close_layer(z, trim, total, state_ref, b_ref, new_ref, act_ref):
+    finish(z, trim + 1, state_ref[...], total, bias_of(b_ref), new_ref, act_ref)
+
+
+def close_image(z, trim, total, *refs):
+    state_ref, b_ref, *outs, image = refs
     total = state_ref[...].astype(F32) + total + bias_of(b_ref)
     groups = lane_groups(z)
     for g, (lane, n) in enumerate(groups):
@@ -471,9 +435,7 @@
     kernel = lambda f, *a: functools.partial(f, z, *a)
     groups = len(lane_groups(z))
     single = sds((z.cells, z.per))
-    pair = sds((2, z.cells, z.per))
     total = sds((z.cells, z.per), F32)
-    totals = sds((2, z.cells, z.per), F32)
     message = lambda trim: z.packed(z.kept(trim))
 
     raw = (z.rows, z.per, z.width)
@@ -490,13 +452,10 @@
         compiler_params=pltpu.CompilerParams(vmem_limit_bytes=4 << 20),
     )(in_hbm(latent.swapaxes(1, 2)), in_hbm(control_hint.swapaxes(1, 2)))
     blocks = over_bands(blocks)
-    cw1, mw1 = load(cw1, mw1)
-    cw2, mw2 = load(cw2, mw2)
-    (dw1,) = load(dw1)
-    (dw2,) = load(dw2)
-    state, act = call(
+    cw1, mw1, cw2, mw2 = load(cw1, mw1, cw2, mw2)
+    *states, control, main = call(
         kernel(join_kernel),
-        [pair, sds((2,) + message(0))],
+        [single, single, sds(message(0)), sds(message(0))],
         *blocks,
         scratch=[
             pltpu.VMEM((2, groups, z.cells, LANES), F32),
@@ -504,51 +463,49 @@
         ],
     )
 
-    def layer(step, body, received, weights, rest, partial_out, outs, sums=(), extra=(), wide=1):
+    def convolution(step, received, w, base, outs, end=None, rest=(), sums=(), extra=()):
         received = [(names, pieces) for names, pieces in received if names]
         for at, (names, pieces) in enumerate(received):
-            end = at == len(received) - 1
-            shape = (z.held, len(names) * z.span * wide)
-            if len(weights) > 1:
-                shape = (len(weights),) + shape
+            ends = at == len(received) - 1
             result = call(
-                kernel(body, step, names, len(sums), end),
-                outs if end else partial_out,
+                kernel(block_kernel, step, base, names, len(sums), end if ends else None),
+                outs if ends else total,
                 *pieces,
                 *sums,
-                *weights,
-                *(rest if end else ()),
-                scratch=(list(extra) if end else []) + [pltpu.VMEM(shape, BF16)],
-                flops=2 * 9 * z.cells * z.per * z.per * len(names) * len(weights) * wide,
+                w,
+                *(rest if ends else ()),
+                scratch=(list(extra) if ends else [])
+                + [pltpu.VMEM((z.held, len(names) * z.span), BF16)],
+                flops=2 * 9 * z.cells * z.per * z.per * len(names),
             )
             sums = (result,)
         return result
 
     for step, (cw, cb, mw, mb) in enumerate(((cw1, cb1, mw1, mb1), (cw2, cb2, mw2, mb2))):
-        received = gather(act)
-        outs = [pair, sds((2,) + message(step + 1))]
-        rest = (state, cb, mb)
-        state, act = layer(step, pair_kernel, received, (cw, mw), rest, totals, outs)
-    received = gather(act)
-    skips = {d: p for names, pieces in received for d, p in zip(names, pieces)}
+        outs = [single, sds(message(step + 1))]
+        received = gather(control)
+        rest = (states[0], cb)
+        states[0], control = convolution(step, received, cw, 0, outs, close_layer, rest)
+        received = gather(main)
+        rest = (states[1], mb)
+        states[1], main = convolution(step, received, mw, 0, outs, close_layer, rest)
+    skip = gather(control)
+    near, *others = skip
+    merged = tuple(sum((list(part) for part in parts), []) for parts in zip(*others))
+    first = convolution(2, [near, merged], dw1, z.depth, total)
     outs = [single, sds(message(3))]
-    state, act = layer(2, decode_kernel, received, (dw1,), (state, db1), total, outs, wide=2)
-    part = call(
-        kernel(skip_kernel, 2),
-        total,
-        *[skips[d] for d in range(z.shards)],
+    rest = (states[1], db1)
+    state, act = convolution(2, gather(main), dw1, 0, outs, close_layer, rest, sums=(first,))
+    every = tuple(sum((list(part) for part in parts), []) for parts in zip(*skip))
+    part = convolution(2, [every], dw2, z.depth, total)
+    blocks = convolution(
+        3,
+        gather(act),
         dw2,
-        scratch=[pltpu.VMEM((z.held, z.shards * z.span), BF16)],
-        flops=2 * 9 * z.cells * z.per * z.depth,
-    )
-    blocks = layer(
-        3,
-        last_kernel,
-        gather(act),
-        (dw2,),
+        0,
+        [sds(z.packed(z.rows * z.columns))] * z.bands,
+        close_image,
         (state, db2),
-        total,
-        [sds(z.packed(z.rows * z.columns))] * z.bands,
         sums=(part,),
         extra=[pltpu.VMEM((groups, z.cells, LANES), F32)],
     )

time: 66.3 us -> 64.5 us (0.973)
  waiting for transfers between devices: 24.9 us -> 22.4 us
  starting transfers between devices: 17 us -> 19.4 us
  Pallas kernels: 23.7 us -> 21.7 us
    pallas_call x4 -> x1, Pallas kernels: 8.25 us -> 3.2 us  [load(): pl.pallas_call(functools.partial(load_kernel, count), out_shape=[sds(w.sh...]
    pallas_call x15 -> x23, Pallas kernels: 14.2 us -> 17.3 us  [call(): pl.pallas_call(kernel, out_shape=outs, in_specs=whole(len(args)), out_spe...]
    ppermute x18 -> x27, waiting for transfers between devices: 24.9 us -> 22.4 us  [exchange(): return lax.ppermute(cells, axis, [(i, i ^ distance) for i in range(count)])]
    ppermute x18 -> x27, starting transfers between devices: 17 us -> 19.4 us  [exchange(): return lax.ppermute(cells, axis, [(i, i ^ distance) for i in range(count)])]
  transfers between devices with their start and end apart: 18 -> 27, of which waited for: 8 -> 11; matrix products, arithmetic and copies ran while one was open for 0% -> 0% of each run, Pallas kernels for 26% -> 28%
where the time goes in v9:
time: 64.5 us; the launch traced here: 64.3 us
  waiting for transfers between devices  22.4 us (35%)
  Pallas kernels  21.7 us (34%)
  starting transfers between devices  19.4 us (30%)
    ppermute x27, waiting for transfers between devices, exchange(): return lax.ppermute(cells, axis, [(i, i ^ distance) for i in range(count)])  22.4 us
    ppermute x27, starting transfers between devices, exchange(): return lax.ppermute(cells, axis, [(i, i ^ distance) for i in range(count)])  19.4 us
    pallas_call x23, Pallas kernels, call(): pl.pallas_call(kernel, out_shape=outs, in_specs=whole(len(args)), out_spe...  17.3 us
    pallas_call x1, Pallas kernels, load(): pl.pallas_call(functools.partial(load_kernel, count), out_shape=[sds(w.sh...  3.2 us
  transfers between devices with their start and end apart: 27, of which 11 were waited for; matrix products, arithmetic and copies ran while one was open for 0% of the time, Pallas kernels for 28%

profile of v9, /device:TPU:0, one launch (start us, length us, event | category | flops | bytes accessed | tf_op | source)
XLA Modules:
  0.0 64.3 jit_solution(11829046652844083889)
XLA Ops:
  0.0 1.2 %shard_map.136 = (bf16[200,128]{1,0:T(8,128)(2,1)S(1)}, bf16[200,128]{1,0:T(8,128)(2,1)S(1)}, bf16[200,128]{1,0:T(8,128)(2,1)S(1)}, bf16[200,128]{1,0:T(8,128)(2,1)S(1)}) custom-call(bf16[2,160,128]{2,1,0:T(8,128)(2,1)} %bitcast.3, bf16[2,160,128]{2,1,0:T(8,128)(2,1)} %bitcast.4), custom_call_target="tpu_custom_call" | custom-call | tf_op jit(solution)/shard_map/pallas_call | solution.py:442
  1.2 3.1 %collective-permute-start = (bf16[200,128]{1,0:T(8,128)(2,1)S(1)}, bf16[200,128]{1,0:T(8,128)(2,1)S(1)}, u32[]{:S(2)}, u32[]{:S(2)}) collective-permute-start(bf16[200,128]{1,0:T(8,128)(2,1)S(1)} %get-tuple-element.31), channel_id=1, source_target_pairs={{0,2},{2,0},{4,6},{6,4},{1,3},{3,1},{5,7},{7,5},{8,10},{10,8},{12,... | collective-permute-start | bytes 153608 | tf_op jit(solution)/shard_map/ppermute | solution.py:25
  4.3 2.6 %collective-permute-start.1 = (bf16[200,128]{1,0:T(8,128)(2,1)S(1)}, bf16[200,128]{1,0:T(8,128)(2,1)S(1)}, u32[]{:S(2)}, u32[]{:S(2)}) collective-permute-start(bf16[200,128]{1,0:T(8,128)(2,1)S(1)} %get-tuple-element.32), channel_id=1, source_target_pairs={{0,4},{2,6},{4,0},{6,2},{1,5},{3,7},{5,1},{7,3},{8,12},{10,14},{12... | collective-permute-start | bytes 153608 | tf_op jit(solution)/shard_map/ppermute | solution.py:25
  6.9 3.4 %collective-permute-done.1.refs_2_ = bf16[200,128]{1,0:T(8,128)(2,1)S(1)} collective-permute-done((bf16[200,128]{1,0:T(8,128)(2,1)S(1)}, bf16[200,128]{1,0:T(8,128)(2,1)S(1)}, u32[]{:S(2)}, u32[]{:S(2)}) %collective-permute-start.1) | collective-permute-done | bytes 51232 | tf_op jit(solution)/shard_map/ppermute | solution.py:25
  10.3 2.5 %collective-permute-done.2.refs_3_ = bf16[200,128]{1,0:T(8,128)(2,1)S(1)} collective-permute-done((bf16[200,128]{1,0:T(8,128)(2,1)S(1)}, bf16[200,128]{1,0:T(8,128)(2,1)S(1)}, u32[]{:S(2)}, u32[]{:S(2)}) %collective-permute-start.2) | collective-permute-done | bytes 51232 | tf_op jit(solution)/shard_map/ppermute | solution.py:25
  13.3 1.5 %collective-permute-start.12 = (bf16[400,128]{1,0:T(8,128)(2,1)S(1)}, bf16[400,128]{1,0:T(8,128)(2,1)S(1)}, u32[]{:S(2)}, u32[]{:S(2)}) collective-permute-start(bf16[400,128]{1,0:T(8,128)(2,1)S(1)} %get-tuple-element.41.refs_0_), channel_id=1, source_target_pairs={{0,8},{8,0},{1,9},{9,1},{2,10},{10,2},{3,11},{11,3},{4,12},{12,4},... | collective-permute-start | bytes 307208 | tf_op jit(solution)/shard_map/ppermute | solution.py:25
  14.9 0.5 collective-permute-start.3
  15.4 2.6 %collective-permute-done.12.refs_0_ = bf16[400,128]{1,0:T(8,128)(2,1)S(1)} collective-permute-done((bf16[400,128]{1,0:T(8,128)(2,1)S(1)}, bf16[400,128]{1,0:T(8,128)(2,1)S(1)}, u32[]{:S(2)}, u32[]{:S(2)}) %collective-permute-start.12) | collective-permute-done | bytes 102432 | tf_op jit(solution)/shard_map/ppermute | solution.py:25
  18.0 0.5 collective-permute-start.5
  18.5 1.0 %collective-permute-done.3.refs_0_ = bf16[400,128]{1,0:T(8,128)(2,1)S(1)} collective-permute-done((bf16[400,128]{1,0:T(8,128)(2,1)S(1)}, bf16[400,128]{1,0:T(8,128)(2,1)S(1)}, u32[]{:S(2)}, u32[]{:S(2)}) %collective-permute-start.3) | collective-permute-done | bytes 102432 | tf_op jit(solution)/shard_map/ppermute | solution.py:25
  19.5 3.2 %shard_map.138 = (bf16[3,3,160,640]{3,2,1,0:T(8,128)(2,1)S(1)}, bf16[3,3,160,640]{3,2,1,0:T(8,128)(2,1)S(1)}, bf16[3,3,160,640]{3,2,1,0:T(8,128)(2,1)S(1)}, bf16[3,3,160,640]{3,2,1,0:T(8,128)(2,1)S(1)}) custom-call(bf16[3,3,160,640]{3,2,1,0:T(8,128)(2,1)} %refs_0_.1, bf16[3,3,160,640]{3,2,1,0:T(8,128)(2,1)} %refs_1_.1, bf16[3,3,160,640]{3,2,1,0:T(8,128)(2,1)} %refs_2_.6, ...), custom_call_target="tpu_custom_call" | custom-call | bytes 7372800 | tf_op jit(solution)/shard_map/pallas_call | solution.py:193
  22.7 0.8 %shard_map.145.refs_1_ = f32[320,160]{1,0:T(8,128)S(1)} custom-call(bf16[400,128]{1,0:T(8,128)(2,1)S(1)} %get-tuple-element.41.refs_0_, bf16[400,128]{1,0:T(8,128)(2,1)S(1)} %collective-permute-done.14.refs_1_, bf16[3,3,160,640]{3,2,1,0:T(8,128)(2,1)S(1)} %get-tuple-element.42.refs_2_), custom_call_target="tpu_custom_call" | custom-call | flops 294912000 | bytes 2252800 | tf_op jit(solution)/shard_map/pallas_call | solution.py:44
  23.6 0.5 shard_map.146.refs_1_
  24.2 0.8 %shard_map.147 = (bf16[320,160]{1,0:T(8,128)(2,1)S(1)}, bf16[384,128]{1,0:T(8,128)(2,1)S(1)}) custom-call(bf16[400,128]{1,0:T(8,128)(2,1)S(1)} %collective-permute-done.13.refs_0_, f32[320,160]{1,0:T(8,128)S(1)} %shard_map.146.refs_1_, bf16[3,3,160,640]{3,2,1,0:T(8,128)(2,1)S(1)} %get-tuple-element.42.refs_2_, ...), custom_call_target="tpu_custom_call" | custom-call | flops 147456000 | bytes 2453824 | tf_op jit(solution)/shard_map/pallas_call | solution.py:44
  25.0 1.1 %collective-permute-start.15 = (bf16[384,128]{1,0:T(8,128)(2,1)S(1)}, bf16[384,128]{1,0:T(8,128)(2,1)S(1)}, u32[]{:S(2)}, u32[]{:S(2)}) collective-permute-start(bf16[384,128]{1,0:T(8,128)(2,1)S(1)} %get-tuple-element.44.refs_0_), channel_id=1, source_target_pairs={{0,8},{8,0},{1,9},{9,1},{2,10},{10,2},{3,11},{11,3},{4,12},{12,4},... | collective-permute-start | bytes 294920 | tf_op jit(solution)/shard_map/ppermute | solution.py:25
  26.1 0.8 %shard_map.139.refs_1_ = f32[320,160]{1,0:T(8,128)S(1)} custom-call(bf16[400,128]{1,0:T(8,128)(2,1)S(1)} %get-tuple-element.34.refs_0_, bf16[400,128]{1,0:T(8,128)(2,1)S(1)} %collective-permute-done.5.refs_1_, bf16[3,3,160,640]{3,2,1,0:T(8,128)(2,1)S(1)} %get-tuple-element.35.refs_2_), custom_call_target="tpu_custom_call" | custom-call | flops 294912000 | bytes 2252800 | tf_op jit(solution)/shard_map/pallas_call | solution.py:44
  26.9 0.5 shard_map.140.refs_1_
  27.6 0.7 %shard_map.141 = (bf16[320,160]{1,0:T(8,128)(2,1)S(1)}, bf16[384,128]{1,0:T(8,128)(2,1)S(1)}) custom-call(bf16[400,128]{1,0:T(8,128)(2,1)S(1)} %collective-permute-done.4.refs_0_, f32[320,160]{1,0:T(8,128)S(1)} %shard_map.140.refs_1_, bf16[3,3,160,640]{3,2,1,0:T(8,128)(2,1)S(1)} %get-tuple-element.35.refs_2_, ...), custom_call_target="tpu_custom_call" | custom-call | flops 147456000 | bytes 2453824 | tf_op jit(solution)/shard_map/pallas_call | solution.py:44
  28.3 1.0 %collective-permute-start.6 = (bf16[384,128]{1,0:T(8,128)(2,1)S(1)}, bf16[384,128]{1,0:T(8,128)(2,1)S(1)}, u32[]{:S(2)}, u32[]{:S(2)}) collective-permute-start(bf16[384,128]{1,0:T(8,128)(2,1)S(1)} %get-tuple-element.37.refs_0_), channel_id=1, source_target_pairs={{0,8},{8,0},{1,9},{9,1},{2,10},{10,2},{3,11},{11,3},{4,12},{12,4},... | collective-permute-start | bytes 294920 | tf_op jit(solution)/shard_map/ppermute | solution.py:25
  29.3 0.9 %collective-permute-done.15.refs_0_ = bf16[384,128]{1,0:T(8,128)(2,1)S(1)} collective-permute-done((bf16[384,128]{1,0:T(8,128)(2,1)S(1)}, bf16[384,128]{1,0:T(8,128)(2,1)S(1)}, u32[]{:S(2)}, u32[]{:S(2)}) %collective-permute-start.15) | collective-permute-done | bytes 98336 | tf_op jit(solution)/shard_map/ppermute | solution.py:25
  30.7 2.6 %collective-permute-done.6.refs_0_ = bf16[384,128]{1,0:T(8,128)(2,1)S(1)} collective-permute-done((bf16[384,128]{1,0:T(8,128)(2,1)S(1)}, bf16[384,128]{1,0:T(8,128)(2,1)S(1)}, u32[]{:S(2)}, u32[]{:S(2)}) %collective-permute-start.6) | collective-permute-done | bytes 98336 | tf_op jit(solution)/shard_map/ppermute | solution.py:25
  33.3 0.8 %shard_map.148.refs_1_ = f32[320,160]{1,0:T(8,128)S(1)} custom-call(bf16[384,128]{1,0:T(8,128)(2,1)S(1)} %get-tuple-element.44.refs_0_, bf16[384,128]{1,0:T(8,128)(2,1)S(1)} %collective-permute-done.17.refs_1_, bf16[3,3,160,640]{3,2,1,0:T(8,128)(2,1)S(1)} %get-tuple-element.45.refs_2_), custom_call_target="tpu_custom_call" | custom-call | flops 294912000 | bytes 2244608 | tf_op jit(solution)/shard_map/pallas_call | solution.py:44
  34.1 0.5 shard_map.149.refs_1_
  34.8 1.3 %shard_map.150 = (bf16[320,160]{1,0:T(8,128)(2,1)}, bf16[360,128]{1,0:T(8,128)(2,1)S(1)}) custom-call(bf16[384,128]{1,0:T(8,128)(2,1)S(1)} %collective-permute-done.16.refs_0_, f32[320,160]{1,0:T(8,128)S(1)} %shard_map.149.refs_1_, bf16[3,3,160,640]{3,2,1,0:T(8,128)(2,1)S(1)} %get-tuple-element.45.refs_2_, bf16[320,160]{1,0:T(8,128)(2,1)S(1)} %get-tuple-element.46.refs_3_, ...), custom_call_target="tpu_custom_call" | custom-call | flops 147456000 | bytes 2443584 | tf_op jit(solution)/shard_map/pallas_call | solution.py:44
  36.1 0.9 %collective-permute-start.18 = (bf16[360,128]{1,0:T(8,128)(2,1)S(1)}, bf16[360,128]{1,0:T(8,128)(2,1)S(1)}, u32[]{:S(2)}, u32[]{:S(2)}) collective-permute-start(bf16[360,128]{1,0:T(8,128)(2,1)S(1)} %get-tuple-element.47.refs_0_), channel_id=1, source_target_pairs={{0,8},{8,0},{1,9},{9,1},{2,10},{10,2},{3,11},{11,3},{4,12},{12,4},... | collective-permute-start | bytes 276488 | tf_op jit(solution)/shard_map/ppermute | solution.py:25
  37.0 0.8 %shard_map.142.refs_1_ = f32[320,160]{1,0:T(8,128)S(1)} custom-call(bf16[384,128]{1,0:T(8,128)(2,1)S(1)} %get-tuple-element.37.refs_0_, bf16[384,128]{1,0:T(8,128)(2,1)S(1)} %collective-permute-done.8.refs_1_, bf16[3,3,160,640]{3,2,1,0:T(8,128)(2,1)S(1)} %get-tuple-element.38.refs_2_), custom_call_target="tpu_custom_call" | custom-call | flops 294912000 | bytes 2244608 | tf_op jit(solution)/shard_map/pallas_call | solution.py:44
  37.8 0.5 shard_map.143.refs_1_
  38.4 0.7 %shard_map.144 = (bf16[320,160]{1,0:T(8,128)(2,1)S(1)}, bf16[360,128]{1,0:T(8,128)(2,1)S(1)}) custom-call(bf16[384,128]{1,0:T(8,128)(2,1)S(1)} %collective-permute-done.7.refs_0_, f32[320,160]{1,0:T(8,128)S(1)} %shard_map.143.refs_1_, bf16[3,3,160,640]{3,2,1,0:T(8,128)(2,1)S(1)} %get-tuple-element.38.refs_2_, ...), custom_call_target="tpu_custom_call" | custom-call | flops 147456000 | bytes 2443584 | tf_op jit(solution)/shard_map/pallas_call | solution.py:44
  39.2 1.1 %collective-permute-start.9 = (bf16[360,128]{1,0:T(8,128)(2,1)S(1)}, bf16[360,128]{1,0:T(8,128)(2,1)S(1)}, u32[]{:S(2)}, u32[]{:S(2)}) collective-permute-start(bf16[360,128]{1,0:T(8,128)(2,1)S(1)} %get-tuple-element.40.refs_0_), channel_id=1, source_target_pairs={{0,8},{8,0},{1,9},{9,1},{2,10},{10,2},{3,11},{11,3},{4,12},{12,4},... | collective-permute-start | bytes 276488 | tf_op jit(solution)/shard_map/ppermute | solution.py:25
  40.3 0.9 %collective-permute-done.18.refs_0_.refs_2_ = bf16[360,128]{1,0:T(8,128)(2,1)S(1)} collective-permute-done((bf16[360,128]{1,0:T(8,128)(2,1)S(1)}, bf16[360,128]{1,0:T(8,128)(2,1)S(1)}, u32[]{:S(2)}, u32[]{:S(2)}) %collective-permute-start.18) | collective-permute-done | bytes 92192 | tf_op jit(solution)/shard_map/ppermute | solution.py:25
  41.2 0.5 collective-permute-start.11
  41.7 2.3 %collective-permute-done.9.refs_0_ = bf16[360,128]{1,0:T(8,128)(2,1)S(1)} collective-permute-done((bf16[360,128]{1,0:T(8,128)(2,1)S(1)}, bf16[360,128]{1,0:T(8,128)(2,1)S(1)}, u32[]{:S(2)}, u32[]{:S(2)}) %collective-permute-start.9) | collective-permute-done | bytes 92192 | tf_op jit(solution)/shard_map/ppermute | solution.py:25
  44.0 0.8 %shard_map.151.refs_2_ = f32[320,160]{1,0:T(8,128)S(1)} custom-call(bf16[360,128]{1,0:T(8,128)(2,1)S(1)} %get-tuple-element.47.refs_0_, bf16[360,128]{1,0:T(8,128)(2,1)S(1)} %collective-permute-done.20.refs_1_, bf16[3,3,160,1280]{3,2,1,0:T(8,128)(2,1)S(1)} %copy-done), custom_call_target="tpu_custom_call" | custom-call | flops 294912000 | bytes 4075520 | tf_op jit(solution)/shard_map/pallas_call | solution.py:44
  44.8 0.8 %shard_map.152.refs_2_ = f32[320,160]{1,0:T(8,128)S(1)} custom-call(bf16[360,128]{1,0:T(8,128)(2,1)S(1)} %collective-permute-done.18.refs_0_.refs_2_, bf16[360,128]{1,0:T(8,128)(2,1)S(1)} %collective-permute-done.19.refs_1_.refs_3_, f32[320,160]{1,0:T(8,128)S(1)} %shard_map.151.refs_2_, bf16[3,3,160,1280]{3,2,1,0:T(8,128)(2,1)S(1)} %copy-done), custom_call_target="tpu_custom_call" | custom-call | flops 294912000 | bytes 4280320 | tf_op jit(solution)/shard_map/pallas_call | solution.py:44
  45.6 0.8 %shard_map.153.refs_1_ = f32[320,160]{1,0:T(8,128)S(1)} custom-call(bf16[360,128]{1,0:T(8,128)(2,1)S(1)} %get-tuple-element.40.refs_0_, bf16[360,128]{1,0:T(8,128)(2,1)S(1)} %collective-permute-done.11.refs_1_, f32[320,160]{1,0:T(8,128)S(1)} %shard_map.152.refs_2_, bf16[3,3,160,1280]{3,2,1,0:T(8,128)(2,1)S(1)} %copy-done), custom_call_target="tpu_custom_call" | custom-call | flops 294912000 | bytes 4280320 | tf_op jit(solution)/shard_map/pallas_call | solution.py:44
  46.5 0.5 shard_map.154.refs_1_
  47.1 0.7 %shard_map.155 = (bf16[320,160]{1,0:T(8,128)(2,1)S(1)}, bf16[344,128]{1,0:T(8,128)(2,1)S(1)}) custom-call(bf16[360,128]{1,0:T(8,128)(2,1)S(1)} %collective-permute-done.10.refs_0_, f32[320,160]{1,0:T(8,128)S(1)} %shard_map.154.refs_1_, bf16[3,3,160,1280]{3,2,1,0:T(8,128)(2,1)S(1)} %copy-done, bf16[320,160]{1,0:T(8,128)(2,1)S(1)} %get-tuple-element.48.refs_3_, ...), custom_call_target="tpu_custom_call" | custom-call | flops 147456000 | bytes 4276544 | tf_op jit(solution)/shard_map/pallas_call | solution.py:44
  47.8 1.2 %collective-permute-start.21 = (bf16[344,128]{1,0:T(8,128)(2,1)S(1)}, bf16[344,128]{1,0:T(8,128)(2,1)S(1)}, u32[]{:S(2)}, u32[]{:S(2)}) collective-permute-start(bf16[344,128]{1,0:T(8,128)(2,1)S(1)} %get-tuple-element.49.refs_0_), channel_id=1, source_target_pairs={{0,8},{8,0},{1,9},{9,1},{2,10},{10,2},{3,11},{11,3},{4,12},{12,4},... | collective-permute-start | bytes 264200 | tf_op jit(solution)/shard_map/ppermute | solution.py:25
  49.3 3.6 %collective-permute-done.21.refs_0_ = bf16[344,128]{1,0:T(8,128)(2,1)S(1)} collective-permute-done((bf16[344,128]{1,0:T(8,128)(2,1)S(1)}, bf16[344,128]{1,0:T(8,128)(2,1)S(1)}, u32[]{:S(2)}, u32[]{:S(2)}) %collective-permute-start.21) | collective-permute-done | bytes 88096 | tf_op jit(solution)/shard_map/ppermute | solution.py:25
  52.9 1.3 %shard_map.156.refs_2_ = f32[320,160]{1,0:T(8,128)S(1)} custom-call(bf16[360,128]{1,0:T(8,128)(2,1)S(1)} %get-tuple-element.47.refs_0_, bf16[360,128]{1,0:T(8,128)(2,1)S(1)} %collective-permute-done.20.refs_1_, bf16[360,128]{1,0:T(8,128)(2,1)S(1)} %collective-permute-done.18.refs_0_.refs_2_, bf16[360,128]{1,0:T(8,128)(2,1)S(1)} %collective-permute-done.19.refs_1_.refs_3_, ...), custom_call_target="tpu_custom_call" | custom-call | flops 589824000 | bytes 4259840 | tf_op jit(solution)/shard_map/pallas_call | solution.py:44
  54.3 0.8 %shard_map.157.refs_1_ = f32[320,160]{1,0:T(8,128)S(1)} custom-call(bf16[344,128]{1,0:T(8,128)(2,1)S(1)} %get-tuple-element.49.refs_0_, bf16[344,128]{1,0:T(8,128)(2,1)S(1)} %collective-permute-done.23.refs_1_, f32[320,160]{1,0:T(8,128)S(1)} %shard_map.156.refs_2_, bf16[3,3,160,1280]{3,2,1,0:T(8,128)(2,1)S(1)} %copy-done.1), custom_call_target="tpu_custom_call" | custom-call | flops 294912000 | bytes 4272128 | tf_op jit(solution)/shard_map/pallas_call | solution.py:44
  55.1 0.5 shard_map.158.refs_1_
  55.7 0.6 shard_map.159
  56.4 1.4 %collective-permute-start.25 = (bf16[80,128]{1,0:T(8,128)(2,1)S(1)}, bf16[80,128]{1,0:T(8,128)(2,1)S(1)}, u32[]{:S(2)}, u32[]{:S(2)}) collective-permute-start(bf16[80,128]{1,0:T(8,128)(2,1)S(1)} %get-tuple-element.53), channel_id=1, source_target_pairs={{0,4},{2,6},{4,0},{6,2},{1,5},{3,7},{5,1},{7,3},{8,12},{10,14},{12... | collective-permute-start | bytes 61448 | tf_op jit(solution)/shard_map/ppermute | solution.py:25
  57.9 3.0 %collective-permute-start.26 = (bf16[80,128]{1,0:T(8,128)(2,1)S(1)}, bf16[80,128]{1,0:T(8,128)(2,1)S(1)}, u32[]{:S(2)}, u32[]{:S(2)}) collective-permute-start(bf16[80,128]{1,0:T(8,128)(2,1)S(1)} %get-tuple-element.54), channel_id=1, source_target_pairs={{0,6},{2,4},{4,2},{6,0},{1,7},{3,5},{5,3},{7,1},{8,14},{10,12},{12... | collective-permute-start | bytes 61448 | tf_op jit(solution)/shard_map/ppermute | solution.py:25
  60.8 0.5 collective-permute-done.25.refs_2_
  61.4 2.1 %collective-permute-done.26.refs_3_ = bf16[80,128]{1,0:T(8,128)(2,1)S(1)} collective-permute-done((bf16[80,128]{1,0:T(8,128)(2,1)S(1)}, bf16[80,128]{1,0:T(8,128)(2,1)S(1)}, u32[]{:S(2)}, u32[]{:S(2)}) %collective-permute-start.26) | collective-permute-done | bytes 20512 | tf_op jit(solution)/shard_map/ppermute | solution.py:25
  63.4 0.8 %shard_map.160 = bf16[2,160,128]{2,1,0:T(8,128)(2,1)} custom-call(bf16[80,128]{1,0:T(8,128)(2,1)S(1)} %get-tuple-element.51.refs_0_, bf16[80,128]{1,0:T(8,128)(2,1)S(1)} %collective-permute-done.24.refs_1_, bf16[80,128]{1,0:T(8,128)(2,1)S(1)} %collective-permute-done.25.refs_2_, bf16[80,128]{1,0:T(8,128)(2,1)S(1)} %collective-permute-done.26.refs_3_), custom_call_target="tpu_custom_call" | custom-call | bytes 163840 | tf_op jit(solution)/shard_map/pallas_call | solution.py:44
  (47 shorter events, 1.8 us)
Async XLA Ops:
  1.2 5.7 %collective-permute-start = (bf16[200,128]{1,0:T(8,128)(2,1)S(1)}, bf16[200,128]{1,0:T(8,128)(2,1)S(1)}, u32[]{:S(2)}, u32[]{:S(2)}) collective-permute-start(bf16[200,128]{1,0:T(8,128)(2,1)S(1)} %get-tuple-element.31), channel_id=1, source_target_pairs={{0,2},{2,0},{4,6},{6,4},{1,3},{3,1},{5,7},{7,5},{8,10},{10,8},{12,... | collective-permute-start | bytes 153608 | tf_op jit(solution)/shard_map/ppermute | solution.py:25
  4.3 6.0 %collective-permute-start.1 = (bf16[200,128]{1,0:T(8,128)(2,1)S(1)}, bf16[200,128]{1,0:T(8,128)(2,1)S(1)}, u32[]{:S(2)}, u32[]{:S(2)}) collective-permute-start(bf16[200,128]{1,0:T(8,128)(2,1)S(1)} %get-tuple-element.32), channel_id=1, source_target_pairs={{0,4},{2,6},{4,0},{6,2},{1,5},{3,7},{5,1},{7,3},{8,12},{10,14},{12... | collective-permute-start | bytes 153608 | tf_op jit(solution)/shard_map/ppermute | solution.py:25
  6.9 5.9 %collective-permute-start.2 = (bf16[200,128]{1,0:T(8,128)(2,1)S(1)}, bf16[200,128]{1,0:T(8,128)(2,1)S(1)}, u32[]{:S(2)}, u32[]{:S(2)}) collective-permute-start(bf16[200,128]{1,0:T(8,128)(2,1)S(1)} %get-tuple-element.33), channel_id=1, source_target_pairs={{0,6},{2,4},{4,2},{6,0},{1,7},{3,5},{5,3},{7,1},{8,14},{10,12},{12... | collective-permute-start | bytes 153608 | tf_op jit(solution)/shard_map/ppermute | solution.py:25
  13.3 4.7 %collective-permute-start.12 = (bf16[400,128]{1,0:T(8,128)(2,1)S(1)}, bf16[400,128]{1,0:T(8,128)(2,1)S(1)}, u32[]{:S(2)}, u32[]{:S(2)}) collective-permute-start(bf16[400,128]{1,0:T(8,128)(2,1)S(1)} %get-tuple-element.41.refs_0_), channel_id=1, source_target_pairs={{0,8},{8,0},{1,9},{9,1},{2,10},{10,2},{3,11},{11,3},{4,12},{12,4},... | collective-permute-start | bytes 307208 | tf_op jit(solution)/shard_map/ppermute | solution.py:25
  14.9 4.7 %collective-permute-start.3 = (bf16[400,128]{1,0:T(8,128)(2,1)S(1)}, bf16[400,128]{1,0:T(8,128)(2,1)S(1)}, u32[]{:S(2)}, u32[]{:S(2)}) collective-permute-start(bf16[400,128]{1,0:T(8,128)(2,1)S(1)} %get-tuple-element.34.refs_0_), channel_id=1, source_target_pairs={{0,8},{8,0},{1,9},{9,1},{2,10},{10,2},{3,11},{11,3},{4,12},{12,4},... | collective-permute-start | bytes 307208 | tf_op jit(solution)/shard_map/ppermute | solution.py:25
  15.4 7.3 %collective-permute-start.14 = (bf16[400,128]{1,0:T(8,128)(2,1)S(1)}, bf16[400,128]{1,0:T(8,128)(2,1)S(1)}, u32[]{:S(2)}, u32[]{:S(2)}) collective-permute-start(bf16[400,128]{1,0:T(8,128)(2,1)S(1)} %get-tuple-element.41.refs_0_), channel_id=1, source_target_pairs={{0,1},{1,0},{2,3},{3,2},{4,5},{5,4},{6,7},{7,6},{8,9},{9,8},{10,11... | collective-permute-start | bytes 307208 | tf_op jit(solution)/shard_map/ppermute | solution.py:25
  18.0 6.1 %collective-permute-start.13 = (bf16[400,128]{1,0:T(8,128)(2,1)S(1)}, bf16[400,128]{1,0:T(8,128)(2,1)S(1)}, u32[]{:S(2)}, u32[]{:S(2)}) collective-permute-start(bf16[400,128]{1,0:T(8,128)(2,1)S(1)} %collective-permute-done.12.refs_0_), channel_id=1, source_target_pairs={{0,1},{1,0},{2,3},{3,2},{4,5},{5,4},{6,7},{7,6},{8,9},{9,8},{10,11... | collective-permute-start | bytes 307208 | tf_op jit(solution)/shard_map/ppermute | solution.py:25
  18.0 8.1 %collective-permute-start.5 = (bf16[400,128]{1,0:T(8,128)(2,1)S(1)}, bf16[400,128]{1,0:T(8,128)(2,1)S(1)}, u32[]{:S(2)}, u32[]{:S(2)}) collective-permute-start(bf16[400,128]{1,0:T(8,128)(2,1)S(1)} %get-tuple-element.34.refs_0_), channel_id=1, source_target_pairs={{0,1},{1,0},{2,3},{3,2},{4,5},{5,4},{6,7},{7,6},{8,9},{9,8},{10,11... | collective-permute-start | bytes 307208 | tf_op jit(solution)/shard_map/ppermute | solution.py:25
  19.5 7.9 %collective-permute-start.4 = (bf16[400,128]{1,0:T(8,128)(2,1)S(1)}, bf16[400,128]{1,0:T(8,128)(2,1)S(1)}, u32[]{:S(2)}, u32[]{:S(2)}) collective-permute-start(bf16[400,128]{1,0:T(8,128)(2,1)S(1)} %collective-permute-done.3.refs_0_), channel_id=1, source_target_pairs={{0,1},{1,0},{2,3},{3,2},{4,5},{5,4},{6,7},{7,6},{8,9},{9,8},{10,11... | collective-permute-start | bytes 307208 | tf_op jit(solution)/shard_map/ppermute | solution.py:25
  23.5 0.7 %copy-start.4 = (bf16[160]{0:T(256)(128)(2,1)S(1)}, bf16[160]{0:T(256)(128)(2,1)}, u32[]{:S(2)}) copy-start(bf16[160]{0:T(256)(128)(2,1)} %refs_4_.9) | copy-start | bytes 964
  25.0 5.2 %collective-permute-start.15 = (bf16[384,128]{1,0:T(8,128)(2,1)S(1)}, bf16[384,128]{1,0:T(8,128)(2,1)S(1)}, u32[]{:S(2)}, u32[]{:S(2)}) collective-permute-start(bf16[384,128]{1,0:T(8,128)(2,1)S(1)} %get-tuple-element.44.refs_0_), channel_id=1, source_target_pairs={{0,8},{8,0},{1,9},{9,1},{2,10},{10,2},{3,11},{11,3},{4,12},{12,4},... | collective-permute-start | bytes 294920 | tf_op jit(solution)/shard_map/ppermute | solution.py:25
  26.9 0.7 %copy-start.5 = (bf16[160]{0:T(256)(128)(2,1)S(1)}, bf16[160]{0:T(256)(128)(2,1)}, u32[]{:S(2)}) copy-start(bf16[160]{0:T(256)(128)(2,1)} %refs_4_.7) | copy-start | bytes 964
  28.3 5.0 %collective-permute-start.6 = (bf16[384,128]{1,0:T(8,128)(2,1)S(1)}, bf16[384,128]{1,0:T(8,128)(2,1)S(1)}, u32[]{:S(2)}, u32[]{:S(2)}) collective-permute-start(bf16[384,128]{1,0:T(8,128)(2,1)S(1)} %get-tuple-element.37.refs_0_), channel_id=1, source_target_pairs={{0,8},{8,0},{1,9},{9,1},{2,10},{10,2},{3,11},{11,3},{4,12},{12,4},... | collective-permute-start | bytes 294920 | tf_op jit(solution)/shard_map/ppermute | solution.py:25
  29.3 4.0 %collective-permute-start.17 = (bf16[384,128]{1,0:T(8,128)(2,1)S(1)}, bf16[384,128]{1,0:T(8,128)(2,1)S(1)}, u32[]{:S(2)}, u32[]{:S(2)}) collective-permute-start(bf16[384,128]{1,0:T(8,128)(2,1)S(1)} %get-tuple-element.44.refs_0_), channel_id=1, source_target_pairs={{0,1},{1,0},{2,3},{3,2},{4,5},{5,4},{6,7},{7,6},{8,9},{9,8},{10,11... | collective-permute-start | bytes 294920 | tf_op jit(solution)/shard_map/ppermute | solution.py:25
  30.2 4.5 %collective-permute-start.16 = (bf16[384,128]{1,0:T(8,128)(2,1)S(1)}, bf16[384,128]{1,0:T(8,128)(2,1)S(1)}, u32[]{:S(2)}, u32[]{:S(2)}) collective-permute-start(bf16[384,128]{1,0:T(8,128)(2,1)S(1)} %collective-permute-done.15.refs_0_), channel_id=1, source_target_pairs={{0,1},{1,0},{2,3},{3,2},{4,5},{5,4},{6,7},{7,6},{8,9},{9,8},{10,11... | collective-permute-start | bytes 294920 | tf_op jit(solution)/shard_map/ppermute | solution.py:25
  30.2 6.8 %collective-permute-start.8 = (bf16[384,128]{1,0:T(8,128)(2,1)S(1)}, bf16[384,128]{1,0:T(8,128)(2,1)S(1)}, u32[]{:S(2)}, u32[]{:S(2)}) collective-permute-start(bf16[384,128]{1,0:T(8,128)(2,1)S(1)} %get-tuple-element.37.refs_0_), channel_id=1, source_target_pairs={{0,1},{1,0},{2,3},{3,2},{4,5},{5,4},{6,7},{7,6},{8,9},{9,8},{10,11... | collective-permute-start | bytes 294920 | tf_op jit(solution)/shard_map/ppermute | solution.py:25
  33.3 5.1 %collective-permute-start.7 = (bf16[384,128]{1,0:T(8,128)(2,1)S(1)}, bf16[384,128]{1,0:T(8,128)(2,1)S(1)}, u32[]{:S(2)}, u32[]{:S(2)}) collective-permute-start(bf16[384,128]{1,0:T(8,128)(2,1)S(1)} %collective-permute-done.6.refs_0_), channel_id=1, source_target_pairs={{0,1},{1,0},{2,3},{3,2},{4,5},{5,4},{6,7},{7,6},{8,9},{9,8},{10,11... | collective-permute-start | bytes 294920 | tf_op jit(solution)/shard_map/ppermute | solution.py:25
  34.1 0.7 %copy-start.6 = (bf16[160]{0:T(256)(128)(2,1)S(1)}, bf16[160]{0:T(256)(128)(2,1)}, u32[]{:S(2)}) copy-start(bf16[160]{0:T(256)(128)(2,1)} %refs_4_.10) | copy-start | bytes 964
  36.1 5.1 %collective-permute-start.18 = (bf16[360,128]{1,0:T(8,128)(2,1)S(1)}, bf16[360,128]{1,0:T(8,128)(2,1)S(1)}, u32[]{:S(2)}, u32[]{:S(2)}) collective-permute-start(bf16[360,128]{1,0:T(8,128)(2,1)S(1)} %get-tuple-element.47.refs_0_), channel_id=1, source_target_pairs={{0,8},{8,0},{1,9},{9,1},{2,10},{10,2},{3,11},{11,3},{4,12},{12,4},... | collective-permute-start | bytes 276488 | tf_op jit(solution)/shard_map/ppermute | solution.py:25
  37.0 1.4 %copy-start.7 = (bf16[160]{0:T(256)(128)(2,1)S(1)}, bf16[160]{0:T(256)(128)(2,1)}, u32[]{:S(2)}) copy-start(bf16[160]{0:T(256)(128)(2,1)} %refs_4_.8) | copy-start | bytes 964
  37.8 6.2 %copy-start = (bf16[3,3,160,1280]{3,2,1,0:T(8,128)(2,1)S(1)}, bf16[3,3,160,1280]{3,2,1,0:T(8,128)(2,1)}, u32[]{:S(2)}) copy-start(bf16[3,3,160,1280]{3,2,1,0:T(8,128)(2,1)} %refs_2_.9) | copy-start | bytes 11059204
  39.2 4.8 %collective-permute-start.9 = (bf16[360,128]{1,0:T(8,128)(2,1)S(1)}, bf16[360,128]{1,0:T(8,128)(2,1)S(1)}, u32[]{:S(2)}, u32[]{:S(2)}) collective-permute-start(bf16[360,128]{1,0:T(8,128)(2,1)S(1)} %get-tuple-element.40.refs_0_), channel_id=1, source_target_pairs={{0,8},{8,0},{1,9},{9,1},{2,10},{10,2},{3,11},{11,3},{4,12},{12,4},... | collective-permute-start | bytes 276488 | tf_op jit(solution)/shard_map/ppermute | solution.py:25
  40.3 3.7 %collective-permute-start.20 = (bf16[360,128]{1,0:T(8,128)(2,1)S(1)}, bf16[360,128]{1,0:T(8,128)(2,1)S(1)}, u32[]{:S(2)}, u32[]{:S(2)}) collective-permute-start(bf16[360,128]{1,0:T(8,128)(2,1)S(1)} %get-tuple-element.47.refs_0_), channel_id=1, source_target_pairs={{0,1},{1,0},{2,3},{3,2},{4,5},{5,4},{6,7},{7,6},{8,9},{9,8},{10,11... | collective-permute-start | bytes 276488 | tf_op jit(solution)/shard_map/ppermute | solution.py:25
  41.2 3.6 %collective-permute-start.19 = (bf16[360,128]{1,0:T(8,128)(2,1)S(1)}, bf16[360,128]{1,0:T(8,128)(2,1)S(1)}, u32[]{:S(2)}, u32[]{:S(2)}) collective-permute-start(bf16[360,128]{1,0:T(8,128)(2,1)S(1)} %collective-permute-done.18.refs_0_.refs_2_), channel_id=1, source_target_pairs={{0,1},{1,0},{2,3},{3,2},{4,5},{5,4},{6,7},{7,6},{8,9},{9,8},{10,11... | collective-permute-start | bytes 276488 | tf_op jit(solution)/shard_map/ppermute | solution.py:25
  41.2 4.5 %collective-permute-start.11 = (bf16[360,128]{1,0:T(8,128)(2,1)S(1)}, bf16[360,128]{1,0:T(8,128)(2,1)S(1)}, u32[]{:S(2)}, u32[]{:S(2)}) collective-permute-start(bf16[360,128]{1,0:T(8,128)(2,1)S(1)} %get-tuple-element.40.refs_0_), channel_id=1, source_target_pairs={{0,1},{1,0},{2,3},{3,2},{4,5},{5,4},{6,7},{7,6},{8,9},{9,8},{10,11... | collective-permute-start | bytes 276488 | tf_op jit(solution)/shard_map/ppermute | solution.py:25
  44.0 3.0 %collective-permute-start.10 = (bf16[360,128]{1,0:T(8,128)(2,1)S(1)}, bf16[360,128]{1,0:T(8,128)(2,1)S(1)}, u32[]{:S(2)}, u32[]{:S(2)}) collective-permute-start(bf16[360,128]{1,0:T(8,128)(2,1)S(1)} %collective-permute-done.9.refs_0_), channel_id=1, source_target_pairs={{0,1},{1,0},{2,3},{3,2},{4,5},{5,4},{6,7},{7,6},{8,9},{9,8},{10,11... | collective-permute-start | bytes 276488 | tf_op jit(solution)/shard_map/ppermute | solution.py:25
  46.5 0.7 %copy-start.2 = (bf16[160]{0:T(256)(128)(2,1)S(1)}, bf16[160]{0:T(256)(128)(2,1)}, u32[]{:S(2)}) copy-start(bf16[160]{0:T(256)(128)(2,1)} %refs_4_.11) | copy-start | bytes 964
  47.1 5.8 %copy-start.1 = (bf16[3,3,160,1280]{3,2,1,0:T(8,128)(2,1)S(1)}, bf16[3,3,160,1280]{3,2,1,0:T(8,128)(2,1)}, u32[]{:S(2)}) copy-start(bf16[3,3,160,1280]{3,2,1,0:T(8,128)(2,1)} %refs_2_.11) | copy-start | bytes 11059204
  47.8 5.0 %collective-permute-start.21 = (bf16[344,128]{1,0:T(8,128)(2,1)S(1)}, bf16[344,128]{1,0:T(8,128)(2,1)S(1)}, u32[]{:S(2)}, u32[]{:S(2)}) collective-permute-start(bf16[344,128]{1,0:T(8,128)(2,1)S(1)} %get-tuple-element.49.refs_0_), channel_id=1, source_target_pairs={{0,8},{8,0},{1,9},{9,1},{2,10},{10,2},{3,11},{11,3},{4,12},{12,4},... | collective-permute-start | bytes 264200 | tf_op jit(solution)/shard_map/ppermute | solution.py:25
  49.0 5.2 %collective-permute-start.23 = (bf16[344,128]{1,0:T(8,128)(2,1)S(1)}, bf16[344,128]{1,0:T(8,128)(2,1)S(1)}, u32[]{:S(2)}, u32[]{:S(2)}) collective-permute-start(bf16[344,128]{1,0:T(8,128)(2,1)S(1)} %get-tuple-element.49.refs_0_), channel_id=1, source_target_pairs={{0,1},{1,0},{2,3},{3,2},{4,5},{5,4},{6,7},{7,6},{8,9},{9,8},{10,11... | collective-permute-start | bytes 264200 | tf_op jit(solution)/shard_map/ppermute | solution.py:25
  52.9 2.7 %collective-permute-start.22 = (bf16[344,128]{1,0:T(8,128)(2,1)S(1)}, bf16[344,128]{1,0:T(8,128)(2,1)S(1)}, u32[]{:S(2)}, u32[]{:S(2)}) collective-permute-start(bf16[344,128]{1,0:T(8,128)(2,1)S(1)} %collective-permute-done.21.refs_0_), channel_id=1, source_target_pairs={{0,1},{1,0},{2,3},{3,2},{4,5},{5,4},{6,7},{7,6},{8,9},{9,8},{10,11... | collective-permute-start | bytes 264200 | tf_op jit(solution)/shard_map/ppermute | solution.py:25
  55.1 0.7 %copy-start.3 = (bf16[160]{0:T(256)(128)(2,1)S(1)}, bf16[160]{0:T(256)(128)(2,1)}, u32[]{:S(2)}) copy-start(bf16[160]{0:T(256)(128)(2,1)} %refs_4_.13) | copy-start | bytes 964
  56.4 4.5 %collective-permute-start.24 = (bf16[80,128]{1,0:T(8,128)(2,1)S(1)}, bf16[80,128]{1,0:T(8,128)(2,1)S(1)}, u32[]{:S(2)}, u32[]{:S(2)}) collective-permute-start(bf16[80,128]{1,0:T(8,128)(2,1)S(1)} %get-tuple-element.52), channel_id=1, source_target_pairs={{0,2},{2,0},{4,6},{6,4},{1,3},{3,1},{5,7},{7,5},{8,10},{10,8},{12,... | collective-permute-start | bytes 61448 | tf_op jit(solution)/shard_map/ppermute | solution.py:25
  56.4 4.9 %collective-permute-start.25 = (bf16[80,128]{1,0:T(8,128)(2,1)S(1)}, bf16[80,128]{1,0:T(8,128)(2,1)S(1)}, u32[]{:S(2)}, u32[]{:S(2)}) collective-permute-start(bf16[80,128]{1,0:T(8,128)(2,1)S(1)} %get-tuple-element.53), channel_id=1, source_target_pairs={{0,4},{2,6},{4,0},{6,2},{1,5},{3,7},{5,1},{7,3},{8,12},{10,14},{12... | collective-permute-start | bytes 61448 | tf_op jit(solution)/shard_map/ppermute | solution.py:25
  57.9 5.6 %collective-permute-start.26 = (bf16[80,128]{1,0:T(8,128)(2,1)S(1)}, bf16[80,128]{1,0:T(8,128)(2,1)S(1)}, u32[]{:S(2)}, u32[]{:S(2)}) collective-permute-start(bf16[80,128]{1,0:T(8,128)(2,1)S(1)} %get-tuple-element.54), channel_id=1, source_target_pairs={{0,6},{2,4},{4,2},{6,0},{1,7},{3,5},{5,3},{7,1},{8,14},{10,12},{12... | collective-permute-start | bytes 61448 | tf_op jit(solution)/shard_map/ppermute | solution.py:25

commit v10 on v9

--- a/solution.py
+++ b/solution.py
@@ -334,9 +334,7 @@
     return lambda j: jnp.concatenate([rows(j, at) for at in slices], axis=1)
 
 
-def finish(z, trim, state, result, bias, new_ref, act_ref):
-    new = (state.astype(F32) + result + bias).astype(BF16)
-    new_ref[...] = new
+def send(z, trim, new, act_ref):
     edge = trim * z.height
     act = masked_silu(z, new.astype(F32))[edge : z.cells - edge]
     pack(z, act_ref, act, roll=True)
@@ -363,7 +361,14 @@
 
 
 def close_layer(z, trim, total, state_ref, b_ref, new_ref, act_ref):
-    finish(z, trim + 1, state_ref[...], total, bias_of(b_ref), new_ref, act_ref)
+    new = (state_ref[...].astype(F32) + total + bias_of(b_ref)).astype(BF16)
+    new_ref[...] = new
+    send(z, trim + 1, new, act_ref)
+
+
+def close_control(z, trim, total, state_ref, b_ref, act_ref):
+    new = (state_ref[...].astype(F32) + total + bias_of(b_ref)).astype(BF16)
+    send(z, trim + 1, new, act_ref)
 
 
 def close_image(z, trim, total, *refs):
@@ -428,6 +433,15 @@
         tuple(at * cores + k for at in range(1, len(chips) + 1) for k in range(1, cores)),
     )
     return list(zip(names, (near, chips, far)))
+
+
+def together(received):
+    return tuple(sum((list(part) for part in parts), []) for parts in zip(*received))
+
+
+def late_together(received):
+    near, *others = received
+    return [near, together(others)]
 
 
 def per_device(latent, control_hint, cw1, cb1, cw2, cb2, mw1, mb1, mw2, mb2, dw1, db1, dw2, db2):
@@ -485,18 +499,19 @@
         outs = [single, sds(message(step + 1))]
         received = gather(control)
         rest = (states[0], cb)
-        states[0], control = convolution(step, received, cw, 0, outs, close_layer, rest)
-        received = gather(main)
+        if step == 0:
+            states[0], control = convolution(step, received, cw, 0, outs, close_layer, rest)
+        else:
+            control = convolution(step, received, cw, 0, outs[1], close_control, rest)
+        received = late_together(gather(main))
         rest = (states[1], mb)
         states[1], main = convolution(step, received, mw, 0, outs, close_layer, rest)
     skip = gather(control)
-    near, *others = skip
-    merged = tuple(sum((list(part) for part in parts), []) for parts in zip(*others))
-    first = convolution(2, [near, merged], dw1, z.depth, total)
+    first = convolution(2, late_together(skip), dw1, z.depth, total)
     outs = [single, sds(message(3))]
     rest = (states[1], db1)
     state, act = convolution(2, gather(main), dw1, 0, outs, close_layer, rest, sums=(first,))
-    every = tuple(sum((list(part) for part in parts), []) for parts in zip(*skip))
+    every = together(skip)
     part = convolution(2, [every], dw2, z.depth, total)
     blocks = convolution(
         3,

time: 64.5 us -> 63.2 us (0.980)
  Pallas kernels: 21.7 us -> 20.5 us
    pallas_call x23 -> x21, Pallas kernels: 17.3 us -> 16.1 us  [call(): pl.pallas_call(kernel, out_shape=outs, in_specs=whole(len(args)), out_spe...]
  transfers between devices with their start and end apart: 27 -> 27, of which waited for: 11 -> 11; matrix products, arithmetic and copies ran while one was open for 0% -> 0% of each run, Pallas kernels for 28% -> 26%
where the time goes in v10:
time: 63.2 us; the launch traced here: 63 us
  waiting for transfers between devices  22.5 us (36%)
  Pallas kernels  20.5 us (32%)
  starting transfers between devices  19.4 us (31%)
    ppermute x27, waiting for transfers between devices, exchange(): return lax.ppermute(cells, axis, [(i, i ^ distance) for i in range(count)])  22.5 us
    ppermute x27, starting transfers between devices, exchange(): return lax.ppermute(cells, axis, [(i, i ^ distance) for i in range(count)])  19.4 us
    pallas_call x21, Pallas kernels, call(): pl.pallas_call(kernel, out_shape=outs, in_specs=whole(len(args)), out_spe...  16.1 us
    pallas_call x1, Pallas kernels, load(): pl.pallas_call(functools.partial(load_kernel, count), out_shape=[sds(w.sh...  3.2 us
  transfers between devices with their start and end apart: 27, of which 11 were waited for; matrix products, arithmetic and copies ran while one was open for 0% of the time, Pallas kernels for 26%

profile of v10, /device:TPU:0, one launch (start us, length us, event | category | flops | bytes accessed | tf_op | source)
XLA Modules:
  0.0 63.0 jit_solution(2974802669805716795)
XLA Ops:
  0.0 1.2 %shard_map.136 = (bf16[200,128]{1,0:T(8,128)(2,1)S(1)}, bf16[200,128]{1,0:T(8,128)(2,1)S(1)}, bf16[200,128]{1,0:T(8,128)(2,1)S(1)}, bf16[200,128]{1,0:T(8,128)(2,1)S(1)}) custom-call(bf16[2,160,128]{2,1,0:T(8,128)(2,1)} %bitcast.3, bf16[2,160,128]{2,1,0:T(8,128)(2,1)} %bitcast.4), custom_call_target="tpu_custom_call" | custom-call | tf_op jit(solution)/shard_map/pallas_call | solution.py:456
  1.2 3.1 %collective-permute-start = (bf16[200,128]{1,0:T(8,128)(2,1)S(1)}, bf16[200,128]{1,0:T(8,128)(2,1)S(1)}, u32[]{:S(2)}, u32[]{:S(2)}) collective-permute-start(bf16[200,128]{1,0:T(8,128)(2,1)S(1)} %get-tuple-element.30), channel_id=1, source_target_pairs={{0,2},{2,0},{4,6},{6,4},{1,3},{3,1},{5,7},{7,5},{8,10},{10,8},{12,... | collective-permute-start | bytes 153608 | tf_op jit(solution)/shard_map/ppermute | solution.py:25
  4.3 2.6 %collective-permute-start.1 = (bf16[200,128]{1,0:T(8,128)(2,1)S(1)}, bf16[200,128]{1,0:T(8,128)(2,1)S(1)}, u32[]{:S(2)}, u32[]{:S(2)}) collective-permute-start(bf16[200,128]{1,0:T(8,128)(2,1)S(1)} %get-tuple-element.31), channel_id=1, source_target_pairs={{0,4},{2,6},{4,0},{6,2},{1,5},{3,7},{5,1},{7,3},{8,12},{10,14},{12... | collective-permute-start | bytes 153608 | tf_op jit(solution)/shard_map/ppermute | solution.py:25
  6.9 3.4 %collective-permute-done.1.refs_2_ = bf16[200,128]{1,0:T(8,128)(2,1)S(1)} collective-permute-done((bf16[200,128]{1,0:T(8,128)(2,1)S(1)}, bf16[200,128]{1,0:T(8,128)(2,1)S(1)}, u32[]{:S(2)}, u32[]{:S(2)}) %collective-permute-start.1) | collective-permute-done | bytes 51232 | tf_op jit(solution)/shard_map/ppermute | solution.py:25
  10.3 2.5 %collective-permute-done.2.refs_3_ = bf16[200,128]{1,0:T(8,128)(2,1)S(1)} collective-permute-done((bf16[200,128]{1,0:T(8,128)(2,1)S(1)}, bf16[200,128]{1,0:T(8,128)(2,1)S(1)}, u32[]{:S(2)}, u32[]{:S(2)}) %collective-permute-start.2) | collective-permute-done | bytes 51232 | tf_op jit(solution)/shard_map/ppermute | solution.py:25
  12.8 0.5 shard_map.137
  13.3 1.5 %collective-permute-start.12 = (bf16[400,128]{1,0:T(8,128)(2,1)S(1)}, bf16[400,128]{1,0:T(8,128)(2,1)S(1)}, u32[]{:S(2)}, u32[]{:S(2)}) collective-permute-start(bf16[400,128]{1,0:T(8,128)(2,1)S(1)} %get-tuple-element.40.refs_0_), channel_id=1, source_target_pairs={{0,8},{8,0},{1,9},{9,1},{2,10},{10,2},{3,11},{11,3},{4,12},{12,4},... | collective-permute-start | bytes 307208 | tf_op jit(solution)/shard_map/ppermute | solution.py:25
  14.9 0.5 collective-permute-start.3
  15.4 2.6 %collective-permute-done.12.refs_0_ = bf16[400,128]{1,0:T(8,128)(2,1)S(1)} collective-permute-done((bf16[400,128]{1,0:T(8,128)(2,1)S(1)}, bf16[400,128]{1,0:T(8,128)(2,1)S(1)}, u32[]{:S(2)}, u32[]{:S(2)}) %collective-permute-start.12) | collective-permute-done | bytes 102432 | tf_op jit(solution)/shard_map/ppermute | solution.py:25
  18.0 0.5 collective-permute-start.5
  18.5 1.0 %collective-permute-done.3.refs_0_ = bf16[400,128]{1,0:T(8,128)(2,1)S(1)} collective-permute-done((bf16[400,128]{1,0:T(8,128)(2,1)S(1)}, bf16[400,128]{1,0:T(8,128)(2,1)S(1)}, u32[]{:S(2)}, u32[]{:S(2)}) %collective-permute-start.3) | collective-permute-done | bytes 102432 | tf_op jit(solution)/shard_map/ppermute | solution.py:25
  19.5 3.2 %shard_map.138 = (bf16[3,3,160,640]{3,2,1,0:T(8,128)(2,1)S(1)}, bf16[3,3,160,640]{3,2,1,0:T(8,128)(2,1)S(1)}, bf16[3,3,160,640]{3,2,1,0:T(8,128)(2,1)S(1)}, bf16[3,3,160,640]{3,2,1,0:T(8,128)(2,1)S(1)}) custom-call(bf16[3,3,160,640]{3,2,1,0:T(8,128)(2,1)} %refs_0_.1, bf16[3,3,160,640]{3,2,1,0:T(8,128)(2,1)} %refs_1_.1, bf16[3,3,160,640]{3,2,1,0:T(8,128)(2,1)} %refs_2_.6, ...), custom_call_target="tpu_custom_call" | custom-call | bytes 7372800 | tf_op jit(solution)/shard_map/pallas_call | solution.py:193
  22.7 0.8 %shard_map.143.refs_1_ = f32[320,160]{1,0:T(8,128)S(1)} custom-call(bf16[400,128]{1,0:T(8,128)(2,1)S(1)} %get-tuple-element.40.refs_0_, bf16[400,128]{1,0:T(8,128)(2,1)S(1)} %collective-permute-done.14.refs_1_, bf16[3,3,160,640]{3,2,1,0:T(8,128)(2,1)S(1)} %get-tuple-element.41.refs_2_), custom_call_target="tpu_custom_call" | custom-call | flops 294912000 | bytes 2252800 | tf_op jit(solution)/shard_map/pallas_call | solution.py:44
  23.6 0.5 shard_map.144.refs_1_
  24.2 0.8 %shard_map.145 = (bf16[320,160]{1,0:T(8,128)(2,1)S(1)}, bf16[384,128]{1,0:T(8,128)(2,1)S(1)}) custom-call(bf16[400,128]{1,0:T(8,128)(2,1)S(1)} %collective-permute-done.13.refs_0_, f32[320,160]{1,0:T(8,128)S(1)} %shard_map.144.refs_1_, bf16[3,3,160,640]{3,2,1,0:T(8,128)(2,1)S(1)} %get-tuple-element.41.refs_2_, ...), custom_call_target="tpu_custom_call" | custom-call | flops 147456000 | bytes 2453824 | tf_op jit(solution)/shard_map/pallas_call | solution.py:44
  25.0 1.1 %collective-permute-start.15 = (bf16[384,128]{1,0:T(8,128)(2,1)S(1)}, bf16[384,128]{1,0:T(8,128)(2,1)S(1)}, u32[]{:S(2)}, u32[]{:S(2)}) collective-permute-start(bf16[384,128]{1,0:T(8,128)(2,1)S(1)} %get-tuple-element.43.refs_0_), channel_id=1, source_target_pairs={{0,8},{8,0},{1,9},{9,1},{2,10},{10,2},{3,11},{11,3},{4,12},{12,4},... | collective-permute-start | bytes 294920 | tf_op jit(solution)/shard_map/ppermute | solution.py:25
  26.1 0.8 %shard_map.139.refs_2_ = f32[320,160]{1,0:T(8,128)S(1)} custom-call(bf16[400,128]{1,0:T(8,128)(2,1)S(1)} %get-tuple-element.33.refs_0_, bf16[400,128]{1,0:T(8,128)(2,1)S(1)} %collective-permute-done.5.refs_1_, bf16[3,3,160,640]{3,2,1,0:T(8,128)(2,1)S(1)} %get-tuple-element.34.refs_2_.refs_3_), custom_call_target="tpu_custom_call" | custom-call | flops 294912000 | bytes 2252800 | tf_op jit(solution)/shard_map/pallas_call | solution.py:44
  26.9 1.0 %shard_map.140 = (bf16[320,160]{1,0:T(8,128)(2,1)S(1)}, bf16[384,128]{1,0:T(8,128)(2,1)S(1)}) custom-call(bf16[400,128]{1,0:T(8,128)(2,1)S(1)} %collective-permute-done.3.refs_0_, bf16[400,128]{1,0:T(8,128)(2,1)S(1)} %collective-permute-done.4.refs_1_, f32[320,160]{1,0:T(8,128)S(1)} %shard_map.139.refs_2_, ...), custom_call_target="tpu_custom_call" | custom-call | flops 294912000 | bytes 2556224 | tf_op jit(solution)/shard_map/pallas_call | solution.py:44
  27.9 1.0 %collective-permute-start.6 = (bf16[384,128]{1,0:T(8,128)(2,1)S(1)}, bf16[384,128]{1,0:T(8,128)(2,1)S(1)}, u32[]{:S(2)}, u32[]{:S(2)}) collective-permute-start(bf16[384,128]{1,0:T(8,128)(2,1)S(1)} %get-tuple-element.36.refs_0_), channel_id=1, source_target_pairs={{0,8},{8,0},{1,9},{9,1},{2,10},{10,2},{3,11},{11,3},{4,12},{12,4},... | collective-permute-start | bytes 294920 | tf_op jit(solution)/shard_map/ppermute | solution.py:25
  28.9 1.3 %collective-permute-done.15.refs_0_ = bf16[384,128]{1,0:T(8,128)(2,1)S(1)} collective-permute-done((bf16[384,128]{1,0:T(8,128)(2,1)S(1)}, bf16[384,128]{1,0:T(8,128)(2,1)S(1)}, u32[]{:S(2)}, u32[]{:S(2)}) %collective-permute-start.15) | collective-permute-done | bytes 98336 | tf_op jit(solution)/shard_map/ppermute | solution.py:25
  30.2 0.5 collective-permute-start.8
  30.7 2.2 %collective-permute-done.6.refs_0_ = bf16[384,128]{1,0:T(8,128)(2,1)S(1)} collective-permute-done((bf16[384,128]{1,0:T(8,128)(2,1)S(1)}, bf16[384,128]{1,0:T(8,128)(2,1)S(1)}, u32[]{:S(2)}, u32[]{:S(2)}) %collective-permute-start.6) | collective-permute-done | bytes 98336 | tf_op jit(solution)/shard_map/ppermute | solution.py:25
  32.9 0.8 %shard_map.146.refs_1_ = f32[320,160]{1,0:T(8,128)S(1)} custom-call(bf16[384,128]{1,0:T(8,128)(2,1)S(1)} %get-tuple-element.43.refs_0_, bf16[384,128]{1,0:T(8,128)(2,1)S(1)} %collective-permute-done.17.refs_1_, bf16[3,3,160,640]{3,2,1,0:T(8,128)(2,1)S(1)} %get-tuple-element.44.refs_2_), custom_call_target="tpu_custom_call" | custom-call | flops 294912000 | bytes 2244608 | tf_op jit(solution)/shard_map/pallas_call | solution.py:44
  33.7 0.5 shard_map.147.refs_1_
  34.4 0.7 %shard_map.148.refs_0_ = bf16[360,128]{1,0:T(8,128)(2,1)S(1)} custom-call(bf16[384,128]{1,0:T(8,128)(2,1)S(1)} %collective-permute-done.16.refs_0_, f32[320,160]{1,0:T(8,128)S(1)} %shard_map.147.refs_1_, bf16[3,3,160,640]{3,2,1,0:T(8,128)(2,1)S(1)} %get-tuple-element.44.refs_2_, bf16[320,160]{1,0:T(8,128)(2,1)S(1)} %get-tuple-element.45.refs_3_, ...), custom_call_target="tpu_custom_call" | custom-call | flops 147456000 | bytes 2341184 | tf_op jit(solution)/shard_map/pallas_call | solution.py:44
  35.1 1.0 %collective-permute-start.18 = (bf16[360,128]{1,0:T(8,128)(2,1)S(1)}, bf16[360,128]{1,0:T(8,128)(2,1)S(1)}, u32[]{:S(2)}, u32[]{:S(2)}) collective-permute-start(bf16[360,128]{1,0:T(8,128)(2,1)S(1)} %shard_map.148.refs_0_), channel_id=1, source_target_pairs={{0,8},{8,0},{1,9},{9,1},{2,10},{10,2},{3,11},{11,3},{4,12},{12,4},... | collective-permute-start | bytes 276488 | tf_op jit(solution)/shard_map/ppermute | solution.py:25
  36.1 0.8 %shard_map.141.refs_2_ = f32[320,160]{1,0:T(8,128)S(1)} custom-call(bf16[384,128]{1,0:T(8,128)(2,1)S(1)} %get-tuple-element.36.refs_0_, bf16[384,128]{1,0:T(8,128)(2,1)S(1)} %collective-permute-done.8.refs_1_, bf16[3,3,160,640]{3,2,1,0:T(8,128)(2,1)S(1)} %get-tuple-element.37.refs_2_.refs_3_), custom_call_target="tpu_custom_call" | custom-call | flops 294912000 | bytes 2244608 | tf_op jit(solution)/shard_map/pallas_call | solution.py:44
  36.9 1.0 %shard_map.142 = (bf16[320,160]{1,0:T(8,128)(2,1)S(1)}, bf16[360,128]{1,0:T(8,128)(2,1)S(1)}) custom-call(bf16[384,128]{1,0:T(8,128)(2,1)S(1)} %collective-permute-done.6.refs_0_, bf16[384,128]{1,0:T(8,128)(2,1)S(1)} %collective-permute-done.7.refs_1_, f32[320,160]{1,0:T(8,128)S(1)} %shard_map.141.refs_2_, ...), custom_call_target="tpu_custom_call" | custom-call | flops 294912000 | bytes 2541888 | tf_op jit(solution)/shard_map/pallas_call | solution.py:44
  37.9 1.2 %collective-permute-start.9 = (bf16[360,128]{1,0:T(8,128)(2,1)S(1)}, bf16[360,128]{1,0:T(8,128)(2,1)S(1)}, u32[]{:S(2)}, u32[]{:S(2)}) collective-permute-start(bf16[360,128]{1,0:T(8,128)(2,1)S(1)} %get-tuple-element.39.refs_0_), channel_id=1, source_target_pairs={{0,8},{8,0},{1,9},{9,1},{2,10},{10,2},{3,11},{11,3},{4,12},{12,4},... | collective-permute-start | bytes 276488 | tf_op jit(solution)/shard_map/ppermute | solution.py:25
  39.1 1.1 %collective-permute-done.18.refs_0_.refs_2_ = bf16[360,128]{1,0:T(8,128)(2,1)S(1)} collective-permute-done((bf16[360,128]{1,0:T(8,128)(2,1)S(1)}, bf16[360,128]{1,0:T(8,128)(2,1)S(1)}, u32[]{:S(2)}, u32[]{:S(2)}) %collective-permute-start.18) | collective-permute-done | bytes 92192 | tf_op jit(solution)/shard_map/ppermute | solution.py:25
  40.2 0.5 collective-permute-start.11
  40.7 2.0 %collective-permute-done.9.refs_0_ = bf16[360,128]{1,0:T(8,128)(2,1)S(1)} collective-permute-done((bf16[360,128]{1,0:T(8,128)(2,1)S(1)}, bf16[360,128]{1,0:T(8,128)(2,1)S(1)}, u32[]{:S(2)}, u32[]{:S(2)}) %collective-permute-start.9) | collective-permute-done | bytes 92192 | tf_op jit(solution)/shard_map/ppermute | solution.py:25
  42.8 0.8 %shard_map.149.refs_2_ = f32[320,160]{1,0:T(8,128)S(1)} custom-call(bf16[360,128]{1,0:T(8,128)(2,1)S(1)} %shard_map.148.refs_0_, bf16[360,128]{1,0:T(8,128)(2,1)S(1)} %collective-permute-done.20.refs_1_, bf16[3,3,160,1280]{3,2,1,0:T(8,128)(2,1)S(1)} %copy-done), custom_call_target="tpu_custom_call" | custom-call | flops 294912000 | bytes 4075520 | tf_op jit(solution)/shard_map/pallas_call | solution.py:44
  43.6 0.8 %shard_map.150.refs_2_ = f32[320,160]{1,0:T(8,128)S(1)} custom-call(bf16[360,128]{1,0:T(8,128)(2,1)S(1)} %collective-permute-done.18.refs_0_.refs_2_, bf16[360,128]{1,0:T(8,128)(2,1)S(1)} %collective-permute-done.19.refs_1_.refs_3_, f32[320,160]{1,0:T(8,128)S(1)} %shard_map.149.refs_2_, bf16[3,3,160,1280]{3,2,1,0:T(8,128)(2,1)S(1)} %copy-done), custom_call_target="tpu_custom_call" | custom-call | flops 294912000 | bytes 4280320 | tf_op jit(solution)/shard_map/pallas_call | solution.py:44
  44.4 0.8 %shard_map.151.refs_1_ = f32[320,160]{1,0:T(8,128)S(1)} custom-call(bf16[360,128]{1,0:T(8,128)(2,1)S(1)} %get-tuple-element.39.refs_0_, bf16[360,128]{1,0:T(8,128)(2,1)S(1)} %collective-permute-done.11.refs_1_, f32[320,160]{1,0:T(8,128)S(1)} %shard_map.150.refs_2_, bf16[3,3,160,1280]{3,2,1,0:T(8,128)(2,1)S(1)} %copy-done), custom_call_target="tpu_custom_call" | custom-call | flops 294912000 | bytes 4280320 | tf_op jit(solution)/shard_map/pallas_call | solution.py:44
  45.2 0.5 shard_map.152.refs_1_
  45.9 0.7 %shard_map.153 = (bf16[320,160]{1,0:T(8,128)(2,1)S(1)}, bf16[344,128]{1,0:T(8,128)(2,1)S(1)}) custom-call(bf16[360,128]{1,0:T(8,128)(2,1)S(1)} %collective-permute-done.10.refs_0_, f32[320,160]{1,0:T(8,128)S(1)} %shard_map.152.refs_1_, bf16[3,3,160,1280]{3,2,1,0:T(8,128)(2,1)S(1)} %copy-done, bf16[320,160]{1,0:T(8,128)(2,1)S(1)} %get-tuple-element.46.refs_3_, ...), custom_call_target="tpu_custom_call" | custom-call | flops 147456000 | bytes 4276544 | tf_op jit(solution)/shard_map/pallas_call | solution.py:44
  46.6 1.1 %collective-permute-start.21 = (bf16[344,128]{1,0:T(8,128)(2,1)S(1)}, bf16[344,128]{1,0:T(8,128)(2,1)S(1)}, u32[]{:S(2)}, u32[]{:S(2)}) collective-permute-start(bf16[344,128]{1,0:T(8,128)(2,1)S(1)} %get-tuple-element.47.refs_0_), channel_id=1, source_target_pairs={{0,8},{8,0},{1,9},{9,1},{2,10},{10,2},{3,11},{11,3},{4,12},{12,4},... | collective-permute-start | bytes 264200 | tf_op jit(solution)/shard_map/ppermute | solution.py:25
  48.0 3.7 %collective-permute-done.21.refs_0_ = bf16[344,128]{1,0:T(8,128)(2,1)S(1)} collective-permute-done((bf16[344,128]{1,0:T(8,128)(2,1)S(1)}, bf16[344,128]{1,0:T(8,128)(2,1)S(1)}, u32[]{:S(2)}, u32[]{:S(2)}) %collective-permute-start.21) | collective-permute-done | bytes 88096 | tf_op jit(solution)/shard_map/ppermute | solution.py:25
  51.7 1.3 %shard_map.154.refs_2_ = f32[320,160]{1,0:T(8,128)S(1)} custom-call(bf16[360,128]{1,0:T(8,128)(2,1)S(1)} %shard_map.148.refs_0_, bf16[360,128]{1,0:T(8,128)(2,1)S(1)} %collective-permute-done.20.refs_1_, bf16[360,128]{1,0:T(8,128)(2,1)S(1)} %collective-permute-done.18.refs_0_.refs_2_, bf16[360,128]{1,0:T(8,128)(2,1)S(1)} %collective-permute-done.19.refs_1_.refs_3_, ...), custom_call_target="tpu_custom_call" | custom-call | flops 589824000 | bytes 4259840 | tf_op jit(solution)/shard_map/pallas_call | solution.py:44
  53.0 0.8 %shard_map.155.refs_1_ = f32[320,160]{1,0:T(8,128)S(1)} custom-call(bf16[344,128]{1,0:T(8,128)(2,1)S(1)} %get-tuple-element.47.refs_0_, bf16[344,128]{1,0:T(8,128)(2,1)S(1)} %collective-permute-done.23.refs_1_, f32[320,160]{1,0:T(8,128)S(1)} %shard_map.154.refs_2_, bf16[3,3,160,1280]{3,2,1,0:T(8,128)(2,1)S(1)} %copy-done.1), custom_call_target="tpu_custom_call" | custom-call | flops 294912000 | bytes 4272128 | tf_op jit(solution)/shard_map/pallas_call | solution.py:44
  53.8 0.5 shard_map.156.refs_1_
  54.5 0.6 %shard_map.157 = (bf16[80,128]{1,0:T(8,128)(2,1)S(1)}, bf16[80,128]{1,0:T(8,128)(2,1)S(1)}, bf16[80,128]{1,0:T(8,128)(2,1)S(1)}, bf16[80,128]{1,0:T(8,128)(2,1)S(1)}) custom-call(bf16[344,128]{1,0:T(8,128)(2,1)S(1)} %collective-permute-done.22.refs_0_, f32[320,160]{1,0:T(8,128)S(1)} %shard_map.156.refs_1_, bf16[3,3,160,1280]{3,2,1,0:T(8,128)(2,1)S(1)} %copy-done.1, ...), custom_call_target="tpu_custom_call" | custom-call | flops 147456000 | bytes 4163904 | tf_op jit(solution)/shard_map/pallas_call | solution.py:44
  55.2 1.4 %collective-permute-start.25 = (bf16[80,128]{1,0:T(8,128)(2,1)S(1)}, bf16[80,128]{1,0:T(8,128)(2,1)S(1)}, u32[]{:S(2)}, u32[]{:S(2)}) collective-permute-start(bf16[80,128]{1,0:T(8,128)(2,1)S(1)} %get-tuple-element.51), channel_id=1, source_target_pairs={{0,4},{2,6},{4,0},{6,2},{1,5},{3,7},{5,1},{7,3},{8,12},{10,14},{12... | collective-permute-start | bytes 61448 | tf_op jit(solution)/shard_map/ppermute | solution.py:25
  56.6 3.0 %collective-permute-start.26 = (bf16[80,128]{1,0:T(8,128)(2,1)S(1)}, bf16[80,128]{1,0:T(8,128)(2,1)S(1)}, u32[]{:S(2)}, u32[]{:S(2)}) collective-permute-start(bf16[80,128]{1,0:T(8,128)(2,1)S(1)} %get-tuple-element.52), channel_id=1, source_target_pairs={{0,6},{2,4},{4,2},{6,0},{1,7},{3,5},{5,3},{7,1},{8,14},{10,12},{12... | collective-permute-start | bytes 61448 | tf_op jit(solution)/shard_map/ppermute | solution.py:25
  59.6 0.5 collective-permute-done.25.refs_2_
  60.1 2.1 %collective-permute-done.26.refs_3_ = bf16[80,128]{1,0:T(8,128)(2,1)S(1)} collective-permute-done((bf16[80,128]{1,0:T(8,128)(2,1)S(1)}, bf16[80,128]{1,0:T(8,128)(2,1)S(1)}, u32[]{:S(2)}, u32[]{:S(2)}) %collective-permute-start.26) | collective-permute-done | bytes 20512 | tf_op jit(solution)/shard_map/ppermute | solution.py:25
  62.2 0.8 %shard_map.158 = bf16[2,160,128]{2,1,0:T(8,128)(2,1)} custom-call(bf16[80,128]{1,0:T(8,128)(2,1)S(1)} %get-tuple-element.49.refs_0_, bf16[80,128]{1,0:T(8,128)(2,1)S(1)} %collective-permute-done.24.refs_1_, bf16[80,128]{1,0:T(8,128)(2,1)S(1)} %collective-permute-done.25.refs_2_, bf16[80,128]{1,0:T(8,128)(2,1)S(1)} %collective-permute-done.26.refs_3_), custom_call_target="tpu_custom_call" | custom-call | bytes 163840 | tf_op jit(solution)/shard_map/pallas_call | solution.py:44
  (45 shorter events, 0.8 us)
Async XLA Ops:
  1.2 5.7 %collective-permute-start = (bf16[200,128]{1,0:T(8,128)(2,1)S(1)}, bf16[200,128]{1,0:T(8,128)(2,1)S(1)}, u32[]{:S(2)}, u32[]{:S(2)}) collective-permute-start(bf16[200,128]{1,0:T(8,128)(2,1)S(1)} %get-tuple-element.30), channel_id=1, source_target_pairs={{0,2},{2,0},{4,6},{6,4},{1,3},{3,1},{5,7},{7,5},{8,10},{10,8},{12,... | collective-permute-start | bytes 153608 | tf_op jit(solution)/shard_map/ppermute | solution.py:25
  4.3 6.0 %collective-permute-start.1 = (bf16[200,128]{1,0:T(8,128)(2,1)S(1)}, bf16[200,128]{1,0:T(8,128)(2,1)S(1)}, u32[]{:S(2)}, u32[]{:S(2)}) collective-permute-start(bf16[200,128]{1,0:T(8,128)(2,1)S(1)} %get-tuple-element.31), channel_id=1, source_target_pairs={{0,4},{2,6},{4,0},{6,2},{1,5},{3,7},{5,1},{7,3},{8,12},{10,14},{12... | collective-permute-start | bytes 153608 | tf_op jit(solution)/shard_map/ppermute | solution.py:25
  6.9 5.9 %collective-permute-start.2 = (bf16[200,128]{1,0:T(8,128)(2,1)S(1)}, bf16[200,128]{1,0:T(8,128)(2,1)S(1)}, u32[]{:S(2)}, u32[]{:S(2)}) collective-permute-start(bf16[200,128]{1,0:T(8,128)(2,1)S(1)} %get-tuple-element.32), channel_id=1, source_target_pairs={{0,6},{2,4},{4,2},{6,0},{1,7},{3,5},{5,3},{7,1},{8,14},{10,12},{12... | collective-permute-start | bytes 153608 | tf_op jit(solution)/shard_map/ppermute | solution.py:25
  13.3 4.7 %collective-permute-start.12 = (bf16[400,128]{1,0:T(8,128)(2,1)S(1)}, bf16[400,128]{1,0:T(8,128)(2,1)S(1)}, u32[]{:S(2)}, u32[]{:S(2)}) collective-permute-start(bf16[400,128]{1,0:T(8,128)(2,1)S(1)} %get-tuple-element.40.refs_0_), channel_id=1, source_target_pairs={{0,8},{8,0},{1,9},{9,1},{2,10},{10,2},{3,11},{11,3},{4,12},{12,4},... | collective-permute-start | bytes 307208 | tf_op jit(solution)/shard_map/ppermute | solution.py:25
  14.9 4.7 %collective-permute-start.3 = (bf16[400,128]{1,0:T(8,128)(2,1)S(1)}, bf16[400,128]{1,0:T(8,128)(2,1)S(1)}, u32[]{:S(2)}, u32[]{:S(2)}) collective-permute-start(bf16[400,128]{1,0:T(8,128)(2,1)S(1)} %get-tuple-element.33.refs_0_), channel_id=1, source_target_pairs={{0,8},{8,0},{1,9},{9,1},{2,10},{10,2},{3,11},{11,3},{4,12},{12,4},... | collective-permute-start | bytes 307208 | tf_op jit(solution)/shard_map/ppermute | solution.py:25
  15.4 7.3 %collective-permute-start.14 = (bf16[400,128]{1,0:T(8,128)(2,1)S(1)}, bf16[400,128]{1,0:T(8,128)(2,1)S(1)}, u32[]{:S(2)}, u32[]{:S(2)}) collective-permute-start(bf16[400,128]{1,0:T(8,128)(2,1)S(1)} %get-tuple-element.40.refs_0_), channel_id=1, source_target_pairs={{0,1},{1,0},{2,3},{3,2},{4,5},{5,4},{6,7},{7,6},{8,9},{9,8},{10,11... | collective-permute-start | bytes 307208 | tf_op jit(solution)/shard_map/ppermute | solution.py:25
  18.0 6.1 %collective-permute-start.13 = (bf16[400,128]{1,0:T(8,128)(2,1)S(1)}, bf16[400,128]{1,0:T(8,128)(2,1)S(1)}, u32[]{:S(2)}, u32[]{:S(2)}) collective-permute-start(bf16[400,128]{1,0:T(8,128)(2,1)S(1)} %collective-permute-done.12.refs_0_), channel_id=1, source_target_pairs={{0,1},{1,0},{2,3},{3,2},{4,5},{5,4},{6,7},{7,6},{8,9},{9,8},{10,11... | collective-permute-start | bytes 307208 | tf_op jit(solution)/shard_map/ppermute | solution.py:25
  18.0 8.1 %collective-permute-start.5 = (bf16[400,128]{1,0:T(8,128)(2,1)S(1)}, bf16[400,128]{1,0:T(8,128)(2,1)S(1)}, u32[]{:S(2)}, u32[]{:S(2)}) collective-permute-start(bf16[400,128]{1,0:T(8,128)(2,1)S(1)} %get-tuple-element.33.refs_0_), channel_id=1, source_target_pairs={{0,1},{1,0},{2,3},{3,2},{4,5},{5,4},{6,7},{7,6},{8,9},{9,8},{10,11... | collective-permute-start | bytes 307208 | tf_op jit(solution)/shard_map/ppermute | solution.py:25
  19.5 7.4 %collective-permute-start.4 = (bf16[400,128]{1,0:T(8,128)(2,1)S(1)}, bf16[400,128]{1,0:T(8,128)(2,1)S(1)}, u32[]{:S(2)}, u32[]{:S(2)}) collective-permute-start(bf16[400,128]{1,0:T(8,128)(2,1)S(1)} %collective-permute-done.3.refs_0_), channel_id=1, source_target_pairs={{0,1},{1,0},{2,3},{3,2},{4,5},{5,4},{6,7},{7,6},{8,9},{9,8},{10,11... | collective-permute-start | bytes 307208 | tf_op jit(solution)/shard_map/ppermute | solution.py:25
  23.6 0.7 %copy-start.5 = (bf16[160]{0:T(256)(128)(2,1)S(1)}, bf16[160]{0:T(256)(128)(2,1)}, u32[]{:S(2)}) copy-start(bf16[160]{0:T(256)(128)(2,1)} %refs_4_.5) | copy-start | bytes 964
  24.2 2.7 %copy-start.6 = (bf16[160]{0:T(256)(128)(2,1)S(1)}, bf16[160]{0:T(256)(128)(2,1)}, u32[]{:S(2)}) copy-start(bf16[160]{0:T(256)(128)(2,1)} %refs_5_.2) | copy-start | bytes 964
  25.0 5.2 %collective-permute-start.15 = (bf16[384,128]{1,0:T(8,128)(2,1)S(1)}, bf16[384,128]{1,0:T(8,128)(2,1)S(1)}, u32[]{:S(2)}, u32[]{:S(2)}) collective-permute-start(bf16[384,128]{1,0:T(8,128)(2,1)S(1)} %get-tuple-element.43.refs_0_), channel_id=1, source_target_pairs={{0,8},{8,0},{1,9},{9,1},{2,10},{10,2},{3,11},{11,3},{4,12},{12,4},... | collective-permute-start | bytes 294920 | tf_op jit(solution)/shard_map/ppermute | solution.py:25
  27.9 5.0 %collective-permute-start.6 = (bf16[384,128]{1,0:T(8,128)(2,1)S(1)}, bf16[384,128]{1,0:T(8,128)(2,1)S(1)}, u32[]{:S(2)}, u32[]{:S(2)}) collective-permute-start(bf16[384,128]{1,0:T(8,128)(2,1)S(1)} %get-tuple-element.36.refs_0_), channel_id=1, source_target_pairs={{0,8},{8,0},{1,9},{9,1},{2,10},{10,2},{3,11},{11,3},{4,12},{12,4},... | collective-permute-start | bytes 294920 | tf_op jit(solution)/shard_map/ppermute | solution.py:25
  28.9 4.0 %collective-permute-start.17 = (bf16[384,128]{1,0:T(8,128)(2,1)S(1)}, bf16[384,128]{1,0:T(8,128)(2,1)S(1)}, u32[]{:S(2)}, u32[]{:S(2)}) collective-permute-start(bf16[384,128]{1,0:T(8,128)(2,1)S(1)} %get-tuple-element.43.refs_0_), channel_id=1, source_target_pairs={{0,1},{1,0},{2,3},{3,2},{4,5},{5,4},{6,7},{7,6},{8,9},{9,8},{10,11... | collective-permute-start | bytes 294920 | tf_op jit(solution)/shard_map/ppermute | solution.py:25
  30.2 4.1 %collective-permute-start.16 = (bf16[384,128]{1,0:T(8,128)(2,1)S(1)}, bf16[384,128]{1,0:T(8,128)(2,1)S(1)}, u32[]{:S(2)}, u32[]{:S(2)}) collective-permute-start(bf16[384,128]{1,0:T(8,128)(2,1)S(1)} %collective-permute-done.15.refs_0_), channel_id=1, source_target_pairs={{0,1},{1,0},{2,3},{3,2},{4,5},{5,4},{6,7},{7,6},{8,9},{9,8},{10,11... | collective-permute-start | bytes 294920 | tf_op jit(solution)/shard_map/ppermute | solution.py:25
  30.2 5.9 %collective-permute-start.8 = (bf16[384,128]{1,0:T(8,128)(2,1)S(1)}, bf16[384,128]{1,0:T(8,128)(2,1)S(1)}, u32[]{:S(2)}, u32[]{:S(2)}) collective-permute-start(bf16[384,128]{1,0:T(8,128)(2,1)S(1)} %get-tuple-element.36.refs_0_), channel_id=1, source_target_pairs={{0,1},{1,0},{2,3},{3,2},{4,5},{5,4},{6,7},{7,6},{8,9},{9,8},{10,11... | collective-permute-start | bytes 294920 | tf_op jit(solution)/shard_map/ppermute | solution.py:25
  32.9 4.0 %collective-permute-start.7 = (bf16[384,128]{1,0:T(8,128)(2,1)S(1)}, bf16[384,128]{1,0:T(8,128)(2,1)S(1)}, u32[]{:S(2)}, u32[]{:S(2)}) collective-permute-start(bf16[384,128]{1,0:T(8,128)(2,1)S(1)} %collective-permute-done.6.refs_0_), channel_id=1, source_target_pairs={{0,1},{1,0},{2,3},{3,2},{4,5},{5,4},{6,7},{7,6},{8,9},{9,8},{10,11... | collective-permute-start | bytes 294920 | tf_op jit(solution)/shard_map/ppermute | solution.py:25
  33.7 0.7 %copy-start.2 = (bf16[160]{0:T(256)(128)(2,1)S(1)}, bf16[160]{0:T(256)(128)(2,1)}, u32[]{:S(2)}) copy-start(bf16[160]{0:T(256)(128)(2,1)} %refs_4_.6) | copy-start | bytes 964
  34.4 2.5 %copy-start.7 = (bf16[160]{0:T(256)(128)(2,1)S(1)}, bf16[160]{0:T(256)(128)(2,1)}, u32[]{:S(2)}) copy-start(bf16[160]{0:T(256)(128)(2,1)} %refs_5_.3) | copy-start | bytes 964
  35.1 5.1 %collective-permute-start.18 = (bf16[360,128]{1,0:T(8,128)(2,1)S(1)}, bf16[360,128]{1,0:T(8,128)(2,1)S(1)}, u32[]{:S(2)}, u32[]{:S(2)}) collective-permute-start(bf16[360,128]{1,0:T(8,128)(2,1)S(1)} %shard_map.148.refs_0_), channel_id=1, source_target_pairs={{0,8},{8,0},{1,9},{9,1},{2,10},{10,2},{3,11},{11,3},{4,12},{12,4},... | collective-permute-start | bytes 276488 | tf_op jit(solution)/shard_map/ppermute | solution.py:25
  36.1 6.7 %copy-start = (bf16[3,3,160,1280]{3,2,1,0:T(8,128)(2,1)S(1)}, bf16[3,3,160,1280]{3,2,1,0:T(8,128)(2,1)}, u32[]{:S(2)}) copy-start(bf16[3,3,160,1280]{3,2,1,0:T(8,128)(2,1)} %refs_2_.9) | copy-start | bytes 11059204
  37.9 4.8 %collective-permute-start.9 = (bf16[360,128]{1,0:T(8,128)(2,1)S(1)}, bf16[360,128]{1,0:T(8,128)(2,1)S(1)}, u32[]{:S(2)}, u32[]{:S(2)}) collective-permute-start(bf16[360,128]{1,0:T(8,128)(2,1)S(1)} %get-tuple-element.39.refs_0_), channel_id=1, source_target_pairs={{0,8},{8,0},{1,9},{9,1},{2,10},{10,2},{3,11},{11,3},{4,12},{12,4},... | collective-permute-start | bytes 276488 | tf_op jit(solution)/shard_map/ppermute | solution.py:25
  39.1 3.7 %collective-permute-start.20 = (bf16[360,128]{1,0:T(8,128)(2,1)S(1)}, bf16[360,128]{1,0:T(8,128)(2,1)S(1)}, u32[]{:S(2)}, u32[]{:S(2)}) collective-permute-start(bf16[360,128]{1,0:T(8,128)(2,1)S(1)} %shard_map.148.refs_0_), channel_id=1, source_target_pairs={{0,1},{1,0},{2,3},{3,2},{4,5},{5,4},{6,7},{7,6},{8,9},{9,8},{10,11... | collective-permute-start | bytes 276488 | tf_op jit(solution)/shard_map/ppermute | solution.py:25
  40.2 3.4 %collective-permute-start.19 = (bf16[360,128]{1,0:T(8,128)(2,1)S(1)}, bf16[360,128]{1,0:T(8,128)(2,1)S(1)}, u32[]{:S(2)}, u32[]{:S(2)}) collective-permute-start(bf16[360,128]{1,0:T(8,128)(2,1)S(1)} %collective-permute-done.18.refs_0_.refs_2_), channel_id=1, source_target_pairs={{0,1},{1,0},{2,3},{3,2},{4,5},{5,4},{6,7},{7,6},{8,9},{9,8},{10,11... | collective-permute-start | bytes 276488 | tf_op jit(solution)/shard_map/ppermute | solution.py:25
  40.2 4.2 %collective-permute-start.11 = (bf16[360,128]{1,0:T(8,128)(2,1)S(1)}, bf16[360,128]{1,0:T(8,128)(2,1)S(1)}, u32[]{:S(2)}, u32[]{:S(2)}) collective-permute-start(bf16[360,128]{1,0:T(8,128)(2,1)S(1)} %get-tuple-element.39.refs_0_), channel_id=1, source_target_pairs={{0,1},{1,0},{2,3},{3,2},{4,5},{5,4},{6,7},{7,6},{8,9},{9,8},{10,11... | collective-permute-start | bytes 276488 | tf_op jit(solution)/shard_map/ppermute | solution.py:25
  42.8 3.0 %collective-permute-start.10 = (bf16[360,128]{1,0:T(8,128)(2,1)S(1)}, bf16[360,128]{1,0:T(8,128)(2,1)S(1)}, u32[]{:S(2)}, u32[]{:S(2)}) collective-permute-start(bf16[360,128]{1,0:T(8,128)(2,1)S(1)} %collective-permute-done.9.refs_0_), channel_id=1, source_target_pairs={{0,1},{1,0},{2,3},{3,2},{4,5},{5,4},{6,7},{7,6},{8,9},{9,8},{10,11... | collective-permute-start | bytes 276488 | tf_op jit(solution)/shard_map/ppermute | solution.py:25
  45.2 0.7 %copy-start.3 = (bf16[160]{0:T(256)(128)(2,1)S(1)}, bf16[160]{0:T(256)(128)(2,1)}, u32[]{:S(2)}) copy-start(bf16[160]{0:T(256)(128)(2,1)} %refs_4_.7) | copy-start | bytes 964
  45.9 5.8 %copy-start.1 = (bf16[3,3,160,1280]{3,2,1,0:T(8,128)(2,1)S(1)}, bf16[3,3,160,1280]{3,2,1,0:T(8,128)(2,1)}, u32[]{:S(2)}) copy-start(bf16[3,3,160,1280]{3,2,1,0:T(8,128)(2,1)} %refs_2_.11) | copy-start | bytes 11059204
  46.6 5.0 %collective-permute-start.21 = (bf16[344,128]{1,0:T(8,128)(2,1)S(1)}, bf16[344,128]{1,0:T(8,128)(2,1)S(1)}, u32[]{:S(2)}, u32[]{:S(2)}) collective-permute-start(bf16[344,128]{1,0:T(8,128)(2,1)S(1)} %get-tuple-element.47.refs_0_), channel_id=1, source_target_pairs={{0,8},{8,0},{1,9},{9,1},{2,10},{10,2},{3,11},{11,3},{4,12},{12,4},... | collective-permute-start | bytes 264200 | tf_op jit(solution)/shard_map/ppermute | solution.py:25
  47.8 5.2 %collective-permute-start.23 = (bf16[344,128]{1,0:T(8,128)(2,1)S(1)}, bf16[344,128]{1,0:T(8,128)(2,1)S(1)}, u32[]{:S(2)}, u32[]{:S(2)}) collective-permute-start(bf16[344,128]{1,0:T(8,128)(2,1)S(1)} %get-tuple-element.47.refs_0_), channel_id=1, source_target_pairs={{0,1},{1,0},{2,3},{3,2},{4,5},{5,4},{6,7},{7,6},{8,9},{9,8},{10,11... | collective-permute-start | bytes 264200 | tf_op jit(solution)/shard_map/ppermute | solution.py:25
  51.7 2.7 %collective-permute-start.22 = (bf16[344,128]{1,0:T(8,128)(2,1)S(1)}, bf16[344,128]{1,0:T(8,128)(2,1)S(1)}, u32[]{:S(2)}, u32[]{:S(2)}) collective-permute-start(bf16[344,128]{1,0:T(8,128)(2,1)S(1)} %collective-permute-done.21.refs_0_), channel_id=1, source_target_pairs={{0,1},{1,0},{2,3},{3,2},{4,5},{5,4},{6,7},{7,6},{8,9},{9,8},{10,11... | collective-permute-start | bytes 264200 | tf_op jit(solution)/shard_map/ppermute | solution.py:25
  53.8 0.7 %copy-start.4 = (bf16[160]{0:T(256)(128)(2,1)S(1)}, bf16[160]{0:T(256)(128)(2,1)}, u32[]{:S(2)}) copy-start(bf16[160]{0:T(256)(128)(2,1)} %refs_4_.9) | copy-start | bytes 964
  55.1 4.5 %collective-permute-start.24 = (bf16[80,128]{1,0:T(8,128)(2,1)S(1)}, bf16[80,128]{1,0:T(8,128)(2,1)S(1)}, u32[]{:S(2)}, u32[]{:S(2)}) collective-permute-start(bf16[80,128]{1,0:T(8,128)(2,1)S(1)} %get-tuple-element.50), channel_id=1, source_target_pairs={{0,2},{2,0},{4,6},{6,4},{1,3},{3,1},{5,7},{7,5},{8,10},{10,8},{12,... | collective-permute-start | bytes 61448 | tf_op jit(solution)/shard_map/ppermute | solution.py:25
  55.2 4.9 %collective-permute-start.25 = (bf16[80,128]{1,0:T(8,128)(2,1)S(1)}, bf16[80,128]{1,0:T(8,128)(2,1)S(1)}, u32[]{:S(2)}, u32[]{:S(2)}) collective-permute-start(bf16[80,128]{1,0:T(8,128)(2,1)S(1)} %get-tuple-element.51), channel_id=1, source_target_pairs={{0,4},{2,6},{4,0},{6,2},{1,5},{3,7},{5,1},{7,3},{8,12},{10,14},{12... | collective-permute-start | bytes 61448 | tf_op jit(solution)/shard_map/ppermute | solution.py:25
  56.6 5.6 %collective-permute-start.26 = (bf16[80,128]{1,0:T(8,128)(2,1)S(1)}, bf16[80,128]{1,0:T(8,128)(2,1)S(1)}, u32[]{:S(2)}, u32[]{:S(2)}) collective-permute-start(bf16[80,128]{1,0:T(8,128)(2,1)S(1)} %get-tuple-element.52), channel_id=1, source_target_pairs={{0,6},{2,4},{4,2},{6,0},{1,7},{3,5},{5,3},{7,1},{8,14},{10,12},{12... | collective-permute-start | bytes 61448 | tf_op jit(solution)/shard_map/ppermute | solution.py:25

commit v11 on v10

--- a/solution.py
+++ b/solution.py
@@ -207,30 +207,28 @@
     return [(at, min(LANES, z.per - at)) for at in range(0, z.per, LANES)]
 
 
-def join_kernel(z, *refs):
-    blocks, (*states, act_zero, act_one, image, block_image) = refs[: z.bands], refs[z.bands :]
-    acts = (act_zero, act_one)
+def join_kernel(z, t, *refs):
+    blocks, (state_ref, act_ref, image, block_image) = refs[: z.bands], refs[z.bands :]
     band = lax.axis_index("band")
     size = z.rows * z.wide
 
     def put(row, lane, piece):
         rows, lanes = piece.shape
         group, lane = lane // LANES, lane % LANES
-        block_image[group, row : row + rows, lane : lane + lanes] = piece
+        if t * size < row + rows and row < (t + 1) * size:
+            block_image[group, row : row + rows, lane : lane + lanes] = piece
 
     for k, block in enumerate(blocks):
         unpack(z, 2 * size, block[...].astype(F32), put)
-        for t in range(2):
-            for row in range(z.rows):
-                to = pl.ds((band ^ k) * z.rows + row, z.wide, stride=z.height)
-                at = t * size + row * z.wide
-                for g in range(len(lane_groups(z))):
-                    image[t, g, to] = block_image[g, at : at + z.wide]
-    for t in range(2):
-        parts = [image[t, g][:, :n] for g, (_, n) in enumerate(lane_groups(z))]
-        value = jnp.concatenate(parts, axis=1)
-        states[t][...] = value.astype(BF16)
-        pack(z, acts[t], masked_silu(z, value), roll=True)
+        for row in range(z.rows):
+            to = pl.ds((band ^ k) * z.rows + row, z.wide, stride=z.height)
+            at = t * size + row * z.wide
+            for g in range(len(lane_groups(z))):
+                image[g, to] = block_image[g, at : at + z.wide]
+    parts = [image[g][:, :n] for g, (_, n) in enumerate(lane_groups(z))]
+    value = jnp.concatenate(parts, axis=1)
+    state_ref[...] = value.astype(BF16)
+    pack(z, act_ref, masked_silu(z, value), roll=True)
 
 
 def place(z, trim, a_ref, at, message, distance):
@@ -466,21 +464,29 @@
         compiler_params=pltpu.CompilerParams(vmem_limit_bytes=4 << 20),
     )(in_hbm(latent.swapaxes(1, 2)), in_hbm(control_hint.swapaxes(1, 2)))
     blocks = over_bands(blocks)
-    cw1, mw1, cw2, mw2 = load(cw1, mw1, cw2, mw2)
-    *states, control, main = call(
-        kernel(join_kernel),
-        [single, single, sds(message(0)), sds(message(0))],
-        *blocks,
-        scratch=[
-            pltpu.VMEM((2, groups, z.cells, LANES), F32),
-            pltpu.VMEM((groups, 2 * z.rows * z.wide, LANES), F32),
-        ],
-    )
-
-    def convolution(step, received, w, base, outs, end=None, rest=(), sums=(), extra=()):
+    cw1, mw1 = load(cw1, mw1)
+    joined = []
+    for t in range(2):
+        joined.append(
+            call(
+                kernel(join_kernel, t),
+                [single, sds(message(0))],
+                *blocks,
+                scratch=[
+                    pltpu.VMEM((groups, z.cells, LANES), F32),
+                    pltpu.VMEM((groups, 2 * z.rows * z.wide, LANES), F32),
+                ],
+            )
+        )
+    states = [state for state, _ in joined]
+    control, main = [act for _, act in joined]
+
+    def convolution(step, received, w, base, outs, end=None, rest=(), late=(), extra=()):
         received = [(names, pieces) for names, pieces in received if names]
+        sums = ()
         for at, (names, pieces) in enumerate(received):
             ends = at == len(received) - 1
+            sums += late if ends else ()
             result = call(
                 kernel(block_kernel, step, base, names, len(sums), end if ends else None),
                 outs if ends else total,
@@ -503,14 +509,14 @@
             states[0], control = convolution(step, received, cw, 0, outs, close_layer, rest)
         else:
             control = convolution(step, received, cw, 0, outs[1], close_control, rest)
-        received = late_together(gather(main))
+        received = gather(main)
         rest = (states[1], mb)
         states[1], main = convolution(step, received, mw, 0, outs, close_layer, rest)
     skip = gather(control)
     first = convolution(2, late_together(skip), dw1, z.depth, total)
     outs = [single, sds(message(3))]
     rest = (states[1], db1)
-    state, act = convolution(2, gather(main), dw1, 0, outs, close_layer, rest, sums=(first,))
+    state, act = convolution(2, gather(main), dw1, 0, outs, close_layer, rest, late=(first,))
     every = together(skip)
     part = convolution(2, [every], dw2, z.depth, total)
     blocks = convolution(
@@ -521,7 +527,7 @@
         [sds(z.packed(z.rows * z.columns))] * z.bands,
         close_image,
         (state, db2),
-        sums=(part,),
+        late=(part,),
         extra=[pltpu.VMEM((groups, z.cells, LANES), F32)],
     )
     out = call(

time: 63.2 us -> 63.8 us (level)
  local copies, waits for them, and re-layouts: 0.41 us -> 1.07 us
    pallas_call x1, Pallas kernels: 3.2 us -> 2.07 us  [load(): pl.pallas_call(functools.partial(load_kernel, count), out_shape=[sds(w.sh...]
    pallas_call x21 -> x24, Pallas kernels: 16.1 us -> 16.9 us  [call(): pl.pallas_call(kernel, out_shape=outs, in_specs=whole(len(args)), out_spe...]
    unnamed x16 -> x20, local copies, waits for them, and re-layouts: 0.41 us -> 1.07 us
where the time goes in v11:
time: 63.8 us; the launch traced here: 63.6 us
  waiting for transfers between devices  22.6 us (35%)
  Pallas kernels  20.2 us (32%)
  starting transfers between devices  19.4 us (30%)
  local copies, waits for them, and re-layouts  1.07 us (2%)
    ppermute x27, waiting for transfers between devices, exchange(): return lax.ppermute(cells, axis, [(i, i ^ distance) for i in range(count)])  22.6 us
    ppermute x27, starting transfers between devices, exchange(): return lax.ppermute(cells, axis, [(i, i ^ distance) for i in range(count)])  19.4 us
    pallas_call x24, Pallas kernels, call(): pl.pallas_call(kernel, out_shape=outs, in_specs=whole(len(args)), out_spe...  16.9 us
    pallas_call x1, Pallas kernels, load(): pl.pallas_call(functools.partial(load_kernel, count), out_shape=[sds(w.sh...  2.07 us
  transfers between devices with their start and end apart: 27, of which 11 were waited for; matrix products, arithmetic and copies ran while one was open for 0% of the time, Pallas kernels for 26%

profile of v11, /device:TPU:0, one launch (start us, length us, event | category | flops | bytes accessed | tf_op | source)
XLA Modules:
  0.0 63.6 jit_solution(13656584288158177591)
XLA Ops:
  0.0 1.2 %shard_map.136 = (bf16[200,128]{1,0:T(8,128)(2,1)S(1)}, bf16[200,128]{1,0:T(8,128)(2,1)S(1)}, bf16[200,128]{1,0:T(8,128)(2,1)S(1)}, bf16[200,128]{1,0:T(8,128)(2,1)S(1)}) custom-call(bf16[2,160,128]{2,1,0:T(8,128)(2,1)} %bitcast.3, bf16[2,160,128]{2,1,0:T(8,128)(2,1)} %bitcast.4), custom_call_target="tpu_custom_call" | custom-call | tf_op jit(solution)/shard_map/pallas_call | solution.py:454
  1.2 3.1 %collective-permute-start = (bf16[200,128]{1,0:T(8,128)(2,1)S(1)}, bf16[200,128]{1,0:T(8,128)(2,1)S(1)}, u32[]{:S(2)}, u32[]{:S(2)}) collective-permute-start(bf16[200,128]{1,0:T(8,128)(2,1)S(1)} %get-tuple-element.28), channel_id=1, source_target_pairs={{0,2},{2,0},{4,6},{6,4},{1,3},{3,1},{5,7},{7,5},{8,10},{10,8},{12,... | collective-permute-start | bytes 153608 | tf_op jit(solution)/shard_map/ppermute | solution.py:25
  4.3 2.6 %collective-permute-start.1 = (bf16[200,128]{1,0:T(8,128)(2,1)S(1)}, bf16[200,128]{1,0:T(8,128)(2,1)S(1)}, u32[]{:S(2)}, u32[]{:S(2)}) collective-permute-start(bf16[200,128]{1,0:T(8,128)(2,1)S(1)} %get-tuple-element.29), channel_id=1, source_target_pairs={{0,4},{2,6},{4,0},{6,2},{1,5},{3,7},{5,1},{7,3},{8,12},{10,14},{12... | collective-permute-start | bytes 153608 | tf_op jit(solution)/shard_map/ppermute | solution.py:25
  6.9 3.4 %collective-permute-done.1.refs_2_ = bf16[200,128]{1,0:T(8,128)(2,1)S(1)} collective-permute-done((bf16[200,128]{1,0:T(8,128)(2,1)S(1)}, bf16[200,128]{1,0:T(8,128)(2,1)S(1)}, u32[]{:S(2)}, u32[]{:S(2)}) %collective-permute-start.1) | collective-permute-done | bytes 51232 | tf_op jit(solution)/shard_map/ppermute | solution.py:25
  10.3 2.5 %collective-permute-done.2.refs_3_ = bf16[200,128]{1,0:T(8,128)(2,1)S(1)} collective-permute-done((bf16[200,128]{1,0:T(8,128)(2,1)S(1)}, bf16[200,128]{1,0:T(8,128)(2,1)S(1)}, u32[]{:S(2)}, u32[]{:S(2)}) %collective-permute-start.2) | collective-permute-done | bytes 51232 | tf_op jit(solution)/shard_map/ppermute | solution.py:25
  13.2 1.5 %collective-permute-start.12 = (bf16[400,128]{1,0:T(8,128)(2,1)S(1)}, bf16[400,128]{1,0:T(8,128)(2,1)S(1)}, u32[]{:S(2)}, u32[]{:S(2)}) collective-permute-start(bf16[400,128]{1,0:T(8,128)(2,1)S(1)} %get-tuple-element.37.refs_0_), channel_id=1, source_target_pairs={{0,8},{8,0},{1,9},{9,1},{2,10},{10,2},{3,11},{11,3},{4,12},{12,4},... | collective-permute-start | bytes 307208 | tf_op jit(solution)/shard_map/ppermute | solution.py:25
  15.1 0.6 collective-permute-start.3
  16.2 1.7 %collective-permute-done.12.refs_0_ = bf16[400,128]{1,0:T(8,128)(2,1)S(1)} collective-permute-done((bf16[400,128]{1,0:T(8,128)(2,1)S(1)}, bf16[400,128]{1,0:T(8,128)(2,1)S(1)}, u32[]{:S(2)}, u32[]{:S(2)}) %collective-permute-start.12) | collective-permute-done | bytes 102432 | tf_op jit(solution)/shard_map/ppermute | solution.py:25
  17.9 1.9 %collective-permute-done.3.refs_0_ = bf16[400,128]{1,0:T(8,128)(2,1)S(1)} collective-permute-done((bf16[400,128]{1,0:T(8,128)(2,1)S(1)}, bf16[400,128]{1,0:T(8,128)(2,1)S(1)}, u32[]{:S(2)}, u32[]{:S(2)}) %collective-permute-start.3) | collective-permute-done | bytes 102432 | tf_op jit(solution)/shard_map/ppermute | solution.py:25
  19.8 2.1 %shard_map.138 = (bf16[3,3,160,640]{3,2,1,0:T(8,128)(2,1)S(1)}, bf16[3,3,160,640]{3,2,1,0:T(8,128)(2,1)S(1)}) custom-call(bf16[3,3,160,640]{3,2,1,0:T(8,128)(2,1)} %refs_0_.1, bf16[3,3,160,640]{3,2,1,0:T(8,128)(2,1)} %refs_1_.1), custom_call_target="tpu_custom_call" | custom-call | bytes 3686400 | tf_op jit(solution)/shard_map/pallas_call | solution.py:193
  21.9 0.8 %shard_map.148.refs_1_ = f32[320,160]{1,0:T(8,128)S(1)} custom-call(bf16[400,128]{1,0:T(8,128)(2,1)S(1)} %get-tuple-element.37.refs_0_, bf16[400,128]{1,0:T(8,128)(2,1)S(1)} %collective-permute-done.14.refs_1_, bf16[3,3,160,640]{3,2,1,0:T(8,128)(2,1)S(1)} %get-tuple-element.38.refs_2_), custom_call_target="tpu_custom_call" | custom-call | flops 294912000 | bytes 2252800 | tf_op jit(solution)/shard_map/pallas_call | solution.py:44
  22.7 0.5 shard_map.149.refs_1_
  23.3 0.8 %shard_map.139.refs_1_ = f32[320,160]{1,0:T(8,128)S(1)} custom-call(bf16[400,128]{1,0:T(8,128)(2,1)S(1)} %get-tuple-element.31.refs_0_, bf16[400,128]{1,0:T(8,128)(2,1)S(1)} %collective-permute-done.5.refs_1_, bf16[3,3,160,640]{3,2,1,0:T(8,128)(2,1)S(1)} %get-tuple-element.32.refs_2_), custom_call_target="tpu_custom_call" | custom-call | flops 294912000 | bytes 2252800 | tf_op jit(solution)/shard_map/pallas_call | solution.py:44
  24.1 0.8 %shard_map.150 = (bf16[320,160]{1,0:T(8,128)(2,1)S(1)}, bf16[384,128]{1,0:T(8,128)(2,1)S(1)}) custom-call(bf16[400,128]{1,0:T(8,128)(2,1)S(1)} %collective-permute-done.13.refs_0_, f32[320,160]{1,0:T(8,128)S(1)} %shard_map.149.refs_1_, bf16[3,3,160,640]{3,2,1,0:T(8,128)(2,1)S(1)} %get-tuple-element.38.refs_2_, ...), custom_call_target="tpu_custom_call" | custom-call | flops 147456000 | bytes 2453824 | tf_op jit(solution)/shard_map/pallas_call | solution.py:44
  24.8 0.7 %collective-permute-start.15 = (bf16[384,128]{1,0:T(8,128)(2,1)S(1)}, bf16[384,128]{1,0:T(8,128)(2,1)S(1)}, u32[]{:S(2)}, u32[]{:S(2)}) collective-permute-start(bf16[384,128]{1,0:T(8,128)(2,1)S(1)} %get-tuple-element.40.refs_0_), channel_id=1, source_target_pairs={{0,8},{8,0},{1,9},{9,1},{2,10},{10,2},{3,11},{11,3},{4,12},{12,4},... | collective-permute-start | bytes 294920 | tf_op jit(solution)/shard_map/ppermute | solution.py:25
  25.6 0.5 shard_map.140.refs_1_
  26.2 0.8 %shard_map.141 = (bf16[320,160]{1,0:T(8,128)(2,1)S(1)}, bf16[384,128]{1,0:T(8,128)(2,1)S(1)}) custom-call(bf16[400,128]{1,0:T(8,128)(2,1)S(1)} %collective-permute-done.4.refs_0_, f32[320,160]{1,0:T(8,128)S(1)} %shard_map.140.refs_1_, bf16[3,3,160,640]{3,2,1,0:T(8,128)(2,1)S(1)} %get-tuple-element.32.refs_2_, ...), custom_call_target="tpu_custom_call" | custom-call | flops 147456000 | bytes 2453824 | tf_op jit(solution)/shard_map/pallas_call | solution.py:44
  26.9 1.4 %collective-permute-start.6 = (bf16[384,128]{1,0:T(8,128)(2,1)S(1)}, bf16[384,128]{1,0:T(8,128)(2,1)S(1)}, u32[]{:S(2)}, u32[]{:S(2)}) collective-permute-start(bf16[384,128]{1,0:T(8,128)(2,1)S(1)} %get-tuple-element.34.refs_0_), channel_id=1, source_target_pairs={{0,8},{8,0},{1,9},{9,1},{2,10},{10,2},{3,11},{11,3},{4,12},{12,4},... | collective-permute-start | bytes 294920 | tf_op jit(solution)/shard_map/ppermute | solution.py:25
  28.3 0.5 collective-permute-start.8
  28.8 1.6 %collective-permute-done.15.refs_0_ = bf16[384,128]{1,0:T(8,128)(2,1)S(1)} collective-permute-done((bf16[384,128]{1,0:T(8,128)(2,1)S(1)}, bf16[384,128]{1,0:T(8,128)(2,1)S(1)}, u32[]{:S(2)}, u32[]{:S(2)}) %collective-permute-start.15) | collective-permute-done | bytes 98336 | tf_op jit(solution)/shard_map/ppermute | solution.py:25
  30.4 1.8 %collective-permute-done.6.refs_0_ = bf16[384,128]{1,0:T(8,128)(2,1)S(1)} collective-permute-done((bf16[384,128]{1,0:T(8,128)(2,1)S(1)}, bf16[384,128]{1,0:T(8,128)(2,1)S(1)}, u32[]{:S(2)}, u32[]{:S(2)}) %collective-permute-start.6) | collective-permute-done | bytes 98336 | tf_op jit(solution)/shard_map/ppermute | solution.py:25
  32.2 0.8 %shard_map.151.refs_1_ = f32[320,160]{1,0:T(8,128)S(1)} custom-call(bf16[384,128]{1,0:T(8,128)(2,1)S(1)} %get-tuple-element.40.refs_0_, bf16[384,128]{1,0:T(8,128)(2,1)S(1)} %collective-permute-done.17.refs_1_, bf16[3,3,160,640]{3,2,1,0:T(8,128)(2,1)S(1)} %copy-done.2), custom_call_target="tpu_custom_call" | custom-call | flops 294912000 | bytes 2244608 | tf_op jit(solution)/shard_map/pallas_call | solution.py:44
  33.0 0.5 shard_map.152.refs_1_
  33.6 0.9 %copy-done.3 = bf16[3,3,160,640]{3,2,1,0:T(8,128)(2,1)S(1)} copy-done((bf16[3,3,160,640]{3,2,1,0:T(8,128)(2,1)S(1)}, bf16[3,3,160,640]{3,2,1,0:T(8,128)(2,1)}, u32[]{:S(2)}) %copy-start.3) | copy-done | bytes 1843224
  34.5 0.8 %shard_map.142.refs_1_ = f32[320,160]{1,0:T(8,128)S(1)} custom-call(bf16[384,128]{1,0:T(8,128)(2,1)S(1)} %get-tuple-element.34.refs_0_, bf16[384,128]{1,0:T(8,128)(2,1)S(1)} %collective-permute-done.8.refs_1_, bf16[3,3,160,640]{3,2,1,0:T(8,128)(2,1)S(1)} %copy-done.3), custom_call_target="tpu_custom_call" | custom-call | flops 294912000 | bytes 2244608 | tf_op jit(solution)/shard_map/pallas_call | solution.py:44
  35.3 0.7 %shard_map.153.refs_0_ = bf16[360,128]{1,0:T(8,128)(2,1)S(1)} custom-call(bf16[384,128]{1,0:T(8,128)(2,1)S(1)} %collective-permute-done.16.refs_0_, f32[320,160]{1,0:T(8,128)S(1)} %shard_map.152.refs_1_, bf16[3,3,160,640]{3,2,1,0:T(8,128)(2,1)S(1)} %copy-done.2, bf16[320,160]{1,0:T(8,128)(2,1)S(1)} %get-tuple-element.41.refs_3_, bf16[160]{0:T(256)(128)(2,1)S(1)} %copy-done.4), custom_call_target="tpu_custom_call" | custom-call | flops 147456000 | bytes 2341184 | tf_op jit(solution)/shard_map/pallas_call | solution.py:44
  36.1 1.1 %collective-permute-start.18 = (bf16[360,128]{1,0:T(8,128)(2,1)S(1)}, bf16[360,128]{1,0:T(8,128)(2,1)S(1)}, u32[]{:S(2)}, u32[]{:S(2)}) collective-permute-start(bf16[360,128]{1,0:T(8,128)(2,1)S(1)} %shard_map.153.refs_0_), channel_id=1, source_target_pairs={{0,8},{8,0},{1,9},{9,1},{2,10},{10,2},{3,11},{11,3},{4,12},{12,4},... | collective-permute-start | bytes 276488 | tf_op jit(solution)/shard_map/ppermute | solution.py:25
  37.2 0.5 shard_map.143.refs_1_
  37.7 0.7 %shard_map.144 = (bf16[320,160]{1,0:T(8,128)(2,1)S(1)}, bf16[360,128]{1,0:T(8,128)(2,1)S(1)}) custom-call(bf16[384,128]{1,0:T(8,128)(2,1)S(1)} %collective-permute-done.7.refs_0_, f32[320,160]{1,0:T(8,128)S(1)} %shard_map.143.refs_1_, bf16[3,3,160,640]{3,2,1,0:T(8,128)(2,1)S(1)} %copy-done.3, bf16[320,160]{1,0:T(8,128)(2,1)S(1)} %get-tuple-element.35.refs_3_, ...), custom_call_target="tpu_custom_call" | custom-call | flops 147456000 | bytes 2443584 | tf_op jit(solution)/shard_map/pallas_call | solution.py:44
  38.5 1.0 %collective-permute-start.9 = (bf16[360,128]{1,0:T(8,128)(2,1)S(1)}, bf16[360,128]{1,0:T(8,128)(2,1)S(1)}, u32[]{:S(2)}, u32[]{:S(2)}) collective-permute-start(bf16[360,128]{1,0:T(8,128)(2,1)S(1)} %get-tuple-element.36.refs_0_), channel_id=1, source_target_pairs={{0,8},{8,0},{1,9},{9,1},{2,10},{10,2},{3,11},{11,3},{4,12},{12,4},... | collective-permute-start | bytes 276488 | tf_op jit(solution)/shard_map/ppermute | solution.py:25
  40.0 1.2 %collective-permute-done.18.refs_0_.refs_2_ = bf16[360,128]{1,0:T(8,128)(2,1)S(1)} collective-permute-done((bf16[360,128]{1,0:T(8,128)(2,1)S(1)}, bf16[360,128]{1,0:T(8,128)(2,1)S(1)}, u32[]{:S(2)}, u32[]{:S(2)}) %collective-permute-start.18) | collective-permute-done | bytes 92192 | tf_op jit(solution)/shard_map/ppermute | solution.py:25
  41.2 2.1 %collective-permute-done.9.refs_0_ = bf16[360,128]{1,0:T(8,128)(2,1)S(1)} collective-permute-done((bf16[360,128]{1,0:T(8,128)(2,1)S(1)}, bf16[360,128]{1,0:T(8,128)(2,1)S(1)}, u32[]{:S(2)}, u32[]{:S(2)}) %collective-permute-start.9) | collective-permute-done | bytes 92192 | tf_op jit(solution)/shard_map/ppermute | solution.py:25
  43.3 0.8 %shard_map.145.refs_1_ = f32[320,160]{1,0:T(8,128)S(1)} custom-call(bf16[360,128]{1,0:T(8,128)(2,1)S(1)} %get-tuple-element.36.refs_0_, bf16[360,128]{1,0:T(8,128)(2,1)S(1)} %collective-permute-done.11.refs_1_, bf16[3,3,160,1280]{3,2,1,0:T(8,128)(2,1)S(1)} %copy-done), custom_call_target="tpu_custom_call" | custom-call | flops 294912000 | bytes 4075520 | tf_op jit(solution)/shard_map/pallas_call | solution.py:44
  44.1 0.5 shard_map.146.refs_1_
  44.7 0.8 %shard_map.154.refs_2_ = f32[320,160]{1,0:T(8,128)S(1)} custom-call(bf16[360,128]{1,0:T(8,128)(2,1)S(1)} %shard_map.153.refs_0_, bf16[360,128]{1,0:T(8,128)(2,1)S(1)} %collective-permute-done.20.refs_1_, bf16[3,3,160,1280]{3,2,1,0:T(8,128)(2,1)S(1)} %copy-done), custom_call_target="tpu_custom_call" | custom-call | flops 294912000 | bytes 4075520 | tf_op jit(solution)/shard_map/pallas_call | solution.py:44
  45.5 0.8 %shard_map.155.refs_2_ = f32[320,160]{1,0:T(8,128)S(1)} custom-call(bf16[360,128]{1,0:T(8,128)(2,1)S(1)} %collective-permute-done.18.refs_0_.refs_2_, bf16[360,128]{1,0:T(8,128)(2,1)S(1)} %collective-permute-done.19.refs_1_.refs_3_, f32[320,160]{1,0:T(8,128)S(1)} %shard_map.154.refs_2_, bf16[3,3,160,1280]{3,2,1,0:T(8,128)(2,1)S(1)} %copy-done), custom_call_target="tpu_custom_call" | custom-call | flops 294912000 | bytes 4280320 | tf_op jit(solution)/shard_map/pallas_call | solution.py:44
  46.4 0.7 %shard_map.156 = (bf16[320,160]{1,0:T(8,128)(2,1)S(1)}, bf16[344,128]{1,0:T(8,128)(2,1)S(1)}) custom-call(bf16[360,128]{1,0:T(8,128)(2,1)S(1)} %collective-permute-done.10.refs_0_, f32[320,160]{1,0:T(8,128)S(1)} %shard_map.146.refs_1_, f32[320,160]{1,0:T(8,128)S(1)} %shard_map.155.refs_2_, bf16[3,3,160,1280]{3,2,1,0:T(8,128)(2,1)S(1)} %copy-done, ...), custom_call_target="tpu_custom_call" | custom-call | flops 147456000 | bytes 4481344 | tf_op jit(solution)/shard_map/pallas_call | solution.py:44
  47.1 1.1 %collective-permute-start.21 = (bf16[344,128]{1,0:T(8,128)(2,1)S(1)}, bf16[344,128]{1,0:T(8,128)(2,1)S(1)}, u32[]{:S(2)}, u32[]{:S(2)}) collective-permute-start(bf16[344,128]{1,0:T(8,128)(2,1)S(1)} %get-tuple-element.43.refs_0_), channel_id=1, source_target_pairs={{0,8},{8,0},{1,9},{9,1},{2,10},{10,2},{3,11},{11,3},{4,12},{12,4},... | collective-permute-start | bytes 264200 | tf_op jit(solution)/shard_map/ppermute | solution.py:25
  48.4 3.7 %collective-permute-done.21.refs_0_ = bf16[344,128]{1,0:T(8,128)(2,1)S(1)} collective-permute-done((bf16[344,128]{1,0:T(8,128)(2,1)S(1)}, bf16[344,128]{1,0:T(8,128)(2,1)S(1)}, u32[]{:S(2)}, u32[]{:S(2)}) %collective-permute-start.21) | collective-permute-done | bytes 88096 | tf_op jit(solution)/shard_map/ppermute | solution.py:25
  52.1 1.4 %shard_map.159.refs_2_ = f32[320,160]{1,0:T(8,128)S(1)} custom-call(bf16[360,128]{1,0:T(8,128)(2,1)S(1)} %shard_map.153.refs_0_, bf16[360,128]{1,0:T(8,128)(2,1)S(1)} %collective-permute-done.20.refs_1_, bf16[360,128]{1,0:T(8,128)(2,1)S(1)} %collective-permute-done.18.refs_0_.refs_2_, bf16[360,128]{1,0:T(8,128)(2,1)S(1)} %collective-permute-done.19.refs_1_.refs_3_, ...), custom_call_target="tpu_custom_call" | custom-call | flops 589824000 | bytes 4259840 | tf_op jit(solution)/shard_map/pallas_call | solution.py:44
  53.5 0.8 %shard_map.157.refs_1_ = f32[320,160]{1,0:T(8,128)S(1)} custom-call(bf16[344,128]{1,0:T(8,128)(2,1)S(1)} %get-tuple-element.43.refs_0_, bf16[344,128]{1,0:T(8,128)(2,1)S(1)} %collective-permute-done.23.refs_1_, bf16[3,3,160,1280]{3,2,1,0:T(8,128)(2,1)S(1)} %copy-done.1), custom_call_target="tpu_custom_call" | custom-call | flops 294912000 | bytes 4067328 | tf_op jit(solution)/shard_map/pallas_call | solution.py:44
  54.3 0.5 shard_map.158.refs_1_
  55.0 0.7 %shard_map.160 = (bf16[80,128]{1,0:T(8,128)(2,1)S(1)}, bf16[80,128]{1,0:T(8,128)(2,1)S(1)}, bf16[80,128]{1,0:T(8,128)(2,1)S(1)}, bf16[80,128]{1,0:T(8,128)(2,1)S(1)}) custom-call(bf16[344,128]{1,0:T(8,128)(2,1)S(1)} %collective-permute-done.22.refs_0_, f32[320,160]{1,0:T(8,128)S(1)} %shard_map.158.refs_1_, f32[320,160]{1,0:T(8,128)S(1)} %shard_map.159.refs_2_, ...), custom_call_target="tpu_custom_call" | custom-call | flops 147456000 | bytes 4368704 | tf_op jit(solution)/shard_map/pallas_call | solution.py:44
  55.7 1.4 %collective-permute-start.25 = (bf16[80,128]{1,0:T(8,128)(2,1)S(1)}, bf16[80,128]{1,0:T(8,128)(2,1)S(1)}, u32[]{:S(2)}, u32[]{:S(2)}) collective-permute-start(bf16[80,128]{1,0:T(8,128)(2,1)S(1)} %get-tuple-element.47), channel_id=1, source_target_pairs={{0,4},{2,6},{4,0},{6,2},{1,5},{3,7},{5,1},{7,3},{8,12},{10,14},{12... | collective-permute-start | bytes 61448 | tf_op jit(solution)/shard_map/ppermute | solution.py:25
  57.1 3.0 %collective-permute-start.26 = (bf16[80,128]{1,0:T(8,128)(2,1)S(1)}, bf16[80,128]{1,0:T(8,128)(2,1)S(1)}, u32[]{:S(2)}, u32[]{:S(2)}) collective-permute-start(bf16[80,128]{1,0:T(8,128)(2,1)S(1)} %get-tuple-element.48), channel_id=1, source_target_pairs={{0,6},{2,4},{4,2},{6,0},{1,7},{3,5},{5,3},{7,1},{8,14},{10,12},{12... | collective-permute-start | bytes 61448 | tf_op jit(solution)/shard_map/ppermute | solution.py:25
  60.1 0.5 collective-permute-done.25.refs_2_
  60.6 2.1 %collective-permute-done.26.refs_3_ = bf16[80,128]{1,0:T(8,128)(2,1)S(1)} collective-permute-done((bf16[80,128]{1,0:T(8,128)(2,1)S(1)}, bf16[80,128]{1,0:T(8,128)(2,1)S(1)}, u32[]{:S(2)}, u32[]{:S(2)}) %collective-permute-start.26) | collective-permute-done | bytes 20512 | tf_op jit(solution)/shard_map/ppermute | solution.py:25
  62.7 0.8 %shard_map.161 = bf16[2,160,128]{2,1,0:T(8,128)(2,1)} custom-call(bf16[80,128]{1,0:T(8,128)(2,1)S(1)} %get-tuple-element.45.refs_0_, bf16[80,128]{1,0:T(8,128)(2,1)S(1)} %collective-permute-done.24.refs_1_, bf16[80,128]{1,0:T(8,128)(2,1)S(1)} %collective-permute-done.25.refs_2_, bf16[80,128]{1,0:T(8,128)(2,1)S(1)} %collective-permute-done.26.refs_3_), custom_call_target="tpu_custom_call" | custom-call | bytes 163840 | tf_op jit(solution)/shard_map/pallas_call | solution.py:44
  (52 shorter events, 2.2 us)
Async XLA Ops:
  1.2 5.7 %collective-permute-start = (bf16[200,128]{1,0:T(8,128)(2,1)S(1)}, bf16[200,128]{1,0:T(8,128)(2,1)S(1)}, u32[]{:S(2)}, u32[]{:S(2)}) collective-permute-start(bf16[200,128]{1,0:T(8,128)(2,1)S(1)} %get-tuple-element.28), channel_id=1, source_target_pairs={{0,2},{2,0},{4,6},{6,4},{1,3},{3,1},{5,7},{7,5},{8,10},{10,8},{12,... | collective-permute-start | bytes 153608 | tf_op jit(solution)/shard_map/ppermute | solution.py:25
  4.3 6.0 %collective-permute-start.1 = (bf16[200,128]{1,0:T(8,128)(2,1)S(1)}, bf16[200,128]{1,0:T(8,128)(2,1)S(1)}, u32[]{:S(2)}, u32[]{:S(2)}) collective-permute-start(bf16[200,128]{1,0:T(8,128)(2,1)S(1)} %get-tuple-element.29), channel_id=1, source_target_pairs={{0,4},{2,6},{4,0},{6,2},{1,5},{3,7},{5,1},{7,3},{8,12},{10,14},{12... | collective-permute-start | bytes 153608 | tf_op jit(solution)/shard_map/ppermute | solution.py:25
  6.9 5.9 %collective-permute-start.2 = (bf16[200,128]{1,0:T(8,128)(2,1)S(1)}, bf16[200,128]{1,0:T(8,128)(2,1)S(1)}, u32[]{:S(2)}, u32[]{:S(2)}) collective-permute-start(bf16[200,128]{1,0:T(8,128)(2,1)S(1)} %get-tuple-element.30), channel_id=1, source_target_pairs={{0,6},{2,4},{4,2},{6,0},{1,7},{3,5},{5,3},{7,1},{8,14},{10,12},{12... | collective-permute-start | bytes 153608 | tf_op jit(solution)/shard_map/ppermute | solution.py:25
  13.2 4.7 %collective-permute-start.12 = (bf16[400,128]{1,0:T(8,128)(2,1)S(1)}, bf16[400,128]{1,0:T(8,128)(2,1)S(1)}, u32[]{:S(2)}, u32[]{:S(2)}) collective-permute-start(bf16[400,128]{1,0:T(8,128)(2,1)S(1)} %get-tuple-element.37.refs_0_), channel_id=1, source_target_pairs={{0,8},{8,0},{1,9},{9,1},{2,10},{10,2},{3,11},{11,3},{4,12},{12,4},... | collective-permute-start | bytes 307208 | tf_op jit(solution)/shard_map/ppermute | solution.py:25
  15.1 4.7 %collective-permute-start.3 = (bf16[400,128]{1,0:T(8,128)(2,1)S(1)}, bf16[400,128]{1,0:T(8,128)(2,1)S(1)}, u32[]{:S(2)}, u32[]{:S(2)}) collective-permute-start(bf16[400,128]{1,0:T(8,128)(2,1)S(1)} %get-tuple-element.31.refs_0_), channel_id=1, source_target_pairs={{0,8},{8,0},{1,9},{9,1},{2,10},{10,2},{3,11},{11,3},{4,12},{12,4},... | collective-permute-start | bytes 307208 | tf_op jit(solution)/shard_map/ppermute | solution.py:25
  15.6 6.2 %collective-permute-start.14 = (bf16[400,128]{1,0:T(8,128)(2,1)S(1)}, bf16[400,128]{1,0:T(8,128)(2,1)S(1)}, u32[]{:S(2)}, u32[]{:S(2)}) collective-permute-start(bf16[400,128]{1,0:T(8,128)(2,1)S(1)} %get-tuple-element.37.refs_0_), channel_id=1, source_target_pairs={{0,1},{1,0},{2,3},{3,2},{4,5},{5,4},{6,7},{7,6},{8,9},{9,8},{10,11... | collective-permute-start | bytes 307208 | tf_op jit(solution)/shard_map/ppermute | solution.py:25
  15.6 7.6 %collective-permute-start.5 = (bf16[400,128]{1,0:T(8,128)(2,1)S(1)}, bf16[400,128]{1,0:T(8,128)(2,1)S(1)}, u32[]{:S(2)}, u32[]{:S(2)}) collective-permute-start(bf16[400,128]{1,0:T(8,128)(2,1)S(1)} %get-tuple-element.31.refs_0_), channel_id=1, source_target_pairs={{0,1},{1,0},{2,3},{3,2},{4,5},{5,4},{6,7},{7,6},{8,9},{9,8},{10,11... | collective-permute-start | bytes 307208 | tf_op jit(solution)/shard_map/ppermute | solution.py:25
  17.9 6.2 %collective-permute-start.13 = (bf16[400,128]{1,0:T(8,128)(2,1)S(1)}, bf16[400,128]{1,0:T(8,128)(2,1)S(1)}, u32[]{:S(2)}, u32[]{:S(2)}) collective-permute-start(bf16[400,128]{1,0:T(8,128)(2,1)S(1)} %collective-permute-done.12.refs_0_), channel_id=1, source_target_pairs={{0,1},{1,0},{2,3},{3,2},{4,5},{5,4},{6,7},{7,6},{8,9},{9,8},{10,11... | collective-permute-start | bytes 307208 | tf_op jit(solution)/shard_map/ppermute | solution.py:25
  19.8 6.4 %collective-permute-start.4 = (bf16[400,128]{1,0:T(8,128)(2,1)S(1)}, bf16[400,128]{1,0:T(8,128)(2,1)S(1)}, u32[]{:S(2)}, u32[]{:S(2)}) collective-permute-start(bf16[400,128]{1,0:T(8,128)(2,1)S(1)} %collective-permute-done.3.refs_0_), channel_id=1, source_target_pairs={{0,1},{1,0},{2,3},{3,2},{4,5},{5,4},{6,7},{7,6},{8,9},{9,8},{10,11... | collective-permute-start | bytes 307208 | tf_op jit(solution)/shard_map/ppermute | solution.py:25
  22.7 1.4 %copy-start.7 = (bf16[160]{0:T(256)(128)(2,1)S(1)}, bf16[160]{0:T(256)(128)(2,1)}, u32[]{:S(2)}) copy-start(bf16[160]{0:T(256)(128)(2,1)} %refs_4_.7) | copy-start | bytes 964
  24.8 1.3 %copy-start.8 = (bf16[160]{0:T(256)(128)(2,1)S(1)}, bf16[160]{0:T(256)(128)(2,1)}, u32[]{:S(2)}) copy-start(bf16[160]{0:T(256)(128)(2,1)} %refs_4_.5) | copy-start | bytes 964
  24.8 5.6 %collective-permute-start.15 = (bf16[384,128]{1,0:T(8,128)(2,1)S(1)}, bf16[384,128]{1,0:T(8,128)(2,1)S(1)}, u32[]{:S(2)}, u32[]{:S(2)}) collective-permute-start(bf16[384,128]{1,0:T(8,128)(2,1)S(1)} %get-tuple-element.40.refs_0_), channel_id=1, source_target_pairs={{0,8},{8,0},{1,9},{9,1},{2,10},{10,2},{3,11},{11,3},{4,12},{12,4},... | collective-permute-start | bytes 294920 | tf_op jit(solution)/shard_map/ppermute | solution.py:25
  26.1 6.1 %copy-start.2 = (bf16[3,3,160,640]{3,2,1,0:T(8,128)(2,1)S(1)}, bf16[3,3,160,640]{3,2,1,0:T(8,128)(2,1)}, u32[]{:S(2)}) copy-start(bf16[3,3,160,640]{3,2,1,0:T(8,128)(2,1)} %refs_2_.18) | copy-start | bytes 5529604
  26.9 5.3 %collective-permute-start.6 = (bf16[384,128]{1,0:T(8,128)(2,1)S(1)}, bf16[384,128]{1,0:T(8,128)(2,1)S(1)}, u32[]{:S(2)}, u32[]{:S(2)}) collective-permute-start(bf16[384,128]{1,0:T(8,128)(2,1)S(1)} %get-tuple-element.34.refs_0_), channel_id=1, source_target_pairs={{0,8},{8,0},{1,9},{9,1},{2,10},{10,2},{3,11},{11,3},{4,12},{12,4},... | collective-permute-start | bytes 294920 | tf_op jit(solution)/shard_map/ppermute | solution.py:25
  28.3 3.9 %collective-permute-start.17 = (bf16[384,128]{1,0:T(8,128)(2,1)S(1)}, bf16[384,128]{1,0:T(8,128)(2,1)S(1)}, u32[]{:S(2)}, u32[]{:S(2)}) collective-permute-start(bf16[384,128]{1,0:T(8,128)(2,1)S(1)} %get-tuple-element.40.refs_0_), channel_id=1, source_target_pairs={{0,1},{1,0},{2,3},{3,2},{4,5},{5,4},{6,7},{7,6},{8,9},{9,8},{10,11... | collective-permute-start | bytes 294920 | tf_op jit(solution)/shard_map/ppermute | solution.py:25
  28.3 5.3 %collective-permute-start.8 = (bf16[384,128]{1,0:T(8,128)(2,1)S(1)}, bf16[384,128]{1,0:T(8,128)(2,1)S(1)}, u32[]{:S(2)}, u32[]{:S(2)}) collective-permute-start(bf16[384,128]{1,0:T(8,128)(2,1)S(1)} %get-tuple-element.34.refs_0_), channel_id=1, source_target_pairs={{0,1},{1,0},{2,3},{3,2},{4,5},{5,4},{6,7},{7,6},{8,9},{9,8},{10,11... | collective-permute-start | bytes 294920 | tf_op jit(solution)/shard_map/ppermute | solution.py:25
  30.4 4.9 %collective-permute-start.16 = (bf16[384,128]{1,0:T(8,128)(2,1)S(1)}, bf16[384,128]{1,0:T(8,128)(2,1)S(1)}, u32[]{:S(2)}, u32[]{:S(2)}) collective-permute-start(bf16[384,128]{1,0:T(8,128)(2,1)S(1)} %collective-permute-done.15.refs_0_), channel_id=1, source_target_pairs={{0,1},{1,0},{2,3},{3,2},{4,5},{5,4},{6,7},{7,6},{8,9},{9,8},{10,11... | collective-permute-start | bytes 294920 | tf_op jit(solution)/shard_map/ppermute | solution.py:25
  32.2 5.5 %collective-permute-start.7 = (bf16[384,128]{1,0:T(8,128)(2,1)S(1)}, bf16[384,128]{1,0:T(8,128)(2,1)S(1)}, u32[]{:S(2)}, u32[]{:S(2)}) collective-permute-start(bf16[384,128]{1,0:T(8,128)(2,1)S(1)} %collective-permute-done.6.refs_0_), channel_id=1, source_target_pairs={{0,1},{1,0},{2,3},{3,2},{4,5},{5,4},{6,7},{7,6},{8,9},{9,8},{10,11... | collective-permute-start | bytes 294920 | tf_op jit(solution)/shard_map/ppermute | solution.py:25
  33.0 1.5 %copy-start.3 = (bf16[3,3,160,640]{3,2,1,0:T(8,128)(2,1)S(1)}, bf16[3,3,160,640]{3,2,1,0:T(8,128)(2,1)}, u32[]{:S(2)}) copy-start(bf16[3,3,160,640]{3,2,1,0:T(8,128)(2,1)} %refs_2_.13) | copy-start | bytes 5529604
  33.0 2.3 %copy-start.4 = (bf16[160]{0:T(256)(128)(2,1)S(1)}, bf16[160]{0:T(256)(128)(2,1)}, u32[]{:S(2)}) copy-start(bf16[160]{0:T(256)(128)(2,1)} %refs_4_.8) | copy-start | bytes 964
  36.1 1.7 %copy-start.9 = (bf16[160]{0:T(256)(128)(2,1)S(1)}, bf16[160]{0:T(256)(128)(2,1)}, u32[]{:S(2)}) copy-start(bf16[160]{0:T(256)(128)(2,1)} %refs_4_.6) | copy-start | bytes 964
  36.1 5.2 %collective-permute-start.18 = (bf16[360,128]{1,0:T(8,128)(2,1)S(1)}, bf16[360,128]{1,0:T(8,128)(2,1)S(1)}, u32[]{:S(2)}, u32[]{:S(2)}) collective-permute-start(bf16[360,128]{1,0:T(8,128)(2,1)S(1)} %shard_map.153.refs_0_), channel_id=1, source_target_pairs={{0,8},{8,0},{1,9},{9,1},{2,10},{10,2},{3,11},{11,3},{4,12},{12,4},... | collective-permute-start | bytes 276488 | tf_op jit(solution)/shard_map/ppermute | solution.py:25
  37.2 6.2 %copy-start = (bf16[3,3,160,1280]{3,2,1,0:T(8,128)(2,1)S(1)}, bf16[3,3,160,1280]{3,2,1,0:T(8,128)(2,1)}, u32[]{:S(2)}) copy-start(bf16[3,3,160,1280]{3,2,1,0:T(8,128)(2,1)} %refs_3_.4) | copy-start | bytes 11059204
  38.5 4.8 %collective-permute-start.9 = (bf16[360,128]{1,0:T(8,128)(2,1)S(1)}, bf16[360,128]{1,0:T(8,128)(2,1)S(1)}, u32[]{:S(2)}, u32[]{:S(2)}) collective-permute-start(bf16[360,128]{1,0:T(8,128)(2,1)S(1)} %get-tuple-element.36.refs_0_), channel_id=1, source_target_pairs={{0,8},{8,0},{1,9},{9,1},{2,10},{10,2},{3,11},{11,3},{4,12},{12,4},... | collective-permute-start | bytes 276488 | tf_op jit(solution)/shard_map/ppermute | solution.py:25
  39.5 3.8 %collective-permute-start.11 = (bf16[360,128]{1,0:T(8,128)(2,1)S(1)}, bf16[360,128]{1,0:T(8,128)(2,1)S(1)}, u32[]{:S(2)}, u32[]{:S(2)}) collective-permute-start(bf16[360,128]{1,0:T(8,128)(2,1)S(1)} %get-tuple-element.36.refs_0_), channel_id=1, source_target_pairs={{0,1},{1,0},{2,3},{3,2},{4,5},{5,4},{6,7},{7,6},{8,9},{9,8},{10,11... | collective-permute-start | bytes 276488 | tf_op jit(solution)/shard_map/ppermute | solution.py:25
  39.5 5.1 %collective-permute-start.20 = (bf16[360,128]{1,0:T(8,128)(2,1)S(1)}, bf16[360,128]{1,0:T(8,128)(2,1)S(1)}, u32[]{:S(2)}, u32[]{:S(2)}) collective-permute-start(bf16[360,128]{1,0:T(8,128)(2,1)S(1)} %shard_map.153.refs_0_), channel_id=1, source_target_pairs={{0,1},{1,0},{2,3},{3,2},{4,5},{5,4},{6,7},{7,6},{8,9},{9,8},{10,11... | collective-permute-start | bytes 276488 | tf_op jit(solution)/shard_map/ppermute | solution.py:25
  41.2 4.3 %collective-permute-start.19 = (bf16[360,128]{1,0:T(8,128)(2,1)S(1)}, bf16[360,128]{1,0:T(8,128)(2,1)S(1)}, u32[]{:S(2)}, u32[]{:S(2)}) collective-permute-start(bf16[360,128]{1,0:T(8,128)(2,1)S(1)} %collective-permute-done.18.refs_0_.refs_2_), channel_id=1, source_target_pairs={{0,1},{1,0},{2,3},{3,2},{4,5},{5,4},{6,7},{7,6},{8,9},{9,8},{10,11... | collective-permute-start | bytes 276488 | tf_op jit(solution)/shard_map/ppermute | solution.py:25
  43.3 3.0 %collective-permute-start.10 = (bf16[360,128]{1,0:T(8,128)(2,1)S(1)}, bf16[360,128]{1,0:T(8,128)(2,1)S(1)}, u32[]{:S(2)}, u32[]{:S(2)}) collective-permute-start(bf16[360,128]{1,0:T(8,128)(2,1)S(1)} %collective-permute-done.9.refs_0_), channel_id=1, source_target_pairs={{0,1},{1,0},{2,3},{3,2},{4,5},{5,4},{6,7},{7,6},{8,9},{9,8},{10,11... | collective-permute-start | bytes 276488 | tf_op jit(solution)/shard_map/ppermute | solution.py:25
  45.5 0.8 %copy-start.5 = (bf16[160]{0:T(256)(128)(2,1)S(1)}, bf16[160]{0:T(256)(128)(2,1)}, u32[]{:S(2)}) copy-start(bf16[160]{0:T(256)(128)(2,1)} %refs_5_.2) | copy-start | bytes 964
  46.4 5.8 %copy-start.1 = (bf16[3,3,160,1280]{3,2,1,0:T(8,128)(2,1)S(1)}, bf16[3,3,160,1280]{3,2,1,0:T(8,128)(2,1)}, u32[]{:S(2)}) copy-start(bf16[3,3,160,1280]{3,2,1,0:T(8,128)(2,1)} %refs_3_.5) | copy-start | bytes 11059204
  47.1 5.0 %collective-permute-start.21 = (bf16[344,128]{1,0:T(8,128)(2,1)S(1)}, bf16[344,128]{1,0:T(8,128)(2,1)S(1)}, u32[]{:S(2)}, u32[]{:S(2)}) collective-permute-start(bf16[344,128]{1,0:T(8,128)(2,1)S(1)} %get-tuple-element.43.refs_0_), channel_id=1, source_target_pairs={{0,8},{8,0},{1,9},{9,1},{2,10},{10,2},{3,11},{11,3},{4,12},{12,4},... | collective-permute-start | bytes 264200 | tf_op jit(solution)/shard_map/ppermute | solution.py:25
  48.2 5.3 %collective-permute-start.23 = (bf16[344,128]{1,0:T(8,128)(2,1)S(1)}, bf16[344,128]{1,0:T(8,128)(2,1)S(1)}, u32[]{:S(2)}, u32[]{:S(2)}) collective-permute-start(bf16[344,128]{1,0:T(8,128)(2,1)S(1)} %get-tuple-element.43.refs_0_), channel_id=1, source_target_pairs={{0,1},{1,0},{2,3},{3,2},{4,5},{5,4},{6,7},{7,6},{8,9},{9,8},{10,11... | collective-permute-start | bytes 264200 | tf_op jit(solution)/shard_map/ppermute | solution.py:25
  52.1 2.7 %collective-permute-start.22 = (bf16[344,128]{1,0:T(8,128)(2,1)S(1)}, bf16[344,128]{1,0:T(8,128)(2,1)S(1)}, u32[]{:S(2)}, u32[]{:S(2)}) collective-permute-start(bf16[344,128]{1,0:T(8,128)(2,1)S(1)} %collective-permute-done.21.refs_0_), channel_id=1, source_target_pairs={{0,1},{1,0},{2,3},{3,2},{4,5},{5,4},{6,7},{7,6},{8,9},{9,8},{10,11... | collective-permute-start | bytes 264200 | tf_op jit(solution)/shard_map/ppermute | solution.py:25
  54.3 0.7 %copy-start.6 = (bf16[160]{0:T(256)(128)(2,1)S(1)}, bf16[160]{0:T(256)(128)(2,1)}, u32[]{:S(2)}) copy-start(bf16[160]{0:T(256)(128)(2,1)} %refs_5_.3) | copy-start | bytes 964
  55.7 4.5 %collective-permute-start.24 = (bf16[80,128]{1,0:T(8,128)(2,1)S(1)}, bf16[80,128]{1,0:T(8,128)(2,1)S(1)}, u32[]{:S(2)}, u32[]{:S(2)}) collective-permute-start(bf16[80,128]{1,0:T(8,128)(2,1)S(1)} %get-tuple-element.46), channel_id=1, source_target_pairs={{0,2},{2,0},{4,6},{6,4},{1,3},{3,1},{5,7},{7,5},{8,10},{10,8},{12,... | collective-permute-start | bytes 61448 | tf_op jit(solution)/shard_map/ppermute | solution.py:25
  55.7 4.9 %collective-permute-start.25 = (bf16[80,128]{1,0:T(8,128)(2,1)S(1)}, bf16[80,128]{1,0:T(8,128)(2,1)S(1)}, u32[]{:S(2)}, u32[]{:S(2)}) collective-permute-start(bf16[80,128]{1,0:T(8,128)(2,1)S(1)} %get-tuple-element.47), channel_id=1, source_target_pairs={{0,4},{2,6},{4,0},{6,2},{1,5},{3,7},{5,1},{7,3},{8,12},{10,14},{12... | collective-permute-start | bytes 61448 | tf_op jit(solution)/shard_map/ppermute | solution.py:25
  57.1 5.6 %collective-permute-start.26 = (bf16[80,128]{1,0:T(8,128)(2,1)S(1)}, bf16[80,128]{1,0:T(8,128)(2,1)S(1)}, u32[]{:S(2)}, u32[]{:S(2)}) collective-permute-start(bf16[80,128]{1,0:T(8,128)(2,1)S(1)} %get-tuple-element.48), channel_id=1, source_target_pairs={{0,6},{2,4},{4,2},{6,0},{1,7},{3,5},{5,3},{7,1},{8,14},{10,12},{12... | collective-permute-start | bytes 61448 | tf_op jit(solution)/shard_map/ppermute | solution.py:25

commit v12 on v11

--- a/solution.py
+++ b/solution.py
@@ -64,7 +64,6 @@
         self.wide = self.columns + 2 * LAYERS
         self.height = self.rows * self.bands
         self.cells = self.height * self.wide
-        self.held = self.cells + 2 * self.height
         self.shards = channel_count()
         self.depth = self.shards * self.per
         self.rest = self.per % LANES
@@ -144,10 +143,10 @@
         put(g * part, full * LANES, rest[:rows, g * z.rest : (g + 1) * z.rest])
 
 
-def masked_silu(z, state):
-    value = silu(state).reshape(z.wide, z.height, z.per)
+def masked_silu(z, trim, state):
+    value = silu(state).reshape(-1, z.height, z.per)
     at = lax.broadcasted_iota(jnp.int32, value.shape, 0)
-    at = at + (lax.axis_index("band") * z.columns - LAYERS)
+    at = at + (lax.axis_index("band") * z.columns - LAYERS + trim)
     value = jnp.where((at >= 0) & (at < z.width), value, 0.0)
     return value.reshape(-1, z.per)
 
@@ -228,11 +227,10 @@
     parts = [image[g][:, :n] for g, (_, n) in enumerate(lane_groups(z))]
     value = jnp.concatenate(parts, axis=1)
     state_ref[...] = value.astype(BF16)
-    pack(z, act_ref, masked_silu(z, value), roll=True)
+    pack(z, act_ref, masked_silu(z, 0, value), roll=True)
 
 
 def place(z, trim, a_ref, at, message, distance):
-    first = (1 + trim) * z.height
     owner = channel_place() ^ distance
     offset = pick(z.offsets, owner)
     cells = z.kept(trim)
@@ -248,8 +246,8 @@
         lane = lax.broadcasted_iota(jnp.int32, main.shape, 1)
         low = jnp.where(lane >= offset, main, 0.0)
         high = jnp.where(lane < offset, main, jnp.where(lane < offset + z.rest, rest, 0.0))
-        a_ref[first : first + cells, at : at + LANES] = low.astype(BF16)
-        a_ref[first : first + cells, at + LANES : at + 2 * LANES] = high.astype(BF16)
+        a_ref[:, at : at + LANES] = low.astype(BF16)
+        a_ref[:, at + LANES : at + 2 * LANES] = high.astype(BF16)
     else:
         for known in sorted(set(z.offsets)):
 
@@ -258,7 +256,6 @@
                 def put(row, lane, piece):
                     rows, lanes = piece.shape
                     lane = at + known + lane
-                    row = row + first
                     a_ref[row : row + rows, lane : lane + lanes] = piece
 
                 unpack(z, cells, message, put)
@@ -266,37 +263,30 @@
     return pick(z.starts, owner)
 
 
-def clear(z, trim, a_ref):
-    if z.rolled():
-        first = (1 + trim) * z.height
-        edge = jnp.zeros((first, a_ref.shape[1]), BF16)
-        a_ref[:first] = edge
-        a_ref[z.held - first :] = edge
-    else:
+def accumulate(z, trim, drop, distances, sources, w_ref, a_ref):
+    if not z.rolled():
         a_ref[...] = jnp.zeros(a_ref.shape, BF16)
-
-
-def accumulate(z, trim, distances, sources, w_ref, a_ref):
-    clear(z, trim, a_ref)
     slices = []
     for base, messages in sources:
         for distance, message in zip(distances, messages):
             start = place(z, trim, a_ref, len(slices) * z.span, message, distance)
             slices.append(pl.ds(pl.multiple_of(base + start, LANES), z.span))
-    return convolve(z, moves(z, a_ref), taps(z, w_ref, slices))
+    return convolve(z, moves(z, trim, drop, a_ref), taps(z, w_ref, slices))
 
 
 def up(z, value):
-    value = value.reshape(z.wide, z.height, -1)
+    cells = value.shape[0]
+    value = value.reshape(cells // z.height, z.height, -1)
     row = lax.broadcasted_iota(jnp.int32, value.shape, 1)
-    return jnp.where(row == 0, 0.0, pltpu.roll(value, 1, 1)).reshape(z.cells, -1)
+    return jnp.where(row == 0, 0.0, pltpu.roll(value, 1, 1)).reshape(cells, -1)
 
 
 def down(z, value):
-    value = value.reshape(z.wide, z.height, -1)
+    cells = value.shape[0]
+    value = value.reshape(cells // z.height, z.height, -1)
     row = lax.broadcasted_iota(jnp.int32, value.shape, 1)
     last = z.height - 1
-    return jnp.where(row == last, 0.0, pltpu.roll(value, last, 1)).reshape(z.cells, -1)
+    return jnp.where(row == last, 0.0, pltpu.roll(value, last, 1)).reshape(cells, -1)
 
 
 def convolve(z, cells, weight):
@@ -316,8 +306,9 @@
     return jnp.concatenate(parts, axis=1) if len(parts) > 1 else parts[0]
 
 
-def moves(z, a_ref):
-    return lambda j: a_ref[j * z.height : j * z.height + z.cells]
+def moves(z, trim, drop, a_ref):
+    cells = z.kept(trim + 1 + drop)
+    return lambda j: a_ref[(j + drop) * z.height : (j + drop) * z.height + cells]
 
 
 def taps(z, w_ref, slices):
@@ -333,23 +324,25 @@
 
 
 def send(z, trim, new, act_ref):
-    edge = trim * z.height
-    act = masked_silu(z, new.astype(F32))[edge : z.cells - edge]
-    pack(z, act_ref, act, roll=True)
+    pack(z, act_ref, masked_silu(z, trim, new.astype(F32)), roll=True)
+
+
+def inner(z, trim, state_ref):
+    return state_ref[z.height : z.height + z.kept(trim + 1)].astype(F32)
 
 
 def bias_of(ref):
     return ref[...].astype(F32).reshape(1, -1)
 
 
-def block_kernel(z, trim, base, distances, add, end, *refs):
+def block_kernel(z, trim, drop, base, distances, add, end, *refs):
     n = len(distances)
     blocks, refs = refs[:n], refs[n:]
     sums, refs = refs[:add], refs[add:]
     w_ref, *refs = refs
     a_ref = refs.pop()
     sources = [(base, [block[...] for block in blocks])]
-    total = accumulate(z, trim, distances, sources, w_ref, a_ref)
+    total = accumulate(z, trim, drop, distances, sources, w_ref, a_ref)
     for other in sums:
         total = total + other[...]
     if end:
@@ -359,19 +352,19 @@
 
 
 def close_layer(z, trim, total, state_ref, b_ref, new_ref, act_ref):
-    new = (state_ref[...].astype(F32) + total + bias_of(b_ref)).astype(BF16)
+    new = (inner(z, trim, state_ref) + total + bias_of(b_ref)).astype(BF16)
     new_ref[...] = new
     send(z, trim + 1, new, act_ref)
 
 
 def close_control(z, trim, total, state_ref, b_ref, act_ref):
-    new = (state_ref[...].astype(F32) + total + bias_of(b_ref)).astype(BF16)
+    new = (inner(z, trim, state_ref) + total + bias_of(b_ref)).astype(BF16)
     send(z, trim + 1, new, act_ref)
 
 
 def close_image(z, trim, total, *refs):
     state_ref, b_ref, *outs, image = refs
-    total = state_ref[...].astype(F32) + total + bias_of(b_ref)
+    total = inner(z, trim, state_ref) + total + bias_of(b_ref)
     groups = lane_groups(z)
     for g, (lane, n) in enumerate(groups):
         image[g, :, :n] = total[:, lane : lane + n]
@@ -379,7 +372,7 @@
     for k, out in enumerate(outs):
         rows = []
         for row in range(z.rows):
-            first = LAYERS * z.height + (band ^ k) * z.rows + row
+            first = (band ^ k) * z.rows + row
             at = pl.ds(first, z.columns, stride=z.height)
             rows.append(
                 jnp.concatenate([image[g, at][:, :n] for g, (_, n) in enumerate(groups)], axis=1)
@@ -446,8 +439,7 @@
     z = Sizes(latent)
     kernel = lambda f, *a: functools.partial(f, z, *a)
     groups = len(lane_groups(z))
-    single = sds((z.cells, z.per))
-    total = sds((z.cells, z.per), F32)
+    state_of = lambda trim: sds((z.kept(trim), z.per))
     message = lambda trim: z.packed(z.kept(trim))
 
     raw = (z.rows, z.per, z.width)
@@ -464,13 +456,13 @@
         compiler_params=pltpu.CompilerParams(vmem_limit_bytes=4 << 20),
     )(in_hbm(latent.swapaxes(1, 2)), in_hbm(control_hint.swapaxes(1, 2)))
     blocks = over_bands(blocks)
-    cw1, mw1 = load(cw1, mw1)
+    cw1, mw1, mw2 = load(cw1, mw1, mw2)
     joined = []
     for t in range(2):
         joined.append(
             call(
                 kernel(join_kernel, t),
-                [single, sds(message(0))],
+                [state_of(0), sds(message(0))],
                 *blocks,
                 scratch=[
                     pltpu.VMEM((groups, z.cells, LANES), F32),
@@ -481,44 +473,47 @@
     states = [state for state, _ in joined]
     control, main = [act for _, act in joined]
 
-    def convolution(step, received, w, base, outs, end=None, rest=(), late=(), extra=()):
+    def convolution(
+        step, received, w, base, outs=None, end=None, rest=(), late=(), extra=(), drop=0
+    ):
         received = [(names, pieces) for names, pieces in received if names]
         sums = ()
+        total = sds((z.kept(step + 1 + drop), z.per), F32)
         for at, (names, pieces) in enumerate(received):
             ends = at == len(received) - 1
             sums += late if ends else ()
             result = call(
-                kernel(block_kernel, step, base, names, len(sums), end if ends else None),
-                outs if ends else total,
+                kernel(block_kernel, step, drop, base, names, len(sums), end if ends else None),
+                outs if ends and end else total,
                 *pieces,
                 *sums,
                 w,
                 *(rest if ends else ()),
                 scratch=(list(extra) if ends else [])
-                + [pltpu.VMEM((z.held, len(names) * z.span), BF16)],
+                + [pltpu.VMEM((z.kept(step), len(names) * z.span), BF16)],
                 flops=2 * 9 * z.cells * z.per * z.per * len(names),
             )
             sums = (result,)
         return result
 
     for step, (cw, cb, mw, mb) in enumerate(((cw1, cb1, mw1, mb1), (cw2, cb2, mw2, mb2))):
-        outs = [single, sds(message(step + 1))]
+        outs = [state_of(step + 1), sds(message(step + 1))]
         received = gather(control)
         rest = (states[0], cb)
         if step == 0:
             states[0], control = convolution(step, received, cw, 0, outs, close_layer, rest)
         else:
             control = convolution(step, received, cw, 0, outs[1], close_control, rest)
-        received = gather(main)
+        received = late_together(gather(main))
         rest = (states[1], mb)
         states[1], main = convolution(step, received, mw, 0, outs, close_layer, rest)
     skip = gather(control)
-    first = convolution(2, late_together(skip), dw1, z.depth, total)
-    outs = [single, sds(message(3))]
+    first = convolution(2, late_together(skip), dw1, z.depth)
+    outs = [state_of(3), sds(message(3))]
     rest = (states[1], db1)
     state, act = convolution(2, gather(main), dw1, 0, outs, close_layer, rest, late=(first,))
     every = together(skip)
-    part = convolution(2, [every], dw2, z.depth, total)
+    part = convolution(2, [every], dw2, z.depth, drop=1)
     blocks = convolution(
         3,
         gather(act),
@@ -528,7 +523,7 @@
         close_image,
         (state, db2),
         late=(part,),
-        extra=[pltpu.VMEM((groups, z.cells, LANES), F32)],
+        extra=[pltpu.VMEM((groups, z.kept(LAYERS), LANES), F32)],
     )
     out = call(
         kernel(rows_kernel),

time: 63.8 us -> 62.3 us (0.976)
  Pallas kernels: 20.2 us -> 19.2 us
  local copies, waits for them, and re-layouts: 1.07 us -> 0.2 us
  waiting for transfers between devices: 22.6 us -> 23.4 us
    pallas_call x24 -> x22, Pallas kernels: 16.9 us -> 15.3 us  [call(): pl.pallas_call(kernel, out_shape=outs, in_specs=whole(len(args)), out_spe...]
    unnamed x20 -> x18, local copies, waits for them, and re-layouts: 1.07 us -> 0.2 us
    ppermute x27, waiting for transfers between devices: 22.6 us -> 23.4 us  [exchange(): return lax.ppermute(cells, axis, [(i, i ^ distance) for i in range(count)])]
  transfers between devices with their start and end apart: 27 -> 27, of which waited for: 11 -> 11; matrix products, arithmetic and copies ran while one was open for 0% -> 0% of each run, Pallas kernels for 26% -> 25%
where the time goes in v12:
time: 62.3 us; the launch traced here: 62.2 us
  waiting for transfers between devices  23.4 us (38%)
  Pallas kernels  19.2 us (31%)
  starting transfers between devices  19.1 us (31%)
    ppermute x27, waiting for transfers between devices, exchange(): return lax.ppermute(cells, axis, [(i, i ^ distance) for i in range(count)])  23.4 us
    ppermute x27, starting transfers between devices, exchange(): return lax.ppermute(cells, axis, [(i, i ^ distance) for i in range(count)])  19.1 us
    pallas_call x22, Pallas kernels, call(): pl.pallas_call(kernel, out_shape=outs, in_specs=whole(len(args)), out_spe...  15.3 us
    pallas_call x1, Pallas kernels, load(): pl.pallas_call(functools.partial(load_kernel, count), out_shape=[sds(w.sh...  2.64 us
  transfers between devices with their start and end apart: 27, of which 11 were waited for; matrix products, arithmetic and copies ran while one was open for 0% of the time, Pallas kernels for 25%

profile of v12, /device:TPU:0, one launch (start us, length us, event | category | flops | bytes accessed | tf_op | source)
XLA Modules:
  0.0 62.2 jit_solution(1218622705095563586)
XLA Ops:
  0.0 1.2 %shard_map.136 = (bf16[200,128]{1,0:T(8,128)(2,1)S(1)}, bf16[200,128]{1,0:T(8,128)(2,1)S(1)}, bf16[200,128]{1,0:T(8,128)(2,1)S(1)}, bf16[200,128]{1,0:T(8,128)(2,1)S(1)}) custom-call(bf16[2,160,128]{2,1,0:T(8,128)(2,1)} %bitcast.3, bf16[2,160,128]{2,1,0:T(8,128)(2,1)} %bitcast.4), custom_call_target="tpu_custom_call" | custom-call | tf_op jit(solution)/shard_map/pallas_call | solution.py:446
  1.2 3.1 %collective-permute-start = (bf16[200,128]{1,0:T(8,128)(2,1)S(1)}, bf16[200,128]{1,0:T(8,128)(2,1)S(1)}, u32[]{:S(2)}, u32[]{:S(2)}) collective-permute-start(bf16[200,128]{1,0:T(8,128)(2,1)S(1)} %get-tuple-element.29), channel_id=1, source_target_pairs={{0,2},{2,0},{4,6},{6,4},{1,3},{3,1},{5,7},{7,5},{8,10},{10,8},{12,... | collective-permute-start | bytes 153608 | tf_op jit(solution)/shard_map/ppermute | solution.py:25
  4.3 2.6 %collective-permute-start.1 = (bf16[200,128]{1,0:T(8,128)(2,1)S(1)}, bf16[200,128]{1,0:T(8,128)(2,1)S(1)}, u32[]{:S(2)}, u32[]{:S(2)}) collective-permute-start(bf16[200,128]{1,0:T(8,128)(2,1)S(1)} %get-tuple-element.30), channel_id=1, source_target_pairs={{0,4},{2,6},{4,0},{6,2},{1,5},{3,7},{5,1},{7,3},{8,12},{10,14},{12... | collective-permute-start | bytes 153608 | tf_op jit(solution)/shard_map/ppermute | solution.py:25
  6.9 3.4 %collective-permute-done.1.refs_2_ = bf16[200,128]{1,0:T(8,128)(2,1)S(1)} collective-permute-done((bf16[200,128]{1,0:T(8,128)(2,1)S(1)}, bf16[200,128]{1,0:T(8,128)(2,1)S(1)}, u32[]{:S(2)}, u32[]{:S(2)}) %collective-permute-start.1) | collective-permute-done | bytes 51232 | tf_op jit(solution)/shard_map/ppermute | solution.py:25
  10.3 2.5 %collective-permute-done.2.refs_3_ = bf16[200,128]{1,0:T(8,128)(2,1)S(1)} collective-permute-done((bf16[200,128]{1,0:T(8,128)(2,1)S(1)}, bf16[200,128]{1,0:T(8,128)(2,1)S(1)}, u32[]{:S(2)}, u32[]{:S(2)}) %collective-permute-start.2) | collective-permute-done | bytes 51232 | tf_op jit(solution)/shard_map/ppermute | solution.py:25
  13.2 1.5 %collective-permute-start.12 = (bf16[400,128]{1,0:T(8,128)(2,1)S(1)}, bf16[400,128]{1,0:T(8,128)(2,1)S(1)}, u32[]{:S(2)}, u32[]{:S(2)}) collective-permute-start(bf16[400,128]{1,0:T(8,128)(2,1)S(1)} %get-tuple-element.39.refs_0_), channel_id=1, source_target_pairs={{0,8},{8,0},{1,9},{9,1},{2,10},{10,2},{3,11},{11,3},{4,12},{12,4},... | collective-permute-start | bytes 307208 | tf_op jit(solution)/shard_map/ppermute | solution.py:25
  14.7 0.4 shard_map.137
  15.1 0.6 collective-permute-start.3
  15.6 0.5 collective-permute-start.5
  16.2 1.7 %collective-permute-done.12.refs_0_ = bf16[400,128]{1,0:T(8,128)(2,1)S(1)} collective-permute-done((bf16[400,128]{1,0:T(8,128)(2,1)S(1)}, bf16[400,128]{1,0:T(8,128)(2,1)S(1)}, u32[]{:S(2)}, u32[]{:S(2)}) %collective-permute-start.12) | collective-permute-done | bytes 102432 | tf_op jit(solution)/shard_map/ppermute | solution.py:25
  17.9 1.9 %collective-permute-done.3.refs_0_ = bf16[400,128]{1,0:T(8,128)(2,1)S(1)} collective-permute-done((bf16[400,128]{1,0:T(8,128)(2,1)S(1)}, bf16[400,128]{1,0:T(8,128)(2,1)S(1)}, u32[]{:S(2)}, u32[]{:S(2)}) %collective-permute-start.3) | collective-permute-done | bytes 102432 | tf_op jit(solution)/shard_map/ppermute | solution.py:25
  19.8 2.6 %shard_map.138 = (bf16[3,3,160,640]{3,2,1,0:T(8,128)(2,1)S(1)}, bf16[3,3,160,640]{3,2,1,0:T(8,128)(2,1)S(1)}, bf16[3,3,160,640]{3,2,1,0:T(8,128)(2,1)S(1)}) custom-call(bf16[3,3,160,640]{3,2,1,0:T(8,128)(2,1)} %refs_0_.1, bf16[3,3,160,640]{3,2,1,0:T(8,128)(2,1)} %refs_1_.1, bf16[3,3,160,640]{3,2,1,0:T(8,128)(2,1)} %refs_2_.9), custom_call_target="tpu_custom_call" | custom-call | bytes 5529600 | tf_op jit(solution)/shard_map/pallas_call | solution.py:192
  22.4 0.8 %shard_map.146.refs_1_ = f32[304,160]{1,0:T(8,128)S(1)} custom-call(bf16[400,128]{1,0:T(8,128)(2,1)S(1)} %get-tuple-element.39.refs_0_, bf16[400,128]{1,0:T(8,128)(2,1)S(1)} %collective-permute-done.14.refs_1_, bf16[3,3,160,640]{3,2,1,0:T(8,128)(2,1)S(1)} %get-tuple-element.40.refs_2_), custom_call_target="tpu_custom_call" | custom-call | flops 294912000 | bytes 2242560 | tf_op jit(solution)/shard_map/pallas_call | solution.py:44
  23.2 0.5 shard_map.147.refs_1_
  23.8 0.8 %shard_map.139.refs_2_ = f32[304,160]{1,0:T(8,128)S(1)} custom-call(bf16[400,128]{1,0:T(8,128)(2,1)S(1)} %get-tuple-element.32.refs_0_, bf16[400,128]{1,0:T(8,128)(2,1)S(1)} %collective-permute-done.5.refs_1_, bf16[3,3,160,640]{3,2,1,0:T(8,128)(2,1)S(1)} %get-tuple-element.33.refs_2_.refs_3_), custom_call_target="tpu_custom_call" | custom-call | flops 294912000 | bytes 2242560 | tf_op jit(solution)/shard_map/pallas_call | solution.py:44
  24.6 0.7 %shard_map.148 = (bf16[304,160]{1,0:T(8,128)(2,1)S(1)}, bf16[384,128]{1,0:T(8,128)(2,1)S(1)}) custom-call(bf16[400,128]{1,0:T(8,128)(2,1)S(1)} %collective-permute-done.13.refs_0_, f32[304,160]{1,0:T(8,128)S(1)} %shard_map.147.refs_1_, bf16[3,3,160,640]{3,2,1,0:T(8,128)(2,1)S(1)} %get-tuple-element.40.refs_2_, ...), custom_call_target="tpu_custom_call" | custom-call | flops 147456000 | bytes 2438464 | tf_op jit(solution)/shard_map/pallas_call | solution.py:44
  25.3 0.8 %collective-permute-start.15 = (bf16[384,128]{1,0:T(8,128)(2,1)S(1)}, bf16[384,128]{1,0:T(8,128)(2,1)S(1)}, u32[]{:S(2)}, u32[]{:S(2)}) collective-permute-start(bf16[384,128]{1,0:T(8,128)(2,1)S(1)} %get-tuple-element.42.refs_0_), channel_id=1, source_target_pairs={{0,8},{8,0},{1,9},{9,1},{2,10},{10,2},{3,11},{11,3},{4,12},{12,4},... | collective-permute-start | bytes 294920 | tf_op jit(solution)/shard_map/ppermute | solution.py:25
  26.1 1.0 %shard_map.140 = (bf16[304,160]{1,0:T(8,128)(2,1)S(1)}, bf16[384,128]{1,0:T(8,128)(2,1)S(1)}) custom-call(bf16[400,128]{1,0:T(8,128)(2,1)S(1)} %collective-permute-done.3.refs_0_, bf16[400,128]{1,0:T(8,128)(2,1)S(1)} %collective-permute-done.4.refs_1_, f32[304,160]{1,0:T(8,128)S(1)} %shard_map.139.refs_2_, ...), custom_call_target="tpu_custom_call" | custom-call | flops 294912000 | bytes 2540864 | tf_op jit(solution)/shard_map/pallas_call | solution.py:44
  27.1 1.4 %collective-permute-start.6 = (bf16[384,128]{1,0:T(8,128)(2,1)S(1)}, bf16[384,128]{1,0:T(8,128)(2,1)S(1)}, u32[]{:S(2)}, u32[]{:S(2)}) collective-permute-start(bf16[384,128]{1,0:T(8,128)(2,1)S(1)} %get-tuple-element.35.refs_0_), channel_id=1, source_target_pairs={{0,8},{8,0},{1,9},{9,1},{2,10},{10,2},{3,11},{11,3},{4,12},{12,4},... | collective-permute-start | bytes 294920 | tf_op jit(solution)/shard_map/ppermute | solution.py:25
  28.4 0.5 collective-permute-start.8
  29.0 2.1 %collective-permute-done.15.refs_0_ = bf16[384,128]{1,0:T(8,128)(2,1)S(1)} collective-permute-done((bf16[384,128]{1,0:T(8,128)(2,1)S(1)}, bf16[384,128]{1,0:T(8,128)(2,1)S(1)}, u32[]{:S(2)}, u32[]{:S(2)}) %collective-permute-start.15) | collective-permute-done | bytes 98336 | tf_op jit(solution)/shard_map/ppermute | solution.py:25
  31.0 1.6 %collective-permute-done.6.refs_0_ = bf16[384,128]{1,0:T(8,128)(2,1)S(1)} collective-permute-done((bf16[384,128]{1,0:T(8,128)(2,1)S(1)}, bf16[384,128]{1,0:T(8,128)(2,1)S(1)}, u32[]{:S(2)}, u32[]{:S(2)}) %collective-permute-start.6) | collective-permute-done | bytes 98336 | tf_op jit(solution)/shard_map/ppermute | solution.py:25
  32.7 0.7 %shard_map.149.refs_1_ = f32[288,160]{1,0:T(8,128)S(1)} custom-call(bf16[384,128]{1,0:T(8,128)(2,1)S(1)} %get-tuple-element.42.refs_0_, bf16[384,128]{1,0:T(8,128)(2,1)S(1)} %collective-permute-done.17.refs_1_, bf16[3,3,160,640]{3,2,1,0:T(8,128)(2,1)S(1)} %copy-done.2), custom_call_target="tpu_custom_call" | custom-call | flops 294912000 | bytes 2224128 | tf_op jit(solution)/shard_map/pallas_call | solution.py:44
  33.5 0.5 shard_map.150.refs_1_
  34.0 0.7 %shard_map.141.refs_2_ = f32[288,160]{1,0:T(8,128)S(1)} custom-call(bf16[384,128]{1,0:T(8,128)(2,1)S(1)} %get-tuple-element.35.refs_0_, bf16[384,128]{1,0:T(8,128)(2,1)S(1)} %collective-permute-done.8.refs_1_, bf16[3,3,160,640]{3,2,1,0:T(8,128)(2,1)S(1)} %get-tuple-element.36.refs_2_.refs_3_), custom_call_target="tpu_custom_call" | custom-call | flops 294912000 | bytes 2224128 | tf_op jit(solution)/shard_map/pallas_call | solution.py:44
  34.8 0.7 %shard_map.151.refs_0_ = bf16[360,128]{1,0:T(8,128)(2,1)S(1)} custom-call(bf16[384,128]{1,0:T(8,128)(2,1)S(1)} %collective-permute-done.16.refs_0_, f32[288,160]{1,0:T(8,128)S(1)} %shard_map.150.refs_1_, bf16[3,3,160,640]{3,2,1,0:T(8,128)(2,1)S(1)} %copy-done.2, bf16[304,160]{1,0:T(8,128)(2,1)S(1)} %get-tuple-element.43.refs_3_, bf16[160]{0:T(256)(128)(2,1)S(1)} %copy-done.3), custom_call_target="tpu_custom_call" | custom-call | flops 147456000 | bytes 2315584 | tf_op jit(solution)/shard_map/pallas_call | solution.py:44
  35.5 0.8 %collective-permute-start.18 = (bf16[360,128]{1,0:T(8,128)(2,1)S(1)}, bf16[360,128]{1,0:T(8,128)(2,1)S(1)}, u32[]{:S(2)}, u32[]{:S(2)}) collective-permute-start(bf16[360,128]{1,0:T(8,128)(2,1)S(1)} %shard_map.151.refs_0_), channel_id=1, source_target_pairs={{0,8},{8,0},{1,9},{9,1},{2,10},{10,2},{3,11},{11,3},{4,12},{12,4},... | collective-permute-start | bytes 276488 | tf_op jit(solution)/shard_map/ppermute | solution.py:25
  36.3 1.0 %shard_map.142 = (bf16[288,160]{1,0:T(8,128)(2,1)S(1)}, bf16[360,128]{1,0:T(8,128)(2,1)S(1)}) custom-call(bf16[384,128]{1,0:T(8,128)(2,1)S(1)} %collective-permute-done.6.refs_0_, bf16[384,128]{1,0:T(8,128)(2,1)S(1)} %collective-permute-done.7.refs_1_, f32[288,160]{1,0:T(8,128)S(1)} %shard_map.141.refs_2_, ...), custom_call_target="tpu_custom_call" | custom-call | flops 294912000 | bytes 2506048 | tf_op jit(solution)/shard_map/pallas_call | solution.py:44
  37.3 1.3 %collective-permute-start.9 = (bf16[360,128]{1,0:T(8,128)(2,1)S(1)}, bf16[360,128]{1,0:T(8,128)(2,1)S(1)}, u32[]{:S(2)}, u32[]{:S(2)}) collective-permute-start(bf16[360,128]{1,0:T(8,128)(2,1)S(1)} %get-tuple-element.38.refs_0_), channel_id=1, source_target_pairs={{0,8},{8,0},{1,9},{9,1},{2,10},{10,2},{3,11},{11,3},{4,12},{12,4},... | collective-permute-start | bytes 276488 | tf_op jit(solution)/shard_map/ppermute | solution.py:25
  38.6 0.5 collective-permute-start.20
  39.1 2.0 %collective-permute-done.18.refs_0_.refs_2_ = bf16[360,128]{1,0:T(8,128)(2,1)S(1)} collective-permute-done((bf16[360,128]{1,0:T(8,128)(2,1)S(1)}, bf16[360,128]{1,0:T(8,128)(2,1)S(1)}, u32[]{:S(2)}, u32[]{:S(2)}) %collective-permute-start.18) | collective-permute-done | bytes 92192 | tf_op jit(solution)/shard_map/ppermute | solution.py:25
  41.1 1.5 %collective-permute-done.9.refs_0_ = bf16[360,128]{1,0:T(8,128)(2,1)S(1)} collective-permute-done((bf16[360,128]{1,0:T(8,128)(2,1)S(1)}, bf16[360,128]{1,0:T(8,128)(2,1)S(1)}, u32[]{:S(2)}, u32[]{:S(2)}) %collective-permute-start.9) | collective-permute-done | bytes 92192 | tf_op jit(solution)/shard_map/ppermute | solution.py:25
  42.6 0.7 %shard_map.143.refs_1_ = f32[272,160]{1,0:T(8,128)S(1)} custom-call(bf16[360,128]{1,0:T(8,128)(2,1)S(1)} %get-tuple-element.38.refs_0_, bf16[360,128]{1,0:T(8,128)(2,1)S(1)} %collective-permute-done.11.refs_1_, bf16[3,3,160,1280]{3,2,1,0:T(8,128)(2,1)S(1)} %copy-done), custom_call_target="tpu_custom_call" | custom-call | flops 294912000 | bytes 4044800 | tf_op jit(solution)/shard_map/pallas_call | solution.py:44
  43.4 0.5 shard_map.144.refs_1_
  43.9 0.7 %shard_map.152.refs_2_ = f32[272,160]{1,0:T(8,128)S(1)} custom-call(bf16[360,128]{1,0:T(8,128)(2,1)S(1)} %shard_map.151.refs_0_, bf16[360,128]{1,0:T(8,128)(2,1)S(1)} %collective-permute-done.20.refs_1_, bf16[3,3,160,1280]{3,2,1,0:T(8,128)(2,1)S(1)} %copy-done), custom_call_target="tpu_custom_call" | custom-call | flops 294912000 | bytes 4044800 | tf_op jit(solution)/shard_map/pallas_call | solution.py:44
  44.7 0.7 %shard_map.153.refs_2_ = f32[272,160]{1,0:T(8,128)S(1)} custom-call(bf16[360,128]{1,0:T(8,128)(2,1)S(1)} %collective-permute-done.18.refs_0_.refs_2_, bf16[360,128]{1,0:T(8,128)(2,1)S(1)} %collective-permute-done.19.refs_1_.refs_3_, f32[272,160]{1,0:T(8,128)S(1)} %shard_map.152.refs_2_, bf16[3,3,160,1280]{3,2,1,0:T(8,128)(2,1)S(1)} %copy-done), custom_call_target="tpu_custom_call" | custom-call | flops 294912000 | bytes 4218880 | tf_op jit(solution)/shard_map/pallas_call | solution.py:44
  45.4 0.7 %shard_map.154 = (bf16[272,160]{1,0:T(8,128)(2,1)S(1)}, bf16[344,128]{1,0:T(8,128)(2,1)S(1)}) custom-call(bf16[360,128]{1,0:T(8,128)(2,1)S(1)} %collective-permute-done.10.refs_0_, f32[272,160]{1,0:T(8,128)S(1)} %shard_map.144.refs_1_, f32[272,160]{1,0:T(8,128)S(1)} %shard_map.153.refs_2_, bf16[3,3,160,1280]{3,2,1,0:T(8,128)(2,1)S(1)} %copy-done, ...), custom_call_target="tpu_custom_call" | custom-call | flops 147456000 | bytes 4394304 | tf_op jit(solution)/shard_map/pallas_call | solution.py:44
  46.1 0.8 %collective-permute-start.21 = (bf16[344,128]{1,0:T(8,128)(2,1)S(1)}, bf16[344,128]{1,0:T(8,128)(2,1)S(1)}, u32[]{:S(2)}, u32[]{:S(2)}) collective-permute-start(bf16[344,128]{1,0:T(8,128)(2,1)S(1)} %get-tuple-element.45.refs_0_), channel_id=1, source_target_pairs={{0,8},{8,0},{1,9},{9,1},{2,10},{10,2},{3,11},{11,3},{4,12},{12,4},... | collective-permute-start | bytes 264200 | tf_op jit(solution)/shard_map/ppermute | solution.py:25
  47.2 4.0 %collective-permute-done.21.refs_0_ = bf16[344,128]{1,0:T(8,128)(2,1)S(1)} collective-permute-done((bf16[344,128]{1,0:T(8,128)(2,1)S(1)}, bf16[344,128]{1,0:T(8,128)(2,1)S(1)}, u32[]{:S(2)}, u32[]{:S(2)}) %collective-permute-start.21) | collective-permute-done | bytes 88096 | tf_op jit(solution)/shard_map/ppermute | solution.py:25
  51.1 1.1 %shard_map.157.refs_2_ = f32[256,160]{1,0:T(8,128)S(1)} custom-call(bf16[360,128]{1,0:T(8,128)(2,1)S(1)} %shard_map.151.refs_0_, bf16[360,128]{1,0:T(8,128)(2,1)S(1)} %collective-permute-done.20.refs_1_, bf16[360,128]{1,0:T(8,128)(2,1)S(1)} %collective-permute-done.18.refs_0_.refs_2_, bf16[360,128]{1,0:T(8,128)(2,1)S(1)} %collective-permute-done.19.refs_1_.refs_3_, ...), custom_call_target="tpu_custom_call" | custom-call | flops 589824000 | bytes 4218880 | tf_op jit(solution)/shard_map/pallas_call | solution.py:44
  52.3 0.7 %shard_map.155.refs_1_ = f32[256,160]{1,0:T(8,128)S(1)} custom-call(bf16[344,128]{1,0:T(8,128)(2,1)S(1)} %get-tuple-element.45.refs_0_, bf16[344,128]{1,0:T(8,128)(2,1)S(1)} %collective-permute-done.23.refs_1_, bf16[3,3,160,1280]{3,2,1,0:T(8,128)(2,1)S(1)} %copy-done.1), custom_call_target="tpu_custom_call" | custom-call | flops 294912000 | bytes 4026368 | tf_op jit(solution)/shard_map/pallas_call | solution.py:44
  53.0 0.5 shard_map.156.refs_1_
  53.6 0.6 shard_map.158
  54.3 1.4 %collective-permute-start.25 = (bf16[80,128]{1,0:T(8,128)(2,1)S(1)}, bf16[80,128]{1,0:T(8,128)(2,1)S(1)}, u32[]{:S(2)}, u32[]{:S(2)}) collective-permute-start(bf16[80,128]{1,0:T(8,128)(2,1)S(1)} %get-tuple-element.49), channel_id=1, source_target_pairs={{0,4},{2,6},{4,0},{6,2},{1,5},{3,7},{5,1},{7,3},{8,12},{10,14},{12... | collective-permute-start | bytes 61448 | tf_op jit(solution)/shard_map/ppermute | solution.py:25
  55.7 2.9 %collective-permute-start.26 = (bf16[80,128]{1,0:T(8,128)(2,1)S(1)}, bf16[80,128]{1,0:T(8,128)(2,1)S(1)}, u32[]{:S(2)}, u32[]{:S(2)}) collective-permute-start(bf16[80,128]{1,0:T(8,128)(2,1)S(1)} %get-tuple-element.50), channel_id=1, source_target_pairs={{0,6},{2,4},{4,2},{6,0},{1,7},{3,5},{5,3},{7,1},{8,14},{10,12},{12... | collective-permute-start | bytes 61448 | tf_op jit(solution)/shard_map/ppermute | solution.py:25
  58.7 0.6 collective-permute-done.25.refs_2_
  59.2 2.1 %collective-permute-done.26.refs_3_ = bf16[80,128]{1,0:T(8,128)(2,1)S(1)} collective-permute-done((bf16[80,128]{1,0:T(8,128)(2,1)S(1)}, bf16[80,128]{1,0:T(8,128)(2,1)S(1)}, u32[]{:S(2)}, u32[]{:S(2)}) %collective-permute-start.26) | collective-permute-done | bytes 20512 | tf_op jit(solution)/shard_map/ppermute | solution.py:25
  61.3 0.8 %shard_map.159 = bf16[2,160,128]{2,1,0:T(8,128)(2,1)} custom-call(bf16[80,128]{1,0:T(8,128)(2,1)S(1)} %get-tuple-element.47.refs_0_, bf16[80,128]{1,0:T(8,128)(2,1)S(1)} %collective-permute-done.24.refs_1_, bf16[80,128]{1,0:T(8,128)(2,1)S(1)} %collective-permute-done.25.refs_2_, bf16[80,128]{1,0:T(8,128)(2,1)S(1)} %collective-permute-done.26.refs_3_), custom_call_target="tpu_custom_call" | custom-call | bytes 163840 | tf_op jit(solution)/shard_map/pallas_call | solution.py:44
  (48 shorter events, 0.9 us)
Async XLA Ops:
  1.2 5.7 %collective-permute-start = (bf16[200,128]{1,0:T(8,128)(2,1)S(1)}, bf16[200,128]{1,0:T(8,128)(2,1)S(1)}, u32[]{:S(2)}, u32[]{:S(2)}) collective-permute-start(bf16[200,128]{1,0:T(8,128)(2,1)S(1)} %get-tuple-element.29), channel_id=1, source_target_pairs={{0,2},{2,0},{4,6},{6,4},{1,3},{3,1},{5,7},{7,5},{8,10},{10,8},{12,... | collective-permute-start | bytes 153608 | tf_op jit(solution)/shard_map/ppermute | solution.py:25
  4.3 6.0 %collective-permute-start.1 = (bf16[200,128]{1,0:T(8,128)(2,1)S(1)}, bf16[200,128]{1,0:T(8,128)(2,1)S(1)}, u32[]{:S(2)}, u32[]{:S(2)}) collective-permute-start(bf16[200,128]{1,0:T(8,128)(2,1)S(1)} %get-tuple-element.30), channel_id=1, source_target_pairs={{0,4},{2,6},{4,0},{6,2},{1,5},{3,7},{5,1},{7,3},{8,12},{10,14},{12... | collective-permute-start | bytes 153608 | tf_op jit(solution)/shard_map/ppermute | solution.py:25
  6.9 5.9 %collective-permute-start.2 = (bf16[200,128]{1,0:T(8,128)(2,1)S(1)}, bf16[200,128]{1,0:T(8,128)(2,1)S(1)}, u32[]{:S(2)}, u32[]{:S(2)}) collective-permute-start(bf16[200,128]{1,0:T(8,128)(2,1)S(1)} %get-tuple-element.31), channel_id=1, source_target_pairs={{0,6},{2,4},{4,2},{6,0},{1,7},{3,5},{5,3},{7,1},{8,14},{10,12},{12... | collective-permute-start | bytes 153608 | tf_op jit(solution)/shard_map/ppermute | solution.py:25
  13.2 4.7 %collective-permute-start.12 = (bf16[400,128]{1,0:T(8,128)(2,1)S(1)}, bf16[400,128]{1,0:T(8,128)(2,1)S(1)}, u32[]{:S(2)}, u32[]{:S(2)}) collective-permute-start(bf16[400,128]{1,0:T(8,128)(2,1)S(1)} %get-tuple-element.39.refs_0_), channel_id=1, source_target_pairs={{0,8},{8,0},{1,9},{9,1},{2,10},{10,2},{3,11},{11,3},{4,12},{12,4},... | collective-permute-start | bytes 307208 | tf_op jit(solution)/shard_map/ppermute | solution.py:25
  15.1 4.7 %collective-permute-start.3 = (bf16[400,128]{1,0:T(8,128)(2,1)S(1)}, bf16[400,128]{1,0:T(8,128)(2,1)S(1)}, u32[]{:S(2)}, u32[]{:S(2)}) collective-permute-start(bf16[400,128]{1,0:T(8,128)(2,1)S(1)} %get-tuple-element.32.refs_0_), channel_id=1, source_target_pairs={{0,8},{8,0},{1,9},{9,1},{2,10},{10,2},{3,11},{11,3},{4,12},{12,4},... | collective-permute-start | bytes 307208 | tf_op jit(solution)/shard_map/ppermute | solution.py:25
  15.6 6.8 %collective-permute-start.14 = (bf16[400,128]{1,0:T(8,128)(2,1)S(1)}, bf16[400,128]{1,0:T(8,128)(2,1)S(1)}, u32[]{:S(2)}, u32[]{:S(2)}) collective-permute-start(bf16[400,128]{1,0:T(8,128)(2,1)S(1)} %get-tuple-element.39.refs_0_), channel_id=1, source_target_pairs={{0,1},{1,0},{2,3},{3,2},{4,5},{5,4},{6,7},{7,6},{8,9},{9,8},{10,11... | collective-permute-start | bytes 307208 | tf_op jit(solution)/shard_map/ppermute | solution.py:25
  15.6 8.1 %collective-permute-start.5 = (bf16[400,128]{1,0:T(8,128)(2,1)S(1)}, bf16[400,128]{1,0:T(8,128)(2,1)S(1)}, u32[]{:S(2)}, u32[]{:S(2)}) collective-permute-start(bf16[400,128]{1,0:T(8,128)(2,1)S(1)} %get-tuple-element.32.refs_0_), channel_id=1, source_target_pairs={{0,1},{1,0},{2,3},{3,2},{4,5},{5,4},{6,7},{7,6},{8,9},{9,8},{10,11... | collective-permute-start | bytes 307208 | tf_op jit(solution)/shard_map/ppermute | solution.py:25
  17.9 6.7 %collective-permute-start.13 = (bf16[400,128]{1,0:T(8,128)(2,1)S(1)}, bf16[400,128]{1,0:T(8,128)(2,1)S(1)}, u32[]{:S(2)}, u32[]{:S(2)}) collective-permute-start(bf16[400,128]{1,0:T(8,128)(2,1)S(1)} %collective-permute-done.12.refs_0_), channel_id=1, source_target_pairs={{0,1},{1,0},{2,3},{3,2},{4,5},{5,4},{6,7},{7,6},{8,9},{9,8},{10,11... | collective-permute-start | bytes 307208 | tf_op jit(solution)/shard_map/ppermute | solution.py:25
  19.8 6.3 %collective-permute-start.4 = (bf16[400,128]{1,0:T(8,128)(2,1)S(1)}, bf16[400,128]{1,0:T(8,128)(2,1)S(1)}, u32[]{:S(2)}, u32[]{:S(2)}) collective-permute-start(bf16[400,128]{1,0:T(8,128)(2,1)S(1)} %collective-permute-done.3.refs_0_), channel_id=1, source_target_pairs={{0,1},{1,0},{2,3},{3,2},{4,5},{5,4},{6,7},{7,6},{8,9},{9,8},{10,11... | collective-permute-start | bytes 307208 | tf_op jit(solution)/shard_map/ppermute | solution.py:25
  23.2 1.4 %copy-start.6 = (bf16[160]{0:T(256)(128)(2,1)S(1)}, bf16[160]{0:T(256)(128)(2,1)}, u32[]{:S(2)}) copy-start(bf16[160]{0:T(256)(128)(2,1)} %refs_4_.3) | copy-start | bytes 964
  23.8 2.3 %copy-start.7 = (bf16[160]{0:T(256)(128)(2,1)S(1)}, bf16[160]{0:T(256)(128)(2,1)}, u32[]{:S(2)}) copy-start(bf16[160]{0:T(256)(128)(2,1)} %refs_5_.4) | copy-start | bytes 964
  25.3 7.4 %copy-start.2 = (bf16[3,3,160,640]{3,2,1,0:T(8,128)(2,1)S(1)}, bf16[3,3,160,640]{3,2,1,0:T(8,128)(2,1)}, u32[]{:S(2)}) copy-start(bf16[3,3,160,640]{3,2,1,0:T(8,128)(2,1)} %refs_2_.14) | copy-start | bytes 5529604
  25.3 5.7 %collective-permute-start.15 = (bf16[384,128]{1,0:T(8,128)(2,1)S(1)}, bf16[384,128]{1,0:T(8,128)(2,1)S(1)}, u32[]{:S(2)}, u32[]{:S(2)}) collective-permute-start(bf16[384,128]{1,0:T(8,128)(2,1)S(1)} %get-tuple-element.42.refs_0_), channel_id=1, source_target_pairs={{0,8},{8,0},{1,9},{9,1},{2,10},{10,2},{3,11},{11,3},{4,12},{12,4},... | collective-permute-start | bytes 294920 | tf_op jit(solution)/shard_map/ppermute | solution.py:25
  27.1 5.6 %collective-permute-start.6 = (bf16[384,128]{1,0:T(8,128)(2,1)S(1)}, bf16[384,128]{1,0:T(8,128)(2,1)S(1)}, u32[]{:S(2)}, u32[]{:S(2)}) collective-permute-start(bf16[384,128]{1,0:T(8,128)(2,1)S(1)} %get-tuple-element.35.refs_0_), channel_id=1, source_target_pairs={{0,8},{8,0},{1,9},{9,1},{2,10},{10,2},{3,11},{11,3},{4,12},{12,4},... | collective-permute-start | bytes 294920 | tf_op jit(solution)/shard_map/ppermute | solution.py:25
  28.4 4.3 %collective-permute-start.17 = (bf16[384,128]{1,0:T(8,128)(2,1)S(1)}, bf16[384,128]{1,0:T(8,128)(2,1)S(1)}, u32[]{:S(2)}, u32[]{:S(2)}) collective-permute-start(bf16[384,128]{1,0:T(8,128)(2,1)S(1)} %get-tuple-element.42.refs_0_), channel_id=1, source_target_pairs={{0,1},{1,0},{2,3},{3,2},{4,5},{5,4},{6,7},{7,6},{8,9},{9,8},{10,11... | collective-permute-start | bytes 294920 | tf_op jit(solution)/shard_map/ppermute | solution.py:25
  28.4 5.6 %collective-permute-start.8 = (bf16[384,128]{1,0:T(8,128)(2,1)S(1)}, bf16[384,128]{1,0:T(8,128)(2,1)S(1)}, u32[]{:S(2)}, u32[]{:S(2)}) collective-permute-start(bf16[384,128]{1,0:T(8,128)(2,1)S(1)} %get-tuple-element.35.refs_0_), channel_id=1, source_target_pairs={{0,1},{1,0},{2,3},{3,2},{4,5},{5,4},{6,7},{7,6},{8,9},{9,8},{10,11... | collective-permute-start | bytes 294920 | tf_op jit(solution)/shard_map/ppermute | solution.py:25
  31.0 3.7 %collective-permute-start.16 = (bf16[384,128]{1,0:T(8,128)(2,1)S(1)}, bf16[384,128]{1,0:T(8,128)(2,1)S(1)}, u32[]{:S(2)}, u32[]{:S(2)}) collective-permute-start(bf16[384,128]{1,0:T(8,128)(2,1)S(1)} %collective-permute-done.15.refs_0_), channel_id=1, source_target_pairs={{0,1},{1,0},{2,3},{3,2},{4,5},{5,4},{6,7},{7,6},{8,9},{9,8},{10,11... | collective-permute-start | bytes 294920 | tf_op jit(solution)/shard_map/ppermute | solution.py:25
  32.7 3.6 %collective-permute-start.7 = (bf16[384,128]{1,0:T(8,128)(2,1)S(1)}, bf16[384,128]{1,0:T(8,128)(2,1)S(1)}, u32[]{:S(2)}, u32[]{:S(2)}) collective-permute-start(bf16[384,128]{1,0:T(8,128)(2,1)S(1)} %collective-permute-done.6.refs_0_), channel_id=1, source_target_pairs={{0,1},{1,0},{2,3},{3,2},{4,5},{5,4},{6,7},{7,6},{8,9},{9,8},{10,11... | collective-permute-start | bytes 294920 | tf_op jit(solution)/shard_map/ppermute | solution.py:25
  33.5 1.3 %copy-start.3 = (bf16[160]{0:T(256)(128)(2,1)S(1)}, bf16[160]{0:T(256)(128)(2,1)}, u32[]{:S(2)}) copy-start(bf16[160]{0:T(256)(128)(2,1)} %refs_4_.4) | copy-start | bytes 964
  34.0 2.3 %copy-start.8 = (bf16[160]{0:T(256)(128)(2,1)S(1)}, bf16[160]{0:T(256)(128)(2,1)}, u32[]{:S(2)}) copy-start(bf16[160]{0:T(256)(128)(2,1)} %refs_5_.5) | copy-start | bytes 964
  34.8 7.8 %copy-start = (bf16[3,3,160,1280]{3,2,1,0:T(8,128)(2,1)S(1)}, bf16[3,3,160,1280]{3,2,1,0:T(8,128)(2,1)}, u32[]{:S(2)}) copy-start(bf16[3,3,160,1280]{3,2,1,0:T(8,128)(2,1)} %refs_3_.4) | copy-start | bytes 11059204
  35.5 5.6 %collective-permute-start.18 = (bf16[360,128]{1,0:T(8,128)(2,1)S(1)}, bf16[360,128]{1,0:T(8,128)(2,1)S(1)}, u32[]{:S(2)}, u32[]{:S(2)}) collective-permute-start(bf16[360,128]{1,0:T(8,128)(2,1)S(1)} %shard_map.151.refs_0_), channel_id=1, source_target_pairs={{0,8},{8,0},{1,9},{9,1},{2,10},{10,2},{3,11},{11,3},{4,12},{12,4},... | collective-permute-start | bytes 276488 | tf_op jit(solution)/shard_map/ppermute | solution.py:25
  37.3 5.4 %collective-permute-start.9 = (bf16[360,128]{1,0:T(8,128)(2,1)S(1)}, bf16[360,128]{1,0:T(8,128)(2,1)S(1)}, u32[]{:S(2)}, u32[]{:S(2)}) collective-permute-start(bf16[360,128]{1,0:T(8,128)(2,1)S(1)} %get-tuple-element.38.refs_0_), channel_id=1, source_target_pairs={{0,8},{8,0},{1,9},{9,1},{2,10},{10,2},{3,11},{11,3},{4,12},{12,4},... | collective-permute-start | bytes 276488 | tf_op jit(solution)/shard_map/ppermute | solution.py:25
  38.6 4.0 %collective-permute-start.11 = (bf16[360,128]{1,0:T(8,128)(2,1)S(1)}, bf16[360,128]{1,0:T(8,128)(2,1)S(1)}, u32[]{:S(2)}, u32[]{:S(2)}) collective-permute-start(bf16[360,128]{1,0:T(8,128)(2,1)S(1)} %get-tuple-element.38.refs_0_), channel_id=1, source_target_pairs={{0,1},{1,0},{2,3},{3,2},{4,5},{5,4},{6,7},{7,6},{8,9},{9,8},{10,11... | collective-permute-start | bytes 276488 | tf_op jit(solution)/shard_map/ppermute | solution.py:25
  38.6 5.3 %collective-permute-start.20 = (bf16[360,128]{1,0:T(8,128)(2,1)S(1)}, bf16[360,128]{1,0:T(8,128)(2,1)S(1)}, u32[]{:S(2)}, u32[]{:S(2)}) collective-permute-start(bf16[360,128]{1,0:T(8,128)(2,1)S(1)} %shard_map.151.refs_0_), channel_id=1, source_target_pairs={{0,1},{1,0},{2,3},{3,2},{4,5},{5,4},{6,7},{7,6},{8,9},{9,8},{10,11... | collective-permute-start | bytes 276488 | tf_op jit(solution)/shard_map/ppermute | solution.py:25
  41.1 3.5 %collective-permute-start.19 = (bf16[360,128]{1,0:T(8,128)(2,1)S(1)}, bf16[360,128]{1,0:T(8,128)(2,1)S(1)}, u32[]{:S(2)}, u32[]{:S(2)}) collective-permute-start(bf16[360,128]{1,0:T(8,128)(2,1)S(1)} %collective-permute-done.18.refs_0_.refs_2_), channel_id=1, source_target_pairs={{0,1},{1,0},{2,3},{3,2},{4,5},{5,4},{6,7},{7,6},{8,9},{9,8},{10,11... | collective-permute-start | bytes 276488 | tf_op jit(solution)/shard_map/ppermute | solution.py:25
  42.6 2.8 %collective-permute-start.10 = (bf16[360,128]{1,0:T(8,128)(2,1)S(1)}, bf16[360,128]{1,0:T(8,128)(2,1)S(1)}, u32[]{:S(2)}, u32[]{:S(2)}) collective-permute-start(bf16[360,128]{1,0:T(8,128)(2,1)S(1)} %collective-permute-done.9.refs_0_), channel_id=1, source_target_pairs={{0,1},{1,0},{2,3},{3,2},{4,5},{5,4},{6,7},{7,6},{8,9},{9,8},{10,11... | collective-permute-start | bytes 276488 | tf_op jit(solution)/shard_map/ppermute | solution.py:25
  44.6 0.8 %copy-start.4 = (bf16[160]{0:T(256)(128)(2,1)S(1)}, bf16[160]{0:T(256)(128)(2,1)}, u32[]{:S(2)}) copy-start(bf16[160]{0:T(256)(128)(2,1)} %refs_5_.6) | copy-start | bytes 964
  45.4 5.7 %copy-start.1 = (bf16[3,3,160,1280]{3,2,1,0:T(8,128)(2,1)S(1)}, bf16[3,3,160,1280]{3,2,1,0:T(8,128)(2,1)}, u32[]{:S(2)}) copy-start(bf16[3,3,160,1280]{3,2,1,0:T(8,128)(2,1)} %refs_3_.5) | copy-start | bytes 11059204
  46.1 5.0 %collective-permute-start.21 = (bf16[344,128]{1,0:T(8,128)(2,1)S(1)}, bf16[344,128]{1,0:T(8,128)(2,1)S(1)}, u32[]{:S(2)}, u32[]{:S(2)}) collective-permute-start(bf16[344,128]{1,0:T(8,128)(2,1)S(1)} %get-tuple-element.45.refs_0_), channel_id=1, source_target_pairs={{0,8},{8,0},{1,9},{9,1},{2,10},{10,2},{3,11},{11,3},{4,12},{12,4},... | collective-permute-start | bytes 264200 | tf_op jit(solution)/shard_map/ppermute | solution.py:25
  46.9 5.3 %collective-permute-start.23 = (bf16[344,128]{1,0:T(8,128)(2,1)S(1)}, bf16[344,128]{1,0:T(8,128)(2,1)S(1)}, u32[]{:S(2)}, u32[]{:S(2)}) collective-permute-start(bf16[344,128]{1,0:T(8,128)(2,1)S(1)} %get-tuple-element.45.refs_0_), channel_id=1, source_target_pairs={{0,1},{1,0},{2,3},{3,2},{4,5},{5,4},{6,7},{7,6},{8,9},{9,8},{10,11... | collective-permute-start | bytes 264200 | tf_op jit(solution)/shard_map/ppermute | solution.py:25
  51.1 2.3 %collective-permute-start.22 = (bf16[344,128]{1,0:T(8,128)(2,1)S(1)}, bf16[344,128]{1,0:T(8,128)(2,1)S(1)}, u32[]{:S(2)}, u32[]{:S(2)}) collective-permute-start(bf16[344,128]{1,0:T(8,128)(2,1)S(1)} %collective-permute-done.21.refs_0_), channel_id=1, source_target_pairs={{0,1},{1,0},{2,3},{3,2},{4,5},{5,4},{6,7},{7,6},{8,9},{9,8},{10,11... | collective-permute-start | bytes 264200 | tf_op jit(solution)/shard_map/ppermute | solution.py:25
  53.0 0.7 %copy-start.5 = (bf16[160]{0:T(256)(128)(2,1)S(1)}, bf16[160]{0:T(256)(128)(2,1)}, u32[]{:S(2)}) copy-start(bf16[160]{0:T(256)(128)(2,1)} %refs_5_.7) | copy-start | bytes 964
  54.2 4.5 %collective-permute-start.24 = (bf16[80,128]{1,0:T(8,128)(2,1)S(1)}, bf16[80,128]{1,0:T(8,128)(2,1)S(1)}, u32[]{:S(2)}, u32[]{:S(2)}) collective-permute-start(bf16[80,128]{1,0:T(8,128)(2,1)S(1)} %get-tuple-element.48), channel_id=1, source_target_pairs={{0,2},{2,0},{4,6},{6,4},{1,3},{3,1},{5,7},{7,5},{8,10},{10,8},{12,... | collective-permute-start | bytes 61448 | tf_op jit(solution)/shard_map/ppermute | solution.py:25
  54.3 4.9 %collective-permute-start.25 = (bf16[80,128]{1,0:T(8,128)(2,1)S(1)}, bf16[80,128]{1,0:T(8,128)(2,1)S(1)}, u32[]{:S(2)}, u32[]{:S(2)}) collective-permute-start(bf16[80,128]{1,0:T(8,128)(2,1)S(1)} %get-tuple-element.49), channel_id=1, source_target_pairs={{0,4},{2,6},{4,0},{6,2},{1,5},{3,7},{5,1},{7,3},{8,12},{10,14},{12... | collective-permute-start | bytes 61448 | tf_op jit(solution)/shard_map/ppermute | solution.py:25
  55.7 5.6 %collective-permute-start.26 = (bf16[80,128]{1,0:T(8,128)(2,1)S(1)}, bf16[80,128]{1,0:T(8,128)(2,1)S(1)}, u32[]{:S(2)}, u32[]{:S(2)}) collective-permute-start(bf16[80,128]{1,0:T(8,128)(2,1)S(1)} %get-tuple-element.50), channel_id=1, source_target_pairs={{0,6},{2,4},{4,2},{6,0},{1,7},{3,5},{5,3},{7,1},{8,14},{10,12},{12... | collective-permute-start | bytes 61448 | tf_op jit(solution)/shard_map/ppermute | solution.py:25

commit v13 on v12

--- a/solution.py
+++ b/solution.py
@@ -381,7 +381,7 @@
 
 
 def rows_kernel(z, *refs):
-    blocks, (out_ref, image, block_image) = refs[:-3], refs[-3:]
+    blocks, (out_hbm, image, block_image, out_ref, sems) = refs[:-5], refs[-5:]
     band = lax.axis_index("band")
 
     def put(row, lane, piece):
@@ -395,8 +395,13 @@
             image[row, pl.ds(start, z.columns)] = block_image[
                 row * z.columns : (row + 1) * z.columns
             ]
+    copies = []
     for row in range(z.rows):
         out_ref[row] = image[row].T.astype(BF16)
+        copies.append(pltpu.make_async_copy(out_ref.at[row], out_hbm.at[row], sems.at[row]))
+        copies[-1].start()
+    for copy in copies:
+        copy.wait()
 
 
 def over_bands(blocks):
@@ -525,15 +530,20 @@
         late=(part,),
         extra=[pltpu.VMEM((groups, z.kept(LAYERS), LANES), F32)],
     )
-    out = call(
+    blocks = over_bands(blocks)
+    out = pl.pallas_call(
         kernel(rows_kernel),
-        sds(raw),
-        *over_bands(blocks),
-        scratch=[
+        out_shape=sds(raw),
+        in_specs=whole(z.bands),
+        out_specs=pl.BlockSpec(memory_space=pltpu.HBM),
+        scratch_shapes=[
             pltpu.VMEM((z.rows, z.width, z.per), F32),
             pltpu.VMEM((z.rows * z.columns, z.per), F32),
+            pltpu.VMEM(raw, BF16),
+            pltpu.SemaphoreType.DMA((z.rows,)),
         ],
-    )
+        compiler_params=pltpu.CompilerParams(vmem_limit_bytes=4 << 20),
+    )(*blocks)
     return out.swapaxes(1, 2)
 
 

time: 62.3 us -> 62.3 us (level)
    pallas_call x0 -> x1, Pallas kernels: none -> 0.86 us  [per_device(): pl.pallas_call(kernel(rows_kernel), out_shape=sds(raw), in_specs=whole(z....]
    pallas_call x22 -> x21, Pallas kernels: 15.3 us -> 14.5 us  [call(): pl.pallas_call(kernel, out_shape=outs, in_specs=whole(len(args)), out_spe...]
where the time goes in v13:
time: 62.3 us; the launch traced here: 62.2 us
  waiting for transfers between devices  23.4 us (38%)
  Pallas kernels  19.2 us (31%)
  starting transfers between devices  19.1 us (31%)
    ppermute x27, waiting for transfers between devices, exchange(): return lax.ppermute(cells, axis, [(i, i ^ distance) for i in range(count)])  23.4 us
    ppermute x27, starting transfers between devices, exchange(): return lax.ppermute(cells, axis, [(i, i ^ distance) for i in range(count)])  19.1 us
    pallas_call x21, Pallas kernels, call(): pl.pallas_call(kernel, out_shape=outs, in_specs=whole(len(args)), out_spe...  14.5 us
    pallas_call x1, Pallas kernels, load(): pl.pallas_call(functools.partial(load_kernel, count), out_shape=[sds(w.sh...  2.64 us
  transfers between devices with their start and end apart: 27, of which 11 were waited for; matrix products, arithmetic and copies ran while one was open for 0% of the time, Pallas kernels for 25%

profile of v13, /device:TPU:0, one launch (start us, length us, event | category | flops | bytes accessed | tf_op | source)
XLA Modules:
  0.0 62.2 jit_solution(12105773026728037291)
XLA Ops:
  0.0 1.2 %shard_map.136 = (bf16[200,128]{1,0:T(8,128)(2,1)S(1)}, bf16[200,128]{1,0:T(8,128)(2,1)S(1)}, bf16[200,128]{1,0:T(8,128)(2,1)S(1)}, bf16[200,128]{1,0:T(8,128)(2,1)S(1)}) custom-call(bf16[2,160,128]{2,1,0:T(8,128)(2,1)} %bitcast.3, bf16[2,160,128]{2,1,0:T(8,128)(2,1)} %bitcast.4), custom_call_target="tpu_custom_call" | custom-call | tf_op jit(solution)/shard_map/pallas_call | solution.py:451
  1.2 3.1 %collective-permute-start = (bf16[200,128]{1,0:T(8,128)(2,1)S(1)}, bf16[200,128]{1,0:T(8,128)(2,1)S(1)}, u32[]{:S(2)}, u32[]{:S(2)}) collective-permute-start(bf16[200,128]{1,0:T(8,128)(2,1)S(1)} %get-tuple-element.29), channel_id=1, source_target_pairs={{0,2},{2,0},{4,6},{6,4},{1,3},{3,1},{5,7},{7,5},{8,10},{10,8},{12,... | collective-permute-start | bytes 153608 | tf_op jit(solution)/shard_map/ppermute | solution.py:25
  4.3 2.6 %collective-permute-start.1 = (bf16[200,128]{1,0:T(8,128)(2,1)S(1)}, bf16[200,128]{1,0:T(8,128)(2,1)S(1)}, u32[]{:S(2)}, u32[]{:S(2)}) collective-permute-start(bf16[200,128]{1,0:T(8,128)(2,1)S(1)} %get-tuple-element.30), channel_id=1, source_target_pairs={{0,4},{2,6},{4,0},{6,2},{1,5},{3,7},{5,1},{7,3},{8,12},{10,14},{12... | collective-permute-start | bytes 153608 | tf_op jit(solution)/shard_map/ppermute | solution.py:25
  6.9 3.4 %collective-permute-done.1.refs_2_ = bf16[200,128]{1,0:T(8,128)(2,1)S(1)} collective-permute-done((bf16[200,128]{1,0:T(8,128)(2,1)S(1)}, bf16[200,128]{1,0:T(8,128)(2,1)S(1)}, u32[]{:S(2)}, u32[]{:S(2)}) %collective-permute-start.1) | collective-permute-done | bytes 51232 | tf_op jit(solution)/shard_map/ppermute | solution.py:25
  10.3 2.5 %collective-permute-done.2.refs_3_ = bf16[200,128]{1,0:T(8,128)(2,1)S(1)} collective-permute-done((bf16[200,128]{1,0:T(8,128)(2,1)S(1)}, bf16[200,128]{1,0:T(8,128)(2,1)S(1)}, u32[]{:S(2)}, u32[]{:S(2)}) %collective-permute-start.2) | collective-permute-done | bytes 51232 | tf_op jit(solution)/shard_map/ppermute | solution.py:25
  13.2 1.5 %collective-permute-start.12 = (bf16[400,128]{1,0:T(8,128)(2,1)S(1)}, bf16[400,128]{1,0:T(8,128)(2,1)S(1)}, u32[]{:S(2)}, u32[]{:S(2)}) collective-permute-start(bf16[400,128]{1,0:T(8,128)(2,1)S(1)} %get-tuple-element.39.refs_0_), channel_id=1, source_target_pairs={{0,8},{8,0},{1,9},{9,1},{2,10},{10,2},{3,11},{11,3},{4,12},{12,4},... | collective-permute-start | bytes 307208 | tf_op jit(solution)/shard_map/ppermute | solution.py:25
  14.7 0.4 shard_map.137
  15.1 0.6 collective-permute-start.3
  15.6 0.5 collective-permute-start.5
  16.2 1.7 %collective-permute-done.12.refs_0_ = bf16[400,128]{1,0:T(8,128)(2,1)S(1)} collective-permute-done((bf16[400,128]{1,0:T(8,128)(2,1)S(1)}, bf16[400,128]{1,0:T(8,128)(2,1)S(1)}, u32[]{:S(2)}, u32[]{:S(2)}) %collective-permute-start.12) | collective-permute-done | bytes 102432 | tf_op jit(solution)/shard_map/ppermute | solution.py:25
  17.9 1.9 %collective-permute-done.3.refs_0_ = bf16[400,128]{1,0:T(8,128)(2,1)S(1)} collective-permute-done((bf16[400,128]{1,0:T(8,128)(2,1)S(1)}, bf16[400,128]{1,0:T(8,128)(2,1)S(1)}, u32[]{:S(2)}, u32[]{:S(2)}) %collective-permute-start.3) | collective-permute-done | bytes 102432 | tf_op jit(solution)/shard_map/ppermute | solution.py:25
  19.8 2.6 %shard_map.138 = (bf16[3,3,160,640]{3,2,1,0:T(8,128)(2,1)S(1)}, bf16[3,3,160,640]{3,2,1,0:T(8,128)(2,1)S(1)}, bf16[3,3,160,640]{3,2,1,0:T(8,128)(2,1)S(1)}) custom-call(bf16[3,3,160,640]{3,2,1,0:T(8,128)(2,1)} %refs_0_.1, bf16[3,3,160,640]{3,2,1,0:T(8,128)(2,1)} %refs_1_.1, bf16[3,3,160,640]{3,2,1,0:T(8,128)(2,1)} %refs_2_.9), custom_call_target="tpu_custom_call" | custom-call | bytes 5529600 | tf_op jit(solution)/shard_map/pallas_call | solution.py:192
  22.4 0.8 %shard_map.146.refs_1_ = f32[304,160]{1,0:T(8,128)S(1)} custom-call(bf16[400,128]{1,0:T(8,128)(2,1)S(1)} %get-tuple-element.39.refs_0_, bf16[400,128]{1,0:T(8,128)(2,1)S(1)} %collective-permute-done.14.refs_1_, bf16[3,3,160,640]{3,2,1,0:T(8,128)(2,1)S(1)} %get-tuple-element.40.refs_2_), custom_call_target="tpu_custom_call" | custom-call | flops 294912000 | bytes 2242560 | tf_op jit(solution)/shard_map/pallas_call | solution.py:44
  23.2 0.5 shard_map.147.refs_1_
  23.8 0.8 %shard_map.139.refs_2_ = f32[304,160]{1,0:T(8,128)S(1)} custom-call(bf16[400,128]{1,0:T(8,128)(2,1)S(1)} %get-tuple-element.32.refs_0_, bf16[400,128]{1,0:T(8,128)(2,1)S(1)} %collective-permute-done.5.refs_1_, bf16[3,3,160,640]{3,2,1,0:T(8,128)(2,1)S(1)} %get-tuple-element.33.refs_2_.refs_3_), custom_call_target="tpu_custom_call" | custom-call | flops 294912000 | bytes 2242560 | tf_op jit(solution)/shard_map/pallas_call | solution.py:44
  24.6 0.7 %shard_map.148 = (bf16[304,160]{1,0:T(8,128)(2,1)S(1)}, bf16[384,128]{1,0:T(8,128)(2,1)S(1)}) custom-call(bf16[400,128]{1,0:T(8,128)(2,1)S(1)} %collective-permute-done.13.refs_0_, f32[304,160]{1,0:T(8,128)S(1)} %shard_map.147.refs_1_, bf16[3,3,160,640]{3,2,1,0:T(8,128)(2,1)S(1)} %get-tuple-element.40.refs_2_, ...), custom_call_target="tpu_custom_call" | custom-call | flops 147456000 | bytes 2438464 | tf_op jit(solution)/shard_map/pallas_call | solution.py:44
  25.3 0.8 %collective-permute-start.15 = (bf16[384,128]{1,0:T(8,128)(2,1)S(1)}, bf16[384,128]{1,0:T(8,128)(2,1)S(1)}, u32[]{:S(2)}, u32[]{:S(2)}) collective-permute-start(bf16[384,128]{1,0:T(8,128)(2,1)S(1)} %get-tuple-element.42.refs_0_), channel_id=1, source_target_pairs={{0,8},{8,0},{1,9},{9,1},{2,10},{10,2},{3,11},{11,3},{4,12},{12,4},... | collective-permute-start | bytes 294920 | tf_op jit(solution)/shard_map/ppermute | solution.py:25
  26.1 1.0 %shard_map.140 = (bf16[304,160]{1,0:T(8,128)(2,1)S(1)}, bf16[384,128]{1,0:T(8,128)(2,1)S(1)}) custom-call(bf16[400,128]{1,0:T(8,128)(2,1)S(1)} %collective-permute-done.3.refs_0_, bf16[400,128]{1,0:T(8,128)(2,1)S(1)} %collective-permute-done.4.refs_1_, f32[304,160]{1,0:T(8,128)S(1)} %shard_map.139.refs_2_, ...), custom_call_target="tpu_custom_call" | custom-call | flops 294912000 | bytes 2540864 | tf_op jit(solution)/shard_map/pallas_call | solution.py:44
  27.1 1.4 %collective-permute-start.6 = (bf16[384,128]{1,0:T(8,128)(2,1)S(1)}, bf16[384,128]{1,0:T(8,128)(2,1)S(1)}, u32[]{:S(2)}, u32[]{:S(2)}) collective-permute-start(bf16[384,128]{1,0:T(8,128)(2,1)S(1)} %get-tuple-element.35.refs_0_), channel_id=1, source_target_pairs={{0,8},{8,0},{1,9},{9,1},{2,10},{10,2},{3,11},{11,3},{4,12},{12,4},... | collective-permute-start | bytes 294920 | tf_op jit(solution)/shard_map/ppermute | solution.py:25
  28.4 0.5 collective-permute-start.8
  29.0 2.1 %collective-permute-done.15.refs_0_ = bf16[384,128]{1,0:T(8,128)(2,1)S(1)} collective-permute-done((bf16[384,128]{1,0:T(8,128)(2,1)S(1)}, bf16[384,128]{1,0:T(8,128)(2,1)S(1)}, u32[]{:S(2)}, u32[]{:S(2)}) %collective-permute-start.15) | collective-permute-done | bytes 98336 | tf_op jit(solution)/shard_map/ppermute | solution.py:25
  31.0 1.6 %collective-permute-done.6.refs_0_ = bf16[384,128]{1,0:T(8,128)(2,1)S(1)} collective-permute-done((bf16[384,128]{1,0:T(8,128)(2,1)S(1)}, bf16[384,128]{1,0:T(8,128)(2,1)S(1)}, u32[]{:S(2)}, u32[]{:S(2)}) %collective-permute-start.6) | collective-permute-done | bytes 98336 | tf_op jit(solution)/shard_map/ppermute | solution.py:25
  32.7 0.7 %shard_map.149.refs_1_ = f32[288,160]{1,0:T(8,128)S(1)} custom-call(bf16[384,128]{1,0:T(8,128)(2,1)S(1)} %get-tuple-element.42.refs_0_, bf16[384,128]{1,0:T(8,128)(2,1)S(1)} %collective-permute-done.17.refs_1_, bf16[3,3,160,640]{3,2,1,0:T(8,128)(2,1)S(1)} %copy-done.2), custom_call_target="tpu_custom_call" | custom-call | flops 294912000 | bytes 2224128 | tf_op jit(solution)/shard_map/pallas_call | solution.py:44
  33.5 0.5 shard_map.150.refs_1_
  34.0 0.7 %shard_map.141.refs_2_ = f32[288,160]{1,0:T(8,128)S(1)} custom-call(bf16[384,128]{1,0:T(8,128)(2,1)S(1)} %get-tuple-element.35.refs_0_, bf16[384,128]{1,0:T(8,128)(2,1)S(1)} %collective-permute-done.8.refs_1_, bf16[3,3,160,640]{3,2,1,0:T(8,128)(2,1)S(1)} %get-tuple-element.36.refs_2_.refs_3_), custom_call_target="tpu_custom_call" | custom-call | flops 294912000 | bytes 2224128 | tf_op jit(solution)/shard_map/pallas_call | solution.py:44
  34.8 0.7 %shard_map.151.refs_0_ = bf16[360,128]{1,0:T(8,128)(2,1)S(1)} custom-call(bf16[384,128]{1,0:T(8,128)(2,1)S(1)} %collective-permute-done.16.refs_0_, f32[288,160]{1,0:T(8,128)S(1)} %shard_map.150.refs_1_, bf16[3,3,160,640]{3,2,1,0:T(8,128)(2,1)S(1)} %copy-done.2, bf16[304,160]{1,0:T(8,128)(2,1)S(1)} %get-tuple-element.43.refs_3_, bf16[160]{0:T(256)(128)(2,1)S(1)} %copy-done.3), custom_call_target="tpu_custom_call" | custom-call | flops 147456000 | bytes 2315584 | tf_op jit(solution)/shard_map/pallas_call | solution.py:44
  35.5 0.8 %collective-permute-start.18 = (bf16[360,128]{1,0:T(8,128)(2,1)S(1)}, bf16[360,128]{1,0:T(8,128)(2,1)S(1)}, u32[]{:S(2)}, u32[]{:S(2)}) collective-permute-start(bf16[360,128]{1,0:T(8,128)(2,1)S(1)} %shard_map.151.refs_0_), channel_id=1, source_target_pairs={{0,8},{8,0},{1,9},{9,1},{2,10},{10,2},{3,11},{11,3},{4,12},{12,4},... | collective-permute-start | bytes 276488 | tf_op jit(solution)/shard_map/ppermute | solution.py:25
  36.3 1.0 %shard_map.142 = (bf16[288,160]{1,0:T(8,128)(2,1)S(1)}, bf16[360,128]{1,0:T(8,128)(2,1)S(1)}) custom-call(bf16[384,128]{1,0:T(8,128)(2,1)S(1)} %collective-permute-done.6.refs_0_, bf16[384,128]{1,0:T(8,128)(2,1)S(1)} %collective-permute-done.7.refs_1_, f32[288,160]{1,0:T(8,128)S(1)} %shard_map.141.refs_2_, ...), custom_call_target="tpu_custom_call" | custom-call | flops 294912000 | bytes 2506048 | tf_op jit(solution)/shard_map/pallas_call | solution.py:44
  37.3 1.3 %collective-permute-start.9 = (bf16[360,128]{1,0:T(8,128)(2,1)S(1)}, bf16[360,128]{1,0:T(8,128)(2,1)S(1)}, u32[]{:S(2)}, u32[]{:S(2)}) collective-permute-start(bf16[360,128]{1,0:T(8,128)(2,1)S(1)} %get-tuple-element.38.refs_0_), channel_id=1, source_target_pairs={{0,8},{8,0},{1,9},{9,1},{2,10},{10,2},{3,11},{11,3},{4,12},{12,4},... | collective-permute-start | bytes 276488 | tf_op jit(solution)/shard_map/ppermute | solution.py:25
  38.6 0.5 collective-permute-start.20
  39.1 2.0 %collective-permute-done.18.refs_0_.refs_2_ = bf16[360,128]{1,0:T(8,128)(2,1)S(1)} collective-permute-done((bf16[360,128]{1,0:T(8,128)(2,1)S(1)}, bf16[360,128]{1,0:T(8,128)(2,1)S(1)}, u32[]{:S(2)}, u32[]{:S(2)}) %collective-permute-start.18) | collective-permute-done | bytes 92192 | tf_op jit(solution)/shard_map/ppermute | solution.py:25
  41.1 1.5 %collective-permute-done.9.refs_0_ = bf16[360,128]{1,0:T(8,128)(2,1)S(1)} collective-permute-done((bf16[360,128]{1,0:T(8,128)(2,1)S(1)}, bf16[360,128]{1,0:T(8,128)(2,1)S(1)}, u32[]{:S(2)}, u32[]{:S(2)}) %collective-permute-start.9) | collective-permute-done | bytes 92192 | tf_op jit(solution)/shard_map/ppermute | solution.py:25
  42.6 0.7 %shard_map.143.refs_1_ = f32[272,160]{1,0:T(8,128)S(1)} custom-call(bf16[360,128]{1,0:T(8,128)(2,1)S(1)} %get-tuple-element.38.refs_0_, bf16[360,128]{1,0:T(8,128)(2,1)S(1)} %collective-permute-done.11.refs_1_, bf16[3,3,160,1280]{3,2,1,0:T(8,128)(2,1)S(1)} %copy-done), custom_call_target="tpu_custom_call" | custom-call | flops 294912000 | bytes 4044800 | tf_op jit(solution)/shard_map/pallas_call | solution.py:44
  43.4 0.5 shard_map.144.refs_1_
  43.9 0.7 %shard_map.152.refs_2_ = f32[272,160]{1,0:T(8,128)S(1)} custom-call(bf16[360,128]{1,0:T(8,128)(2,1)S(1)} %shard_map.151.refs_0_, bf16[360,128]{1,0:T(8,128)(2,1)S(1)} %collective-permute-done.20.refs_1_, bf16[3,3,160,1280]{3,2,1,0:T(8,128)(2,1)S(1)} %copy-done), custom_call_target="tpu_custom_call" | custom-call | flops 294912000 | bytes 4044800 | tf_op jit(solution)/shard_map/pallas_call | solution.py:44
  44.7 0.7 %shard_map.153.refs_2_ = f32[272,160]{1,0:T(8,128)S(1)} custom-call(bf16[360,128]{1,0:T(8,128)(2,1)S(1)} %collective-permute-done.18.refs_0_.refs_2_, bf16[360,128]{1,0:T(8,128)(2,1)S(1)} %collective-permute-done.19.refs_1_.refs_3_, f32[272,160]{1,0:T(8,128)S(1)} %shard_map.152.refs_2_, bf16[3,3,160,1280]{3,2,1,0:T(8,128)(2,1)S(1)} %copy-done), custom_call_target="tpu_custom_call" | custom-call | flops 294912000 | bytes 4218880 | tf_op jit(solution)/shard_map/pallas_call | solution.py:44
  45.4 0.7 %shard_map.154 = (bf16[272,160]{1,0:T(8,128)(2,1)S(1)}, bf16[344,128]{1,0:T(8,128)(2,1)S(1)}) custom-call(bf16[360,128]{1,0:T(8,128)(2,1)S(1)} %collective-permute-done.10.refs_0_, f32[272,160]{1,0:T(8,128)S(1)} %shard_map.144.refs_1_, f32[272,160]{1,0:T(8,128)S(1)} %shard_map.153.refs_2_, bf16[3,3,160,1280]{3,2,1,0:T(8,128)(2,1)S(1)} %copy-done, ...), custom_call_target="tpu_custom_call" | custom-call | flops 147456000 | bytes 4394304 | tf_op jit(solution)/shard_map/pallas_call | solution.py:44
  46.1 0.8 %collective-permute-start.21 = (bf16[344,128]{1,0:T(8,128)(2,1)S(1)}, bf16[344,128]{1,0:T(8,128)(2,1)S(1)}, u32[]{:S(2)}, u32[]{:S(2)}) collective-permute-start(bf16[344,128]{1,0:T(8,128)(2,1)S(1)} %get-tuple-element.45.refs_0_), channel_id=1, source_target_pairs={{0,8},{8,0},{1,9},{9,1},{2,10},{10,2},{3,11},{11,3},{4,12},{12,4},... | collective-permute-start | bytes 264200 | tf_op jit(solution)/shard_map/ppermute | solution.py:25
  47.2 4.0 %collective-permute-done.21.refs_0_ = bf16[344,128]{1,0:T(8,128)(2,1)S(1)} collective-permute-done((bf16[344,128]{1,0:T(8,128)(2,1)S(1)}, bf16[344,128]{1,0:T(8,128)(2,1)S(1)}, u32[]{:S(2)}, u32[]{:S(2)}) %collective-permute-start.21) | collective-permute-done | bytes 88096 | tf_op jit(solution)/shard_map/ppermute | solution.py:25
  51.1 1.1 %shard_map.157.refs_2_ = f32[256,160]{1,0:T(8,128)S(1)} custom-call(bf16[360,128]{1,0:T(8,128)(2,1)S(1)} %shard_map.151.refs_0_, bf16[360,128]{1,0:T(8,128)(2,1)S(1)} %collective-permute-done.20.refs_1_, bf16[360,128]{1,0:T(8,128)(2,1)S(1)} %collective-permute-done.18.refs_0_.refs_2_, bf16[360,128]{1,0:T(8,128)(2,1)S(1)} %collective-permute-done.19.refs_1_.refs_3_, ...), custom_call_target="tpu_custom_call" | custom-call | flops 589824000 | bytes 4218880 | tf_op jit(solution)/shard_map/pallas_call | solution.py:44
  52.3 0.7 %shard_map.155.refs_1_ = f32[256,160]{1,0:T(8,128)S(1)} custom-call(bf16[344,128]{1,0:T(8,128)(2,1)S(1)} %get-tuple-element.45.refs_0_, bf16[344,128]{1,0:T(8,128)(2,1)S(1)} %collective-permute-done.23.refs_1_, bf16[3,3,160,1280]{3,2,1,0:T(8,128)(2,1)S(1)} %copy-done.1), custom_call_target="tpu_custom_call" | custom-call | flops 294912000 | bytes 4026368 | tf_op jit(solution)/shard_map/pallas_call | solution.py:44
  53.0 0.5 shard_map.156.refs_1_
  53.6 0.6 shard_map.158
  54.3 1.4 %collective-permute-start.25 = (bf16[80,128]{1,0:T(8,128)(2,1)S(1)}, bf16[80,128]{1,0:T(8,128)(2,1)S(1)}, u32[]{:S(2)}, u32[]{:S(2)}) collective-permute-start(bf16[80,128]{1,0:T(8,128)(2,1)S(1)} %get-tuple-element.49), channel_id=1, source_target_pairs={{0,4},{2,6},{4,0},{6,2},{1,5},{3,7},{5,1},{7,3},{8,12},{10,14},{12... | collective-permute-start | bytes 61448 | tf_op jit(solution)/shard_map/ppermute | solution.py:25
  55.7 2.9 %collective-permute-start.26 = (bf16[80,128]{1,0:T(8,128)(2,1)S(1)}, bf16[80,128]{1,0:T(8,128)(2,1)S(1)}, u32[]{:S(2)}, u32[]{:S(2)}) collective-permute-start(bf16[80,128]{1,0:T(8,128)(2,1)S(1)} %get-tuple-element.50), channel_id=1, source_target_pairs={{0,6},{2,4},{4,2},{6,0},{1,7},{3,5},{5,3},{7,1},{8,14},{10,12},{12... | collective-permute-start | bytes 61448 | tf_op jit(solution)/shard_map/ppermute | solution.py:25
  58.7 0.6 collective-permute-done.25.refs_2_
  59.2 2.1 %collective-permute-done.26.refs_3_ = bf16[80,128]{1,0:T(8,128)(2,1)S(1)} collective-permute-done((bf16[80,128]{1,0:T(8,128)(2,1)S(1)}, bf16[80,128]{1,0:T(8,128)(2,1)S(1)}, u32[]{:S(2)}, u32[]{:S(2)}) %collective-permute-start.26) | collective-permute-done | bytes 20512 | tf_op jit(solution)/shard_map/ppermute | solution.py:25
  61.3 0.9 %shard_map.159 = bf16[2,160,128]{2,1,0:T(8,128)(2,1)} custom-call(bf16[80,128]{1,0:T(8,128)(2,1)S(1)} %get-tuple-element.47.refs_0_, bf16[80,128]{1,0:T(8,128)(2,1)S(1)} %collective-permute-done.24.refs_1_, bf16[80,128]{1,0:T(8,128)(2,1)S(1)} %collective-permute-done.25.refs_2_, bf16[80,128]{1,0:T(8,128)(2,1)S(1)} %collective-permute-done.26.refs_3_), custom_call_target="tpu_custom_call" | custom-call | tf_op jit(solution)/shard_map/pallas_call | solution.py:534
  (48 shorter events, 0.9 us)
Async XLA Ops:
  1.2 5.7 %collective-permute-start = (bf16[200,128]{1,0:T(8,128)(2,1)S(1)}, bf16[200,128]{1,0:T(8,128)(2,1)S(1)}, u32[]{:S(2)}, u32[]{:S(2)}) collective-permute-start(bf16[200,128]{1,0:T(8,128)(2,1)S(1)} %get-tuple-element.29), channel_id=1, source_target_pairs={{0,2},{2,0},{4,6},{6,4},{1,3},{3,1},{5,7},{7,5},{8,10},{10,8},{12,... | collective-permute-start | bytes 153608 | tf_op jit(solution)/shard_map/ppermute | solution.py:25
  4.3 6.0 %collective-permute-start.1 = (bf16[200,128]{1,0:T(8,128)(2,1)S(1)}, bf16[200,128]{1,0:T(8,128)(2,1)S(1)}, u32[]{:S(2)}, u32[]{:S(2)}) collective-permute-start(bf16[200,128]{1,0:T(8,128)(2,1)S(1)} %get-tuple-element.30), channel_id=1, source_target_pairs={{0,4},{2,6},{4,0},{6,2},{1,5},{3,7},{5,1},{7,3},{8,12},{10,14},{12... | collective-permute-start | bytes 153608 | tf_op jit(solution)/shard_map/ppermute | solution.py:25
  6.9 5.9 %collective-permute-start.2 = (bf16[200,128]{1,0:T(8,128)(2,1)S(1)}, bf16[200,128]{1,0:T(8,128)(2,1)S(1)}, u32[]{:S(2)}, u32[]{:S(2)}) collective-permute-start(bf16[200,128]{1,0:T(8,128)(2,1)S(1)} %get-tuple-element.31), channel_id=1, source_target_pairs={{0,6},{2,4},{4,2},{6,0},{1,7},{3,5},{5,3},{7,1},{8,14},{10,12},{12... | collective-permute-start | bytes 153608 | tf_op jit(solution)/shard_map/ppermute | solution.py:25
  13.2 4.7 %collective-permute-start.12 = (bf16[400,128]{1,0:T(8,128)(2,1)S(1)}, bf16[400,128]{1,0:T(8,128)(2,1)S(1)}, u32[]{:S(2)}, u32[]{:S(2)}) collective-permute-start(bf16[400,128]{1,0:T(8,128)(2,1)S(1)} %get-tuple-element.39.refs_0_), channel_id=1, source_target_pairs={{0,8},{8,0},{1,9},{9,1},{2,10},{10,2},{3,11},{11,3},{4,12},{12,4},... | collective-permute-start | bytes 307208 | tf_op jit(solution)/shard_map/ppermute | solution.py:25
  15.1 4.7 %collective-permute-start.3 = (bf16[400,128]{1,0:T(8,128)(2,1)S(1)}, bf16[400,128]{1,0:T(8,128)(2,1)S(1)}, u32[]{:S(2)}, u32[]{:S(2)}) collective-permute-start(bf16[400,128]{1,0:T(8,128)(2,1)S(1)} %get-tuple-element.32.refs_0_), channel_id=1, source_target_pairs={{0,8},{8,0},{1,9},{9,1},{2,10},{10,2},{3,11},{11,3},{4,12},{12,4},... | collective-permute-start | bytes 307208 | tf_op jit(solution)/shard_map/ppermute | solution.py:25
  15.6 6.8 %collective-permute-start.14 = (bf16[400,128]{1,0:T(8,128)(2,1)S(1)}, bf16[400,128]{1,0:T(8,128)(2,1)S(1)}, u32[]{:S(2)}, u32[]{:S(2)}) collective-permute-start(bf16[400,128]{1,0:T(8,128)(2,1)S(1)} %get-tuple-element.39.refs_0_), channel_id=1, source_target_pairs={{0,1},{1,0},{2,3},{3,2},{4,5},{5,4},{6,7},{7,6},{8,9},{9,8},{10,11... | collective-permute-start | bytes 307208 | tf_op jit(solution)/shard_map/ppermute | solution.py:25
  15.6 8.1 %collective-permute-start.5 = (bf16[400,128]{1,0:T(8,128)(2,1)S(1)}, bf16[400,128]{1,0:T(8,128)(2,1)S(1)}, u32[]{:S(2)}, u32[]{:S(2)}) collective-permute-start(bf16[400,128]{1,0:T(8,128)(2,1)S(1)} %get-tuple-element.32.refs_0_), channel_id=1, source_target_pairs={{0,1},{1,0},{2,3},{3,2},{4,5},{5,4},{6,7},{7,6},{8,9},{9,8},{10,11... | collective-permute-start | bytes 307208 | tf_op jit(solution)/shard_map/ppermute | solution.py:25
  17.9 6.7 %collective-permute-start.13 = (bf16[400,128]{1,0:T(8,128)(2,1)S(1)}, bf16[400,128]{1,0:T(8,128)(2,1)S(1)}, u32[]{:S(2)}, u32[]{:S(2)}) collective-permute-start(bf16[400,128]{1,0:T(8,128)(2,1)S(1)} %collective-permute-done.12.refs_0_), channel_id=1, source_target_pairs={{0,1},{1,0},{2,3},{3,2},{4,5},{5,4},{6,7},{7,6},{8,9},{9,8},{10,11... | collective-permute-start | bytes 307208 | tf_op jit(solution)/shard_map/ppermute | solution.py:25
  19.8 6.3 %collective-permute-start.4 = (bf16[400,128]{1,0:T(8,128)(2,1)S(1)}, bf16[400,128]{1,0:T(8,128)(2,1)S(1)}, u32[]{:S(2)}, u32[]{:S(2)}) collective-permute-start(bf16[400,128]{1,0:T(8,128)(2,1)S(1)} %collective-permute-done.3.refs_0_), channel_id=1, source_target_pairs={{0,1},{1,0},{2,3},{3,2},{4,5},{5,4},{6,7},{7,6},{8,9},{9,8},{10,11... | collective-permute-start | bytes 307208 | tf_op jit(solution)/shard_map/ppermute | solution.py:25
  23.2 1.4 %copy-start.6 = (bf16[160]{0:T(256)(128)(2,1)S(1)}, bf16[160]{0:T(256)(128)(2,1)}, u32[]{:S(2)}) copy-start(bf16[160]{0:T(256)(128)(2,1)} %refs_4_.3) | copy-start | bytes 964
  23.8 2.3 %copy-start.7 = (bf16[160]{0:T(256)(128)(2,1)S(1)}, bf16[160]{0:T(256)(128)(2,1)}, u32[]{:S(2)}) copy-start(bf16[160]{0:T(256)(128)(2,1)} %refs_5_.4) | copy-start | bytes 964
  25.3 7.4 %copy-start.2 = (bf16[3,3,160,640]{3,2,1,0:T(8,128)(2,1)S(1)}, bf16[3,3,160,640]{3,2,1,0:T(8,128)(2,1)}, u32[]{:S(2)}) copy-start(bf16[3,3,160,640]{3,2,1,0:T(8,128)(2,1)} %refs_2_.14) | copy-start | bytes 5529604
  25.3 5.7 %collective-permute-start.15 = (bf16[384,128]{1,0:T(8,128)(2,1)S(1)}, bf16[384,128]{1,0:T(8,128)(2,1)S(1)}, u32[]{:S(2)}, u32[]{:S(2)}) collective-permute-start(bf16[384,128]{1,0:T(8,128)(2,1)S(1)} %get-tuple-element.42.refs_0_), channel_id=1, source_target_pairs={{0,8},{8,0},{1,9},{9,1},{2,10},{10,2},{3,11},{11,3},{4,12},{12,4},... | collective-permute-start | bytes 294920 | tf_op jit(solution)/shard_map/ppermute | solution.py:25
  27.1 5.6 %collective-permute-start.6 = (bf16[384,128]{1,0:T(8,128)(2,1)S(1)}, bf16[384,128]{1,0:T(8,128)(2,1)S(1)}, u32[]{:S(2)}, u32[]{:S(2)}) collective-permute-start(bf16[384,128]{1,0:T(8,128)(2,1)S(1)} %get-tuple-element.35.refs_0_), channel_id=1, source_target_pairs={{0,8},{8,0},{1,9},{9,1},{2,10},{10,2},{3,11},{11,3},{4,12},{12,4},... | collective-permute-start | bytes 294920 | tf_op jit(solution)/shard_map/ppermute | solution.py:25
  28.4 4.3 %collective-permute-start.17 = (bf16[384,128]{1,0:T(8,128)(2,1)S(1)}, bf16[384,128]{1,0:T(8,128)(2,1)S(1)}, u32[]{:S(2)}, u32[]{:S(2)}) collective-permute-start(bf16[384,128]{1,0:T(8,128)(2,1)S(1)} %get-tuple-element.42.refs_0_), channel_id=1, source_target_pairs={{0,1},{1,0},{2,3},{3,2},{4,5},{5,4},{6,7},{7,6},{8,9},{9,8},{10,11... | collective-permute-start | bytes 294920 | tf_op jit(solution)/shard_map/ppermute | solution.py:25
  28.4 5.6 %collective-permute-start.8 = (bf16[384,128]{1,0:T(8,128)(2,1)S(1)}, bf16[384,128]{1,0:T(8,128)(2,1)S(1)}, u32[]{:S(2)}, u32[]{:S(2)}) collective-permute-start(bf16[384,128]{1,0:T(8,128)(2,1)S(1)} %get-tuple-element.35.refs_0_), channel_id=1, source_target_pairs={{0,1},{1,0},{2,3},{3,2},{4,5},{5,4},{6,7},{7,6},{8,9},{9,8},{10,11... | collective-permute-start | bytes 294920 | tf_op jit(solution)/shard_map/ppermute | solution.py:25
  31.0 3.7 %collective-permute-start.16 = (bf16[384,128]{1,0:T(8,128)(2,1)S(1)}, bf16[384,128]{1,0:T(8,128)(2,1)S(1)}, u32[]{:S(2)}, u32[]{:S(2)}) collective-permute-start(bf16[384,128]{1,0:T(8,128)(2,1)S(1)} %collective-permute-done.15.refs_0_), channel_id=1, source_target_pairs={{0,1},{1,0},{2,3},{3,2},{4,5},{5,4},{6,7},{7,6},{8,9},{9,8},{10,11... | collective-permute-start | bytes 294920 | tf_op jit(solution)/shard_map/ppermute | solution.py:25
  32.7 3.6 %collective-permute-start.7 = (bf16[384,128]{1,0:T(8,128)(2,1)S(1)}, bf16[384,128]{1,0:T(8,128)(2,1)S(1)}, u32[]{:S(2)}, u32[]{:S(2)}) collective-permute-start(bf16[384,128]{1,0:T(8,128)(2,1)S(1)} %collective-permute-done.6.refs_0_), channel_id=1, source_target_pairs={{0,1},{1,0},{2,3},{3,2},{4,5},{5,4},{6,7},{7,6},{8,9},{9,8},{10,11... | collective-permute-start | bytes 294920 | tf_op jit(solution)/shard_map/ppermute | solution.py:25
  33.5 1.3 %copy-start.3 = (bf16[160]{0:T(256)(128)(2,1)S(1)}, bf16[160]{0:T(256)(128)(2,1)}, u32[]{:S(2)}) copy-start(bf16[160]{0:T(256)(128)(2,1)} %refs_4_.4) | copy-start | bytes 964
  34.0 2.3 %copy-start.8 = (bf16[160]{0:T(256)(128)(2,1)S(1)}, bf16[160]{0:T(256)(128)(2,1)}, u32[]{:S(2)}) copy-start(bf16[160]{0:T(256)(128)(2,1)} %refs_5_.5) | copy-start | bytes 964
  34.8 7.8 %copy-start = (bf16[3,3,160,1280]{3,2,1,0:T(8,128)(2,1)S(1)}, bf16[3,3,160,1280]{3,2,1,0:T(8,128)(2,1)}, u32[]{:S(2)}) copy-start(bf16[3,3,160,1280]{3,2,1,0:T(8,128)(2,1)} %refs_3_.4) | copy-start | bytes 11059204
  35.5 5.6 %collective-permute-start.18 = (bf16[360,128]{1,0:T(8,128)(2,1)S(1)}, bf16[360,128]{1,0:T(8,128)(2,1)S(1)}, u32[]{:S(2)}, u32[]{:S(2)}) collective-permute-start(bf16[360,128]{1,0:T(8,128)(2,1)S(1)} %shard_map.151.refs_0_), channel_id=1, source_target_pairs={{0,8},{8,0},{1,9},{9,1},{2,10},{10,2},{3,11},{11,3},{4,12},{12,4},... | collective-permute-start | bytes 276488 | tf_op jit(solution)/shard_map/ppermute | solution.py:25
  37.3 5.4 %collective-permute-start.9 = (bf16[360,128]{1,0:T(8,128)(2,1)S(1)}, bf16[360,128]{1,0:T(8,128)(2,1)S(1)}, u32[]{:S(2)}, u32[]{:S(2)}) collective-permute-start(bf16[360,128]{1,0:T(8,128)(2,1)S(1)} %get-tuple-element.38.refs_0_), channel_id=1, source_target_pairs={{0,8},{8,0},{1,9},{9,1},{2,10},{10,2},{3,11},{11,3},{4,12},{12,4},... | collective-permute-start | bytes 276488 | tf_op jit(solution)/shard_map/ppermute | solution.py:25
  38.6 4.0 %collective-permute-start.11 = (bf16[360,128]{1,0:T(8,128)(2,1)S(1)}, bf16[360,128]{1,0:T(8,128)(2,1)S(1)}, u32[]{:S(2)}, u32[]{:S(2)}) collective-permute-start(bf16[360,128]{1,0:T(8,128)(2,1)S(1)} %get-tuple-element.38.refs_0_), channel_id=1, source_target_pairs={{0,1},{1,0},{2,3},{3,2},{4,5},{5,4},{6,7},{7,6},{8,9},{9,8},{10,11... | collective-permute-start | bytes 276488 | tf_op jit(solution)/shard_map/ppermute | solution.py:25
  38.6 5.3 %collective-permute-start.20 = (bf16[360,128]{1,0:T(8,128)(2,1)S(1)}, bf16[360,128]{1,0:T(8,128)(2,1)S(1)}, u32[]{:S(2)}, u32[]{:S(2)}) collective-permute-start(bf16[360,128]{1,0:T(8,128)(2,1)S(1)} %shard_map.151.refs_0_), channel_id=1, source_target_pairs={{0,1},{1,0},{2,3},{3,2},{4,5},{5,4},{6,7},{7,6},{8,9},{9,8},{10,11... | collective-permute-start | bytes 276488 | tf_op jit(solution)/shard_map/ppermute | solution.py:25
  41.1 3.5 %collective-permute-start.19 = (bf16[360,128]{1,0:T(8,128)(2,1)S(1)}, bf16[360,128]{1,0:T(8,128)(2,1)S(1)}, u32[]{:S(2)}, u32[]{:S(2)}) collective-permute-start(bf16[360,128]{1,0:T(8,128)(2,1)S(1)} %collective-permute-done.18.refs_0_.refs_2_), channel_id=1, source_target_pairs={{0,1},{1,0},{2,3},{3,2},{4,5},{5,4},{6,7},{7,6},{8,9},{9,8},{10,11... | collective-permute-start | bytes 276488 | tf_op jit(solution)/shard_map/ppermute | solution.py:25
  42.6 2.8 %collective-permute-start.10 = (bf16[360,128]{1,0:T(8,128)(2,1)S(1)}, bf16[360,128]{1,0:T(8,128)(2,1)S(1)}, u32[]{:S(2)}, u32[]{:S(2)}) collective-permute-start(bf16[360,128]{1,0:T(8,128)(2,1)S(1)} %collective-permute-done.9.refs_0_), channel_id=1, source_target_pairs={{0,1},{1,0},{2,3},{3,2},{4,5},{5,4},{6,7},{7,6},{8,9},{9,8},{10,11... | collective-permute-start | bytes 276488 | tf_op jit(solution)/shard_map/ppermute | solution.py:25
  44.6 0.8 %copy-start.4 = (bf16[160]{0:T(256)(128)(2,1)S(1)}, bf16[160]{0:T(256)(128)(2,1)}, u32[]{:S(2)}) copy-start(bf16[160]{0:T(256)(128)(2,1)} %refs_5_.6) | copy-start | bytes 964
  45.4 5.7 %copy-start.1 = (bf16[3,3,160,1280]{3,2,1,0:T(8,128)(2,1)S(1)}, bf16[3,3,160,1280]{3,2,1,0:T(8,128)(2,1)}, u32[]{:S(2)}) copy-start(bf16[3,3,160,1280]{3,2,1,0:T(8,128)(2,1)} %refs_3_.5) | copy-start | bytes 11059204
  46.1 5.0 %collective-permute-start.21 = (bf16[344,128]{1,0:T(8,128)(2,1)S(1)}, bf16[344,128]{1,0:T(8,128)(2,1)S(1)}, u32[]{:S(2)}, u32[]{:S(2)}) collective-permute-start(bf16[344,128]{1,0:T(8,128)(2,1)S(1)} %get-tuple-element.45.refs_0_), channel_id=1, source_target_pairs={{0,8},{8,0},{1,9},{9,1},{2,10},{10,2},{3,11},{11,3},{4,12},{12,4},... | collective-permute-start | bytes 264200 | tf_op jit(solution)/shard_map/ppermute | solution.py:25
  46.9 5.3 %collective-permute-start.23 = (bf16[344,128]{1,0:T(8,128)(2,1)S(1)}, bf16[344,128]{1,0:T(8,128)(2,1)S(1)}, u32[]{:S(2)}, u32[]{:S(2)}) collective-permute-start(bf16[344,128]{1,0:T(8,128)(2,1)S(1)} %get-tuple-element.45.refs_0_), channel_id=1, source_target_pairs={{0,1},{1,0},{2,3},{3,2},{4,5},{5,4},{6,7},{7,6},{8,9},{9,8},{10,11... | collective-permute-start | bytes 264200 | tf_op jit(solution)/shard_map/ppermute | solution.py:25
  51.1 2.3 %collective-permute-start.22 = (bf16[344,128]{1,0:T(8,128)(2,1)S(1)}, bf16[344,128]{1,0:T(8,128)(2,1)S(1)}, u32[]{:S(2)}, u32[]{:S(2)}) collective-permute-start(bf16[344,128]{1,0:T(8,128)(2,1)S(1)} %collective-permute-done.21.refs_0_), channel_id=1, source_target_pairs={{0,1},{1,0},{2,3},{3,2},{4,5},{5,4},{6,7},{7,6},{8,9},{9,8},{10,11... | collective-permute-start | bytes 264200 | tf_op jit(solution)/shard_map/ppermute | solution.py:25
  53.0 0.7 %copy-start.5 = (bf16[160]{0:T(256)(128)(2,1)S(1)}, bf16[160]{0:T(256)(128)(2,1)}, u32[]{:S(2)}) copy-start(bf16[160]{0:T(256)(128)(2,1)} %refs_5_.7) | copy-start | bytes 964
  54.2 4.5 %collective-permute-start.24 = (bf16[80,128]{1,0:T(8,128)(2,1)S(1)}, bf16[80,128]{1,0:T(8,128)(2,1)S(1)}, u32[]{:S(2)}, u32[]{:S(2)}) collective-permute-start(bf16[80,128]{1,0:T(8,128)(2,1)S(1)} %get-tuple-element.48), channel_id=1, source_target_pairs={{0,2},{2,0},{4,6},{6,4},{1,3},{3,1},{5,7},{7,5},{8,10},{10,8},{12,... | collective-permute-start | bytes 61448 | tf_op jit(solution)/shard_map/ppermute | solution.py:25
  54.3 4.9 %collective-permute-start.25 = (bf16[80,128]{1,0:T(8,128)(2,1)S(1)}, bf16[80,128]{1,0:T(8,128)(2,1)S(1)}, u32[]{:S(2)}, u32[]{:S(2)}) collective-permute-start(bf16[80,128]{1,0:T(8,128)(2,1)S(1)} %get-tuple-element.49), channel_id=1, source_target_pairs={{0,4},{2,6},{4,0},{6,2},{1,5},{3,7},{5,1},{7,3},{8,12},{10,14},{12... | collective-permute-start | bytes 61448 | tf_op jit(solution)/shard_map/ppermute | solution.py:25
  55.7 5.6 %collective-permute-start.26 = (bf16[80,128]{1,0:T(8,128)(2,1)S(1)}, bf16[80,128]{1,0:T(8,128)(2,1)S(1)}, u32[]{:S(2)}, u32[]{:S(2)}) collective-permute-start(bf16[80,128]{1,0:T(8,128)(2,1)S(1)} %get-tuple-element.50), channel_id=1, source_target_pairs={{0,6},{2,4},{4,2},{6,0},{1,7},{3,5},{5,3},{7,1},{8,14},{10,12},{12... | collective-permute-start | bytes 61448 | tf_op jit(solution)/shard_map/ppermute | solution.py:25
